TPU v7x, 512 devices: a whole 4x4x16 slice. The times are simulated.
512 devices in a mesh: page: 16 (over z_lo, core), tensor: 32 (over x, y, z_hi).
Axes of the slice: x: 4, y: 4, z: 16 (z_hi: 2, z_lo: 8; z = z_hi * 8 + z_lo), core: 2. Of those that a mesh axis runs over, the one named last changes fastest.
Arguments:
- tokens: bfloat16 [2048, 2560], P('tensor'), may hold values from -6 to 6
- norm_gain: float32 [2560], replicated, may hold values from 0.1 to 1.9
- w_query: bfloat16 [2560, 2560], P(None, 'tensor'), may hold values from -0.125 to 0.125
- w_keyvalue: bfloat16 [2560, 1280], P(None, 'tensor'), may hold values from -0.125 to 0.125
- cache: bfloat16 [128, 32, 128, 1280], P('page', 'tensor'), may hold values from -180 to 180, as said below
- page_count: int32 [16, 32], P('page', 'tensor'), may hold values from 1 to 8, as said below
- page_owner: int32 [128, 32], P('page', 'tensor'), may hold values from 0 to 63
- keep_rows: int32 [128, 32, 32], P('page', 'tensor'), may hold values from 0 to 127, as said below
- dest_slot: int32 [128, 32], P('page', 'tensor'), may hold values from 0 to 15, as said below
Outputs:
- attended: bfloat16 [2048, 2560], P('tensor')
- compacted: bfloat16 [256, 32, 32, 1280], P('page', 'tensor')
Inputs may be any that keep to these rules, and one draw needn't show every extreme that they name: `cache`: normal values within 4.5; keys may carry a row scale. `page_count`: in every tensor index some holder has all 8 slots live. `keep_rows`: distinct within each page. `dest_slot`: value q * 1 + c names position c of holder q (with 1 = 1, c = 0); the live slots of one holder and tensor index name distinct destinations, and every holder's first slot of a tensor index goes to position 0 of one common holder of that index.
All inputs are finite; a program needn't handle non-finite values.
Results may differ from a plain program's by a relative error of at most 0.012.
Values may be sent and summed in bfloat16 or wider, within the bound.
No kernel may reach another device: no remote copies, remote signals or barrier semaphores. Data moves between devices by JAX's collectives and lax.ppermute only.
A program may use at most 64 MiB of HBM per device.

v0:
```python
import jax
import jax.numpy as jnp
from jax import lax
from jax.sharding import PartitionSpec as P

HEADS = 32
KV_HEADS = 8
HEAD_DIM = 80


EPSILON = 1e-05
NEGATIVE = -1e30


def per_device(
    tokens, norm_gain, w_query, w_keyvalue, cache, page_count, page_owner, keep_rows, dest_slot
):
    holders = lax.axis_size("page")
    groups = lax.axis_size("tensor")
    rows_here = tokens.shape[0]
    sources = cache.shape[0]
    keep_count = keep_rows.shape[2]
    row_width = cache.shape[3]
    capacity = (sources + holders - 1) // holders
    targets = capacity * holders
    repeat_count = HEADS // KV_HEADS
    score_scale = HEAD_DIM ** (-0.5)
    widened = tokens.astype(jnp.float32)
    normed = (
        widened
        * lax.rsqrt(jnp.mean(widened * widened, axis=-1, keepdims=True) + EPSILON)
        * norm_gain
    ).astype(jnp.bfloat16)
    portion = lax.all_gather(normed, "tensor", axis=0, tiled=True)
    query_part = jnp.dot(portion, w_query, preferred_element_type=jnp.float32)
    pair_part = jnp.dot(portion, w_keyvalue, preferred_element_type=jnp.float32)
    projected = jnp.concatenate([query_part, pair_part], axis=1).astype(jnp.bfloat16)
    local_heads = lax.all_to_all(
        projected, "tensor", split_axis=0, concat_axis=1, tiled=True
    ).reshape(rows_here, groups, -1)
    query_cols = w_query.shape[1]
    queries = local_heads[:, :, :query_cols].reshape(rows_here, KV_HEADS, repeat_count, HEAD_DIM)
    fresh_kv = local_heads[:, :, query_cols:].reshape(rows_here, 2, KV_HEADS, HEAD_DIM)
    new_keys = fresh_kv[:, 0]
    new_values = fresh_kv[:, 1]
    retained = jax.vmap(lambda one_page, row_picks: one_page[row_picks])(
        cache[:, 0], keep_rows[:, 0]
    )
    is_live = jnp.arange(sources) < page_count[0, 0]
    owners = page_owner[:, 0]
    chosen = (dest_slot[:, 0][None, :] == jnp.arange(targets)[:, None]) & is_live[None, :]
    outgoing = jnp.einsum(
        "ts,sjc->tjc", chosen.astype(jnp.bfloat16), retained, preferred_element_type=jnp.float32
    ).astype(jnp.bfloat16)
    out_tags = jnp.sum(jnp.where(chosen, owners[None, :] + 1, 0), axis=1) - 1
    arrived, arrived_tags = (
        lax.all_to_all(
            outgoing.reshape(holders, capacity, keep_count, row_width),
            "page",
            split_axis=0,
            concat_axis=0,
            tiled=True,
        ),
        lax.all_to_all(
            out_tags.reshape(holders, capacity), "page", split_axis=0, concat_axis=0, tiled=True
        ),
    )
    arrived = arrived.reshape(targets, keep_count, row_width)
    arrived_tags = arrived_tags.reshape(targets)
    slot_count = arrived.shape[0]
    active = arrived_tags >= 0
    owner_idx = jnp.maximum(arrived_tags, 0)
    picked = jnp.take(queries, owner_idx, axis=0)
    slot_keys = arrived[:, :, : KV_HEADS * HEAD_DIM].reshape(
        slot_count, keep_count, KV_HEADS, HEAD_DIM
    )
    slot_values = arrived[:, :, KV_HEADS * HEAD_DIM :].reshape(
        slot_count, keep_count, KV_HEADS, HEAD_DIM
    )
    scores = (
        jnp.einsum("sgkd,sjgd->sgkj", picked, slot_keys, preferred_element_type=jnp.float32)
        * score_scale
    )
    member = (owner_idx[None, :] == jnp.arange(rows_here)[:, None]) & active[None, :]
    slot_peak = jnp.max(scores, axis=3)
    local_peak = jnp.max(jnp.where(member[:, :, None, None], slot_peak[None], NEGATIVE), axis=1)
    own_score = (
        jnp.einsum("rgkd,rgd->rgk", queries, new_keys, preferred_element_type=jnp.float32)
        * score_scale
    )
    row_peak = jnp.maximum(lax.pmax(local_peak, "page"), own_score)
    shifted = scores - jnp.take(row_peak, owner_idx, axis=0)[..., None]
    weights = jnp.where(active[:, None, None, None], jnp.exp(shifted), 0.0)
    slot_total = jnp.sum(weights, axis=3)
    slot_out = jnp.einsum(
        "sgkj,sjgd->sgkd",
        weights.astype(jnp.bfloat16),
        slot_values,
        preferred_element_type=jnp.float32,
    )
    member_weight = member.astype(jnp.float32)
    part_total = jnp.einsum(
        "rs,sgk->rgk", member_weight, slot_total, precision=lax.Precision.HIGHEST
    )
    part_out = jnp.einsum("rs,sgkd->rgkd", member_weight, slot_out, precision=lax.Precision.HIGHEST)
    sum_out, sum_total = lax.psum((part_out, part_total), "page")
    own_weight = jnp.exp(own_score - row_peak)
    mixed = sum_out + own_weight[..., None] * new_values[:, :, None, :].astype(jnp.float32)
    result = mixed / (sum_total + own_weight)[..., None]
    return (result.reshape(rows_here, HEADS * HEAD_DIM).astype(jnp.bfloat16), arrived[:, None])


def solution(mesh):
    return jax.shard_map(
        per_device,
        mesh=mesh,
        in_specs=(
            P("tensor", None),
            P(),
            P(None, "tensor"),
            P(None, "tensor"),
            P("page", "tensor", None, None),
            P("page", "tensor"),
            P("page", "tensor"),
            P("page", "tensor", None),
            P("page", "tensor"),
        ),
        out_specs=(P("tensor", None), P("page", "tensor", None, None)),
        check_vma=False,
    )
```

profile of v0, /device:TPU:1, one launch (start us, length us, event | category | flops | bytes accessed | tf_op | source)
XLA Modules:
  0.0 712.3 jit_solution(6468544499792493670)
XLA Ops:
  8.5 1.9 fusion.6
  13.1 14.0 %all-to-all-start = ((s32[16,1,1]{2,1,0:T(1,128)}), s32[16,1,1]{2,1,0:T(1,128)S(1)}, u32[]{:S(2)}, u32[]{:S(2)}) async-start(s32[16,1,1]{2,1,0:T(1,128)} %copy.97), calls=%async_computation | async-start | bytes 16384 | tf_op jit(solution)/shard_map/all_to_all | solution.py:64
  28.0 3.2 gather_fusion.2
  33.3 3.6 all-to-all-done
  36.9 6.4 all-to-all-start.2
  43.2 295.3 %all-gather.2.cloned.1.call-done = bf16[2048,2560]{1,0:T(8,128)(2,1)} async-done(((bf16[64,2560]{1,0:T(8,128)(2,1)}), bf16[2048,2560]{1,0:T(8,128)(2,1)}) %all-gather.2.cloned.1.call-update) | async-done | bytes 10485776 | tf_op jit(solution)/shard_map/all_gather | solution.py:34
  338.6 7.1 convolution_convert_fusion.2
  346.8 8.0 %convolution_convert_fusion.1 = bf16[2048,80]{0,1:T(8,128)(2,1)} fusion(bf16[2048,2560]{1,0:T(8,128)(2,1)} %all-gather.2.cloned.1.call-done, bf16[2560,80]{0,1:T(8,128)(2,1)S(1)} %copy-done.1), kind=kOutput, calls=%fused_computation.5 | convolution fusion | flops 839024640 | bytes 11223040 | tf_op jit(solution)/shard_map/dot_general | solution.py:35
  356.3 2.1 pad_maximum_fusion
  358.5 2.9 copy.98
  361.4 5.3 all-to-all-start.1
  367.8 2.5 fusion.36
  370.3 3.0 reshape.186
  373.3 3.0 reshape.188
  376.2 10.4 %all-to-all-done.1 = bf16[32,64,120]{2,1,0:T(8,128)(2,1)S(1)} async-done(((bf16[32,64,120]{2,1,0:T(8,128)(2,1)}), bf16[32,64,120]{2,1,0:T(8,128)(2,1)S(1)}, u32[]{:S(2)}, u32[]{:S(2)}) %all-to-all-start.1) | async-done | bytes 491552 | tf_op jit(solution)/shard_map/all_to_all | solution.py:38
  388.8 2.0 copy.105
  392.5 1.8 copy.123
  394.4 2.3 gather_fusion
  397.6 3.2 fusion.37
  402.0 95.7 %pmax.7 = f32[64,8,4]{0,1,2:T(8,128)S(1)} all-reduce(f32[64,8,4]{0,1,2:T(8,128)S(1)} %select_reduce_fusion), channel_id=1, replica_groups=mesh['page'=16,'tensor'=32] {'page'}, use_global_device_ids=true, to_apply=%region_4.5 | all-reduce | flops 2048 | bytes 16384 | tf_op jit(solution)/shard_map/pmax | solution.py:91
  501.8 2.3 fusion.8
  506.4 89.3 %psum.15 = f32[64,8,4]{0,1,2:T(8,128)S(1)} all-reduce(f32[64,8,4]{0,1,2:T(8,128)S(1)} %fusion.22), channel_id=1, replica_groups=mesh['page'=16,'tensor'=32] {'page'}, use_global_device_ids=true, to_apply=%region_7.8 | all-reduce | flops 2048 | bytes 16384 | tf_op jit(solution)/shard_map/psum | solution.py:106
  596.4 102.9 %all-reduce.2.cloned.1.call-done = f32[64,8,4,80]{3,0,2,1:T(8,128)} async-done(((f32[64,8,4,80]{3,0,2,1:T(8,128)}), f32[64,8,4,80]{3,0,2,1:T(8,128)}) %all-reduce.2.cloned.1.call-update) | async-done | bytes 655376 | tf_op jit(solution)/shard_map/psum | solution.py:106
  703.0 2.5 copy.150
  (62 shorter events, 26.8 us)
Async XLA Ops:
  7.2 20.8 %copy-start = (bf16[8,1,128,1280]{3,2,1,0:T(8,128)(2,1)S(1)}, bf16[8,1,128,1280]{3,2,1,0:T(8,128)(2,1)}, u32[]{:S(2)}) copy-start(bf16[8,1,128,1280]{3,2,1,0:T(8,128)(2,1)} %param.13) | copy-start | bytes 7864324
  7.2 331.4 %all-gather.2.cloned.1.call-start = ((), (), s32[]{:S(2)}) async-start(), calls=%async_computation.3 | async-start | bytes 10813440 | tf_op jit(solution)/shard_map/all_gather | solution.py:34
  13.1 23.7 %all-to-all-start = ((s32[16,1,1]{2,1,0:T(1,128)}), s32[16,1,1]{2,1,0:T(1,128)S(1)}, u32[]{:S(2)}, u32[]{:S(2)}) async-start(s32[16,1,1]{2,1,0:T(1,128)} %copy.97), calls=%async_computation | async-start | bytes 16384 | tf_op jit(solution)/shard_map/all_to_all | solution.py:64
  28.0 3.2 copy-start.7
  31.9 306.7 %copy-start.3 = (bf16[2560,40]{0,1:T(8,128)(2,1)S(1)}, bf16[2560,40]{0,1:T(8,128)(2,1)}, u32[]{:S(2)}) copy-start(bf16[2560,40]{0,1:T(8,128)(2,1)} %param.12) | copy-start | bytes 614404
  36.9 324.5 %all-to-all-start.2 = ((bf16[16,1,32,1280]{3,2,1,0:T(8,128)(2,1)}), bf16[16,1,32,1280]{3,2,1,0:T(8,128)(2,1)}, u32[]{:S(2)}, u32[]{:S(2)}) async-start(bf16[16,1,32,1280]{3,2,1,0:T(8,128)(2,1)} %copy.101), calls=%async_computation.2 | async-start | bytes 2621440 | tf_op jit(solution)/shard_map/all_to_all | solution.py:57
  43.2 303.5 %copy-start.1 = (bf16[2560,80]{0,1:T(8,128)(2,1)S(1)}, bf16[2560,80]{0,1:T(8,128)(2,1)}, u32[]{:S(2)}) copy-start(bf16[2560,80]{0,1:T(8,128)(2,1)} %param.11) | copy-start | bytes 1228804
  361.4 25.2 %all-to-all-start.1 = ((bf16[32,64,120]{2,1,0:T(8,128)(2,1)}), bf16[32,64,120]{2,1,0:T(8,128)(2,1)S(1)}, u32[]{:S(2)}, u32[]{:S(2)}) async-start(bf16[32,64,120]{2,1,0:T(8,128)(2,1)} %copy.98), calls=%async_computation.1 | async-start | bytes 1048576 | tf_op jit(solution)/shard_map/all_to_all | solution.py:38
  366.7 332.5 %all-reduce.2.cloned.1.call-start = ((), (), s32[]{:S(2)}) async-start(), calls=%async_computation.4 | async-start | bytes 2097152 | tf_op jit(solution)/shard_map/psum | solution.py:106
  367.3 8.9 %copy-start.6 = (s32[16]{0:T(128)}, s32[16]{0:T(128)S(1)}, u32[]{:S(2)}) copy-start(s32[16]{0:T(128)S(1)} %maximum_reduce_fusion) | copy-start | bytes 196
  367.7 8.5 %copy-start.5 = (pred[16]{0:T(512)(128)(4,1)}, pred[16]{0:T(512)(128)(4,1)S(1)}, u32[]{:S(2)}) copy-start(pred[16]{0:T(512)(128)(4,1)S(1)} %compare_reduce_fusion) | copy-start | bytes 52
  497.7 2.0 copy-start.4
  499.0 5.3 copy-start.2
Sparse Core Ops, SparseCore 0:
  12.9 325.6 all-gather.1
  504.2 194.9 all-reduce.1
where the time goes:
time: 713 us; the launch traced here: 712 us
  waiting for transfers between devices  412 us (58%)
  blocking collectives  185 us (26%)
  local copies, waits for them, and re-layouts  34.2 us (5%)
  starting transfers between devices  26 us (4%)
  matrix products  23.9 us (3%)
  other arithmetic  16.1 us (2%)
  between operations  14.9 us (2%)
    all_gather x1, waiting for transfers between devices, per_device(): portion = lax.all_gather(normed, 'tensor', axis=0, tiled=True)  295 us
    psum x1, waiting for transfers between devices, per_device(): sum_out, sum_total = lax.psum((part_out, part_total), 'page')  103 us
    pmax x1, blocking collectives, per_device(): row_peak = jnp.maximum(lax.pmax(local_peak, 'page'), own_score)  95.7 us
    psum x1, blocking collectives, per_device(): sum_out, sum_total = lax.psum((part_out, part_total), 'page')  89.3 us
  transfers between devices with their start and end apart: 5, of which 4 were waited for; matrix products, arithmetic and copies ran while one was open for 6% of the time, Pallas kernels for 0%

commit v1 on v0

v1 whole, which is shorter than its diff:
```python
import functools

import jax
import jax.numpy as jnp
from jax import lax
from jax.experimental import pallas as pl
from jax.experimental.pallas import tpu as pltpu
from jax.sharding import PartitionSpec as P

HEADS = 32
KV_HEADS = 8
HEAD_DIM = 80
EPSILON = 1e-05
NEGATIVE = -1e30

CHIPS = 8
PLANE = 16
SOURCES = 8
KEEP = 32
LANES = SOURCES * KEEP
BLOCK = 2 * HEAD_DIM + 16

PLANE_GROUPS = [[2 * i + half for i in range(PLANE)] for half in range(2)]
RUN_GROUPS = [[2 * z + core for z in range(CHIPS)] for core in range(2)]
OTHER_HALF = [(i, i ^ 1) for i in range(2 * PLANE)]
OTHER_CORE = [(i, i ^ 1) for i in range(2 * CHIPS)]


def select_kernel(count_ref, owner_ref, dest_ref, keep_ref, page_ref, out_ref, kv_ref, kept_ref):
    slot = pl.program_id(0)

    @pl.when(slot == 0)
    def _():
        out_ref[...] = jnp.zeros_like(out_ref)

    rows = page_ref.shape[1]
    picks = jnp.broadcast_to(keep_ref[0], (rows, KEEP))
    chosen = (picks == lax.broadcasted_iota(jnp.int32, (rows, KEEP), 0)).astype(jnp.float32)
    kept = jnp.dot(
        chosen.T.astype(jnp.bfloat16), page_ref[0], preferred_element_type=jnp.float32
    ).astype(jnp.bfloat16)
    kept_ref[pl.ds(pl.multiple_of(slot * KEEP, KEEP), KEEP), :] = kept

    @pl.when(slot < count_ref[0])
    def _():
        out_ref[dest_ref[slot]] = kept

    @pl.when(slot == SOURCES - 1)
    def _():
        turned = kept_ref[...].T
        lane_slot = lax.broadcasted_iota(jnp.int32, (16, LANES), 1) // KEEP
        tags = jnp.full((16, LANES), -1, jnp.int32)
        for s in range(SOURCES):
            tag = jnp.where(s < count_ref[0], owner_ref[s], -1)
            tags = jnp.where(lane_slot == s, tag, tags)
        tags = tags.astype(jnp.float32).astype(jnp.bfloat16)
        values_at = KV_HEADS * HEAD_DIM
        for g in range(KV_HEADS):
            low = g * HEAD_DIM
            kv_ref[g, 0:HEAD_DIM] = turned[low : low + HEAD_DIM]
            kv_ref[g, HEAD_DIM : 2 * HEAD_DIM] = turned[values_at + low : values_at + low + HEAD_DIM]
            kv_ref[g, 2 * HEAD_DIM :] = tags


def select_rows(page_count, page_owner, dest_slot, keep_rows, cache):
    sources, _, rows, width = cache.shape
    holders = 2 * CHIPS
    return pl.pallas_call(
        select_kernel,
        out_shape=(
            jax.ShapeDtypeStruct((holders, KEEP, width), cache.dtype),
            jax.ShapeDtypeStruct((KV_HEADS, BLOCK, LANES), cache.dtype),
        ),
        grid_spec=pltpu.PrefetchScalarGridSpec(
            num_scalar_prefetch=3,
            grid=(sources,),
            in_specs=[
                pl.BlockSpec((1, 1, KEEP), lambda s, *_: (s, 0, 0)),
                pl.BlockSpec((1, rows, width), lambda s, *_: (s, 0, 0)),
            ],
            out_specs=[
                pl.BlockSpec((holders, KEEP, width), lambda s, *_: (0, 0, 0)),
                pl.BlockSpec((KV_HEADS, BLOCK, LANES), lambda s, *_: (0, 0, 0)),
            ],
            scratch_shapes=[pltpu.VMEM((LANES, width), cache.dtype)],
        ),
        name="select_rows",
    )(
        page_count.reshape(1),
        page_owner.reshape(sources),
        dest_slot.reshape(sources),
        keep_rows,
        cache.reshape(sources, rows, width),
    )


def attend_kernel(own_ref, near_ref, far_ref, out_ref, score_ref):
    scale = HEAD_DIM ** (-0.5)
    requests = own_ref.shape[1]
    query = jnp.concatenate([own_ref[0, :, :HEAD_DIM], own_ref[1, :, :HEAD_DIM]], axis=0)
    new_key = own_ref[0, :, HEAD_DIM:].astype(jnp.float32)
    new_value = own_ref[1, :, HEAD_DIM:].astype(jnp.float32)
    new_key = jnp.concatenate([new_key, new_key], axis=0)
    new_value = jnp.concatenate([new_value, new_value], axis=0)
    own = jnp.sum(query.astype(jnp.float32) * new_key, axis=1, keepdims=True) * scale
    request = lax.broadcasted_iota(jnp.int32, (2 * requests, 1), 0) % requests
    request = request.astype(jnp.float32)
    blocks = [near_ref.at[i] for i in range(CHIPS)] + [far_ref.at[i] for i in range(CHIPS)]
    top = jnp.full((2 * requests, LANES), NEGATIVE, jnp.float32)
    for b, block in enumerate(blocks):
        score = jnp.dot(query, block[0:HEAD_DIM, :], preferred_element_type=jnp.float32) * scale
        tag = block[2 * HEAD_DIM : BLOCK, :].astype(jnp.float32)[0:1]
        score = jnp.where(tag == request, score, NEGATIVE)
        score_ref[:, b * LANES : (b + 1) * LANES] = score
        top = jnp.maximum(top, score)
    peak = jnp.maximum(jnp.max(top, axis=1, keepdims=True), own)
    own_weight = jnp.exp(own - peak)
    total = jnp.zeros((2 * requests, LANES), jnp.float32)
    mixed = jnp.zeros((2 * requests, HEAD_DIM), jnp.float32)
    for b, block in enumerate(blocks):
        weight = jnp.exp(score_ref[:, b * LANES : (b + 1) * LANES] - peak)
        total = total + weight
        mixed = mixed + lax.dot_general(
            weight.astype(jnp.bfloat16),
            block[HEAD_DIM : 2 * HEAD_DIM, :],
            (((1,), (1,)), ((), ())),
            preferred_element_type=jnp.float32,
        )
    total = jnp.sum(total, axis=1, keepdims=True) + own_weight
    result = (mixed + own_weight * new_value) / total
    out_ref[...] = result.T.astype(jnp.bfloat16)


def attend(own, near, far):
    requests = own.shape[1]
    return pl.pallas_call(
        attend_kernel,
        out_shape=jax.ShapeDtypeStruct((HEAD_DIM, 2 * requests), jnp.bfloat16),
        in_specs=[pl.BlockSpec(memory_space=pltpu.VMEM)] * 3,
        out_specs=pl.BlockSpec(memory_space=pltpu.VMEM),
        scratch_shapes=[pltpu.VMEM((2 * requests, 2 * CHIPS * LANES), jnp.float32)],
        name="attend",
    )(own, near, far)


def assemble_kernel(core_ref, near_ref, far_ref, out_ref):
    first = core_ref[0] == 0
    requests = out_ref.shape[0]
    for z in range(CHIPS):
        near = near_ref[z].astype(jnp.float32)
        far = far_ref[z].astype(jnp.float32)
        for core in range(2):
            piece = jnp.where(first == (core == 0), near, far).T.astype(jnp.bfloat16)
            for j in range(2):
                at = (4 * z + 2 * core + j) * HEAD_DIM
                out_ref[:, at : at + HEAD_DIM] = piece[j * requests : (j + 1) * requests]


def assemble(core, near, far):
    requests = near.shape[2] // 2
    return pl.pallas_call(
        assemble_kernel,
        out_shape=jax.ShapeDtypeStruct((requests, HEADS * HEAD_DIM), jnp.bfloat16),
        in_specs=[pl.BlockSpec(memory_space=pltpu.SMEM)] + [pl.BlockSpec(memory_space=pltpu.VMEM)] * 2,
        out_specs=pl.BlockSpec(memory_space=pltpu.VMEM),
        name="assemble",
    )(core.reshape(1), near, far)


def per_device(
    tokens, norm_gain, w_query, w_keyvalue, cache, page_count, page_owner, keep_rows, dest_slot
):
    holders = lax.axis_size("page")
    groups = lax.axis_size("tensor")
    holder = lax.axis_index("page")
    half = lax.axis_index("tensor") % 2
    share = tokens.shape[0] // holders

    mine = lax.dynamic_slice_in_dim(tokens, holder * share, share, 0)
    widened = mine.astype(jnp.float32)
    normed = (
        widened
        * lax.rsqrt(jnp.mean(widened * widened, axis=-1, keepdims=True) + EPSILON)
        * norm_gain
    ).astype(jnp.bfloat16)
    across = lax.ppermute(normed, "tensor", OTHER_HALF)

    compact, by_head = select_rows(page_count, page_owner, dest_slot, keep_rows, cache)
    near = lax.all_to_all(
        by_head, "page", 0, 0, axis_index_groups=RUN_GROUPS, tiled=True
    )
    far = lax.ppermute(near, "page", OTHER_CORE)
    arrived = lax.all_to_all(compact, "page", 0, 0, tiled=True)

    both = jnp.where(
        half == 0, jnp.stack([normed, across]), jnp.stack([across, normed])
    )
    rows = lax.all_to_all(
        jnp.broadcast_to(both[None], (PLANE,) + both.shape),
        "tensor",
        0,
        0,
        axis_index_groups=PLANE_GROUPS,
        tiled=True,
    ).reshape(groups * share, -1)
    query_part = jnp.dot(rows, w_query, preferred_element_type=jnp.float32)
    pair_part = jnp.dot(rows, w_keyvalue, preferred_element_type=jnp.float32)
    projected = jnp.concatenate([query_part, pair_part], axis=1).astype(jnp.bfloat16)
    back = lax.all_to_all(
        projected.reshape(groups, share, -1), "tensor", 0, 0, tiled=True
    )
    query = back[:, :, :HEAD_DIM].reshape(CHIPS, 2, 2, share, HEAD_DIM)
    pair = back[:, :, HEAD_DIM:].reshape(2, CHIPS, 2, share, HEAD_DIM // 2)
    pair = jnp.transpose(pair, (1, 0, 3, 2, 4)).reshape(CHIPS, 1, 2, share, HEAD_DIM)
    pair = jnp.broadcast_to(pair, query.shape)
    outgoing = jnp.concatenate([query, pair], axis=-1).reshape(holders, 2, share, 2 * HEAD_DIM)
    own = lax.all_to_all(outgoing, "page", 0, 0, tiled=True)
    own = jnp.transpose(own, (1, 0, 2, 3)).reshape(2, holders * share, 2 * HEAD_DIM)

    piece = attend(own, near, far)
    near_out = lax.all_to_all(
        jnp.broadcast_to(piece[None], (CHIPS,) + piece.shape),
        "page",
        0,
        0,
        axis_index_groups=RUN_GROUPS,
        tiled=True,
    )
    far_out = lax.ppermute(near_out, "page", OTHER_CORE)
    attended = assemble(holder % 2, near_out, far_out)
    return attended, arrived[:, None]


def solution(mesh):
    return jax.shard_map(
        per_device,
        mesh=mesh,
        in_specs=(
            P("tensor", None),
            P(),
            P(None, "tensor"),
            P(None, "tensor"),
            P("page", "tensor", None, None),
            P("page", "tensor"),
            P("page", "tensor"),
            P("page", "tensor", None),
            P("page", "tensor"),
        ),
        out_specs=(P("tensor", None), P("page", "tensor", None, None)),
        check_vma=False,
    )
```

time: 713 us -> 217 us (0.30)
  the two profiles are of different devices: /device:TPU:1 before, /device:TPU:65 now
where the time goes in v1:
time: 217 us; the launch traced here: 216 us
  waiting for transfers between devices  83.6 us (39%)
  blocking collectives  59.9 us (28%)
  starting transfers between devices  48.4 us (22%)
  Pallas kernels  13 us (6%)
  local copies, waits for them, and re-layouts  6.22 us (3%)
  other arithmetic  2.97 us (1%)
    all_to_all x1, waiting for transfers between devices, per_device(): arrived = lax.all_to_all(compact, 'page', 0, 0, tiled=True)  53.3 us
    all_to_all x1, waiting for transfers between devices, per_device(): lax.all_to_all(by_head, 'page', 0, 0, axis_index_groups=RUN_GROUPS, tiled...  27.3 us
    all_to_all x1, blocking collectives, per_device(): lax.all_to_all(projected.reshape(groups, share, -1), 'tensor', 0, 0, tile...  26.7 us
    all_to_all x1, blocking collectives, per_device(): own = lax.all_to_all(outgoing, 'page', 0, 0, tiled=True)  17.7 us
    all_to_all x1, blocking collectives, per_device(): lax.all_to_all(jnp.broadcast_to(piece[None], (CHIPS,) + piece.shape), 'pa...  15.5 us
    ppermute x1, starting transfers between devices, per_device(): across = lax.ppermute(normed, 'tensor', OTHER_HALF)  13.6 us
    all_to_all x1, starting transfers between devices, per_device(): lax.all_to_all(by_head, 'page', 0, 0, axis_index_groups=RUN_GROUPS, tiled...  9.98 us
    all_to_all x1, starting transfers between devices, per_device(): arrived = lax.all_to_all(compact, 'page', 0, 0, tiled=True)  8.13 us
  transfers between devices with their start and end apart: 6, of which 5 were waited for; matrix products, arithmetic and copies ran while one was open for 2% of the time, Pallas kernels for 4%

profile of v1, /device:TPU:65, one launch (start us, length us, event | category | flops | bytes accessed | tf_op | source)
XLA Modules:
  0.0 216.1 jit_solution(17715677123575578807)
XLA Ops:
  0.7 1.0 fusion.2
  1.6 0.9 fusion.4
  2.5 13.6 %collective-permute-start = (bf16[4,2560]{1,0:T(4,128)(2,1)S(1)}, bf16[4,2560]{1,0:T(4,128)(2,1)S(1)}, u32[]{:S(2)}, u32[]{:S(2)}) collective-permute-start(bf16[4,2560]{1,0:T(4,128)(2,1)S(1)} %fusion.4), channel_id=1, source_target_pairs={{0,1},{1,0},{2,3},{3,2},{4,5},{5,4},{6,7},{7,6},{8,9},{9,8},{10,11... | collective-permute-start | bytes 61448 | tf_op jit(solution)/shard_map/ppermute | solution.py:186
  16.2 0.9 fusion.7
  17.4 1.2 broadcast_in_dim.10
  18.6 6.8 %all-to-all-start = ((bf16[16,2,4,2560]{3,1,2,0:T(2,128)(2,1)}), bf16[16,2,4,2560]{3,1,2,0:T(2,128)(2,1)S(1)}, u32[]{:S(2)}, u32[]{:S(2)}) async-start(bf16[16,2,4,2560]{3,1,2,0:T(2,128)(2,1)} %broadcast_in_dim.10), calls=%async_computation | async-start | bytes 1310720 | tf_op jit(solution)/shard_map/all_to_all | solution.py:198
  26.0 7.5 %select_rows.1 = (bf16[16,32,1280]{2,1,0:T(8,128)(2,1)}, bf16[8,176,256]{2,1,0:T(8,128)(2,1)}) custom-call(s32[1]{0:T(128)} %bitcast.31.count_ref, s32[8]{0:T(128)} %bitcast.40, s32[8]{0:T(128)} %bitcast.41, s32[8,1,32]{2,1,0:T(1,128)} %keep_ref.1, bf16[8,128,1280]{2,1,0:T(8,128)(2,1)} %bitcast.33), custom_call_target="tpu_custom_call" | custom-call | tf_op jit(solution)/shard_map/select_rows/pallas_call | solution.py:68
  33.5 1.6 all-to-all-done
  35.2 10.0 %all-to-all-start.3 = ((bf16[8,176,256]{2,1,0:T(8,128)(2,1)}), bf16[8,176,256]{2,1,0:T(8,128)(2,1)S(1)}, u32[]{:S(2)}, u32[]{:S(2)}) async-start(bf16[8,176,256]{2,1,0:T(8,128)(2,1)} %get-tuple-element.4), calls=%async_computation.3 | async-start | bytes 1441792 | tf_op jit(solution)/shard_map/all_to_all | solution.py:189
  46.2 27.3 %all-to-all-done.3.near_ref = bf16[8,176,256]{2,1,0:T(8,128)(2,1)S(1)} async-done(((bf16[8,176,256]{2,1,0:T(8,128)(2,1)}), bf16[8,176,256]{2,1,0:T(8,128)(2,1)S(1)}, u32[]{:S(2)}, u32[]{:S(2)}) %all-to-all-start.3) | async-done | bytes 720928 | tf_op jit(solution)/shard_map/all_to_all | solution.py:189
  73.5 7.6 %collective-permute-start.1 = (bf16[8,176,256]{2,1,0:T(8,128)(2,1)S(1)}, bf16[8,176,256]{2,1,0:T(8,128)(2,1)S(1)}, u32[]{:S(2)}, u32[]{:S(2)}) collective-permute-start(bf16[8,176,256]{2,1,0:T(8,128)(2,1)S(1)} %all-to-all-done.3.near_ref), channel_id=1, source_target_pairs={{0,32},{32,0},{64,96},{96,64},{128,160},{160,128},{192,224},{224,1... | collective-permute-start | bytes 2162696 | tf_op jit(solution)/shard_map/ppermute | solution.py:192
  81.6 26.7 %all_to_all.30 = bf16[32,4,120]{2,1,0:T(4,128)(2,1)S(1)} all-to-all(bf16[32,4,120]{2,1,0:T(4,128)(2,1)S(1)} %copy.22), channel_id=1, replica_groups=mesh['page'=16,'tensor'=32] {'tensor'}, dimensions={0} | all-to-all | bytes 61440 | tf_op jit(solution)/shard_map/all_to_all | solution.py:209
  108.7 17.7 %all_to_all.31 = bf16[16,2,4,160]{3,2,1,0:T(4,128)(2,1)S(1)} all-to-all(bf16[16,2,4,160]{3,2,1,0:T(4,128)(2,1)S(1)} %pad_maximum_fusion), channel_id=1, replica_groups=mesh['page'=16,'tensor'=32] {'page'}, dimensions={0} | all-to-all | bytes 81920 | tf_op jit(solution)/shard_map/all_to_all | solution.py:217
  126.4 0.7 reshape.85.own_ref
  127.1 0.9 copy-done.2
  127.9 3.3 %attend.1 = bf16[80,128]{1,0:T(8,128)(2,1)} custom-call(bf16[2,64,160]{2,1,0:T(8,128)(2,1)} %reshape.85.own_ref, bf16[8,176,256]{2,1,0:T(8,128)(2,1)} %copy-done.1, bf16[8,176,256]{2,1,0:T(8,128)(2,1)} %copy-done.2), custom_call_target="tpu_custom_call" | custom-call | tf_op jit(solution)/shard_map/attend/pallas_call | solution.py:136
  131.2 0.7 broadcast_in_dim.13
  131.9 15.5 %all_to_all.32.near_ref = bf16[8,80,128]{2,1,0:T(8,128)(2,1)S(1)} all-to-all(bf16[8,80,128]{2,1,0:T(8,128)(2,1)S(1)} %broadcast_in_dim.13), channel_id=1, replica_groups={{0,64,128,192,256,320,384,448},{32,96,160,224,288,352,416,480},{1,65,12..., dimensions={0} | all-to-all | bytes 327680 | tf_op jit(solution)/shard_map/all_to_all | solution.py:221
  147.5 8.1 %all-to-all-start.5 = ((bf16[16,32,1280]{2,1,0:T(8,128)(2,1)}), bf16[16,32,1280]{2,1,0:T(8,128)(2,1)S(1)}, u32[]{:S(2)}, u32[]{:S(2)}) async-start(bf16[16,32,1280]{2,1,0:T(8,128)(2,1)} %get-tuple-element.5), calls=%async_computation.5 | async-start | bytes 2621440 | tf_op jit(solution)/shard_map/all_to_all | solution.py:193
  155.6 2.3 %collective-permute-start.2 = (bf16[8,80,128]{2,1,0:T(8,128)(2,1)S(1)}, bf16[8,80,128]{2,1,0:T(8,128)(2,1)S(1)}, u32[]{:S(2)}, u32[]{:S(2)}) collective-permute-start(bf16[8,80,128]{2,1,0:T(8,128)(2,1)S(1)} %all_to_all.32.near_ref), channel_id=1, source_target_pairs={{0,32},{32,0},{64,96},{96,64},{128,160},{160,128},{192,224},{224,1... | collective-permute-start | bytes 491528 | tf_op jit(solution)/shard_map/ppermute | solution.py:229
  157.9 1.0 collective-permute-done.2.far_ref
  159.6 2.2 %assemble.1 = bf16[64,2560]{1,0:T(8,128)(2,1)} custom-call(s32[1]{0:T(128)} %bitcast.core_ref, bf16[8,80,128]{2,1,0:T(8,128)(2,1)} %copy-done.3, bf16[8,80,128]{2,1,0:T(8,128)(2,1)} %copy-done.5), custom_call_target="tpu_custom_call" | custom-call | tf_op jit(solution)/shard_map/assemble/pallas_call | solution.py:161
  161.7 53.3 %all-to-all-done.5 = bf16[16,32,1280]{2,1,0:T(8,128)(2,1)S(1)} async-done(((bf16[16,32,1280]{2,1,0:T(8,128)(2,1)}), bf16[16,32,1280]{2,1,0:T(8,128)(2,1)S(1)}, u32[]{:S(2)}, u32[]{:S(2)}) %all-to-all-start.5) | async-done | bytes 1310752 | tf_op jit(solution)/shard_map/all_to_all | solution.py:193
  215.1 1.1 copy.31
  (29 shorter events, 2.8 us)
Async XLA Ops:
  0.6 45.2 %copy-start = (bf16[2560,80]{0,1:T(8,128)(2,1)S(1)}, bf16[2560,80]{0,1:T(8,128)(2,1)}, u32[]{:S(2)}) copy-start(bf16[2560,80]{0,1:T(8,128)(2,1)} %param.11) | copy-start | bytes 1228804
  2.5 14.8 %collective-permute-start = (bf16[4,2560]{1,0:T(4,128)(2,1)S(1)}, bf16[4,2560]{1,0:T(4,128)(2,1)S(1)}, u32[]{:S(2)}, u32[]{:S(2)}) collective-permute-start(bf16[4,2560]{1,0:T(4,128)(2,1)S(1)} %fusion.4), channel_id=1, source_target_pairs={{0,1},{1,0},{2,3},{3,2},{4,5},{5,4},{6,7},{7,6},{8,9},{9,8},{10,11... | collective-permute-start | bytes 61448 | tf_op jit(solution)/shard_map/ppermute | solution.py:186
  18.6 16.6 %all-to-all-start = ((bf16[16,2,4,2560]{3,1,2,0:T(2,128)(2,1)}), bf16[16,2,4,2560]{3,1,2,0:T(2,128)(2,1)S(1)}, u32[]{:S(2)}, u32[]{:S(2)}) async-start(bf16[16,2,4,2560]{3,1,2,0:T(2,128)(2,1)} %broadcast_in_dim.10), calls=%async_computation | async-start | bytes 1310720 | tf_op jit(solution)/shard_map/all_to_all | solution.py:198
  35.2 38.4 %all-to-all-start.3 = ((bf16[8,176,256]{2,1,0:T(8,128)(2,1)}), bf16[8,176,256]{2,1,0:T(8,128)(2,1)S(1)}, u32[]{:S(2)}, u32[]{:S(2)}) async-start(bf16[8,176,256]{2,1,0:T(8,128)(2,1)} %get-tuple-element.4), calls=%async_computation.3 | async-start | bytes 1441792 | tf_op jit(solution)/shard_map/all_to_all | solution.py:189
  45.6 35.5 %copy-start.4 = (bf16[2560,40]{0,1:T(8,128)(2,1)S(1)}, bf16[2560,40]{0,1:T(8,128)(2,1)}, u32[]{:S(2)}) copy-start(bf16[2560,40]{0,1:T(8,128)(2,1)} %param.12) | copy-start | bytes 614404
  73.5 53.5 %copy-start.1 = (bf16[8,176,256]{2,1,0:T(8,128)(2,1)}, bf16[8,176,256]{2,1,0:T(8,128)(2,1)S(1)}, u32[]{:S(2)}) copy-start(bf16[8,176,256]{2,1,0:T(8,128)(2,1)S(1)} %all-to-all-done.3.near_ref) | copy-start | bytes 2162692
  73.5 53.5 %collective-permute-start.1 = (bf16[8,176,256]{2,1,0:T(8,128)(2,1)S(1)}, bf16[8,176,256]{2,1,0:T(8,128)(2,1)S(1)}, u32[]{:S(2)}, u32[]{:S(2)}) collective-permute-start(bf16[8,176,256]{2,1,0:T(8,128)(2,1)S(1)} %all-to-all-done.3.near_ref), channel_id=1, source_target_pairs={{0,32},{32,0},{64,96},{96,64},{128,160},{160,128},{192,224},{224,1... | collective-permute-start | bytes 2162696 | tf_op jit(solution)/shard_map/ppermute | solution.py:192
  127.1 0.9 copy-start.2
  147.5 8.1 %copy-start.3 = (bf16[8,80,128]{2,1,0:T(8,128)(2,1)}, bf16[8,80,128]{2,1,0:T(8,128)(2,1)S(1)}, u32[]{:S(2)}) copy-start(bf16[8,80,128]{2,1,0:T(8,128)(2,1)S(1)} %all_to_all.32.near_ref) | copy-start | bytes 491524
  147.5 67.6 %all-to-all-start.5 = ((bf16[16,32,1280]{2,1,0:T(8,128)(2,1)}), bf16[16,32,1280]{2,1,0:T(8,128)(2,1)S(1)}, u32[]{:S(2)}, u32[]{:S(2)}) async-start(bf16[16,32,1280]{2,1,0:T(8,128)(2,1)} %get-tuple-element.5), calls=%async_computation.5 | async-start | bytes 2621440 | tf_op jit(solution)/shard_map/all_to_all | solution.py:193
  155.6 3.3 %collective-permute-start.2 = (bf16[8,80,128]{2,1,0:T(8,128)(2,1)S(1)}, bf16[8,80,128]{2,1,0:T(8,128)(2,1)S(1)}, u32[]{:S(2)}, u32[]{:S(2)}) collective-permute-start(bf16[8,80,128]{2,1,0:T(8,128)(2,1)S(1)} %all_to_all.32.near_ref), channel_id=1, source_target_pairs={{0,32},{32,0},{64,96},{96,64},{128,160},{160,128},{192,224},{224,1... | collective-permute-start | bytes 491528 | tf_op jit(solution)/shard_map/ppermute | solution.py:229
  158.9 0.7 copy-start.5

commit v2 on v1

--- a/solution.py
+++ b/solution.py
@@ -24,14 +24,21 @@
 RUN_GROUPS = [[2 * z + core for z in range(CHIPS)] for core in range(2)]
 OTHER_HALF = [(i, i ^ 1) for i in range(2 * PLANE)]
 OTHER_CORE = [(i, i ^ 1) for i in range(2 * CHIPS)]
-
-
-def select_kernel(count_ref, owner_ref, dest_ref, keep_ref, page_ref, out_ref, kv_ref, kept_ref):
+OTHER_CHIP = [[(i, i ^ (2 * d)) for i in range(2 * CHIPS)] for d in range(CHIPS)]
+
+
+def select_kernel(
+    place_ref, count_ref, owner_ref, dest_ref, keep_ref, page_ref, *refs
+):
+    out_refs, kv_refs = refs[:CHIPS], refs[CHIPS : 2 * CHIPS]
+    kept_ref, turned_ref = refs[2 * CHIPS :]
     slot = pl.program_id(0)
+    chip, core = place_ref[0], place_ref[1]
 
     @pl.when(slot == 0)
     def _():
-        out_ref[...] = jnp.zeros_like(out_ref)
+        for ref in out_refs:
+            ref[...] = jnp.zeros_like(ref)
 
     rows = page_ref.shape[1]
     picks = jnp.broadcast_to(keep_ref[0], (rows, KEEP))
@@ -40,14 +47,19 @@
         chosen.T.astype(jnp.bfloat16), page_ref[0], preferred_element_type=jnp.float32
     ).astype(jnp.bfloat16)
     kept_ref[pl.ds(pl.multiple_of(slot * KEEP, KEEP), KEEP), :] = kept
-
-    @pl.when(slot < count_ref[0])
-    def _():
-        out_ref[dest_ref[slot]] = kept
+    target = dest_ref[slot]
+    step = (target // 2) ^ chip
+    cross = (target % 2) ^ core
+    live = slot < count_ref[0]
+    for d in range(CHIPS):
+
+        @pl.when(live & (step == d))
+        def _():
+            out_refs[d][cross] = kept
 
     @pl.when(slot == SOURCES - 1)
     def _():
-        turned = kept_ref[...].T
+        turned_ref[...] = kept_ref[...].T
         lane_slot = lax.broadcasted_iota(jnp.int32, (16, LANES), 1) // KEEP
         tags = jnp.full((16, LANES), -1, jnp.int32)
         for s in range(SOURCES):
@@ -55,46 +67,71 @@
             tags = jnp.where(lane_slot == s, tag, tags)
         tags = tags.astype(jnp.float32).astype(jnp.bfloat16)
         values_at = KV_HEADS * HEAD_DIM
-        for g in range(KV_HEADS):
-            low = g * HEAD_DIM
-            kv_ref[g, 0:HEAD_DIM] = turned[low : low + HEAD_DIM]
-            kv_ref[g, HEAD_DIM : 2 * HEAD_DIM] = turned[values_at + low : values_at + low + HEAD_DIM]
-            kv_ref[g, 2 * HEAD_DIM :] = tags
-
-
-def select_rows(page_count, page_owner, dest_slot, keep_rows, cache):
+        for d in range(CHIPS):
+            low = pl.multiple_of((chip ^ d) * HEAD_DIM, HEAD_DIM)
+            kv_refs[d][0:HEAD_DIM] = turned_ref[pl.ds(low, HEAD_DIM), :]
+            kv_refs[d][HEAD_DIM : 2 * HEAD_DIM] = turned_ref[
+                pl.ds(pl.multiple_of(values_at + low, HEAD_DIM), HEAD_DIM), :
+            ]
+            kv_refs[d][2 * HEAD_DIM :] = tags
+
+
+def select_rows(place, page_count, page_owner, dest_slot, keep_rows, cache):
     sources, _, rows, width = cache.shape
-    holders = 2 * CHIPS
-    return pl.pallas_call(
+    out = jax.ShapeDtypeStruct((2, KEEP, width), cache.dtype)
+    kv = jax.ShapeDtypeStruct((BLOCK, LANES), cache.dtype)
+    results = pl.pallas_call(
         select_kernel,
-        out_shape=(
-            jax.ShapeDtypeStruct((holders, KEEP, width), cache.dtype),
-            jax.ShapeDtypeStruct((KV_HEADS, BLOCK, LANES), cache.dtype),
-        ),
+        out_shape=[out] * CHIPS + [kv] * CHIPS,
         grid_spec=pltpu.PrefetchScalarGridSpec(
-            num_scalar_prefetch=3,
+            num_scalar_prefetch=4,
             grid=(sources,),
             in_specs=[
                 pl.BlockSpec((1, 1, KEEP), lambda s, *_: (s, 0, 0)),
                 pl.BlockSpec((1, rows, width), lambda s, *_: (s, 0, 0)),
             ],
-            out_specs=[
-                pl.BlockSpec((holders, KEEP, width), lambda s, *_: (0, 0, 0)),
-                pl.BlockSpec((KV_HEADS, BLOCK, LANES), lambda s, *_: (0, 0, 0)),
+            out_specs=[pl.BlockSpec(out.shape, lambda s, *_: (0, 0, 0))] * CHIPS
+            + [pl.BlockSpec(kv.shape, lambda s, *_: (0, 0))] * CHIPS,
+            scratch_shapes=[
+                pltpu.VMEM((LANES, width), cache.dtype),
+                pltpu.VMEM((width, LANES), cache.dtype),
             ],
-            scratch_shapes=[pltpu.VMEM((LANES, width), cache.dtype)],
         ),
         name="select_rows",
     )(
+        place,
         page_count.reshape(1),
         page_owner.reshape(sources),
         dest_slot.reshape(sources),
         keep_rows,
         cache.reshape(sources, rows, width),
     )
-
-
-def attend_kernel(own_ref, near_ref, far_ref, out_ref, score_ref):
+    return results[:CHIPS], results[CHIPS:]
+
+
+def place_kernel(place_ref, *refs):
+    got_refs, cross_ref, out_ref = refs[:CHIPS], refs[CHIPS], refs[CHIPS + 1]
+    chip, core = place_ref[0], place_ref[1]
+    for d in range(CHIPS):
+        at = 2 * (chip ^ d)
+        out_ref[at + core] = got_refs[d][0]
+        out_ref[at + 1 - core] = cross_ref[d]
+
+
+def place_pages(place, got, cross):
+    return pl.pallas_call(
+        place_kernel,
+        out_shape=jax.ShapeDtypeStruct((2 * CHIPS,) + cross.shape[1:], cross.dtype),
+        in_specs=[pl.BlockSpec(memory_space=pltpu.SMEM)]
+        + [pl.BlockSpec(memory_space=pltpu.VMEM)] * (CHIPS + 1),
+        out_specs=pl.BlockSpec(memory_space=pltpu.VMEM),
+        name="place_pages",
+    )(place, *got, cross)
+
+
+def attend_kernel(own_ref, *refs):
+    near_refs = refs[:CHIPS]
+    far_ref, out_ref, score_ref = refs[CHIPS:]
     scale = HEAD_DIM ** (-0.5)
     requests = own_ref.shape[1]
     query = jnp.concatenate([own_ref[0, :, :HEAD_DIM], own_ref[1, :, :HEAD_DIM]], axis=0)
@@ -105,7 +142,7 @@
     own = jnp.sum(query.astype(jnp.float32) * new_key, axis=1, keepdims=True) * scale
     request = lax.broadcasted_iota(jnp.int32, (2 * requests, 1), 0) % requests
     request = request.astype(jnp.float32)
-    blocks = [near_ref.at[i] for i in range(CHIPS)] + [far_ref.at[i] for i in range(CHIPS)]
+    blocks = list(near_refs) + [far_ref.at[i] for i in range(CHIPS)]
     top = jnp.full((2 * requests, LANES), NEGATIVE, jnp.float32)
     for b, block in enumerate(blocks):
         score = jnp.dot(query, block[0:HEAD_DIM, :], preferred_element_type=jnp.float32) * scale
@@ -136,11 +173,11 @@
     return pl.pallas_call(
         attend_kernel,
         out_shape=jax.ShapeDtypeStruct((HEAD_DIM, 2 * requests), jnp.bfloat16),
-        in_specs=[pl.BlockSpec(memory_space=pltpu.VMEM)] * 3,
+        in_specs=[pl.BlockSpec(memory_space=pltpu.VMEM)] * (2 + CHIPS),
         out_specs=pl.BlockSpec(memory_space=pltpu.VMEM),
         scratch_shapes=[pltpu.VMEM((2 * requests, 2 * CHIPS * LANES), jnp.float32)],
         name="attend",
-    )(own, near, far)
+    )(own, *near, far)
 
 
 def assemble_kernel(core_ref, near_ref, far_ref, out_ref):
@@ -185,13 +222,20 @@
     ).astype(jnp.bfloat16)
     across = lax.ppermute(normed, "tensor", OTHER_HALF)
 
-    compact, by_head = select_rows(page_count, page_owner, dest_slot, keep_rows, cache)
-    near = lax.all_to_all(
-        by_head, "page", 0, 0, axis_index_groups=RUN_GROUPS, tiled=True
-    )
-    far = lax.ppermute(near, "page", OTHER_CORE)
-    arrived = lax.all_to_all(compact, "page", 0, 0, tiled=True)
-
+    place = jnp.stack([holder // 2, holder % 2])
+    compact, by_head = select_rows(place, page_count, page_owner, dest_slot, keep_rows, cache)
+    near, got = [by_head[0]] + [None] * (CHIPS - 1), [compact[0]] + [None] * (CHIPS - 1)
+
+    def send(after, heads, pages):
+        blocks = [by_head[d] for d in heads] + [compact[d] for d in pages]
+        blocks, after = lax.optimization_barrier((blocks, after))
+        for d in heads:
+            near[d] = lax.ppermute(blocks.pop(0), "page", OTHER_CHIP[d])
+        for d in pages:
+            got[d] = lax.ppermute(blocks.pop(0), "page", OTHER_CHIP[d])
+        return after
+
+    normed = send(normed, (4, 5, 6, 1), ())
     both = jnp.where(
         half == 0, jnp.stack([normed, across]), jnp.stack([across, normed])
     )
@@ -203,12 +247,14 @@
         axis_index_groups=PLANE_GROUPS,
         tiled=True,
     ).reshape(groups * share, -1)
+    rows = send(rows, (7, 2, 3), (4, 1))
     query_part = jnp.dot(rows, w_query, preferred_element_type=jnp.float32)
     pair_part = jnp.dot(rows, w_keyvalue, preferred_element_type=jnp.float32)
     projected = jnp.concatenate([query_part, pair_part], axis=1).astype(jnp.bfloat16)
     back = lax.all_to_all(
         projected.reshape(groups, share, -1), "tensor", 0, 0, tiled=True
     )
+    back = send(back, (), (5, 2))
     query = back[:, :, :HEAD_DIM].reshape(CHIPS, 2, 2, share, HEAD_DIM)
     pair = back[:, :, HEAD_DIM:].reshape(2, CHIPS, 2, share, HEAD_DIM // 2)
     pair = jnp.transpose(pair, (1, 0, 3, 2, 4)).reshape(CHIPS, 1, 2, share, HEAD_DIM)
@@ -217,7 +263,9 @@
     own = lax.all_to_all(outgoing, "page", 0, 0, tiled=True)
     own = jnp.transpose(own, (1, 0, 2, 3)).reshape(2, holders * share, 2 * HEAD_DIM)
 
+    far = lax.ppermute(jnp.stack(near), "page", OTHER_CORE)
     piece = attend(own, near, far)
+    piece = send(piece, (), (6, 7, 3))
     near_out = lax.all_to_all(
         jnp.broadcast_to(piece[None], (CHIPS,) + piece.shape),
         "page",
@@ -228,6 +276,8 @@
     )
     far_out = lax.ppermute(near_out, "page", OTHER_CORE)
     attended = assemble(holder % 2, near_out, far_out)
+    cross = lax.ppermute(jnp.stack([block[1] for block in got]), "page", OTHER_CORE)
+    arrived = place_pages(place, got, cross)
     return attended, arrived[:, None]
 
 

time: 217 us -> 184 us (0.85)
  the two profiles are of different devices: /device:TPU:65 before, /device:TPU:99 now
where the time goes in v2:
time: 184 us; the launch traced here: 182 us
  starting transfers between devices  112 us (61%)
  waiting for transfers between devices  34.6 us (19%)
  Pallas kernels  16.3 us (9%)
  local copies, waits for them, and re-layouts  13.1 us (7%)
  other arithmetic  3.35 us (2%)
  between operations  1.94 us (1%)
    ppermute x7, starting transfers between devices, send(): got[d] = lax.ppermute(blocks.pop(0), 'page', OTHER_CHIP[d])  32.3 us
    ppermute x7, waiting for transfers between devices, send(): got[d] = lax.ppermute(blocks.pop(0), 'page', OTHER_CHIP[d])  29 us
    ppermute x7, starting transfers between devices, send(): near[d] = lax.ppermute(blocks.pop(0), 'page', OTHER_CHIP[d])  24.5 us
    ppermute x1, starting transfers between devices, per_device(): across = lax.ppermute(normed, 'tensor', OTHER_HALF)  12.7 us
    all_to_all x1, starting transfers between devices, per_device(): lax.all_to_all(projected.reshape(groups, share, -1), 'tensor', 0, 0, tile...  10.7 us
    unnamed x62, local copies, waits for them, and re-layouts  8.06 us
    pallas_call x1, Pallas kernels, select_rows(): pl.pallas_call(select_kernel, out_shape=[out] * CHIPS + [kv] * CHIPS, gri...  7.99 us
    all_to_all x1, starting transfers between devices, per_device(): lax.all_to_all(jnp.broadcast_to(both[None], (PLANE,) + both.shape), 'tens...  7.06 us
  transfers between devices with their start and end apart: 22, of which 6 were waited for; matrix products, arithmetic and copies ran while one was open for 6% of the time, Pallas kernels for 7%

profile of v2, /device:TPU:99, one launch (start us, length us, event | category | flops | bytes accessed | tf_op | source)
XLA Modules:
  0.0 182.2 jit_solution(3081601549165733814)
XLA Ops:
  2.5 12.7 %collective-permute-start = (bf16[4,2560]{1,0:T(4,128)(2,1)S(1)}, bf16[4,2560]{1,0:T(4,128)(2,1)S(1)}, u32[]{:S(2)}, u32[]{:S(2)}) collective-permute-start(bf16[4,2560]{1,0:T(4,128)(2,1)S(1)} %fusion.2), channel_id=1, source_target_pairs={{0,1},{1,0},{2,3},{3,2},{4,5},{5,4},{6,7},{7,6},{8,9},{9,8},{10,11... | collective-permute-start | bytes 61448 | tf_op jit(solution)/shard_map/ppermute | solution.py:223
  16.5 8.0 %select_rows.1 = (bf16[2,32,1280]{2,1,0:T(8,128)(2,1)}, bf16[2,32,1280]{2,1,0:T(8,128)(2,1)}, bf16[2,32,1280]{2,1,0:T(8,128)(2,1)}, bf16[2,32,1280]{2,1,0:T(8,12...) custom-call(s32[2]{0:T(128)} %pad_add_fusion.place_ref, ...), custom_call_target="tpu_custom_call" | custom-call | tf_op jit(solution)/shard_map/select_rows/pallas_call | solution.py:83
  25.6 7.1 %all-to-all-start = ((bf16[16,2,4,2560]{3,2,1,0:T(4,128)(2,1)}), bf16[16,2,4,2560]{3,2,1,0:T(4,128)(2,1)S(1)}, u32[]{:S(2)}, u32[]{:S(2)}) async-start(bf16[16,2,4,2560]{3,2,1,0:T(4,128)(2,1)} %broadcast_in_dim.10), calls=%async_computation | async-start | bytes 1310720 | tf_op jit(solution)/shard_map/all_to_all | solution.py:242
  32.7 2.7 %collective-permute-start.1 = (bf16[176,256]{1,0:T(8,128)(2,1)}, bf16[176,256]{1,0:T(8,128)(2,1)S(1)}, u32[]{:S(2)}, u32[]{:S(2)}) collective-permute-start(bf16[176,256]{1,0:T(8,128)(2,1)} %get-tuple-element.54), channel_id=1, source_target_pairs={{0,64},{32,96},{64,0},{96,32},{128,192},{160,224},{192,128},{224,1... | collective-permute-start | bytes 270344 | tf_op jit(solution)/shard_map/ppermute | solution.py:233
  35.4 4.0 %collective-permute-start.4 = (bf16[176,256]{1,0:T(8,128)(2,1)}, bf16[176,256]{1,0:T(8,128)(2,1)S(1)}, u32[]{:S(2)}, u32[]{:S(2)}) collective-permute-start(bf16[176,256]{1,0:T(8,128)(2,1)} %get-tuple-element.57), channel_id=1, source_target_pairs={{0,256},{32,288},{64,320},{96,352},{128,384},{160,416},{192,448},{... | collective-permute-start | bytes 270344 | tf_op jit(solution)/shard_map/ppermute | solution.py:233
  39.5 4.7 %collective-permute-start.5 = (bf16[176,256]{1,0:T(8,128)(2,1)}, bf16[176,256]{1,0:T(8,128)(2,1)S(1)}, u32[]{:S(2)}, u32[]{:S(2)}) collective-permute-start(bf16[176,256]{1,0:T(8,128)(2,1)} %get-tuple-element.58), channel_id=1, source_target_pairs={{0,320},{32,352},{64,256},{96,288},{128,448},{160,480},{192,384},{... | collective-permute-start | bytes 270344 | tf_op jit(solution)/shard_map/ppermute | solution.py:233
  44.2 4.0 %collective-permute-start.6 = (bf16[176,256]{1,0:T(8,128)(2,1)}, bf16[176,256]{1,0:T(8,128)(2,1)S(1)}, u32[]{:S(2)}, u32[]{:S(2)}) collective-permute-start(bf16[176,256]{1,0:T(8,128)(2,1)} %get-tuple-element.59), channel_id=1, source_target_pairs={{0,384},{32,416},{64,448},{96,480},{128,256},{160,288},{192,320},{... | collective-permute-start | bytes 270344 | tf_op jit(solution)/shard_map/ppermute | solution.py:233
  50.2 5.0 %collective-permute-start.2 = (bf16[176,256]{1,0:T(8,128)(2,1)}, bf16[176,256]{1,0:T(8,128)(2,1)S(1)}, u32[]{:S(2)}, u32[]{:S(2)}) collective-permute-start(bf16[176,256]{1,0:T(8,128)(2,1)} %get-tuple-element.55), channel_id=1, source_target_pairs={{0,128},{32,160},{64,192},{96,224},{128,0},{160,32},{192,64},{224,... | collective-permute-start | bytes 270344 | tf_op jit(solution)/shard_map/ppermute | solution.py:233
  56.0 10.7 %all-to-all-start.1 = ((bf16[32,4,120]{2,1,0:T(4,128)(2,1)}), bf16[32,4,120]{2,1,0:T(4,128)(2,1)S(1)}, u32[]{:S(2)}, u32[]{:S(2)}) async-start(bf16[32,4,120]{2,1,0:T(4,128)(2,1)} %pad_maximum_fusion.1), calls=%async_computation.1 | async-start | bytes 65536 | tf_op jit(solution)/shard_map/all_to_all | solution.py:254
  70.7 3.7 %collective-permute-done.3.refs_3_ = bf16[176,256]{1,0:T(8,128)(2,1)S(1)} collective-permute-done((bf16[176,256]{1,0:T(8,128)(2,1)}, bf16[176,256]{1,0:T(8,128)(2,1)S(1)}, u32[]{:S(2)}, u32[]{:S(2)}) %collective-permute-start.3) | collective-permute-done | bytes 90144 | tf_op jit(solution)/shard_map/ppermute | solution.py:233
  76.5 7.0 %collective-permute-start.8 = (bf16[8,176,256]{2,1,0:T(8,128)(2,1)S(1)}, bf16[8,176,256]{2,1,0:T(8,128)(2,1)S(1)}, u32[]{:S(2)}, u32[]{:S(2)}) collective-permute-start(bf16[8,176,256]{2,1,0:T(8,128)(2,1)S(1)} %bitcast_dynamic-update-slice_fusion), channel_id=1, source_target_pairs={{0,32},{32,0},{64,96},{96,64},{128,160},{160,128},{192,224},{224,1... | collective-permute-start | bytes 2162696 | tf_op jit(solution)/shard_map/ppermute | solution.py:266
  84.1 9.6 %collective-permute-start.13 = (bf16[2,32,1280]{2,1,0:T(8,128)(2,1)}, bf16[2,32,1280]{2,1,0:T(8,128)(2,1)S(1)}, u32[]{:S(2)}, u32[]{:S(2)}) collective-permute-start(bf16[2,32,1280]{2,1,0:T(8,128)(2,1)} %get-tuple-element.66), channel_id=1, source_target_pairs={{0,256},{32,288},{64,320},{96,352},{128,384},{160,416},{192,448},{... | collective-permute-start | bytes 491528 | tf_op jit(solution)/shard_map/ppermute | solution.py:235
  94.9 6.8 %all-to-all-start.2 = ((bf16[16,2,4,160]{3,1,2,0:T(2,128)(2,1)}), bf16[16,2,4,160]{3,1,2,0:T(2,128)(2,1)S(1)}, u32[]{:S(2)}, u32[]{:S(2)}) async-start(bf16[16,2,4,160]{3,1,2,0:T(2,128)(2,1)} %copy.24), calls=%async_computation.2 | async-start | bytes 131072 | tf_op jit(solution)/shard_map/all_to_all | solution.py:263
  101.6 2.2 %collective-permute-start.11 = (bf16[2,32,1280]{2,1,0:T(8,128)(2,1)}, bf16[2,32,1280]{2,1,0:T(8,128)(2,1)S(1)}, u32[]{:S(2)}, u32[]{:S(2)}) collective-permute-start(bf16[2,32,1280]{2,1,0:T(8,128)(2,1)} %get-tuple-element.64), channel_id=1, source_target_pairs={{0,128},{32,160},{64,192},{96,224},{128,0},{160,32},{192,64},{224,... | collective-permute-start | bytes 491528 | tf_op jit(solution)/shard_map/ppermute | solution.py:235
  103.8 6.1 %collective-permute-start.14 = (bf16[2,32,1280]{2,1,0:T(8,128)(2,1)}, bf16[2,32,1280]{2,1,0:T(8,128)(2,1)S(1)}, u32[]{:S(2)}, u32[]{:S(2)}) collective-permute-start(bf16[2,32,1280]{2,1,0:T(8,128)(2,1)} %get-tuple-element.67), channel_id=1, source_target_pairs={{0,320},{32,352},{64,256},{96,288},{128,448},{160,480},{192,384},{... | collective-permute-start | bytes 491528 | tf_op jit(solution)/shard_map/ppermute | solution.py:235
  112.6 3.4 %attend.1 = bf16[80,128]{1,0:T(8,128)(2,1)} custom-call(bf16[2,64,160]{2,1,0:T(8,128)(2,1)} %copy.27.own_ref, bf16[176,256]{1,0:T(8,128)(2,1)} %get-tuple-element.53.refs_0_, bf16[176,256]{1,0:T(8,128)(2,1)} %copy-done.12, bf16[176,256]{1,0:T(8,128)(2,1)} %copy-done.16, bf16[176,256]{1,0:T(8,128)(2,1)} %copy-done.17, bf16[176,256]{1,0:T(8,128)(2,1)} %copy-done.13, ...), custom_call_target="tpu_custom_call" | custom-call | tf_op jit(solution)/shard_map/attend/pallas_call | solution.py:173
  116.0 5.4 %collective-permute-start.12 = (bf16[2,32,1280]{2,1,0:T(8,128)(2,1)}, bf16[2,32,1280]{2,1,0:T(8,128)(2,1)S(1)}, u32[]{:S(2)}, u32[]{:S(2)}) collective-permute-start(bf16[2,32,1280]{2,1,0:T(8,128)(2,1)} %get-tuple-element.65), channel_id=1, source_target_pairs={{0,192},{32,224},{64,128},{96,160},{128,64},{160,96},{192,0},{224,... | collective-permute-start | bytes 491528 | tf_op jit(solution)/shard_map/ppermute | solution.py:235
  123.9 6.2 %all-to-all-start.3 = ((bf16[8,80,128]{2,1,0:T(8,128)(2,1)}), bf16[8,80,128]{2,1,0:T(8,128)(2,1)S(1)}, u32[]{:S(2)}, u32[]{:S(2)}) async-start(bf16[8,80,128]{2,1,0:T(8,128)(2,1)} %broadcast_in_dim.13), calls=%async_computation.3 | async-start | bytes 327680 | tf_op jit(solution)/shard_map/all_to_all | solution.py:269
  130.2 5.2 %collective-permute-start.15 = (bf16[2,32,1280]{2,1,0:T(8,128)(2,1)S(1)}, bf16[2,32,1280]{2,1,0:T(8,128)(2,1)S(1)}, u32[]{:S(2)}, u32[]{:S(2)}) collective-permute-start(bf16[2,32,1280]{2,1,0:T(8,128)(2,1)S(1)} %copy-done.22), channel_id=1, source_target_pairs={{0,384},{32,416},{64,448},{96,480},{128,256},{160,288},{192,320},{... | collective-permute-start | bytes 491528 | tf_op jit(solution)/shard_map/ppermute | solution.py:235
  139.4 22.7 %collective-permute-done.15.refs_6_ = bf16[2,32,1280]{2,1,0:T(8,128)(2,1)S(1)} collective-permute-done((bf16[2,32,1280]{2,1,0:T(8,128)(2,1)S(1)}, bf16[2,32,1280]{2,1,0:T(8,128)(2,1)S(1)}, u32[]{:S(2)}, u32[]{:S(2)}) %collective-permute-start.15) | collective-permute-done | bytes 163872 | tf_op jit(solution)/shard_map/ppermute | solution.py:235
  162.8 5.8 %collective-permute-done.16.refs_7_ = bf16[2,32,1280]{2,1,0:T(8,128)(2,1)S(1)} collective-permute-done((bf16[2,32,1280]{2,1,0:T(8,128)(2,1)S(1)}, bf16[2,32,1280]{2,1,0:T(8,128)(2,1)S(1)}, u32[]{:S(2)}, u32[]{:S(2)}) %collective-permute-start.16) | collective-permute-done | bytes 163872 | tf_op jit(solution)/shard_map/ppermute | solution.py:235
  169.2 3.1 %collective-permute-start.17 = (bf16[8,32,1280]{2,1,0:T(8,128)(2,1)}, bf16[8,32,1280]{2,1,0:T(8,128)(2,1)S(1)}, u32[]{:S(2)}, u32[]{:S(2)}) collective-permute-start(bf16[8,32,1280]{2,1,0:T(8,128)(2,1)} %slice_dynamic-update-slice_fusion), channel_id=1, source_target_pairs={{0,32},{32,0},{64,96},{96,64},{128,160},{160,128},{192,224},{224,1... | collective-permute-start | bytes 1966088 | tf_op jit(solution)/shard_map/ppermute | solution.py:279
  176.3 2.2 %assemble.1 = bf16[64,2560]{1,0:T(8,128)(2,1)} custom-call(s32[1]{0:T(128)} %bitcast.core_ref, bf16[8,80,128]{2,1,0:T(8,128)(2,1)} %copy-done.2, bf16[8,80,128]{2,1,0:T(8,128)(2,1)} %copy-done.20), custom_call_target="tpu_custom_call" | custom-call | tf_op jit(solution)/shard_map/assemble/pallas_call | solution.py:198
  179.4 2.8 %place_pages.1 = bf16[16,32,1280]{2,1,0:T(8,128)(2,1)} custom-call(s32[2]{0:T(128)} %pad_add_fusion.place_ref, bf16[2,32,1280]{2,1,0:T(8,128)(2,1)} %get-tuple-element.62.refs_0_, bf16[2,32,1280]{2,1,0:T(8,128)(2,1)} %copy-done.5, bf16[2,32,1280]{2,1,0:T(8,128)(2,1)} %copy-done.7, bf16[2,32,1280]{2,1,0:T(8,128)(2,1)} %copy-done.9, ...), custom_call_target="tpu_custom_call" | custom-call | tf_op jit(solution)/shard_map/place_pages/pallas_call | solution.py:122
  (110 shorter events, 29.1 us)
Async XLA Ops:
  2.5 22.0 %collective-permute-start = (bf16[4,2560]{1,0:T(4,128)(2,1)S(1)}, bf16[4,2560]{1,0:T(4,128)(2,1)S(1)}, u32[]{:S(2)}, u32[]{:S(2)}) collective-permute-start(bf16[4,2560]{1,0:T(4,128)(2,1)S(1)} %fusion.2), channel_id=1, source_target_pairs={{0,1},{1,0},{2,3},{3,2},{4,5},{5,4},{6,7},{7,6},{8,9},{9,8},{10,11... | collective-permute-start | bytes 61448 | tf_op jit(solution)/shard_map/ppermute | solution.py:223
  25.6 23.5 %all-to-all-start = ((bf16[16,2,4,2560]{3,2,1,0:T(4,128)(2,1)}), bf16[16,2,4,2560]{3,2,1,0:T(4,128)(2,1)S(1)}, u32[]{:S(2)}, u32[]{:S(2)}) async-start(bf16[16,2,4,2560]{3,2,1,0:T(4,128)(2,1)} %broadcast_in_dim.10), calls=%async_computation | async-start | bytes 1310720 | tf_op jit(solution)/shard_map/all_to_all | solution.py:242
  32.7 16.4 %collective-permute-start.1 = (bf16[176,256]{1,0:T(8,128)(2,1)}, bf16[176,256]{1,0:T(8,128)(2,1)S(1)}, u32[]{:S(2)}, u32[]{:S(2)}) collective-permute-start(bf16[176,256]{1,0:T(8,128)(2,1)} %get-tuple-element.54), channel_id=1, source_target_pairs={{0,64},{32,96},{64,0},{96,32},{128,192},{160,224},{192,128},{224,1... | collective-permute-start | bytes 270344 | tf_op jit(solution)/shard_map/ppermute | solution.py:233
  35.4 40.9 %collective-permute-start.4 = (bf16[176,256]{1,0:T(8,128)(2,1)}, bf16[176,256]{1,0:T(8,128)(2,1)S(1)}, u32[]{:S(2)}, u32[]{:S(2)}) collective-permute-start(bf16[176,256]{1,0:T(8,128)(2,1)} %get-tuple-element.57), channel_id=1, source_target_pairs={{0,256},{32,288},{64,320},{96,352},{128,384},{160,416},{192,448},{... | collective-permute-start | bytes 270344 | tf_op jit(solution)/shard_map/ppermute | solution.py:233
  39.5 36.9 %collective-permute-start.5 = (bf16[176,256]{1,0:T(8,128)(2,1)}, bf16[176,256]{1,0:T(8,128)(2,1)S(1)}, u32[]{:S(2)}, u32[]{:S(2)}) collective-permute-start(bf16[176,256]{1,0:T(8,128)(2,1)} %get-tuple-element.58), channel_id=1, source_target_pairs={{0,320},{32,352},{64,256},{96,288},{128,448},{160,480},{192,384},{... | collective-permute-start | bytes 270344 | tf_op jit(solution)/shard_map/ppermute | solution.py:233
  44.2 32.2 %collective-permute-start.6 = (bf16[176,256]{1,0:T(8,128)(2,1)}, bf16[176,256]{1,0:T(8,128)(2,1)S(1)}, u32[]{:S(2)}, u32[]{:S(2)}) collective-permute-start(bf16[176,256]{1,0:T(8,128)(2,1)} %get-tuple-element.59), channel_id=1, source_target_pairs={{0,384},{32,416},{64,448},{96,480},{128,256},{160,288},{192,320},{... | collective-permute-start | bytes 270344 | tf_op jit(solution)/shard_map/ppermute | solution.py:233
  50.1 80.1 %copy-start.22 = (bf16[2,32,1280]{2,1,0:T(8,128)(2,1)S(1)}, bf16[2,32,1280]{2,1,0:T(8,128)(2,1)}, u32[]{:S(2)}) copy-start(bf16[2,32,1280]{2,1,0:T(8,128)(2,1)} %get-tuple-element.68) | copy-start | bytes 491524
  50.1 85.3 %copy-start.21 = (bf16[2,32,1280]{2,1,0:T(8,128)(2,1)S(1)}, bf16[2,32,1280]{2,1,0:T(8,128)(2,1)}, u32[]{:S(2)}) copy-start(bf16[2,32,1280]{2,1,0:T(8,128)(2,1)} %get-tuple-element.69) | copy-start | bytes 491524
  50.2 18.4 %collective-permute-start.2 = (bf16[176,256]{1,0:T(8,128)(2,1)}, bf16[176,256]{1,0:T(8,128)(2,1)S(1)}, u32[]{:S(2)}, u32[]{:S(2)}) collective-permute-start(bf16[176,256]{1,0:T(8,128)(2,1)} %get-tuple-element.55), channel_id=1, source_target_pairs={{0,128},{32,160},{64,192},{96,224},{128,0},{160,32},{192,64},{224,... | collective-permute-start | bytes 270344 | tf_op jit(solution)/shard_map/ppermute | solution.py:233
  56.0 37.7 %all-to-all-start.1 = ((bf16[32,4,120]{2,1,0:T(4,128)(2,1)}), bf16[32,4,120]{2,1,0:T(4,128)(2,1)S(1)}, u32[]{:S(2)}, u32[]{:S(2)}) async-start(bf16[32,4,120]{2,1,0:T(4,128)(2,1)} %pad_maximum_fusion.1), calls=%async_computation.1 | async-start | bytes 65536 | tf_op jit(solution)/shard_map/all_to_all | solution.py:254
  66.7 7.7 %collective-permute-start.3 = (bf16[176,256]{1,0:T(8,128)(2,1)}, bf16[176,256]{1,0:T(8,128)(2,1)S(1)}, u32[]{:S(2)}, u32[]{:S(2)}) collective-permute-start(bf16[176,256]{1,0:T(8,128)(2,1)} %get-tuple-element.56), channel_id=1, source_target_pairs={{0,192},{32,224},{64,128},{96,160},{128,64},{160,96},{192,0},{224,... | collective-permute-start | bytes 270344 | tf_op jit(solution)/shard_map/ppermute | solution.py:233
  68.6 7.8 %collective-permute-start.7 = (bf16[176,256]{1,0:T(8,128)(2,1)S(1)}, bf16[176,256]{1,0:T(8,128)(2,1)S(1)}, u32[]{:S(2)}, u32[]{:S(2)}) collective-permute-start(bf16[176,256]{1,0:T(8,128)(2,1)S(1)} %copy-done.23), channel_id=1, source_target_pairs={{0,448},{32,480},{64,384},{96,416},{128,320},{160,352},{192,256},{... | collective-permute-start | bytes 270344 | tf_op jit(solution)/shard_map/ppermute | solution.py:233
  74.4 35.5 %collective-permute-start.10 = (bf16[2,32,1280]{2,1,0:T(8,128)(2,1)}, bf16[2,32,1280]{2,1,0:T(8,128)(2,1)S(1)}, u32[]{:S(2)}, u32[]{:S(2)}) collective-permute-start(bf16[2,32,1280]{2,1,0:T(8,128)(2,1)} %get-tuple-element.63), channel_id=1, source_target_pairs={{0,64},{32,96},{64,0},{96,32},{128,192},{160,224},{192,128},{224,1... | collective-permute-start | bytes 491528 | tf_op jit(solution)/shard_map/ppermute | solution.py:235
  76.5 35.2 %collective-permute-start.8 = (bf16[8,176,256]{2,1,0:T(8,128)(2,1)S(1)}, bf16[8,176,256]{2,1,0:T(8,128)(2,1)S(1)}, u32[]{:S(2)}, u32[]{:S(2)}) collective-permute-start(bf16[8,176,256]{2,1,0:T(8,128)(2,1)S(1)} %bitcast_dynamic-update-slice_fusion), channel_id=1, source_target_pairs={{0,32},{32,0},{64,96},{96,64},{128,160},{160,128},{192,224},{224,1... | collective-permute-start | bytes 2162696 | tf_op jit(solution)/shard_map/ppermute | solution.py:266
  84.1 53.9 %collective-permute-start.13 = (bf16[2,32,1280]{2,1,0:T(8,128)(2,1)}, bf16[2,32,1280]{2,1,0:T(8,128)(2,1)S(1)}, u32[]{:S(2)}, u32[]{:S(2)}) collective-permute-start(bf16[2,32,1280]{2,1,0:T(8,128)(2,1)} %get-tuple-element.66), channel_id=1, source_target_pairs={{0,256},{32,288},{64,320},{96,352},{128,384},{160,416},{192,448},{... | collective-permute-start | bytes 491528 | tf_op jit(solution)/shard_map/ppermute | solution.py:235
  94.9 16.2 %all-to-all-start.2 = ((bf16[16,2,4,160]{3,1,2,0:T(2,128)(2,1)}), bf16[16,2,4,160]{3,1,2,0:T(2,128)(2,1)S(1)}, u32[]{:S(2)}, u32[]{:S(2)}) async-start(bf16[16,2,4,160]{3,1,2,0:T(2,128)(2,1)} %copy.24), calls=%async_computation.2 | async-start | bytes 131072 | tf_op jit(solution)/shard_map/all_to_all | solution.py:263
  101.6 20.2 %collective-permute-start.11 = (bf16[2,32,1280]{2,1,0:T(8,128)(2,1)}, bf16[2,32,1280]{2,1,0:T(8,128)(2,1)S(1)}, u32[]{:S(2)}, u32[]{:S(2)}) collective-permute-start(bf16[2,32,1280]{2,1,0:T(8,128)(2,1)} %get-tuple-element.64), channel_id=1, source_target_pairs={{0,128},{32,160},{64,192},{96,224},{128,0},{160,32},{192,64},{224,... | collective-permute-start | bytes 491528 | tf_op jit(solution)/shard_map/ppermute | solution.py:235
  103.8 34.9 %collective-permute-start.14 = (bf16[2,32,1280]{2,1,0:T(8,128)(2,1)}, bf16[2,32,1280]{2,1,0:T(8,128)(2,1)S(1)}, u32[]{:S(2)}, u32[]{:S(2)}) collective-permute-start(bf16[2,32,1280]{2,1,0:T(8,128)(2,1)} %get-tuple-element.67), channel_id=1, source_target_pairs={{0,320},{32,352},{64,256},{96,288},{128,448},{160,480},{192,384},{... | collective-permute-start | bytes 491528 | tf_op jit(solution)/shard_map/ppermute | solution.py:235
  116.0 21.3 %collective-permute-start.12 = (bf16[2,32,1280]{2,1,0:T(8,128)(2,1)}, bf16[2,32,1280]{2,1,0:T(8,128)(2,1)S(1)}, u32[]{:S(2)}, u32[]{:S(2)}) collective-permute-start(bf16[2,32,1280]{2,1,0:T(8,128)(2,1)} %get-tuple-element.65), channel_id=1, source_target_pairs={{0,192},{32,224},{64,128},{96,160},{128,64},{160,96},{192,0},{224,... | collective-permute-start | bytes 491528 | tf_op jit(solution)/shard_map/ppermute | solution.py:235
  123.9 48.4 %all-to-all-start.3 = ((bf16[8,80,128]{2,1,0:T(8,128)(2,1)}), bf16[8,80,128]{2,1,0:T(8,128)(2,1)S(1)}, u32[]{:S(2)}, u32[]{:S(2)}) async-start(bf16[8,80,128]{2,1,0:T(8,128)(2,1)} %broadcast_in_dim.13), calls=%async_computation.3 | async-start | bytes 327680 | tf_op jit(solution)/shard_map/all_to_all | solution.py:269
  130.2 31.9 %collective-permute-start.15 = (bf16[2,32,1280]{2,1,0:T(8,128)(2,1)S(1)}, bf16[2,32,1280]{2,1,0:T(8,128)(2,1)S(1)}, u32[]{:S(2)}, u32[]{:S(2)}) collective-permute-start(bf16[2,32,1280]{2,1,0:T(8,128)(2,1)S(1)} %copy-done.22), channel_id=1, source_target_pairs={{0,384},{32,416},{64,448},{96,480},{128,256},{160,288},{192,320},{... | collective-permute-start | bytes 491528 | tf_op jit(solution)/shard_map/ppermute | solution.py:235
  135.4 33.2 %collective-permute-start.16 = (bf16[2,32,1280]{2,1,0:T(8,128)(2,1)S(1)}, bf16[2,32,1280]{2,1,0:T(8,128)(2,1)S(1)}, u32[]{:S(2)}, u32[]{:S(2)}) collective-permute-start(bf16[2,32,1280]{2,1,0:T(8,128)(2,1)S(1)} %copy-done.21), channel_id=1, source_target_pairs={{0,448},{32,480},{64,384},{96,416},{128,320},{160,352},{192,256},{... | collective-permute-start | bytes 491528 | tf_op jit(solution)/shard_map/ppermute | solution.py:235
  169.2 9.3 %collective-permute-start.17 = (bf16[8,32,1280]{2,1,0:T(8,128)(2,1)}, bf16[8,32,1280]{2,1,0:T(8,128)(2,1)S(1)}, u32[]{:S(2)}, u32[]{:S(2)}) collective-permute-start(bf16[8,32,1280]{2,1,0:T(8,128)(2,1)} %slice_dynamic-update-slice_fusion), channel_id=1, source_target_pairs={{0,32},{32,0},{64,96},{96,64},{128,160},{160,128},{192,224},{224,1... | collective-permute-start | bytes 1966088 | tf_op jit(solution)/shard_map/ppermute | solution.py:279
  172.4 3.3 %collective-permute-start.9 = (bf16[8,80,128]{2,1,0:T(8,128)(2,1)S(1)}, bf16[8,80,128]{2,1,0:T(8,128)(2,1)S(1)}, u32[]{:S(2)}, u32[]{:S(2)}) collective-permute-start(bf16[8,80,128]{2,1,0:T(8,128)(2,1)S(1)} %all-to-all-done.3.near_ref), channel_id=1, source_target_pairs={{0,32},{32,0},{64,96},{96,64},{128,160},{160,128},{192,224},{224,1... | collective-permute-start | bytes 491528 | tf_op jit(solution)/shard_map/ppermute | solution.py:277
  (22 other events, 721.1 us)

commit v3 on v1

v3 whole, which is shorter than its diff:
```python
import jax
import jax.numpy as jnp
from jax import lax
from jax.experimental import pallas as pl
from jax.experimental.pallas import tpu as pltpu
from jax.sharding import PartitionSpec as P

HEADS = 32
KV_HEADS = 8
REPEAT = HEADS // KV_HEADS
HEAD_DIM = 80
KEYS = KV_HEADS * HEAD_DIM
QUERIES = HEADS * HEAD_DIM
EPSILON = 1e-05
NEGATIVE = -1e30

PLANE = 16
HOLDERS = 16
SOURCES = 8
KEEP = 32
EXTRA = 256

PLANE_GROUPS = [[2 * i + half for i in range(PLANE)] for half in range(2)]
OTHER_HALF = [
    (p * 2 * PLANE + t, (p ^ 8) * 2 * PLANE + (t ^ 1)) for p in range(HOLDERS) for t in range(2 * PLANE)
]

VMEM = pl.BlockSpec(memory_space=pltpu.VMEM)
SMEM = pl.BlockSpec(memory_space=pltpu.SMEM)


def select_kernel(count_ref, dest_ref, keep_ref, page_ref, out_ref, kept_ref):
    slot = pl.program_id(0)

    @pl.when(slot == 0)
    def _():
        out_ref[...] = jnp.zeros_like(out_ref)

    rows = page_ref.shape[1]
    picks = jnp.broadcast_to(keep_ref[0], (rows, KEEP))
    chosen = (picks == lax.broadcasted_iota(jnp.int32, (rows, KEEP), 0)).astype(jnp.float32)
    kept = jnp.dot(
        chosen.T.astype(jnp.bfloat16), page_ref[0], preferred_element_type=jnp.float32
    ).astype(jnp.bfloat16)
    kept_ref[...] = kept

    @pl.when(slot < count_ref[0])
    def _():
        out_ref[dest_ref[slot]] = kept


def select_rows(page_count, dest_slot, keep_rows, cache):
    sources, _, rows, width = cache.shape
    return pl.pallas_call(
        select_kernel,
        out_shape=(
            jax.ShapeDtypeStruct((HOLDERS, KEEP, width), cache.dtype),
            jax.ShapeDtypeStruct((sources * KEEP, width), cache.dtype),
        ),
        grid_spec=pltpu.PrefetchScalarGridSpec(
            num_scalar_prefetch=2,
            grid=(sources,),
            in_specs=[
                pl.BlockSpec((1, 1, KEEP), lambda s, *_: (s, 0, 0)),
                pl.BlockSpec((1, rows, width), lambda s, *_: (s, 0, 0)),
            ],
            out_specs=[
                pl.BlockSpec((HOLDERS, KEEP, width), lambda s, *_: (0, 0, 0)),
                pl.BlockSpec((KEEP, width), lambda s, *_: (s, 0)),
            ],
        ),
        name="select_rows",
    )(page_count, dest_slot, keep_rows, cache.reshape(sources, rows, width))


def arrange_kernel(back_ref, out_ref):
    half = HEAD_DIM // 2
    for h in range(HEADS):
        at = (h % REPEAT * KV_HEADS + h // REPEAT) * HEAD_DIM
        out_ref[:, at : at + HEAD_DIM] = back_ref[h, :, :HEAD_DIM]
        at = QUERIES + h * half
        out_ref[:, at : at + half] = back_ref[h, :, HEAD_DIM:]


def arrange(back):
    return pl.pallas_call(
        arrange_kernel,
        out_shape=jax.ShapeDtypeStruct((back.shape[1], QUERIES + 2 * KEYS), back.dtype),
        in_specs=[VMEM],
        out_specs=VMEM,
        name="arrange",
    )(back)


def pieces(value, count):
    parts = []
    for _ in range(count):
        part = value.astype(jnp.bfloat16)
        parts.append(part)
        value = value - part.astype(jnp.float32)
    return parts


def attend_kernel(count_ref, owner_ref, kept_ref, rows_ref, out_ref, sum_ref, peak_ref, total_ref):
    scale = HEAD_DIM ** (-0.5)
    requests = rows_ref.shape[0]
    slot = lax.broadcasted_iota(jnp.int32, (SOURCES, requests), 0)
    owner = jnp.zeros((SOURCES, requests), jnp.int32)
    for s in range(SOURCES):
        owner = jnp.where(slot == s, owner_ref[s], owner)
    picked = (owner == lax.broadcasted_iota(jnp.int32, (SOURCES, requests), 1)).astype(jnp.float32)
    query = jnp.dot(
        picked.astype(jnp.bfloat16), rows_ref[:, :QUERIES], preferred_element_type=jnp.float32
    )
    head = lax.broadcasted_iota(jnp.int32, (KV_HEADS, KEYS), 0) * HEAD_DIM
    lane = lax.broadcasted_iota(jnp.int32, (KV_HEADS, KEYS), 1)
    mask = ((lane >= head) & (lane < head + HEAD_DIM)).astype(jnp.float32)
    for s in range(SOURCES):
        spread = jnp.concatenate(
            [query[s : s + 1, k * KEYS : (k + 1) * KEYS] * mask for k in range(REPEAT)], axis=0
        ).astype(jnp.bfloat16)
        keys = kept_ref[s * KEEP : (s + 1) * KEEP, :KEYS]
        values = kept_ref[s * KEEP : (s + 1) * KEEP, KEYS:]
        score = scale * lax.dot_general(
            keys, spread, (((1,), (1,)), ((), ())), preferred_element_type=jnp.float32
        )
        peak = jnp.max(score, axis=0, keepdims=True)
        weight = jnp.exp(score - peak)
        total_ref[s : s + 1, :] = jnp.sum(weight, axis=0, keepdims=True)
        peak_ref[s : s + 1, :] = jnp.where(s < count_ref[0], peak, NEGATIVE)
        mixed = lax.dot_general(
            weight.astype(jnp.bfloat16),
            values,
            (((0,), (0,)), ((), ())),
            preferred_element_type=jnp.float32,
        )
        for k in range(REPEAT):
            sum_ref[s : s + 1, k * KEYS : (k + 1) * KEYS] = jnp.sum(
                mixed[k * KV_HEADS : (k + 1) * KV_HEADS] * mask, axis=0, keepdims=True
            )
    out_ref[:, :QUERIES] = sum_ref[...].astype(jnp.bfloat16)
    slots = lax.broadcasted_iota(jnp.int32, (SOURCES, HEADS), 0)
    tag = jnp.full((SOURCES, HEADS), -1, jnp.int32)
    for s in range(SOURCES):
        tag = jnp.where((slots == s) & (s < count_ref[0]), owner_ref[s], tag)
    tag = tag.astype(jnp.float32).astype(jnp.bfloat16)
    columns = pieces(peak_ref[...], 3) + pieces(total_ref[...], 3) + [tag, tag]
    columns = [column.astype(jnp.float32) for column in columns]
    out_ref[:, QUERIES:] = jnp.concatenate(columns, axis=1).astype(jnp.bfloat16)


def attend(page_count, page_owner, kept, rows):
    return pl.pallas_call(
        attend_kernel,
        out_shape=jax.ShapeDtypeStruct((SOURCES, QUERIES + EXTRA), jnp.bfloat16),
        in_specs=[SMEM, SMEM, VMEM, VMEM],
        out_specs=VMEM,
        scratch_shapes=[
            pltpu.VMEM((SOURCES, QUERIES), jnp.float32),
            pltpu.VMEM((SOURCES, HEADS), jnp.float32),
            pltpu.VMEM((SOURCES, HEADS), jnp.float32),
        ],
        name="attend",
    )(page_count, page_owner, kept, rows)


def spread_dot(value, chosen, contract, count, chosen_first=False):
    total = None
    for part in pieces(value, count):
        operands = (chosen, part) if chosen_first else (part, chosen)
        term = lax.dot_general(
            *operands, (contract, ((), ())), preferred_element_type=jnp.float32
        )
        total = term if total is None else total + term
    return total


def combine_kernel(part_ref, rows_ref, out_ref):
    scale = HEAD_DIM ** (-0.5)
    requests = rows_ref.shape[0]
    slots = part_ref.shape[0]
    extra = part_ref[:, QUERIES:].astype(jnp.float32)
    column = [extra[:, i * HEADS : (i + 1) * HEADS] for i in range(7)]
    peaks = column[0] + column[1] + column[2]
    totals = column[3] + column[4] + column[5]
    tag = column[6][:, :1]
    row = lax.broadcasted_iota(jnp.int32, (requests, 1), 0).astype(jnp.float32)
    member = (
        tag == lax.broadcasted_iota(jnp.int32, (slots, requests), 1).astype(jnp.float32)
    ).astype(jnp.float32).astype(jnp.bfloat16)
    head = lax.broadcasted_iota(jnp.int32, (HEADS, QUERIES), 0) * HEAD_DIM
    lane = lax.broadcasted_iota(jnp.int32, (HEADS, QUERIES), 1)
    expand = ((lane >= head) & (lane < head + HEAD_DIM)).astype(jnp.float32).astype(jnp.bfloat16)

    query = rows_ref[:, :QUERIES].astype(jnp.float32)
    key = rows_ref[:, QUERIES : QUERIES + KEYS].astype(jnp.float32)
    value = rows_ref[:, QUERIES + KEYS :].astype(jnp.float32)
    product = query * jnp.concatenate([key] * REPEAT, axis=1)
    own = scale * spread_dot(product, expand, ((1,), (1,)), 3)
    top = own
    for s in range(slots):
        top = jnp.maximum(
            top, jnp.where(tag[s : s + 1] == row, peaks[s : s + 1], NEGATIVE)
        )
    own_weight = jnp.exp(own - top)
    weight = jnp.exp(peaks - spread_dot(top, member, ((1,), (0,)), 3, True))
    total = spread_dot(weight * totals, member, ((0,), (0,)), 3, True) + own_weight
    inverse = 1.0 / total
    weight = weight * spread_dot(inverse, member, ((1,), (0,)), 3, True)
    scaled = part_ref[:, :QUERIES].astype(jnp.float32) * spread_dot(
        weight, expand, ((1,), (0,)), 2
    )
    mixed = spread_dot(scaled, member, ((0,), (0,)), 2, True)
    own_share = spread_dot(own_weight * inverse, expand, ((1,), (0,)), 2)
    mixed = (mixed + own_share * jnp.concatenate([value] * REPEAT, axis=1)).astype(jnp.bfloat16)
    for h in range(HEADS):
        at = (h % REPEAT * KV_HEADS + h // REPEAT) * HEAD_DIM
        out_ref[:, h * HEAD_DIM : (h + 1) * HEAD_DIM] = mixed[:, at : at + HEAD_DIM]


def combine(parts, rows):
    return pl.pallas_call(
        combine_kernel,
        out_shape=jax.ShapeDtypeStruct((rows.shape[0], QUERIES), jnp.bfloat16),
        in_specs=[VMEM] * 2,
        out_specs=VMEM,
        compiler_params=pltpu.CompilerParams(vmem_limit_bytes=48 * 1024 * 1024),
        name="combine",
    )(parts, rows)


def per_device(
    tokens, norm_gain, w_query, w_keyvalue, cache, page_count, page_owner, keep_rows, dest_slot
):
    groups = lax.axis_size("tensor")
    holder = lax.axis_index("page")
    half = lax.axis_index("tensor") % 2
    share = tokens.shape[0] // HOLDERS

    def normalise(rows):
        widened = rows.astype(jnp.float32)
        return (
            widened
            * lax.rsqrt(jnp.mean(widened * widened, axis=-1, keepdims=True) + EPSILON)
            * norm_gain
        ).astype(jnp.bfloat16)

    theirs = lax.dynamic_slice_in_dim(tokens, (holder ^ 8) * share, share, 0)
    across = lax.ppermute(normalise(theirs), ("page", "tensor"), OTHER_HALF)
    mine = normalise(lax.dynamic_slice_in_dim(tokens, holder * share, share, 0))

    page_count = page_count.reshape(1)
    page_owner = page_owner.reshape(SOURCES)
    compact, kept = select_rows(page_count, dest_slot.reshape(SOURCES), keep_rows, cache)

    both = jnp.where(half == 0, jnp.stack([mine, across]), jnp.stack([across, mine]))
    rows = lax.all_to_all(
        jnp.broadcast_to(both[None], (PLANE,) + both.shape),
        "tensor",
        0,
        0,
        axis_index_groups=PLANE_GROUPS,
        tiled=True,
    ).reshape(groups * share, -1)
    query_part = jnp.dot(rows, w_query, preferred_element_type=jnp.float32)
    pair_part = jnp.dot(rows, w_keyvalue, preferred_element_type=jnp.float32)
    projected = jnp.concatenate([query_part, pair_part], axis=1).astype(jnp.bfloat16)
    back = lax.all_to_all(
        projected.reshape(groups, share, -1), "tensor", 0, 0, tiled=True
    )
    back, compact = lax.optimization_barrier((back, compact))
    arrived = lax.all_to_all(compact, "page", 0, 0, tiled=True)
    own_rows = lax.all_gather(arrange(back), "page", axis=0, tiled=True)
    part = attend(page_count, page_owner, kept, own_rows)
    parts = lax.all_gather(part, "page", axis=0, tiled=True)
    return combine(parts, own_rows), arrived[:, None]


def solution(mesh):
    return jax.shard_map(
        per_device,
        mesh=mesh,
        in_specs=(
            P("tensor", None),
            P(),
            P(None, "tensor"),
            P(None, "tensor"),
            P("page", "tensor", None, None),
            P("page", "tensor"),
            P("page", "tensor"),
            P("page", "tensor", None),
            P("page", "tensor"),
        ),
        out_specs=(P("tensor", None), P("page", "tensor", None, None)),
        check_vma=False,
    )
```

time: 217 us -> 191 us (0.88)
  the two profiles are of different devices: /device:TPU:65 before, /device:TPU:1 now
where the time goes in v3:
time: 191 us; the launch traced here: 190 us
  blocking collectives  122 us (64%)
  starting transfers between devices  34.3 us (18%)
  Pallas kernels  16.9 us (9%)
  waiting for transfers between devices  8.94 us (5%)
  local copies, waits for them, and re-layouts  3.91 us (2%)
  other arithmetic  2.69 us (1%)
    all_gather x1, blocking collectives, per_device(): own_rows = lax.all_gather(arrange(back), 'page', axis=0, tiled=True)  63.5 us
    all_gather x1, blocking collectives, per_device(): parts = lax.all_gather(part, 'page', axis=0, tiled=True)  40.9 us
    all_to_all x1, blocking collectives, per_device(): lax.all_to_all(jnp.broadcast_to(both[None], (PLANE,) + both.shape), 'tens...  17.3 us
    ppermute x1, starting transfers between devices, per_device(): across = lax.ppermute(normalise(theirs), ('page', 'tensor'), OTHER_HALF)  13.3 us
    all_to_all x1, starting transfers between devices, per_device(): lax.all_to_all(projected.reshape(groups, share, -1), 'tensor', 0, 0, tile...  11.9 us
    all_to_all x1, starting transfers between devices, per_device(): arrived = lax.all_to_all(compact, 'page', 0, 0, tiled=True)  9.04 us
    all_to_all x1, waiting for transfers between devices, per_device(): lax.all_to_all(projected.reshape(groups, share, -1), 'tensor', 0, 0, tile...  7.68 us
    pallas_call x1, Pallas kernels, select_rows(): pl.pallas_call(select_kernel, out_shape=(jax.ShapeDtypeStruct((HOLDERS, K...  7.5 us
  transfers between devices with their start and end apart: 3, of which 2 were waited for; matrix products, arithmetic and copies ran while one was open for 0% of the time, Pallas kernels for 9%

profile of v3, /device:TPU:1, one launch (start us, length us, event | category | flops | bytes accessed | tf_op | source)
XLA Modules:
  0.0 190.5 jit_solution(5274776708239074835)
XLA Ops:
  0.7 1.0 fusion.4
  1.7 0.9 fusion.10
  2.6 13.3 %collective-permute-start = (bf16[4,2560]{1,0:T(4,128)(2,1)S(1)}, bf16[4,2560]{1,0:T(4,128)(2,1)S(1)}, u32[]{:S(2)}, u32[]{:S(2)}) collective-permute-start(bf16[4,2560]{1,0:T(4,128)(2,1)S(1)} %get-tuple-element.17), channel_id=1, source_target_pairs={{0,257},{1,256},{2,259},{3,258},{4,261},{5,260},{6,263},{7,262},{8... | collective-permute-start | bytes 61448 | tf_op jit(solution)/shard_map/ppermute | solution.py:249
  15.9 1.2 collective-permute-done
  17.2 0.3 broadcast_in_dim.4
  17.6 17.3 %all_to_all.15 = bf16[16,2,4,2560]{3,1,2,0:T(2,128)(2,1)S(1)} all-to-all(bf16[16,2,4,2560]{3,1,2,0:T(2,128)(2,1)S(1)} %broadcast_in_dim.4), channel_id=1, replica_groups={{0,2,4,6,8,10,12,14,16,18,20,22,24,26,28,30},{1,3,5,7,9,11,13,15,17,19,..., dimensions={0} | all-to-all | bytes 1310720 | tf_op jit(solution)/shard_map/all_to_all | solution.py:257
  34.9 0.5 copy.16
  35.4 0.2 dot_general.8
  35.6 0.2 copy-done.2
  35.8 0.3 fusion.2
  36.2 0.3 fusion
  36.5 0.7 pad_maximum_fusion
  37.2 11.9 %all-to-all-start.1 = ((bf16[32,4,120]{2,1,0:T(4,128)(2,1)}), bf16[32,4,120]{2,1,0:T(4,128)(2,1)S(1)}, u32[]{:S(2)}, u32[]{:S(2)}) async-start(bf16[32,4,120]{2,1,0:T(4,128)(2,1)} %pad_maximum_fusion), calls=%async_computation.1 | async-start | bytes 65536 | tf_op jit(solution)/shard_map/all_to_all | solution.py:268
  49.8 7.5 %select_rows.1 = (bf16[16,32,1280]{2,1,0:T(8,128)(2,1)}, bf16[256,1280]{1,0:T(8,128)(2,1)}) custom-call(s32[1]{0:T(128)} %bitcast.21.count_ref, s32[8]{0:T(128)} %bitcast.27, s32[8,1,32]{2,1,0:T(1,128)} %keep_ref.1, bf16[8,128,1280]{2,1,0:T(8,128)(2,1)} %bitcast.24), custom_call_target="tpu_custom_call" | custom-call | tf_op jit(solution)/shard_map/select_rows/pallas_call | solution.py:54
  57.3 7.7 %all-to-all-done.1.back_ref = bf16[32,4,120]{2,1,0:T(4,128)(2,1)S(1)} async-done(((bf16[32,4,120]{2,1,0:T(4,128)(2,1)}), bf16[32,4,120]{2,1,0:T(4,128)(2,1)S(1)}, u32[]{:S(2)}, u32[]{:S(2)}) %all-to-all-start.1) | async-done | bytes 30752 | tf_op jit(solution)/shard_map/all_to_all | solution.py:268
  65.0 0.6 copy-done.3
  65.6 9.0 %all-to-all-start.2 = ((bf16[16,32,1280]{2,1,0:T(8,128)(2,1)}), bf16[16,32,1280]{2,1,0:T(8,128)(2,1)S(1)}, u32[]{:S(2)}, u32[]{:S(2)}) async-start(bf16[16,32,1280]{2,1,0:T(8,128)(2,1)} %get-tuple-element.9), calls=%async_computation.2 | async-start | bytes 2621440 | tf_op jit(solution)/shard_map/all_to_all | solution.py:272
  74.7 1.5 arrange.1
  76.2 63.5 %all-gather = bf16[16,4,3840]{2,1,0:T(4,128)(2,1)S(1)} all-gather(bf16[1,4,3840]{2,1,0:T(4,128)(2,1)} %bitcast.25), channel_id=1, replica_groups=mesh['page'=16,'tensor'=32] {'page'}, dimensions={0}, use_global_device_ids=true | all-gather | bytes 522240 | tf_op jit(solution)/shard_map/all_gather | solution.py:273
  139.6 0.9 reshape.79.rows_ref
  140.5 4.0 %attend.1 = bf16[8,2816]{1,0:T(8,128)(2,1)} custom-call(s32[1]{0:T(128)} %bitcast.22.count_ref, s32[8]{0:T(128)} %bitcast.28, bf16[256,1280]{1,0:T(8,128)(2,1)} %get-tuple-element.6.kept_ref, bf16[64,3840]{1,0:T(8,128)(2,1)} %reshape.79.rows_ref), custom_call_target="tpu_custom_call" | custom-call | tf_op jit(solution)/shard_map/attend/pallas_call | solution.py:153
  144.5 40.9 %all_gather.7.part_ref = bf16[128,2816]{1,0:T(8,128)(2,1)S(1)} all-gather(bf16[8,2816]{1,0:T(8,128)(2,1)} %attend.1), channel_id=1, replica_groups=mesh['page'=16,'tensor'=32] {'page'}, dimensions={0}, use_global_device_ids=true | all-gather | bytes 765952 | tf_op jit(solution)/shard_map/all_gather | solution.py:275
  185.5 3.9 %combine.1 = bf16[64,2560]{1,0:T(8,128)(2,1)} custom-call(bf16[128,2816]{1,0:T(8,128)(2,1)S(1)} %all_gather.7.part_ref, bf16[64,3840]{1,0:T(8,128)(2,1)S(1)} %copy-done.1), custom_call_target="tpu_custom_call" | custom-call | tf_op jit(solution)/shard_map/combine/pallas_call | solution.py:222
  189.4 1.1 copy.26
  (12 shorter events, 0.1 us)
Async XLA Ops:
  0.6 35.5 %copy-start = (bf16[2560,80]{0,1:T(8,128)(2,1)S(1)}, bf16[2560,80]{0,1:T(8,128)(2,1)}, u32[]{:S(2)}) copy-start(bf16[2560,80]{0,1:T(8,128)(2,1)} %param.11) | copy-start | bytes 1228804
  2.6 14.6 %collective-permute-start = (bf16[4,2560]{1,0:T(4,128)(2,1)S(1)}, bf16[4,2560]{1,0:T(4,128)(2,1)S(1)}, u32[]{:S(2)}, u32[]{:S(2)}) collective-permute-start(bf16[4,2560]{1,0:T(4,128)(2,1)S(1)} %get-tuple-element.17), channel_id=1, source_target_pairs={{0,257},{1,256},{2,259},{3,258},{4,261},{5,260},{6,263},{7,262},{8... | collective-permute-start | bytes 61448 | tf_op jit(solution)/shard_map/ppermute | solution.py:249
  34.9 0.9 copy-start.2
  37.2 27.8 %all-to-all-start.1 = ((bf16[32,4,120]{2,1,0:T(4,128)(2,1)}), bf16[32,4,120]{2,1,0:T(4,128)(2,1)S(1)}, u32[]{:S(2)}, u32[]{:S(2)}) async-start(bf16[32,4,120]{2,1,0:T(4,128)(2,1)} %pad_maximum_fusion), calls=%async_computation.1 | async-start | bytes 65536 | tf_op jit(solution)/shard_map/all_to_all | solution.py:268
  65.0 0.6 copy-start.3
  65.6 123.8 %all-to-all-start.2 = ((bf16[16,32,1280]{2,1,0:T(8,128)(2,1)}), bf16[16,32,1280]{2,1,0:T(8,128)(2,1)S(1)}, u32[]{:S(2)}, u32[]{:S(2)}) async-start(bf16[16,32,1280]{2,1,0:T(8,128)(2,1)} %get-tuple-element.9), calls=%async_computation.2 | async-start | bytes 2621440 | tf_op jit(solution)/shard_map/all_to_all | solution.py:272
  140.5 45.0 %copy-start.1 = (bf16[64,3840]{1,0:T(8,128)(2,1)S(1)}, bf16[64,3840]{1,0:T(8,128)(2,1)}, u32[]{:S(2)}) copy-start(bf16[64,3840]{1,0:T(8,128)(2,1)} %reshape.79.rows_ref) | copy-start | bytes 1474564

commit v4 on v3

--- a/solution.py
+++ b/solution.py
@@ -20,33 +20,40 @@
 KEEP = 32
 EXTRA = 256
 
+CHIPS = 8
 PLANE_GROUPS = [[2 * i + half for i in range(PLANE)] for half in range(2)]
 OTHER_HALF = [
     (p * 2 * PLANE + t, (p ^ 8) * 2 * PLANE + (t ^ 1)) for p in range(HOLDERS) for t in range(2 * PLANE)
 ]
 
+RUN_GROUPS = [[2 * z + core for z in range(CHIPS)] for core in range(2)]
+OTHER_CORE = [(i, i ^ 1) for i in range(HOLDERS)]
+STEP = 4
+
 VMEM = pl.BlockSpec(memory_space=pltpu.VMEM)
 SMEM = pl.BlockSpec(memory_space=pltpu.SMEM)
 
 
 def select_kernel(count_ref, dest_ref, keep_ref, page_ref, out_ref, kept_ref):
-    slot = pl.program_id(0)
-
-    @pl.when(slot == 0)
+    step = pl.program_id(0)
+
+    @pl.when(step == 0)
     def _():
         out_ref[...] = jnp.zeros_like(out_ref)
 
     rows = page_ref.shape[1]
-    picks = jnp.broadcast_to(keep_ref[0], (rows, KEEP))
-    chosen = (picks == lax.broadcasted_iota(jnp.int32, (rows, KEEP), 0)).astype(jnp.float32)
-    kept = jnp.dot(
-        chosen.T.astype(jnp.bfloat16), page_ref[0], preferred_element_type=jnp.float32
-    ).astype(jnp.bfloat16)
-    kept_ref[...] = kept
-
-    @pl.when(slot < count_ref[0])
-    def _():
-        out_ref[dest_ref[slot]] = kept
+    for i in range(STEP):
+        slot = step * STEP + i
+        picks = jnp.broadcast_to(keep_ref[i], (rows, KEEP))
+        chosen = (picks == lax.broadcasted_iota(jnp.int32, (rows, KEEP), 0)).astype(jnp.float32)
+        kept = jnp.dot(
+            chosen.T.astype(jnp.bfloat16), page_ref[i], preferred_element_type=jnp.float32
+        ).astype(jnp.bfloat16)
+        kept_ref[i * KEEP : (i + 1) * KEEP] = kept
+
+        @pl.when(slot < count_ref[0])
+        def _():
+            out_ref[dest_ref[slot]] = kept
 
 
 def select_rows(page_count, dest_slot, keep_rows, cache):
@@ -59,37 +66,87 @@
         ),
         grid_spec=pltpu.PrefetchScalarGridSpec(
             num_scalar_prefetch=2,
-            grid=(sources,),
+            grid=(sources // STEP,),
             in_specs=[
-                pl.BlockSpec((1, 1, KEEP), lambda s, *_: (s, 0, 0)),
-                pl.BlockSpec((1, rows, width), lambda s, *_: (s, 0, 0)),
+                pl.BlockSpec((STEP, 1, KEEP), lambda s, *_: (s, 0, 0)),
+                pl.BlockSpec((STEP, rows, width), lambda s, *_: (s, 0, 0)),
             ],
             out_specs=[
                 pl.BlockSpec((HOLDERS, KEEP, width), lambda s, *_: (0, 0, 0)),
-                pl.BlockSpec((KEEP, width), lambda s, *_: (s, 0)),
+                pl.BlockSpec((STEP * KEEP, width), lambda s, *_: (s, 0)),
             ],
         ),
         name="select_rows",
     )(page_count, dest_slot, keep_rows, cache.reshape(sources, rows, width))
 
 
-def arrange_kernel(back_ref, out_ref):
+def project_kernel(rows_ref, query_ref, pair_ref, out_ref):
+    rows = rows_ref[...]
+    for ref, low, high in ((query_ref, 0, HEAD_DIM), (pair_ref, HEAD_DIM, HEAD_DIM * 3 // 2)):
+        out_ref[:, low:high] = lax.dot_general(
+            rows, ref[...], (((1,), (1,)), ((), ())), preferred_element_type=jnp.float32
+        ).astype(jnp.bfloat16)
+
+
+def project(rows, w_query, w_keyvalue):
+    return pl.pallas_call(
+        project_kernel,
+        out_shape=jax.ShapeDtypeStruct((rows.shape[0], HEAD_DIM * 3 // 2), jnp.bfloat16),
+        in_specs=[VMEM] * 3,
+        out_specs=VMEM,
+        name="project",
+    )(rows, w_query.T, w_keyvalue.T)
+
+
+def pick_kernel(place_ref, all_ref, own_ref, other_ref):
+    block = all_ref[...].astype(jnp.float32)
+    share = own_ref.shape[1]
+    low, high = block[:, :share], block[:, share:]
+    first = place_ref[1] == 0
+    own_ref[...] = jnp.where(first, low, high).astype(jnp.bfloat16)
+    other_ref[...] = jnp.where(first, high, low).astype(jnp.bfloat16)
+
+
+def pick(place, everyone):
+    count, rows, width = everyone.shape
+    both = rows // PLANE
+    piece = jax.ShapeDtypeStruct((count, both // 2, width), everyone.dtype)
+    whole = pl.BlockSpec(piece.shape, lambda i, *_: (0, 0, 0))
+    return pl.pallas_call(
+        pick_kernel,
+        out_shape=(piece, piece),
+        grid_spec=pltpu.PrefetchScalarGridSpec(
+            num_scalar_prefetch=1,
+            grid=(1,),
+            in_specs=[pl.BlockSpec((count, both, width), lambda i, place: (0, place[0], 0))],
+            out_specs=[whole, whole],
+        ),
+        name="pick",
+    )(place, everyone)
+
+
+def arrange_kernel(place_ref, own_ref, got_ref, out_ref):
     half = HEAD_DIM // 2
     for h in range(HEADS):
+        block = jnp.where(
+            place_ref[1] == h % 2,
+            own_ref[h // 2].astype(jnp.float32),
+            got_ref[h // 2].astype(jnp.float32),
+        ).astype(jnp.bfloat16)
         at = (h % REPEAT * KV_HEADS + h // REPEAT) * HEAD_DIM
-        out_ref[:, at : at + HEAD_DIM] = back_ref[h, :, :HEAD_DIM]
+        out_ref[:, at : at + HEAD_DIM] = block[:, :HEAD_DIM]
         at = QUERIES + h * half
-        out_ref[:, at : at + half] = back_ref[h, :, HEAD_DIM:]
-
-
-def arrange(back):
+        out_ref[:, at : at + half] = block[:, HEAD_DIM:]
+
+
+def arrange(place, own, got):
     return pl.pallas_call(
         arrange_kernel,
-        out_shape=jax.ShapeDtypeStruct((back.shape[1], QUERIES + 2 * KEYS), back.dtype),
-        in_specs=[VMEM],
+        out_shape=jax.ShapeDtypeStruct((own.shape[1], QUERIES + 2 * KEYS), own.dtype),
+        in_specs=[SMEM, VMEM, VMEM],
         out_specs=VMEM,
         name="arrange",
-    )(back)
+    )(place, own, got)
 
 
 def pieces(value, count):
@@ -101,17 +158,31 @@
     return parts
 
 
-def attend_kernel(count_ref, owner_ref, kept_ref, rows_ref, out_ref, sum_ref, peak_ref, total_ref):
+def from_runs(request, core, near, far):
+    count = near.shape[0]
+    per_holder = count // CHIPS
+    holder = request // per_holder
+    place = holder // 2 * per_holder + request % per_holder
+    spot = lax.broadcasted_iota(jnp.int32, (request.shape[0], count), 1)
+    total = None
+    for rows, same in ((near, True), (far, False)):
+        chosen = (spot == place) & ((holder % 2 == core) == same)
+        term = jnp.dot(
+            chosen.astype(jnp.float32).astype(jnp.bfloat16), rows, preferred_element_type=jnp.float32
+        )
+        total = term if total is None else total + term
+    return total
+
+
+def attend_kernel(
+    place_ref, count_ref, owner_ref, kept_ref, near_ref, far_ref, out_ref, sum_ref, peak_ref, total_ref
+):
     scale = HEAD_DIM ** (-0.5)
-    requests = rows_ref.shape[0]
-    slot = lax.broadcasted_iota(jnp.int32, (SOURCES, requests), 0)
-    owner = jnp.zeros((SOURCES, requests), jnp.int32)
+    slot = lax.broadcasted_iota(jnp.int32, (SOURCES, near_ref.shape[0]), 0)
+    owner = jnp.zeros(slot.shape, jnp.int32)
     for s in range(SOURCES):
         owner = jnp.where(slot == s, owner_ref[s], owner)
-    picked = (owner == lax.broadcasted_iota(jnp.int32, (SOURCES, requests), 1)).astype(jnp.float32)
-    query = jnp.dot(
-        picked.astype(jnp.bfloat16), rows_ref[:, :QUERIES], preferred_element_type=jnp.float32
-    )
+    query = from_runs(owner, place_ref[2], near_ref[:, :QUERIES], far_ref[:, :QUERIES])
     head = lax.broadcasted_iota(jnp.int32, (KV_HEADS, KEYS), 0) * HEAD_DIM
     lane = lax.broadcasted_iota(jnp.int32, (KV_HEADS, KEYS), 1)
     mask = ((lane >= head) & (lane < head + HEAD_DIM)).astype(jnp.float32)
@@ -149,11 +220,11 @@
     out_ref[:, QUERIES:] = jnp.concatenate(columns, axis=1).astype(jnp.bfloat16)
 
 
-def attend(page_count, page_owner, kept, rows):
+def attend(place, page_count, page_owner, kept, near, far):
     return pl.pallas_call(
         attend_kernel,
         out_shape=jax.ShapeDtypeStruct((SOURCES, QUERIES + EXTRA), jnp.bfloat16),
-        in_specs=[SMEM, SMEM, VMEM, VMEM],
+        in_specs=[SMEM] * 3 + [VMEM] * 3,
         out_specs=VMEM,
         scratch_shapes=[
             pltpu.VMEM((SOURCES, QUERIES), jnp.float32),
@@ -161,7 +232,7 @@
             pltpu.VMEM((SOURCES, HEADS), jnp.float32),
         ],
         name="attend",
-    )(page_count, page_owner, kept, rows)
+    )(place, page_count, page_owner, kept, near, far)
 
 
 def spread_dot(value, chosen, contract, count, chosen_first=False):
@@ -175,11 +246,14 @@
     return total
 
 
-def combine_kernel(part_ref, rows_ref, out_ref):
+def combine_kernel(place_ref, near_part_ref, far_part_ref, near_ref, far_ref, out_ref):
     scale = HEAD_DIM ** (-0.5)
-    requests = rows_ref.shape[0]
-    slots = part_ref.shape[0]
-    extra = part_ref[:, QUERIES:].astype(jnp.float32)
+    requests = out_ref.shape[0]
+    part = jnp.concatenate(
+        [near_part_ref[...].astype(jnp.float32), far_part_ref[...].astype(jnp.float32)], axis=0
+    )
+    slots = part.shape[0]
+    extra = part[:, QUERIES:]
     column = [extra[:, i * HEADS : (i + 1) * HEADS] for i in range(7)]
     peaks = column[0] + column[1] + column[2]
     totals = column[3] + column[4] + column[5]
@@ -192,9 +266,11 @@
     lane = lax.broadcasted_iota(jnp.int32, (HEADS, QUERIES), 1)
     expand = ((lane >= head) & (lane < head + HEAD_DIM)).astype(jnp.float32).astype(jnp.bfloat16)
 
-    query = rows_ref[:, :QUERIES].astype(jnp.float32)
-    key = rows_ref[:, QUERIES : QUERIES + KEYS].astype(jnp.float32)
-    value = rows_ref[:, QUERIES + KEYS :].astype(jnp.float32)
+    number = lax.broadcasted_iota(jnp.int32, (requests, near_ref.shape[0]), 0)
+    rows = from_runs(number, place_ref[2], near_ref[...], far_ref[...])
+    query = rows[:, :QUERIES]
+    key = rows[:, QUERIES : QUERIES + KEYS]
+    value = rows[:, QUERIES + KEYS :]
     product = query * jnp.concatenate([key] * REPEAT, axis=1)
     own = scale * spread_dot(product, expand, ((1,), (1,)), 3)
     top = own
@@ -207,7 +283,7 @@
     total = spread_dot(weight * totals, member, ((0,), (0,)), 3, True) + own_weight
     inverse = 1.0 / total
     weight = weight * spread_dot(inverse, member, ((1,), (0,)), 3, True)
-    scaled = part_ref[:, :QUERIES].astype(jnp.float32) * spread_dot(
+    scaled = part[:, :QUERIES] * spread_dot(
         weight, expand, ((1,), (0,)), 2
     )
     mixed = spread_dot(scaled, member, ((0,), (0,)), 2, True)
@@ -218,23 +294,38 @@
         out_ref[:, h * HEAD_DIM : (h + 1) * HEAD_DIM] = mixed[:, at : at + HEAD_DIM]
 
 
-def combine(parts, rows):
+def combine(place, near_part, far_part, near, far):
     return pl.pallas_call(
         combine_kernel,
-        out_shape=jax.ShapeDtypeStruct((rows.shape[0], QUERIES), jnp.bfloat16),
-        in_specs=[VMEM] * 2,
+        out_shape=jax.ShapeDtypeStruct((2 * near.shape[0], QUERIES), jnp.bfloat16),
+        in_specs=[SMEM] + [VMEM] * 4,
         out_specs=VMEM,
         compiler_params=pltpu.CompilerParams(vmem_limit_bytes=48 * 1024 * 1024),
         name="combine",
-    )(parts, rows)
+    )(place, near_part, far_part, near, far)
+
+
+def to_all_holders(block):
+    near = lax.all_to_all(
+        jnp.broadcast_to(block[None], (CHIPS,) + block.shape),
+        "page",
+        0,
+        0,
+        axis_index_groups=RUN_GROUPS,
+        tiled=True,
+    )
+    far = lax.ppermute(near, "page", OTHER_CORE)
+    shape = (CHIPS * block.shape[0], block.shape[1])
+    return near.reshape(shape), far.reshape(shape)
 
 
 def per_device(
     tokens, norm_gain, w_query, w_keyvalue, cache, page_count, page_owner, keep_rows, dest_slot
 ):
-    groups = lax.axis_size("tensor")
     holder = lax.axis_index("page")
-    half = lax.axis_index("tensor") % 2
+    group = lax.axis_index("tensor")
+    half = group % 2
+    place = jnp.stack([group // 2, half, holder % 2])
     share = tokens.shape[0] // HOLDERS
 
     def normalise(rows):
@@ -245,35 +336,35 @@
             * norm_gain
         ).astype(jnp.bfloat16)
 
-    theirs = lax.dynamic_slice_in_dim(tokens, (holder ^ 8) * share, share, 0)
-    across = lax.ppermute(normalise(theirs), ("page", "tensor"), OTHER_HALF)
-    mine = normalise(lax.dynamic_slice_in_dim(tokens, holder * share, share, 0))
-
     page_count = page_count.reshape(1)
     page_owner = page_owner.reshape(SOURCES)
     compact, kept = select_rows(page_count, dest_slot.reshape(SOURCES), keep_rows, cache)
 
-    both = jnp.where(half == 0, jnp.stack([mine, across]), jnp.stack([across, mine]))
-    rows = lax.all_to_all(
-        jnp.broadcast_to(both[None], (PLANE,) + both.shape),
-        "tensor",
-        0,
-        0,
-        axis_index_groups=PLANE_GROUPS,
-        tiled=True,
-    ).reshape(groups * share, -1)
-    query_part = jnp.dot(rows, w_query, preferred_element_type=jnp.float32)
-    pair_part = jnp.dot(rows, w_keyvalue, preferred_element_type=jnp.float32)
-    projected = jnp.concatenate([query_part, pair_part], axis=1).astype(jnp.bfloat16)
-    back = lax.all_to_all(
-        projected.reshape(groups, share, -1), "tensor", 0, 0, tiled=True
-    )
-    back, compact = lax.optimization_barrier((back, compact))
+    mine = normalise(lax.dynamic_slice_in_dim(tokens, holder * share, share, 0))
+    mine, compact = lax.optimization_barrier((mine, compact))
+    across = lax.ppermute(mine, ("page", "tensor"), OTHER_HALF)
     arrived = lax.all_to_all(compact, "page", 0, 0, tiled=True)
-    own_rows = lax.all_gather(arrange(back), "page", axis=0, tiled=True)
-    part = attend(page_count, page_owner, kept, own_rows)
-    parts = lax.all_gather(part, "page", axis=0, tiled=True)
-    return combine(parts, own_rows), arrived[:, None]
+
+    both = jnp.where(
+        half == 0,
+        jnp.concatenate([mine, across], axis=0),
+        jnp.concatenate([across, mine], axis=0),
+    )
+    rows = lax.all_gather(
+        both, "tensor", axis=0, axis_index_groups=PLANE_GROUPS, tiled=True
+    )
+    projected = project(rows, w_query, w_keyvalue)
+    everyone = lax.all_gather(
+        projected, "tensor", axis=0, axis_index_groups=PLANE_GROUPS, tiled=False
+    )
+    own, other = pick(place, everyone)
+    got = lax.ppermute(other, ("page", "tensor"), OTHER_HALF)
+    ordered, arrived = lax.optimization_barrier((arrange(place, own, got), arrived))
+    near, far = to_all_holders(ordered)
+    part = attend(place, page_count, page_owner, kept, near, far)
+    near_part, far_part = to_all_holders(part)
+    attended = combine(place, near_part, far_part, near, far)
+    return attended, arrived[:, None]
 
 
 def solution(mesh):

time: 191 us -> 204 us (1.068)
  waiting for transfers between devices: 8.94 us -> 43.4 us
  blocking collectives: 122 us -> 87.9 us
  starting transfers between devices: 34.3 us -> 43.7 us
  Pallas kernels: 16.9 us -> 19.8 us
    all_gather x2, blocking collectives: 104 us -> 42 us  [the longest x1 21.3 us: per_device(): lax.all_gather(both, 'tensor', axis=0, axis_index_groups=PLANE_GROUPS, ti...]
    ppermute x1 -> x4, waiting for transfers between devices: 1.25 us -> 43.4 us  [the longest x1 35.1 us: per_device(): across = lax.ppermute(mine, ('page', 'tensor'), OTHER_HALF)]
    all_to_all x1 -> x2, blocking collectives: 17.3 us -> 46 us  [to_all_holders(): lax.all_to_all(jnp.broadcast_to(block[None], (CHIPS,) + block.shape), 'pa...]
    ppermute x1 -> x4, starting transfers between devices: 13.3 us -> 29.6 us  [the longest x2 19.6 us: to_all_holders(): far = lax.ppermute(near, 'page', OTHER_CORE)]
    all_to_all x1 -> x0, starting transfers between devices: 11.9 us -> none  [per_device(): lax.all_to_all(projected.reshape(groups, share, -1), 'tensor', 0, 0, tile...]
    all_to_all x1 -> x0, waiting for transfers between devices: 7.68 us -> none  [per_device(): lax.all_to_all(projected.reshape(groups, share, -1), 'tensor', 0, 0, tile...]
    pallas_call x2 -> x4, Pallas kernels: 5.42 us -> 10.5 us  [the longest x1 4.56 us: combine(): pl.pallas_call(combine_kernel, out_shape=jax.ShapeDtypeStruct((2 * near.s...]
    all_to_all x1, starting transfers between devices: 9.04 us -> 14 us  [per_device(): arrived = lax.all_to_all(compact, 'page', 0, 0, tiled=True)]
  transfers between devices with their start and end apart: 3 -> 5, of which waited for: 2 -> 4; matrix products, arithmetic and copies ran while one was open for 0% -> 1% of each run, Pallas kernels for 9% -> 3%
where the time goes in v4:
time: 204 us; the launch traced here: 203 us
  blocking collectives  87.9 us (43%)
  starting transfers between devices  43.7 us (21%)
  waiting for transfers between devices  43.4 us (21%)
  Pallas kernels  19.8 us (10%)
  local copies, waits for them, and re-layouts  4.8 us (2%)
  other arithmetic  2.5 us (1%)
    all_to_all x2, blocking collectives, to_all_holders(): lax.all_to_all(jnp.broadcast_to(block[None], (CHIPS,) + block.shape), 'pa...  46 us
    ppermute x1, waiting for transfers between devices, per_device(): across = lax.ppermute(mine, ('page', 'tensor'), OTHER_HALF)  35.1 us
    all_gather x1, blocking collectives, per_device(): lax.all_gather(both, 'tensor', axis=0, axis_index_groups=PLANE_GROUPS, ti...  21.3 us
    all_gather x1, blocking collectives, per_device(): lax.all_gather(projected, 'tensor', axis=0, axis_index_groups=PLANE_GROUP...  20.7 us
    ppermute x2, starting transfers between devices, to_all_holders(): far = lax.ppermute(near, 'page', OTHER_CORE)  19.6 us
    all_to_all x1, starting transfers between devices, per_device(): arrived = lax.all_to_all(compact, 'page', 0, 0, tiled=True)  14 us
    ppermute x1, starting transfers between devices, per_device(): across = lax.ppermute(mine, ('page', 'tensor'), OTHER_HALF)  8.14 us
    ppermute x1, waiting for transfers between devices, per_device(): got = lax.ppermute(other, ('page', 'tensor'), OTHER_HALF)  6.67 us
  transfers between devices with their start and end apart: 5, of which 4 were waited for; matrix products, arithmetic and copies ran while one was open for 1% of the time, Pallas kernels for 3%

profile of v4, /device:TPU:1, one launch (start us, length us, event | category | flops | bytes accessed | tf_op | source)
XLA Modules:
  0.0 203.5 jit_solution(16959866043405261005)
XLA Ops:
  1.3 0.9 fusion
  2.2 0.9 fusion.2
  3.1 5.2 %select_rows.1 = (bf16[16,32,1280]{2,1,0:T(8,128)(2,1)}, bf16[256,1280]{1,0:T(8,128)(2,1)}) custom-call(s32[1]{0:T(128)} %bitcast.15.count_ref, s32[8]{0:T(128)} %bitcast.25, s32[8,1,32]{2,1,0:T(1,128)} %keep_ref.1, bf16[8,128,1280]{2,1,0:T(8,128)(2,1)} %bitcast.20), custom_call_target="tpu_custom_call" | custom-call | tf_op jit(solution)/shard_map/select_rows/pallas_call | solution.py:61
  8.3 14.0 %all-to-all-start = ((bf16[16,32,1280]{2,1,0:T(8,128)(2,1)}), bf16[16,32,1280]{2,1,0:T(8,128)(2,1)S(1)}, u32[]{:S(2)}, u32[]{:S(2)}) async-start(bf16[16,32,1280]{2,1,0:T(8,128)(2,1)} %get-tuple-element.15), calls=%async_computation | async-start | bytes 2621440 | tf_op jit(solution)/shard_map/all_to_all | solution.py:346
  22.3 8.1 %collective-permute-start = (bf16[4,2560]{1,0:T(4,128)(2,1)S(1)}, bf16[4,2560]{1,0:T(4,128)(2,1)S(1)}, u32[]{:S(2)}, u32[]{:S(2)}) collective-permute-start(bf16[4,2560]{1,0:T(4,128)(2,1)S(1)} %fusion.2), channel_id=1, source_target_pairs={{0,257},{1,256},{2,259},{3,258},{4,261},{5,260},{6,263},{7,262},{8... | collective-permute-start | bytes 61448 | tf_op jit(solution)/shard_map/ppermute | solution.py:345
  31.2 35.1 %collective-permute-done = bf16[4,2560]{1,0:T(4,128)(2,1)S(1)} collective-permute-done((bf16[4,2560]{1,0:T(4,128)(2,1)S(1)}, bf16[4,2560]{1,0:T(4,128)(2,1)S(1)}, u32[]{:S(2)}, u32[]{:S(2)}) %collective-permute-start) | collective-permute-done | bytes 20512 | tf_op jit(solution)/shard_map/ppermute | solution.py:345
  66.3 21.3 %all_gather.9.rows_ref = bf16[128,2560]{1,0:T(8,128)(2,1)} all-gather(bf16[8,2560]{1,0:T(8,128)(2,1)S(1)} %maximum_select_fusion), channel_id=1, replica_groups={{0,2,4,6,8,10,12,14,16,18,20,22,24,26,28,30},{1,3,5,7,9,11,13,15,17,19,..., dimensions={0}, use_global_device_ids=true | all-gather | bytes 696320 | tf_op jit(solution)/shard_map/all_gather | solution.py:353
  87.6 2.4 %project.1 = bf16[128,120]{1,0:T(8,128)(2,1)} custom-call(bf16[128,2560]{1,0:T(8,128)(2,1)} %all_gather.9.rows_ref, bf16[80,2560]{1,0:T(8,128)(2,1)} %bitcast.22, bf16[40,2560]{1,0:T(8,128)(2,1)} %bitcast.23), custom_call_target="tpu_custom_call" | custom-call | tf_op jit(solution)/shard_map/project/pallas_call | solution.py:92
  90.0 20.7 %all-gather = bf16[2048,120]{1,0:T(8,128)(2,1)} all-gather(bf16[128,120]{1,0:T(8,128)(2,1)} %project.1), channel_id=2, replica_groups={{0,2,4,6,8,10,12,14,16,18,20,22,24,26,28,30},{1,3,5,7,9,11,13,15,17,19,..., dimensions={0}, use_global_device_ids=true | all-gather | bytes 522240 | tf_op jit(solution)/shard_map/all_gather | solution.py:357
  110.7 2.0 %pick.1 = (bf16[16,4,120]{2,1,0:T(4,128)(2,1)}, bf16[16,4,120]{2,1,0:T(4,128)(2,1)}) custom-call(s32[3]{0:T(128)} %pad_add_fusion.place_ref, bf16[16,128,120]{2,1,0:T(8,128)(2,1)} %bitcast.21), custom_call_target="tpu_custom_call" | custom-call | tf_op jit(solution)/shard_map/pick/pallas_call | solution.py:115
  112.7 1.9 collective-permute-start.1
  114.6 6.7 %collective-permute-done.1.got_ref = bf16[16,4,120]{2,1,0:T(4,128)(2,1)S(1)} collective-permute-done((bf16[16,4,120]{2,1,0:T(4,128)(2,1)}, bf16[16,4,120]{2,1,0:T(4,128)(2,1)S(1)}, u32[]{:S(2)}, u32[]{:S(2)}) %collective-permute-start.1) | collective-permute-done | bytes 15392 | tf_op jit(solution)/shard_map/ppermute | solution.py:361
  121.9 1.5 arrange.1
  123.4 0.8 broadcast_in_dim.6
  124.2 21.8 %all_to_all.15 = bf16[8,4,3840]{2,1,0:T(4,128)(2,1)S(1)} all-to-all(bf16[8,4,3840]{2,1,0:T(4,128)(2,1)S(1)} %broadcast_in_dim.6), channel_id=1, replica_groups={{0,64,128,192,256,320,384,448},{32,96,160,224,288,352,416,480},{1,65,12..., dimensions={0} | all-to-all | bytes 491520 | tf_op jit(solution)/shard_map/all_to_all | solution.py:309
  146.1 15.0 %collective-permute-start.2 = (bf16[8,4,3840]{2,1,0:T(4,128)(2,1)S(1)}, bf16[8,4,3840]{2,1,0:T(4,128)(2,1)S(1)}, u32[]{:S(2)}, u32[]{:S(2)}) collective-permute-start(bf16[8,4,3840]{2,1,0:T(4,128)(2,1)S(1)} %all_to_all.15), channel_id=1, source_target_pairs={{0,32},{32,0},{64,96},{96,64},{128,160},{160,128},{192,224},{224,1... | collective-permute-start | bytes 737288 | tf_op jit(solution)/shard_map/ppermute | solution.py:317
  161.1 0.8 reshape.43.near_ref
  163.0 4.1 %attend.1 = bf16[8,2816]{1,0:T(8,128)(2,1)} custom-call(s32[3]{0:T(128)} %pad_add_fusion.place_ref, s32[1]{0:T(128)} %bitcast.16.count_ref, s32[8]{0:T(128)} %bitcast.24, bf16[256,1280]{1,0:T(8,128)(2,1)} %get-tuple-element.10.kept_ref, bf16[32,3840]{1,0:T(8,128)(2,1)} %reshape.43.near_ref, bf16[32,3840]{1,0:T(8,128)(2,1)} %reshape.44.far_ref), custom_call_target="tpu_custom_call" | custom-call | tf_op jit(solution)/shard_map/attend/pallas_call | solution.py:224
  167.0 0.8 broadcast_in_dim.7
  167.9 24.1 %all_to_all.16 = bf16[8,8,2816]{2,1,0:T(8,128)(2,1)S(1)} all-to-all(bf16[8,8,2816]{2,1,0:T(8,128)(2,1)S(1)} %broadcast_in_dim.7), channel_id=1, replica_groups={{0,64,128,192,256,320,384,448},{32,96,160,224,288,352,416,480},{1,65,12..., dimensions={0} | all-to-all | bytes 720896 | tf_op jit(solution)/shard_map/all_to_all | solution.py:309
  192.0 4.6 %collective-permute-start.3 = (bf16[8,8,2816]{2,1,0:T(8,128)(2,1)S(1)}, bf16[8,8,2816]{2,1,0:T(8,128)(2,1)S(1)}, u32[]{:S(2)}, u32[]{:S(2)}) collective-permute-start(bf16[8,8,2816]{2,1,0:T(8,128)(2,1)S(1)} %all_to_all.16), channel_id=1, source_target_pairs={{0,32},{32,0},{64,96},{96,64},{128,160},{160,128},{192,224},{224,1... | collective-permute-start | bytes 1081352 | tf_op jit(solution)/shard_map/ppermute | solution.py:317
  196.6 1.3 collective-permute-done.3
  197.8 4.6 %combine.1 = bf16[64,2560]{1,0:T(8,128)(2,1)} custom-call(s32[3]{0:T(128)S(1)} %copy-done.2, bf16[64,2816]{1,0:T(8,128)(2,1)S(1)} %bitcast.17, bf16[64,2816]{1,0:T(8,128)(2,1)S(1)} %bitcast.18, bf16[32,3840]{1,0:T(8,128)(2,1)S(1)} %copy-done, bf16[32,3840]{1,0:T(8,128)(2,1)S(1)} %copy-done.1), custom_call_target="tpu_custom_call" | custom-call | tf_op jit(solution)/shard_map/combine/pallas_call | solution.py:298
  202.4 1.1 copy.14
  (14 shorter events, 2.4 us)
Async XLA Ops:
  8.3 115.1 %all-to-all-start = ((bf16[16,32,1280]{2,1,0:T(8,128)(2,1)}), bf16[16,32,1280]{2,1,0:T(8,128)(2,1)S(1)}, u32[]{:S(2)}, u32[]{:S(2)}) async-start(bf16[16,32,1280]{2,1,0:T(8,128)(2,1)} %get-tuple-element.15), calls=%async_computation | async-start | bytes 2621440 | tf_op jit(solution)/shard_map/all_to_all | solution.py:346
  22.3 43.9 %collective-permute-start = (bf16[4,2560]{1,0:T(4,128)(2,1)S(1)}, bf16[4,2560]{1,0:T(4,128)(2,1)S(1)}, u32[]{:S(2)}, u32[]{:S(2)}) collective-permute-start(bf16[4,2560]{1,0:T(4,128)(2,1)S(1)} %fusion.2), channel_id=1, source_target_pairs={{0,257},{1,256},{2,259},{3,258},{4,261},{5,260},{6,263},{7,262},{8... | collective-permute-start | bytes 61448 | tf_op jit(solution)/shard_map/ppermute | solution.py:345
  112.7 8.6 %collective-permute-start.1 = (bf16[16,4,120]{2,1,0:T(4,128)(2,1)}, bf16[16,4,120]{2,1,0:T(4,128)(2,1)S(1)}, u32[]{:S(2)}, u32[]{:S(2)}) collective-permute-start(bf16[16,4,120]{2,1,0:T(4,128)(2,1)} %get-tuple-element.14), channel_id=1, source_target_pairs={{0,257},{1,256},{2,259},{3,258},{4,261},{5,260},{6,263},{7,262},{8... | collective-permute-start | bytes 46088 | tf_op jit(solution)/shard_map/ppermute | solution.py:361
  121.3 0.6 copy-start.3
  146.1 16.1 %collective-permute-start.2 = (bf16[8,4,3840]{2,1,0:T(4,128)(2,1)S(1)}, bf16[8,4,3840]{2,1,0:T(4,128)(2,1)S(1)}, u32[]{:S(2)}, u32[]{:S(2)}) collective-permute-start(bf16[8,4,3840]{2,1,0:T(4,128)(2,1)S(1)} %all_to_all.15), channel_id=1, source_target_pairs={{0,32},{32,0},{64,96},{96,64},{128,160},{160,128},{192,224},{224,1... | collective-permute-start | bytes 737288 | tf_op jit(solution)/shard_map/ppermute | solution.py:317
  161.8 36.0 %copy-start = (bf16[32,3840]{1,0:T(8,128)(2,1)S(1)}, bf16[32,3840]{1,0:T(8,128)(2,1)}, u32[]{:S(2)}) copy-start(bf16[32,3840]{1,0:T(8,128)(2,1)} %reshape.43.near_ref) | copy-start | bytes 737284
  161.9 36.0 %copy-start.2 = (s32[3]{0:T(128)S(1)}, s32[3]{0:T(128)}, u32[]{:S(2)}) copy-start(s32[3]{0:T(128)} %pad_add_fusion.place_ref) | copy-start | bytes 40
  163.0 34.9 %copy-start.1 = (bf16[32,3840]{1,0:T(8,128)(2,1)S(1)}, bf16[32,3840]{1,0:T(8,128)(2,1)}, u32[]{:S(2)}) copy-start(bf16[32,3840]{1,0:T(8,128)(2,1)} %reshape.44.far_ref) | copy-start | bytes 737284
  192.0 5.9 %collective-permute-start.3 = (bf16[8,8,2816]{2,1,0:T(8,128)(2,1)S(1)}, bf16[8,8,2816]{2,1,0:T(8,128)(2,1)S(1)}, u32[]{:S(2)}, u32[]{:S(2)}) collective-permute-start(bf16[8,8,2816]{2,1,0:T(8,128)(2,1)S(1)} %all_to_all.16), channel_id=1, source_target_pairs={{0,32},{32,0},{64,96},{96,64},{128,160},{160,128},{192,224},{224,1... | collective-permute-start | bytes 1081352 | tf_op jit(solution)/shard_map/ppermute | solution.py:317

commit v5 on v4

--- a/solution.py
+++ b/solution.py
@@ -26,6 +26,12 @@
     (p * 2 * PLANE + t, (p ^ 8) * 2 * PLANE + (t ^ 1)) for p in range(HOLDERS) for t in range(2 * PLANE)
 ]
 
+COLUMN_GROUPS = [
+    [(2 * z + core) * 2 * PLANE + 2 * xy + half for half in range(2) for z in range(CHIPS)]
+    for xy in range(PLANE)
+    for core in range(2)
+]
+HALF_COLUMNS = (QUERIES + 2 * KEYS) // 2
 RUN_GROUPS = [[2 * z + core for z in range(CHIPS)] for core in range(2)]
 OTHER_CORE = [(i, i ^ 1) for i in range(HOLDERS)]
 STEP = 4
@@ -98,55 +104,44 @@
     )(rows, w_query.T, w_keyvalue.T)
 
 
-def pick_kernel(place_ref, all_ref, own_ref, other_ref):
-    block = all_ref[...].astype(jnp.float32)
-    share = own_ref.shape[1]
-    low, high = block[:, :share], block[:, share:]
-    first = place_ref[1] == 0
-    own_ref[...] = jnp.where(first, low, high).astype(jnp.bfloat16)
-    other_ref[...] = jnp.where(first, high, low).astype(jnp.bfloat16)
+def pick_kernel(place_ref, all_ref, out_ref, rows_ref):
+    half = HEAD_DIM // 2
+    for i in range(PLANE):
+        block = all_ref[i].astype(jnp.float32)
+        at = (i % 2 * KV_HEADS + i // 2) * HEAD_DIM
+        rows_ref[:, at : at + HEAD_DIM] = block[:, :HEAD_DIM]
+        at = QUERIES // 2 + i * half
+        rows_ref[:, at : at + half] = block[:, HEAD_DIM:]
+    share = out_ref.shape[1]
+    for h in range(2):
+        piece = rows_ref[h * share : (h + 1) * share].astype(jnp.bfloat16)
+        for z in range(CHIPS):
+            out_ref[h * CHIPS + z] = piece
 
 
 def pick(place, everyone):
     count, rows, width = everyone.shape
     both = rows // PLANE
-    piece = jax.ShapeDtypeStruct((count, both // 2, width), everyone.dtype)
-    whole = pl.BlockSpec(piece.shape, lambda i, *_: (0, 0, 0))
+    piece = jax.ShapeDtypeStruct((2 * CHIPS, both // 2, HALF_COLUMNS), everyone.dtype)
     return pl.pallas_call(
         pick_kernel,
-        out_shape=(piece, piece),
+        out_shape=piece,
         grid_spec=pltpu.PrefetchScalarGridSpec(
             num_scalar_prefetch=1,
             grid=(1,),
             in_specs=[pl.BlockSpec((count, both, width), lambda i, place: (0, place[0], 0))],
-            out_specs=[whole, whole],
+            out_specs=pl.BlockSpec(piece.shape, lambda i, *_: (0, 0, 0)),
+            scratch_shapes=[pltpu.VMEM((both, HALF_COLUMNS), jnp.float32)],
         ),
         name="pick",
     )(place, everyone)
 
 
-def arrange_kernel(place_ref, own_ref, got_ref, out_ref):
-    half = HEAD_DIM // 2
-    for h in range(HEADS):
-        block = jnp.where(
-            place_ref[1] == h % 2,
-            own_ref[h // 2].astype(jnp.float32),
-            got_ref[h // 2].astype(jnp.float32),
-        ).astype(jnp.bfloat16)
-        at = (h % REPEAT * KV_HEADS + h // REPEAT) * HEAD_DIM
-        out_ref[:, at : at + HEAD_DIM] = block[:, :HEAD_DIM]
-        at = QUERIES + h * half
-        out_ref[:, at : at + half] = block[:, HEAD_DIM:]
-
-
-def arrange(place, own, got):
-    return pl.pallas_call(
-        arrange_kernel,
-        out_shape=jax.ShapeDtypeStruct((own.shape[1], QUERIES + 2 * KEYS), own.dtype),
-        in_specs=[SMEM, VMEM, VMEM],
-        out_specs=VMEM,
-        name="arrange",
-    )(place, own, got)
+def held(place_ref, near_ref, far_ref, chip, core, half, columns):
+    spot = half * CHIPS + jnp.where(place_ref[1] == half, chip, chip ^ 4)
+    near = near_ref[spot, :, columns].astype(jnp.float32)
+    far = far_ref[spot, :, columns].astype(jnp.float32)
+    return jnp.where(place_ref[2] == core, near, far)
 
 
 def pieces(value, count):
@@ -158,37 +153,32 @@
     return parts
 
 
-def from_runs(request, core, near, far):
-    count = near.shape[0]
-    per_holder = count // CHIPS
-    holder = request // per_holder
-    place = holder // 2 * per_holder + request % per_holder
-    spot = lax.broadcasted_iota(jnp.int32, (request.shape[0], count), 1)
-    total = None
-    for rows, same in ((near, True), (far, False)):
-        chosen = (spot == place) & ((holder % 2 == core) == same)
-        term = jnp.dot(
-            chosen.astype(jnp.float32).astype(jnp.bfloat16), rows, preferred_element_type=jnp.float32
-        )
-        total = term if total is None else total + term
-    return total
-
-
 def attend_kernel(
     place_ref, count_ref, owner_ref, kept_ref, near_ref, far_ref, out_ref, sum_ref, peak_ref, total_ref
 ):
     scale = HEAD_DIM ** (-0.5)
-    slot = lax.broadcasted_iota(jnp.int32, (SOURCES, near_ref.shape[0]), 0)
-    owner = jnp.zeros(slot.shape, jnp.int32)
-    for s in range(SOURCES):
-        owner = jnp.where(slot == s, owner_ref[s], owner)
-    query = from_runs(owner, place_ref[2], near_ref[:, :QUERIES], far_ref[:, :QUERIES])
+    share = near_ref.shape[1]
+    line = lax.broadcasted_iota(jnp.int32, (share, QUERIES // 2), 0)
     head = lax.broadcasted_iota(jnp.int32, (KV_HEADS, KEYS), 0) * HEAD_DIM
     lane = lax.broadcasted_iota(jnp.int32, (KV_HEADS, KEYS), 1)
     mask = ((lane >= head) & (lane < head + HEAD_DIM)).astype(jnp.float32)
     for s in range(SOURCES):
+        request = owner_ref[s]
+        holder = request // share
+        query = []
+        for half in range(2):
+            block = held(
+                place_ref, near_ref, far_ref, holder // 2, holder % 2, half, pl.ds(0, QUERIES // 2)
+            )
+            query.append(
+                jnp.sum(jnp.where(line == request % share, block, 0.0), axis=0, keepdims=True)
+            )
         spread = jnp.concatenate(
-            [query[s : s + 1, k * KEYS : (k + 1) * KEYS] * mask for k in range(REPEAT)], axis=0
+            [
+                query[k % 2][:, k // 2 * KEYS : (k // 2 + 1) * KEYS] * mask
+                for k in range(REPEAT)
+            ],
+            axis=0,
         ).astype(jnp.bfloat16)
         keys = kept_ref[s * KEEP : (s + 1) * KEEP, :KEYS]
         values = kept_ref[s * KEEP : (s + 1) * KEEP, KEYS:]
@@ -209,7 +199,7 @@
             sum_ref[s : s + 1, k * KEYS : (k + 1) * KEYS] = jnp.sum(
                 mixed[k * KV_HEADS : (k + 1) * KV_HEADS] * mask, axis=0, keepdims=True
             )
-    out_ref[:, :QUERIES] = sum_ref[...].astype(jnp.bfloat16)
+    sums = sum_ref[...].astype(jnp.bfloat16)
     slots = lax.broadcasted_iota(jnp.int32, (SOURCES, HEADS), 0)
     tag = jnp.full((SOURCES, HEADS), -1, jnp.int32)
     for s in range(SOURCES):
@@ -217,13 +207,16 @@
     tag = tag.astype(jnp.float32).astype(jnp.bfloat16)
     columns = pieces(peak_ref[...], 3) + pieces(total_ref[...], 3) + [tag, tag]
     columns = [column.astype(jnp.float32) for column in columns]
-    out_ref[:, QUERIES:] = jnp.concatenate(columns, axis=1).astype(jnp.bfloat16)
+    columns = jnp.concatenate(columns, axis=1).astype(jnp.bfloat16)
+    for z in range(CHIPS):
+        out_ref[z, :, :QUERIES] = sums
+        out_ref[z, :, QUERIES:] = columns
 
 
 def attend(place, page_count, page_owner, kept, near, far):
     return pl.pallas_call(
         attend_kernel,
-        out_shape=jax.ShapeDtypeStruct((SOURCES, QUERIES + EXTRA), jnp.bfloat16),
+        out_shape=jax.ShapeDtypeStruct((CHIPS, SOURCES, QUERIES + EXTRA), jnp.bfloat16),
         in_specs=[SMEM] * 3 + [VMEM] * 3,
         out_specs=VMEM,
         scratch_shapes=[
@@ -246,11 +239,60 @@
     return total
 
 
-def combine_kernel(place_ref, near_part_ref, far_part_ref, near_ref, far_ref, out_ref):
+def head_columns():
+    head = lax.broadcasted_iota(jnp.int32, (HEADS, QUERIES), 0) * HEAD_DIM
+    lane = lax.broadcasted_iota(jnp.int32, (HEADS, QUERIES), 1)
+    return ((lane >= head) & (lane < head + HEAD_DIM)).astype(jnp.float32).astype(jnp.bfloat16)
+
+
+def own_kernel(place_ref, near_ref, far_ref, score_ref, value_ref, query_ref, pair_ref):
     scale = HEAD_DIM ** (-0.5)
+    share = near_ref.shape[1]
+    piece = HEAD_DIM // 2
+    for holder in range(HOLDERS):
+        rows = slice(holder * share, (holder + 1) * share)
+        for half in range(2):
+            block = held(
+                place_ref, near_ref, far_ref, holder // 2, holder % 2, half, pl.ds(0, HALF_COLUMNS)
+            )
+            for k in range(2):
+                at = (2 * k + half) * KEYS
+                query_ref[rows, at : at + KEYS] = block[:, k * KEYS : (k + 1) * KEYS]
+            pair_ref[half, rows, :] = block[:, QUERIES // 2 :]
+    keys, values = [], []
+    for g in range(KV_HEADS):
+        for half in range(2):
+            keys.append(pair_ref[half, :, g * piece : (g + 1) * piece])
+            at = KEYS // 2 + g * piece
+            values.append(pair_ref[half, :, at : at + piece])
+    key = jnp.concatenate(keys, axis=1)
+    value_ref[...] = jnp.concatenate(values, axis=1)
+    product = query_ref[...] * jnp.concatenate([key] * REPEAT, axis=1)
+    score_ref[...] = scale * spread_dot(product, head_columns(), ((1,), (1,)), 3)
+
+
+def own_part(place, near, far):
+    requests = HOLDERS * near.shape[1]
+    return pl.pallas_call(
+        own_kernel,
+        out_shape=(
+            jax.ShapeDtypeStruct((requests, HEADS), jnp.float32),
+            jax.ShapeDtypeStruct((requests, KEYS), jnp.float32),
+        ),
+        in_specs=[SMEM, VMEM, VMEM],
+        out_specs=(VMEM, VMEM),
+        scratch_shapes=[
+            pltpu.VMEM((requests, QUERIES), jnp.float32),
+            pltpu.VMEM((2, requests, KEYS), jnp.float32),
+        ],
+        name="own_part",
+    )(place, near, far)
+
+
+def combine_kernel(near_ref, far_ref, own_ref, value_ref, out_ref):
     requests = out_ref.shape[0]
     part = jnp.concatenate(
-        [near_part_ref[...].astype(jnp.float32), far_part_ref[...].astype(jnp.float32)], axis=0
+        [near_ref[...].astype(jnp.float32), far_ref[...].astype(jnp.float32)], axis=0
     )
     slots = part.shape[0]
     extra = part[:, QUERIES:]
@@ -262,61 +304,38 @@
     member = (
         tag == lax.broadcasted_iota(jnp.int32, (slots, requests), 1).astype(jnp.float32)
     ).astype(jnp.float32).astype(jnp.bfloat16)
-    head = lax.broadcasted_iota(jnp.int32, (HEADS, QUERIES), 0) * HEAD_DIM
-    lane = lax.broadcasted_iota(jnp.int32, (HEADS, QUERIES), 1)
-    expand = ((lane >= head) & (lane < head + HEAD_DIM)).astype(jnp.float32).astype(jnp.bfloat16)
-
-    number = lax.broadcasted_iota(jnp.int32, (requests, near_ref.shape[0]), 0)
-    rows = from_runs(number, place_ref[2], near_ref[...], far_ref[...])
-    query = rows[:, :QUERIES]
-    key = rows[:, QUERIES : QUERIES + KEYS]
-    value = rows[:, QUERIES + KEYS :]
-    product = query * jnp.concatenate([key] * REPEAT, axis=1)
-    own = scale * spread_dot(product, expand, ((1,), (1,)), 3)
-    top = own
+    expand = head_columns()
+    own = own_ref[...]
+    tops = [own] + [jnp.full(own.shape, NEGATIVE, jnp.float32)] * 3
     for s in range(slots):
-        top = jnp.maximum(
-            top, jnp.where(tag[s : s + 1] == row, peaks[s : s + 1], NEGATIVE)
+        tops[s % 4] = jnp.maximum(
+            tops[s % 4], jnp.where(tag[s : s + 1] == row, peaks[s : s + 1], NEGATIVE)
         )
+    top = jnp.maximum(jnp.maximum(tops[0], tops[1]), jnp.maximum(tops[2], tops[3]))
     own_weight = jnp.exp(own - top)
     weight = jnp.exp(peaks - spread_dot(top, member, ((1,), (0,)), 3, True))
     total = spread_dot(weight * totals, member, ((0,), (0,)), 3, True) + own_weight
     inverse = 1.0 / total
     weight = weight * spread_dot(inverse, member, ((1,), (0,)), 3, True)
-    scaled = part[:, :QUERIES] * spread_dot(
-        weight, expand, ((1,), (0,)), 2
-    )
+    scaled = part[:, :QUERIES] * spread_dot(weight, expand, ((1,), (0,)), 2)
     mixed = spread_dot(scaled, member, ((0,), (0,)), 2, True)
     own_share = spread_dot(own_weight * inverse, expand, ((1,), (0,)), 2)
-    mixed = (mixed + own_share * jnp.concatenate([value] * REPEAT, axis=1)).astype(jnp.bfloat16)
+    mixed = mixed + own_share * jnp.concatenate([value_ref[...]] * REPEAT, axis=1)
+    mixed = mixed.astype(jnp.bfloat16)
     for h in range(HEADS):
         at = (h % REPEAT * KV_HEADS + h // REPEAT) * HEAD_DIM
         out_ref[:, h * HEAD_DIM : (h + 1) * HEAD_DIM] = mixed[:, at : at + HEAD_DIM]
 
 
-def combine(place, near_part, far_part, near, far):
+def combine(near, far, own, value):
     return pl.pallas_call(
         combine_kernel,
-        out_shape=jax.ShapeDtypeStruct((2 * near.shape[0], QUERIES), jnp.bfloat16),
-        in_specs=[SMEM] + [VMEM] * 4,
+        out_shape=jax.ShapeDtypeStruct((own.shape[0], QUERIES), jnp.bfloat16),
+        in_specs=[VMEM] * 4,
         out_specs=VMEM,
         compiler_params=pltpu.CompilerParams(vmem_limit_bytes=48 * 1024 * 1024),
         name="combine",
-    )(place, near_part, far_part, near, far)
-
-
-def to_all_holders(block):
-    near = lax.all_to_all(
-        jnp.broadcast_to(block[None], (CHIPS,) + block.shape),
-        "page",
-        0,
-        0,
-        axis_index_groups=RUN_GROUPS,
-        tiled=True,
-    )
-    far = lax.ppermute(near, "page", OTHER_CORE)
-    shape = (CHIPS * block.shape[0], block.shape[1])
-    return near.reshape(shape), far.reshape(shape)
+    )(near, far, own, value)
 
 
 def per_device(
@@ -341,8 +360,8 @@
     compact, kept = select_rows(page_count, dest_slot.reshape(SOURCES), keep_rows, cache)
 
     mine = normalise(lax.dynamic_slice_in_dim(tokens, holder * share, share, 0))
-    mine, compact = lax.optimization_barrier((mine, compact))
     across = lax.ppermute(mine, ("page", "tensor"), OTHER_HALF)
+    across, compact = lax.optimization_barrier((across, compact))
     arrived = lax.all_to_all(compact, "page", 0, 0, tiled=True)
 
     both = jnp.where(
@@ -357,13 +376,20 @@
     everyone = lax.all_gather(
         projected, "tensor", axis=0, axis_index_groups=PLANE_GROUPS, tiled=False
     )
-    own, other = pick(place, everyone)
-    got = lax.ppermute(other, ("page", "tensor"), OTHER_HALF)
-    ordered, arrived = lax.optimization_barrier((arrange(place, own, got), arrived))
-    near, far = to_all_holders(ordered)
+    halves, arrived = lax.optimization_barrier((pick(place, everyone), arrived))
+    near = lax.all_to_all(
+        halves, ("page", "tensor"), 0, 0, axis_index_groups=COLUMN_GROUPS, tiled=True
+    )
+    far = lax.ppermute(near, "page", OTHER_CORE)
     part = attend(place, page_count, page_owner, kept, near, far)
-    near_part, far_part = to_all_holders(part)
-    attended = combine(place, near_part, far_part, near, far)
+    near_part = lax.all_to_all(
+        part, "page", 0, 0, axis_index_groups=RUN_GROUPS, tiled=True
+    )
+    own, value = own_part(place, near, far)
+    near_part, own, value = lax.optimization_barrier((near_part, own, value))
+    far_part = lax.ppermute(near_part, "page", OTHER_CORE)
+    flat = (CHIPS * SOURCES, QUERIES + EXTRA)
+    attended = combine(near_part.reshape(flat), far_part.reshape(flat), own, value)
     return attended, arrived[:, None]
 
 

time: 204 us -> 159 us (0.78)
  waiting for transfers between devices: 43.4 us -> 22 us
  blocking collectives: 87.9 us -> 67.7 us
  starting transfers between devices: 43.7 us -> 41.4 us
    ppermute x1, waiting for transfers between devices: 35.1 us -> 0.01 us  [per_device(): across = lax.ppermute(mine, ('page', 'tensor'), OTHER_HALF)]
    all_to_all x2 -> x1, blocking collectives: 46 us -> 24.7 us  [per_device(): lax.all_to_all(halves, ('page', 'tensor'), 0, 0, axis_index_groups=COLUMN...]
    all_to_all x0 -> x1, waiting for transfers between devices: none -> 14.4 us  [per_device(): lax.all_to_all(part, 'page', 0, 0, axis_index_groups=RUN_GROUPS, tiled=True)]
    all_to_all x1, starting transfers between devices: 14 us -> 7.16 us  [per_device(): arrived = lax.all_to_all(compact, 'page', 0, 0, tiled=True)]
    ppermute x3 -> x2, waiting for transfers between devices: 8.31 us -> 2.4 us  [the longest x1 1.28 us: per_device(): far_part = lax.ppermute(near_part, 'page', OTHER_CORE)]
    ppermute x3 -> x2, starting transfers between devices: 21.5 us -> 15.9 us  [the longest x1 8.23 us: per_device(): far = lax.ppermute(near, 'page', OTHER_CORE)]
    all_to_all x1, waiting for transfers between devices: 0.01 us -> 5.16 us  [per_device(): arrived = lax.all_to_all(compact, 'page', 0, 0, tiled=True)]
    ppermute x1, starting transfers between devices: 8.14 us -> 13.3 us  [per_device(): across = lax.ppermute(mine, ('page', 'tensor'), OTHER_HALF)]
  transfers between devices with their start and end apart: 5 -> 5, of which waited for: 4 -> 4; matrix products, arithmetic and copies ran while one was open for 1% -> 0% of each run, Pallas kernels for 3% -> 8%
where the time goes in v5:
time: 159 us; the launch traced here: 158 us
  blocking collectives  67.7 us (43%)
  starting transfers between devices  41.4 us (26%)
  waiting for transfers between devices  22 us (14%)
  Pallas kernels  19.9 us (13%)
  local copies, waits for them, and re-layouts  3.43 us (2%)
  other arithmetic  2.5 us (2%)
    all_to_all x1, blocking collectives, per_device(): lax.all_to_all(halves, ('page', 'tensor'), 0, 0, axis_index_groups=COLUMN...  24.7 us
    all_gather x1, blocking collectives, per_device(): lax.all_gather(both, 'tensor', axis=0, axis_index_groups=PLANE_GROUPS, ti...  22.1 us
    all_gather x1, blocking collectives, per_device(): lax.all_gather(projected, 'tensor', axis=0, axis_index_groups=PLANE_GROUP...  20.9 us
    all_to_all x1, waiting for transfers between devices, per_device(): lax.all_to_all(part, 'page', 0, 0, axis_index_groups=RUN_GROUPS, tiled=True)  14.4 us
    ppermute x1, starting transfers between devices, per_device(): across = lax.ppermute(mine, ('page', 'tensor'), OTHER_HALF)  13.3 us
    ppermute x1, starting transfers between devices, per_device(): far = lax.ppermute(near, 'page', OTHER_CORE)  8.23 us
    ppermute x1, starting transfers between devices, per_device(): far_part = lax.ppermute(near_part, 'page', OTHER_CORE)  7.7 us
    all_to_all x1, starting transfers between devices, per_device(): arrived = lax.all_to_all(compact, 'page', 0, 0, tiled=True)  7.16 us
  transfers between devices with their start and end apart: 5, of which 4 were waited for; matrix products, arithmetic and copies ran while one was open for 0% of the time, Pallas kernels for 8%

profile of v5, /device:TPU:1, one launch (start us, length us, event | category | flops | bytes accessed | tf_op | source)
XLA Modules:
  0.0 158.2 jit_solution(6934610916777646266)
XLA Ops:
  0.6 0.9 fusion
  1.6 0.9 fusion.2
  2.4 13.3 %collective-permute-start = (bf16[4,2560]{1,0:T(4,128)(2,1)S(1)}, bf16[4,2560]{1,0:T(4,128)(2,1)S(1)}, u32[]{:S(2)}, u32[]{:S(2)}) collective-permute-start(bf16[4,2560]{1,0:T(4,128)(2,1)S(1)} %fusion.2), channel_id=1, source_target_pairs={{0,257},{1,256},{2,259},{3,258},{4,261},{5,260},{6,263},{7,262},{8... | collective-permute-start | bytes 61448 | tf_op jit(solution)/shard_map/ppermute | solution.py:363
  16.4 5.2 %select_rows.1 = (bf16[16,32,1280]{2,1,0:T(8,128)(2,1)}, bf16[256,1280]{1,0:T(8,128)(2,1)}) custom-call(s32[1]{0:T(128)} %bitcast.15.count_ref, s32[8]{0:T(128)} %bitcast.24, s32[8,1,32]{2,1,0:T(1,128)} %keep_ref.1, bf16[8,128,1280]{2,1,0:T(8,128)(2,1)} %bitcast.20), custom_call_target="tpu_custom_call" | custom-call | tf_op jit(solution)/shard_map/select_rows/pallas_call | solution.py:67
  21.6 7.2 %all-to-all-start = ((bf16[16,32,1280]{2,1,0:T(8,128)(2,1)}), bf16[16,32,1280]{2,1,0:T(8,128)(2,1)S(1)}, u32[]{:S(2)}, u32[]{:S(2)}) async-start(bf16[16,32,1280]{2,1,0:T(8,128)(2,1)} %get-tuple-element.16), calls=%async_computation | async-start | bytes 2621440 | tf_op jit(solution)/shard_map/all_to_all | solution.py:365
  29.5 22.1 %all_gather.9.rows_ref = bf16[128,2560]{1,0:T(8,128)(2,1)} all-gather(bf16[8,2560]{1,0:T(8,128)(2,1)S(1)} %maximum_select_fusion), channel_id=1, replica_groups={{0,2,4,6,8,10,12,14,16,18,20,22,24,26,28,30},{1,3,5,7,9,11,13,15,17,19,..., dimensions={0}, use_global_device_ids=true | all-gather | bytes 696320 | tf_op jit(solution)/shard_map/all_gather | solution.py:372
  51.6 2.4 %project.1 = bf16[128,120]{1,0:T(8,128)(2,1)} custom-call(bf16[128,2560]{1,0:T(8,128)(2,1)} %all_gather.9.rows_ref, bf16[80,2560]{1,0:T(8,128)(2,1)} %bitcast.22, bf16[40,2560]{1,0:T(8,128)(2,1)} %bitcast.23), custom_call_target="tpu_custom_call" | custom-call | tf_op jit(solution)/shard_map/project/pallas_call | solution.py:98
  54.0 20.9 %all-gather = bf16[2048,120]{1,0:T(8,128)(2,1)} all-gather(bf16[128,120]{1,0:T(8,128)(2,1)} %project.1), channel_id=2, replica_groups={{0,2,4,6,8,10,12,14,16,18,20,22,24,26,28,30},{1,3,5,7,9,11,13,15,17,19,..., dimensions={0}, use_global_device_ids=true | all-gather | bytes 522240 | tf_op jit(solution)/shard_map/all_gather | solution.py:376
  74.9 2.2 %pick.1 = bf16[16,4,1920]{2,1,0:T(4,128)(2,1)} custom-call(s32[3]{0:T(128)} %pad_add_fusion.place_ref, bf16[16,128,120]{2,1,0:T(8,128)(2,1)} %bitcast.21), custom_call_target="tpu_custom_call" | custom-call | tf_op jit(solution)/shard_map/pick/pallas_call | solution.py:126
  77.2 5.2 %all-to-all-done = bf16[16,32,1280]{2,1,0:T(8,128)(2,1)S(1)} async-done(((bf16[16,32,1280]{2,1,0:T(8,128)(2,1)}), bf16[16,32,1280]{2,1,0:T(8,128)(2,1)S(1)}, u32[]{:S(2)}, u32[]{:S(2)}) %all-to-all-start) | async-done | bytes 1310752 | tf_op jit(solution)/shard_map/all_to_all | solution.py:365
  82.3 24.7 %all_to_all.15.near_ref = bf16[16,4,1920]{2,1,0:T(4,128)(2,1)S(1)} all-to-all(bf16[16,4,1920]{2,1,0:T(4,128)(2,1)} %pick.1), channel_id=1, replica_groups={{0,64,128,192,256,320,384,448,1,65,129,193,257,321,385,449},{32,96,160,..., dimensions={0} | all-to-all | bytes 491520 | tf_op jit(solution)/shard_map/all_to_all | solution.py:380
  107.0 8.2 %collective-permute-start.1 = (bf16[16,4,1920]{2,1,0:T(4,128)(2,1)S(1)}, bf16[16,4,1920]{2,1,0:T(4,128)(2,1)S(1)}, u32[]{:S(2)}, u32[]{:S(2)}) collective-permute-start(bf16[16,4,1920]{2,1,0:T(4,128)(2,1)S(1)} %all_to_all.15.near_ref), channel_id=1, source_target_pairs={{0,32},{32,0},{64,96},{96,64},{128,160},{160,128},{192,224},{224,1... | collective-permute-start | bytes 737288 | tf_op jit(solution)/shard_map/ppermute | solution.py:383
  115.2 1.1 collective-permute-done.1.far_ref
  116.4 0.7 copy-done.3
  117.1 4.0 %attend.1 = bf16[8,8,2816]{2,1,0:T(8,128)(2,1)} custom-call(s32[3]{0:T(128)} %pad_add_fusion.place_ref, s32[1]{0:T(128)} %bitcast.16.count_ref, s32[8]{0:T(128)} %bitcast.25, bf16[256,1280]{1,0:T(8,128)(2,1)} %get-tuple-element.13.kept_ref, bf16[16,4,1920]{2,1,0:T(4,128)(2,1)} %copy-done.2, bf16[16,4,1920]{2,1,0:T(4,128)(2,1)} %copy-done.3), custom_call_target="tpu_custom_call" | custom-call | tf_op jit(solution)/shard_map/attend/pallas_call | solution.py:217
  121.1 5.0 %all-to-all-start.2 = ((bf16[8,8,2816]{2,1,0:T(8,128)(2,1)}), bf16[8,8,2816]{2,1,0:T(8,128)(2,1)S(1)}, u32[]{:S(2)}, u32[]{:S(2)}) async-start(bf16[8,8,2816]{2,1,0:T(8,128)(2,1)} %attend.1), calls=%async_computation.2 | async-start | bytes 720896 | tf_op jit(solution)/shard_map/all_to_all | solution.py:385
  126.1 2.4 %own_part.1 = (f32[64,32]{1,0:T(8,128)}, f32[64,640]{1,0:T(8,128)}) custom-call(s32[3]{0:T(128)} %pad_add_fusion.place_ref, bf16[16,4,1920]{2,1,0:T(4,128)(2,1)} %copy-done.2, bf16[16,4,1920]{2,1,0:T(4,128)(2,1)} %copy-done.3), custom_call_target="tpu_custom_call" | custom-call | tf_op jit(solution)/shard_map/own_part/pallas_call | solution.py:276
  128.5 14.4 %all-to-all-done.2 = bf16[8,8,2816]{2,1,0:T(8,128)(2,1)S(1)} async-done(((bf16[8,8,2816]{2,1,0:T(8,128)(2,1)}), bf16[8,8,2816]{2,1,0:T(8,128)(2,1)S(1)}, u32[]{:S(2)}, u32[]{:S(2)}) %all-to-all-start.2) | async-done | bytes 360480 | tf_op jit(solution)/shard_map/all_to_all | solution.py:385
  143.0 7.7 %collective-permute-start.2 = (bf16[8,8,2816]{2,1,0:T(8,128)(2,1)S(1)}, bf16[8,8,2816]{2,1,0:T(8,128)(2,1)S(1)}, u32[]{:S(2)}, u32[]{:S(2)}) collective-permute-start(bf16[8,8,2816]{2,1,0:T(8,128)(2,1)S(1)} %all-to-all-done.2), channel_id=1, source_target_pairs={{0,32},{32,0},{64,96},{96,64},{128,160},{160,128},{192,224},{224,1... | collective-permute-start | bytes 1081352 | tf_op jit(solution)/shard_map/ppermute | solution.py:390
  150.7 1.3 collective-permute-done.2
  151.9 0.9 copy-done
  152.9 0.8 copy-done.1
  153.6 3.6 %combine.1 = bf16[64,2560]{1,0:T(8,128)(2,1)} custom-call(bf16[64,2816]{1,0:T(8,128)(2,1)S(1)} %bitcast.17, bf16[64,2816]{1,0:T(8,128)(2,1)S(1)} %bitcast.18, f32[64,32]{1,0:T(8,128)S(1)} %copy-done.1, f32[64,640]{1,0:T(8,128)S(1)} %copy-done), custom_call_target="tpu_custom_call" | custom-call | tf_op jit(solution)/shard_map/combine/pallas_call | solution.py:331
  157.2 1.1 copy.14
  (9 shorter events, 0.7 us)
Async XLA Ops:
  2.4 19.2 %collective-permute-start = (bf16[4,2560]{1,0:T(4,128)(2,1)S(1)}, bf16[4,2560]{1,0:T(4,128)(2,1)S(1)}, u32[]{:S(2)}, u32[]{:S(2)}) collective-permute-start(bf16[4,2560]{1,0:T(4,128)(2,1)S(1)} %fusion.2), channel_id=1, source_target_pairs={{0,257},{1,256},{2,259},{3,258},{4,261},{5,260},{6,263},{7,262},{8... | collective-permute-start | bytes 61448 | tf_op jit(solution)/shard_map/ppermute | solution.py:363
  21.6 60.7 %all-to-all-start = ((bf16[16,32,1280]{2,1,0:T(8,128)(2,1)}), bf16[16,32,1280]{2,1,0:T(8,128)(2,1)S(1)}, u32[]{:S(2)}, u32[]{:S(2)}) async-start(bf16[16,32,1280]{2,1,0:T(8,128)(2,1)} %get-tuple-element.16), calls=%async_computation | async-start | bytes 2621440 | tf_op jit(solution)/shard_map/all_to_all | solution.py:365
  107.0 9.4 %copy-start.2 = (bf16[16,4,1920]{2,1,0:T(4,128)(2,1)}, bf16[16,4,1920]{2,1,0:T(4,128)(2,1)S(1)}, u32[]{:S(2)}) copy-start(bf16[16,4,1920]{2,1,0:T(4,128)(2,1)S(1)} %all_to_all.15.near_ref) | copy-start | bytes 737284
  107.0 9.4 %collective-permute-start.1 = (bf16[16,4,1920]{2,1,0:T(4,128)(2,1)S(1)}, bf16[16,4,1920]{2,1,0:T(4,128)(2,1)S(1)}, u32[]{:S(2)}, u32[]{:S(2)}) collective-permute-start(bf16[16,4,1920]{2,1,0:T(4,128)(2,1)S(1)} %all_to_all.15.near_ref), channel_id=1, source_target_pairs={{0,32},{32,0},{64,96},{96,64},{128,160},{160,128},{192,224},{224,1... | collective-permute-start | bytes 737288 | tf_op jit(solution)/shard_map/ppermute | solution.py:383
  116.4 0.7 copy-start.3
  121.1 21.9 %all-to-all-start.2 = ((bf16[8,8,2816]{2,1,0:T(8,128)(2,1)}), bf16[8,8,2816]{2,1,0:T(8,128)(2,1)S(1)}, u32[]{:S(2)}, u32[]{:S(2)}) async-start(bf16[8,8,2816]{2,1,0:T(8,128)(2,1)} %attend.1), calls=%async_computation.2 | async-start | bytes 720896 | tf_op jit(solution)/shard_map/all_to_all | solution.py:385
  143.0 9.0 %collective-permute-start.2 = (bf16[8,8,2816]{2,1,0:T(8,128)(2,1)S(1)}, bf16[8,8,2816]{2,1,0:T(8,128)(2,1)S(1)}, u32[]{:S(2)}, u32[]{:S(2)}) collective-permute-start(bf16[8,8,2816]{2,1,0:T(8,128)(2,1)S(1)} %all-to-all-done.2), channel_id=1, source_target_pairs={{0,32},{32,0},{64,96},{96,64},{128,160},{160,128},{192,224},{224,1... | collective-permute-start | bytes 1081352 | tf_op jit(solution)/shard_map/ppermute | solution.py:390
  151.9 0.9 copy-start
  152.9 0.8 copy-start.1

commit v6 on v5

--- a/solution.py
+++ b/solution.py
@@ -26,14 +26,19 @@
     (p * 2 * PLANE + t, (p ^ 8) * 2 * PLANE + (t ^ 1)) for p in range(HOLDERS) for t in range(2 * PLANE)
 ]
 
-COLUMN_GROUPS = [
-    [(2 * z + core) * 2 * PLANE + 2 * xy + half for half in range(2) for z in range(CHIPS)]
+FOUR_GROUPS = [
+    [
+        (2 * (4 * quad + z) + core) * 2 * PLANE + 2 * xy + half
+        for half in range(2)
+        for quad in range(2)
+    ]
     for xy in range(PLANE)
+    for z in range(CHIPS // 2)
     for core in range(2)
 ]
+QUAD_GROUPS = [[CHIPS * quad + i for i in range(CHIPS)] for quad in range(2)]
+OTHER_QUAD = [(i, i ^ CHIPS) for i in range(HOLDERS)]
 HALF_COLUMNS = (QUERIES + 2 * KEYS) // 2
-RUN_GROUPS = [[2 * z + core for z in range(CHIPS)] for core in range(2)]
-OTHER_CORE = [(i, i ^ 1) for i in range(HOLDERS)]
 STEP = 4
 
 VMEM = pl.BlockSpec(memory_space=pltpu.VMEM)
@@ -104,7 +109,7 @@
     )(rows, w_query.T, w_keyvalue.T)
 
 
-def pick_kernel(place_ref, all_ref, out_ref, rows_ref):
+def pick_kernel(plane_ref, all_ref, out_ref, rows_ref):
     half = HEAD_DIM // 2
     for i in range(PLANE):
         block = all_ref[i].astype(jnp.float32)
@@ -115,33 +120,33 @@
     share = out_ref.shape[1]
     for h in range(2):
         piece = rows_ref[h * share : (h + 1) * share].astype(jnp.bfloat16)
-        for z in range(CHIPS):
-            out_ref[h * CHIPS + z] = piece
-
-
-def pick(place, everyone):
+        for quad in range(2):
+            out_ref[2 * h + quad] = piece
+
+
+def pick(plane, everyone):
     count, rows, width = everyone.shape
     both = rows // PLANE
-    piece = jax.ShapeDtypeStruct((2 * CHIPS, both // 2, HALF_COLUMNS), everyone.dtype)
+    piece = jax.ShapeDtypeStruct((4, both // 2, HALF_COLUMNS), everyone.dtype)
     return pl.pallas_call(
         pick_kernel,
         out_shape=piece,
         grid_spec=pltpu.PrefetchScalarGridSpec(
             num_scalar_prefetch=1,
             grid=(1,),
-            in_specs=[pl.BlockSpec((count, both, width), lambda i, place: (0, place[0], 0))],
+            in_specs=[pl.BlockSpec((count, both, width), lambda i, plane: (0, plane[0], 0))],
             out_specs=pl.BlockSpec(piece.shape, lambda i, *_: (0, 0, 0)),
             scratch_shapes=[pltpu.VMEM((both, HALF_COLUMNS), jnp.float32)],
         ),
         name="pick",
-    )(place, everyone)
-
-
-def held(place_ref, near_ref, far_ref, chip, core, half, columns):
-    spot = half * CHIPS + jnp.where(place_ref[1] == half, chip, chip ^ 4)
-    near = near_ref[spot, :, columns].astype(jnp.float32)
-    far = far_ref[spot, :, columns].astype(jnp.float32)
-    return jnp.where(place_ref[2] == core, near, far)
+    )(plane, everyone)
+
+
+def held(rows_ref, holder, half, columns):
+    quad, inside = holder // CHIPS, holder % CHIPS
+    same = lax.axis_index("tensor") % 2 == half
+    spot = inside * 4 + 2 * half + jnp.where(same, quad, 1 - quad)
+    return rows_ref[spot, :, columns].astype(jnp.float32)
 
 
 def pieces(value, count):
@@ -154,10 +159,10 @@
 
 
 def attend_kernel(
-    place_ref, count_ref, owner_ref, kept_ref, near_ref, far_ref, out_ref, sum_ref, peak_ref, total_ref
+    count_ref, owner_ref, kept_ref, rows_ref, out_ref, sum_ref, peak_ref, total_ref
 ):
     scale = HEAD_DIM ** (-0.5)
-    share = near_ref.shape[1]
+    share = rows_ref.shape[1]
     line = lax.broadcasted_iota(jnp.int32, (share, QUERIES // 2), 0)
     head = lax.broadcasted_iota(jnp.int32, (KV_HEADS, KEYS), 0) * HEAD_DIM
     lane = lax.broadcasted_iota(jnp.int32, (KV_HEADS, KEYS), 1)
@@ -167,9 +172,7 @@
         holder = request // share
         query = []
         for half in range(2):
-            block = held(
-                place_ref, near_ref, far_ref, holder // 2, holder % 2, half, pl.ds(0, QUERIES // 2)
-            )
+            block = held(rows_ref, holder, half, pl.ds(0, QUERIES // 2))
             query.append(
                 jnp.sum(jnp.where(line == request % share, block, 0.0), axis=0, keepdims=True)
             )
@@ -208,16 +211,15 @@
     columns = pieces(peak_ref[...], 3) + pieces(total_ref[...], 3) + [tag, tag]
     columns = [column.astype(jnp.float32) for column in columns]
     columns = jnp.concatenate(columns, axis=1).astype(jnp.bfloat16)
-    for z in range(CHIPS):
-        out_ref[z, :, :QUERIES] = sums
-        out_ref[z, :, QUERIES:] = columns
-
-
-def attend(place, page_count, page_owner, kept, near, far):
+    out_ref[:, :QUERIES] = sums
+    out_ref[:, QUERIES:] = columns
+
+
+def attend(page_count, page_owner, kept, rows):
     return pl.pallas_call(
         attend_kernel,
-        out_shape=jax.ShapeDtypeStruct((CHIPS, SOURCES, QUERIES + EXTRA), jnp.bfloat16),
-        in_specs=[SMEM] * 3 + [VMEM] * 3,
+        out_shape=jax.ShapeDtypeStruct((SOURCES, QUERIES + EXTRA), jnp.bfloat16),
+        in_specs=[SMEM] * 2 + [VMEM] * 2,
         out_specs=VMEM,
         scratch_shapes=[
             pltpu.VMEM((SOURCES, QUERIES), jnp.float32),
@@ -225,7 +227,7 @@
             pltpu.VMEM((SOURCES, HEADS), jnp.float32),
         ],
         name="attend",
-    )(place, page_count, page_owner, kept, near, far)
+    )(page_count, page_owner, kept, rows)
 
 
 def spread_dot(value, chosen, contract, count, chosen_first=False):
@@ -245,16 +247,14 @@
     return ((lane >= head) & (lane < head + HEAD_DIM)).astype(jnp.float32).astype(jnp.bfloat16)
 
 
-def own_kernel(place_ref, near_ref, far_ref, score_ref, value_ref, query_ref, pair_ref):
+def own_kernel(rows_ref, score_ref, value_ref, query_ref, pair_ref):
     scale = HEAD_DIM ** (-0.5)
-    share = near_ref.shape[1]
+    share = rows_ref.shape[1]
     piece = HEAD_DIM // 2
     for holder in range(HOLDERS):
         rows = slice(holder * share, (holder + 1) * share)
         for half in range(2):
-            block = held(
-                place_ref, near_ref, far_ref, holder // 2, holder % 2, half, pl.ds(0, HALF_COLUMNS)
-            )
+            block = held(rows_ref, holder, half, pl.ds(0, HALF_COLUMNS))
             for k in range(2):
                 at = (2 * k + half) * KEYS
                 query_ref[rows, at : at + KEYS] = block[:, k * KEYS : (k + 1) * KEYS]
@@ -271,31 +271,28 @@
     score_ref[...] = scale * spread_dot(product, head_columns(), ((1,), (1,)), 3)
 
 
-def own_part(place, near, far):
-    requests = HOLDERS * near.shape[1]
+def own_part(rows):
+    requests = HOLDERS * rows.shape[1]
     return pl.pallas_call(
         own_kernel,
         out_shape=(
             jax.ShapeDtypeStruct((requests, HEADS), jnp.float32),
             jax.ShapeDtypeStruct((requests, KEYS), jnp.float32),
         ),
-        in_specs=[SMEM, VMEM, VMEM],
+        in_specs=[VMEM],
         out_specs=(VMEM, VMEM),
         scratch_shapes=[
             pltpu.VMEM((requests, QUERIES), jnp.float32),
             pltpu.VMEM((2, requests, KEYS), jnp.float32),
         ],
         name="own_part",
-    )(place, near, far)
-
-
-def combine_kernel(near_ref, far_ref, own_ref, value_ref, out_ref):
+    )(rows)
+
+
+def combine_kernel(part_ref, own_ref, value_ref, out_ref):
     requests = out_ref.shape[0]
-    part = jnp.concatenate(
-        [near_ref[...].astype(jnp.float32), far_ref[...].astype(jnp.float32)], axis=0
-    )
-    slots = part.shape[0]
-    extra = part[:, QUERIES:]
+    slots = part_ref.shape[0]
+    extra = part_ref[:, QUERIES:].astype(jnp.float32)
     column = [extra[:, i * HEADS : (i + 1) * HEADS] for i in range(7)]
     peaks = column[0] + column[1] + column[2]
     totals = column[3] + column[4] + column[5]
@@ -317,7 +314,7 @@
     total = spread_dot(weight * totals, member, ((0,), (0,)), 3, True) + own_weight
     inverse = 1.0 / total
     weight = weight * spread_dot(inverse, member, ((1,), (0,)), 3, True)
-    scaled = part[:, :QUERIES] * spread_dot(weight, expand, ((1,), (0,)), 2)
+    scaled = part_ref[:, :QUERIES].astype(jnp.float32) * spread_dot(weight, expand, ((1,), (0,)), 2)
     mixed = spread_dot(scaled, member, ((0,), (0,)), 2, True)
     own_share = spread_dot(own_weight * inverse, expand, ((1,), (0,)), 2)
     mixed = mixed + own_share * jnp.concatenate([value_ref[...]] * REPEAT, axis=1)
@@ -327,15 +324,31 @@
         out_ref[:, h * HEAD_DIM : (h + 1) * HEAD_DIM] = mixed[:, at : at + HEAD_DIM]
 
 
-def combine(near, far, own, value):
+def combine(parts, own, value):
     return pl.pallas_call(
         combine_kernel,
         out_shape=jax.ShapeDtypeStruct((own.shape[0], QUERIES), jnp.bfloat16),
-        in_specs=[VMEM] * 4,
+        in_specs=[VMEM] * 3,
         out_specs=VMEM,
         compiler_params=pltpu.CompilerParams(vmem_limit_bytes=48 * 1024 * 1024),
         name="combine",
-    )(near, far, own, value)
+    )(parts, own, value)
+
+
+def settle_kernel(in_ref, out_ref):
+    out_ref[...] = in_ref[...]
+
+
+def settle(pages):
+    block = pl.BlockSpec((4,) + pages.shape[1:], lambda i: (i, 0, 0))
+    return pl.pallas_call(
+        settle_kernel,
+        out_shape=jax.ShapeDtypeStruct(pages.shape, pages.dtype),
+        grid=(pages.shape[0] // 4,),
+        in_specs=[block],
+        out_specs=block,
+        name="settle",
+    )(pages)
 
 
 def per_device(
@@ -344,7 +357,6 @@
     holder = lax.axis_index("page")
     group = lax.axis_index("tensor")
     half = group % 2
-    place = jnp.stack([group // 2, half, holder % 2])
     share = tokens.shape[0] // HOLDERS
 
     def normalise(rows):
@@ -376,21 +388,25 @@
     everyone = lax.all_gather(
         projected, "tensor", axis=0, axis_index_groups=PLANE_GROUPS, tiled=False
     )
-    halves, arrived = lax.optimization_barrier((pick(place, everyone), arrived))
-    near = lax.all_to_all(
-        halves, ("page", "tensor"), 0, 0, axis_index_groups=COLUMN_GROUPS, tiled=True
-    )
-    far = lax.ppermute(near, "page", OTHER_CORE)
-    part = attend(place, page_count, page_owner, kept, near, far)
-    near_part = lax.all_to_all(
-        part, "page", 0, 0, axis_index_groups=RUN_GROUPS, tiled=True
-    )
-    own, value = own_part(place, near, far)
-    near_part, own, value = lax.optimization_barrier((near_part, own, value))
-    far_part = lax.ppermute(near_part, "page", OTHER_CORE)
-    flat = (CHIPS * SOURCES, QUERIES + EXTRA)
-    attended = combine(near_part.reshape(flat), far_part.reshape(flat), own, value)
-    return attended, arrived[:, None]
+    halves = pick((group // 2).reshape(1), everyone)
+    halves, arrived = lax.optimization_barrier((halves, arrived))
+    quarter = lax.all_to_all(
+        halves, ("page", "tensor"), 0, 0, axis_index_groups=FOUR_GROUPS, tiled=True
+    )
+    rows = lax.all_gather(quarter, "page", axis=0, axis_index_groups=QUAD_GROUPS, tiled=True)
+    part = attend(page_count, page_owner, kept, rows)
+    far = lax.ppermute(part, "page", OTHER_QUAD)
+    own, value = own_part(rows)
+    settled = settle(arrived)
+    far, own, value, settled = lax.optimization_barrier((far, own, value, settled))
+    parts = lax.all_gather(
+        jnp.concatenate([part, far], axis=0),
+        "page",
+        axis=0,
+        axis_index_groups=QUAD_GROUPS,
+        tiled=True,
+    )
+    return combine(parts, own, value), settled[:, None]
 
 
 def solution(mesh):

time: 159 us -> 162 us (1.019)
  blocking collectives: 67.7 us -> 99.7 us
  starting transfers between devices: 41.4 us -> 22.5 us
  waiting for transfers between devices: 22 us -> 11.3 us
  Pallas kernels: 19.9 us -> 22.3 us
  local copies, waits for them, and re-layouts: 3.43 us -> 1.68 us
    all_gather x0 -> x2, blocking collectives: none -> 33.6 us  [the longest x1 17.7 us: per_device(): lax.all_gather(quarter, 'page', axis=0, axis_index_groups=QUAD_GROUPS, ti...]
    all_to_all x1 -> x0, waiting for transfers between devices: 14.4 us -> none  [per_device(): lax.all_to_all(part, 'page', 0, 0, axis_index_groups=RUN_GROUPS, tiled=True)]
    ppermute x2 -> x1, starting transfers between devices: 15.9 us -> 2.04 us  [per_device(): far = lax.ppermute(part, 'page', OTHER_QUAD)]
    all_to_all x1 -> x0, starting transfers between devices: 5.01 us -> none  [per_device(): lax.all_to_all(part, 'page', 0, 0, axis_index_groups=RUN_GROUPS, tiled=True)]
    pallas_call x1 -> x2, Pallas kernels: 4.02 us -> 7.32 us  [the longest x1 3.85 us: attend(): pl.pallas_call(attend_kernel, out_shape=jax.ShapeDtypeStruct((SOURCES, QU...]
    ppermute x2 -> x1, waiting for transfers between devices: 2.4 us -> 4.72 us  [per_device(): far = lax.ppermute(part, 'page', OTHER_QUAD)]
    unnamed x9 -> x8, local copies, waits for them, and re-layouts: 3.43 us -> 1.68 us
  transfers between devices with their start and end apart: 5 -> 3, of which waited for: 4 -> 2; matrix products, arithmetic and copies ran while one was open for 0% -> 0% of each run, Pallas kernels for 8% -> 9%
where the time goes in v6:
time: 162 us; the launch traced here: 161 us
  blocking collectives  99.7 us (62%)
  starting transfers between devices  22.5 us (14%)
  Pallas kernels  22.3 us (14%)
  waiting for transfers between devices  11.3 us (7%)
  other arithmetic  1.86 us (1%)
  local copies, waits for them, and re-layouts  1.68 us (1%)
    all_to_all x1, blocking collectives, per_device(): lax.all_to_all(halves, ('page', 'tensor'), 0, 0, axis_index_groups=FOUR_G...  23.1 us
    all_gather x1, blocking collectives, per_device(): lax.all_gather(both, 'tensor', axis=0, axis_index_groups=PLANE_GROUPS, ti...  22.1 us
    all_gather x1, blocking collectives, per_device(): lax.all_gather(projected, 'tensor', axis=0, axis_index_groups=PLANE_GROUP...  20.9 us
    all_gather x1, blocking collectives, per_device(): lax.all_gather(quarter, 'page', axis=0, axis_index_groups=QUAD_GROUPS, ti...  17.7 us
    all_gather x1, blocking collectives, per_device(): lax.all_gather(jnp.concatenate([part, far], axis=0), 'page', axis=0, axis...  15.9 us
    ppermute x1, starting transfers between devices, per_device(): across = lax.ppermute(mine, ('page', 'tensor'), OTHER_HALF)  13.3 us
    all_to_all x1, starting transfers between devices, per_device(): arrived = lax.all_to_all(compact, 'page', 0, 0, tiled=True)  7.16 us
    all_to_all x1, waiting for transfers between devices, per_device(): arrived = lax.all_to_all(compact, 'page', 0, 0, tiled=True)  6.55 us
  transfers between devices with their start and end apart: 3, of which 2 were waited for; matrix products, arithmetic and copies ran while one was open for 0% of the time, Pallas kernels for 9%

profile of v6, /device:TPU:1, one launch (start us, length us, event | category | flops | bytes accessed | tf_op | source)
XLA Modules:
  0.0 160.6 jit_solution(14041514106233464913)
XLA Ops:
  0.6 0.9 fusion
  1.6 0.9 fusion.2
  2.4 13.3 %collective-permute-start = (bf16[4,2560]{1,0:T(4,128)(2,1)S(1)}, bf16[4,2560]{1,0:T(4,128)(2,1)S(1)}, u32[]{:S(2)}, u32[]{:S(2)}) collective-permute-start(bf16[4,2560]{1,0:T(4,128)(2,1)S(1)} %fusion.2), channel_id=1, source_target_pairs={{0,257},{1,256},{2,259},{3,258},{4,261},{5,260},{6,263},{7,262},{8... | collective-permute-start | bytes 61448 | tf_op jit(solution)/shard_map/ppermute | solution.py:375
  16.4 5.2 %select_rows.1 = (bf16[16,32,1280]{2,1,0:T(8,128)(2,1)}, bf16[256,1280]{1,0:T(8,128)(2,1)}) custom-call(s32[1]{0:T(128)} %bitcast.11.count_ref, s32[8]{0:T(128)} %bitcast.18, s32[8,1,32]{2,1,0:T(1,128)} %keep_ref.1, bf16[8,128,1280]{2,1,0:T(8,128)(2,1)} %bitcast.13), custom_call_target="tpu_custom_call" | custom-call | tf_op jit(solution)/shard_map/select_rows/pallas_call | solution.py:72
  21.6 0.0 collective-permute-done
  21.6 7.2 %all-to-all-start = ((bf16[16,32,1280]{2,1,0:T(8,128)(2,1)}), bf16[16,32,1280]{2,1,0:T(8,128)(2,1)S(1)}, u32[]{:S(2)}, u32[]{:S(2)}) async-start(bf16[16,32,1280]{2,1,0:T(8,128)(2,1)} %get-tuple-element.17), calls=%async_computation | async-start | bytes 2621440 | tf_op jit(solution)/shard_map/all_to_all | solution.py:377
  28.8 22.1 %all_gather.15.rows_ref = bf16[128,2560]{1,0:T(8,128)(2,1)} all-gather(bf16[8,2560]{1,0:T(8,128)(2,1)S(1)} %maximum_select_fusion), channel_id=1, replica_groups={{0,2,4,6,8,10,12,14,16,18,20,22,24,26,28,30},{1,3,5,7,9,11,13,15,17,19,..., dimensions={0}, use_global_device_ids=true | all-gather | bytes 696320 | tf_op jit(solution)/shard_map/all_gather | solution.py:384
  50.9 2.4 %project.1 = bf16[128,120]{1,0:T(8,128)(2,1)} custom-call(bf16[128,2560]{1,0:T(8,128)(2,1)} %all_gather.15.rows_ref, bf16[80,2560]{1,0:T(8,128)(2,1)} %bitcast.16, bf16[40,2560]{1,0:T(8,128)(2,1)} %bitcast.17), custom_call_target="tpu_custom_call" | custom-call | tf_op jit(solution)/shard_map/project/pallas_call | solution.py:103
  53.4 20.9 %all-gather = bf16[2048,120]{1,0:T(8,128)(2,1)} all-gather(bf16[128,120]{1,0:T(8,128)(2,1)} %project.1), channel_id=2, replica_groups={{0,2,4,6,8,10,12,14,16,18,20,22,24,26,28,30},{1,3,5,7,9,11,13,15,17,19,..., dimensions={0}, use_global_device_ids=true | all-gather | bytes 522240 | tf_op jit(solution)/shard_map/all_gather | solution.py:388
  74.3 1.5 pick.1
  75.8 6.6 %all-to-all-done.in_ref = bf16[16,32,1280]{2,1,0:T(8,128)(2,1)S(1)} async-done(((bf16[16,32,1280]{2,1,0:T(8,128)(2,1)}), bf16[16,32,1280]{2,1,0:T(8,128)(2,1)S(1)}, u32[]{:S(2)}, u32[]{:S(2)}) %all-to-all-start) | async-done | bytes 1310752 | tf_op jit(solution)/shard_map/all_to_all | solution.py:377
  82.3 23.1 %all_to_all.10 = bf16[4,4,1920]{2,1,0:T(4,128)(2,1)S(1)} all-to-all(bf16[4,4,1920]{2,1,0:T(4,128)(2,1)} %pick.1), channel_id=1, replica_groups={{0,256,1,257},{32,288,33,289},{64,320,65,321},{96,352,97,353},{128,384,..., dimensions={0} | all-to-all | bytes 122880 | tf_op jit(solution)/shard_map/all_to_all | solution.py:393
  105.4 17.7 %all_gather.18.rows_ref = bf16[32,4,1920]{2,1,0:T(4,128)(2,1)} all-gather(bf16[4,4,1920]{2,1,0:T(4,128)(2,1)S(1)} %all_to_all.10), channel_id=1, replica_groups={{0,32,64,96,128,160,192,224},{256,288,320,352,384,416,448,480},{1,33,65..., dimensions={0}, use_global_device_ids=true | all-gather | bytes 552960 | tf_op jit(solution)/shard_map/all_gather | solution.py:396
  123.2 3.9 %attend.1 = bf16[8,2816]{1,0:T(8,128)(2,1)} custom-call(s32[1]{0:T(128)} %bitcast.12.count_ref, s32[8]{0:T(128)} %bitcast.19, bf16[256,1280]{1,0:T(8,128)(2,1)} %get-tuple-element.14.kept_ref, bf16[32,4,1920]{2,1,0:T(4,128)(2,1)} %all_gather.18.rows_ref), custom_call_target="tpu_custom_call" | custom-call | tf_op jit(solution)/shard_map/attend/pallas_call | solution.py:219
  127.0 2.0 %collective-permute-start.1 = (bf16[8,2816]{1,0:T(8,128)(2,1)}, bf16[8,2816]{1,0:T(8,128)(2,1)S(1)}, u32[]{:S(2)}, u32[]{:S(2)}) collective-permute-start(bf16[8,2816]{1,0:T(8,128)(2,1)} %attend.1), channel_id=1, source_target_pairs={{0,256},{32,288},{64,320},{96,352},{128,384},{160,416},{192,448},{... | collective-permute-start | bytes 135176 | tf_op jit(solution)/shard_map/ppermute | solution.py:398
  129.1 0.0 copy-done.2
  129.1 3.5 %settle.1 = bf16[16,32,1280]{2,1,0:T(8,128)(2,1)} custom-call(bf16[16,32,1280]{2,1,0:T(8,128)(2,1)} %copy-done.2), custom_call_target="tpu_custom_call" | custom-call | tf_op jit(solution)/shard_map/settle/pallas_call | solution.py:344
  132.5 2.3 %own_part.1 = (f32[64,32]{1,0:T(8,128)}, f32[64,640]{1,0:T(8,128)}) custom-call(bf16[32,4,1920]{2,1,0:T(4,128)(2,1)} %all_gather.18.rows_ref), custom_call_target="tpu_custom_call" | custom-call | tf_op jit(solution)/shard_map/own_part/pallas_call | solution.py:276
  134.8 4.7 %collective-permute-done.1 = bf16[8,2816]{1,0:T(8,128)(2,1)S(1)} collective-permute-done((bf16[8,2816]{1,0:T(8,128)(2,1)}, bf16[8,2816]{1,0:T(8,128)(2,1)S(1)}, u32[]{:S(2)}, u32[]{:S(2)}) %collective-permute-start.1) | collective-permute-done | bytes 45088 | tf_op jit(solution)/shard_map/ppermute | solution.py:398
  139.5 0.0 copy-done.3
  139.5 15.9 %all_gather.19.part_ref = bf16[128,2816]{1,0:T(8,128)(2,1)S(1)} all-gather(bf16[16,2816]{1,0:T(8,128)(2,1)S(1)} %pad_maximum_fusion), channel_id=1, replica_groups={{0,32,64,96,128,160,192,224},{256,288,320,352,384,416,448,480},{1,33,65..., dimensions={0}, use_global_device_ids=true | all-gather | bytes 811008 | tf_op jit(solution)/shard_map/all_gather | solution.py:402
  155.4 0.9 copy-done
  156.3 0.8 copy-done.1
  157.1 3.6 %combine.1 = bf16[64,2560]{1,0:T(8,128)(2,1)} custom-call(bf16[128,2816]{1,0:T(8,128)(2,1)S(1)} %all_gather.19.part_ref, f32[64,32]{1,0:T(8,128)S(1)} %copy-done.1, f32[64,640]{1,0:T(8,128)S(1)} %copy-done), custom_call_target="tpu_custom_call" | custom-call | tf_op jit(solution)/shard_map/combine/pallas_call | solution.py:328
  (7 shorter events, 0.1 us)
Async XLA Ops:
  2.4 19.2 %collective-permute-start = (bf16[4,2560]{1,0:T(4,128)(2,1)S(1)}, bf16[4,2560]{1,0:T(4,128)(2,1)S(1)}, u32[]{:S(2)}, u32[]{:S(2)}) collective-permute-start(bf16[4,2560]{1,0:T(4,128)(2,1)S(1)} %fusion.2), channel_id=1, source_target_pairs={{0,257},{1,256},{2,259},{3,258},{4,261},{5,260},{6,263},{7,262},{8... | collective-permute-start | bytes 61448 | tf_op jit(solution)/shard_map/ppermute | solution.py:375
  21.6 60.7 %all-to-all-start = ((bf16[16,32,1280]{2,1,0:T(8,128)(2,1)}), bf16[16,32,1280]{2,1,0:T(8,128)(2,1)S(1)}, u32[]{:S(2)}, u32[]{:S(2)}) async-start(bf16[16,32,1280]{2,1,0:T(8,128)(2,1)} %get-tuple-element.17), calls=%async_computation | async-start | bytes 2621440 | tf_op jit(solution)/shard_map/all_to_all | solution.py:377
  82.3 46.7 %copy-start.2 = (bf16[16,32,1280]{2,1,0:T(8,128)(2,1)}, bf16[16,32,1280]{2,1,0:T(8,128)(2,1)S(1)}, u32[]{:S(2)}) copy-start(bf16[16,32,1280]{2,1,0:T(8,128)(2,1)S(1)} %all-to-all-done.in_ref) | copy-start | bytes 3932164
  127.0 12.5 %copy-start.3 = (bf16[8,2816]{1,0:T(8,128)(2,1)S(1)}, bf16[8,2816]{1,0:T(8,128)(2,1)}, u32[]{:S(2)}) copy-start(bf16[8,2816]{1,0:T(8,128)(2,1)} %attend.1) | copy-start | bytes 135172
  127.0 12.5 %collective-permute-start.1 = (bf16[8,2816]{1,0:T(8,128)(2,1)}, bf16[8,2816]{1,0:T(8,128)(2,1)S(1)}, u32[]{:S(2)}, u32[]{:S(2)}) collective-permute-start(bf16[8,2816]{1,0:T(8,128)(2,1)} %attend.1), channel_id=1, source_target_pairs={{0,256},{32,288},{64,320},{96,352},{128,384},{160,416},{192,448},{... | collective-permute-start | bytes 135176 | tf_op jit(solution)/shard_map/ppermute | solution.py:398
  155.4 0.9 copy-start
  156.3 0.8 copy-start.1

commit v7 on v6

--- a/solution.py
+++ b/solution.py
@@ -37,6 +37,8 @@
     for core in range(2)
 ]
 QUAD_GROUPS = [[CHIPS * quad + i for i in range(CHIPS)] for quad in range(2)]
+OTHER_CORE = [(i, i ^ 1) for i in range(HOLDERS)]
+OTHER_CHIP = [[(i, i ^ (2 * d)) for i in range(HOLDERS)] for d in range(CHIPS)]
 OTHER_QUAD = [(i, i ^ CHIPS) for i in range(HOLDERS)]
 HALF_COLUMNS = (QUERIES + 2 * KEYS) // 2
 STEP = 4
@@ -45,36 +47,40 @@
 SMEM = pl.BlockSpec(memory_space=pltpu.SMEM)
 
 
-def select_kernel(count_ref, dest_ref, keep_ref, page_ref, out_ref, kept_ref):
-    step = pl.program_id(0)
-
-    @pl.when(step == 0)
+def select_kernel(count_ref, dest_ref, keep_ref, page_ref, *refs):
+    out_refs, kept_ref = refs[:CHIPS], refs[CHIPS]
+    grid_step = pl.program_id(0)
+    holder = lax.axis_index("page")
+
+    @pl.when(grid_step == 0)
     def _():
-        out_ref[...] = jnp.zeros_like(out_ref)
+        for ref in out_refs:
+            ref[...] = jnp.zeros_like(ref)
 
     rows = page_ref.shape[1]
     for i in range(STEP):
-        slot = step * STEP + i
+        slot = grid_step * STEP + i
         picks = jnp.broadcast_to(keep_ref[i], (rows, KEEP))
         chosen = (picks == lax.broadcasted_iota(jnp.int32, (rows, KEEP), 0)).astype(jnp.float32)
         kept = jnp.dot(
             chosen.T.astype(jnp.bfloat16), page_ref[i], preferred_element_type=jnp.float32
         ).astype(jnp.bfloat16)
         kept_ref[i * KEEP : (i + 1) * KEEP] = kept
-
-        @pl.when(slot < count_ref[0])
-        def _():
-            out_ref[dest_ref[slot]] = kept
+        target = dest_ref[slot] ^ holder
+        live = slot < count_ref[0]
+        for d in range(CHIPS):
+
+            @pl.when(live & (target // 2 == d))
+            def _():
+                out_refs[d][target % 2] = kept_ref[i * KEEP : (i + 1) * KEEP]
 
 
 def select_rows(page_count, dest_slot, keep_rows, cache):
     sources, _, rows, width = cache.shape
-    return pl.pallas_call(
+    block = jax.ShapeDtypeStruct((2, KEEP, width), cache.dtype)
+    results = pl.pallas_call(
         select_kernel,
-        out_shape=(
-            jax.ShapeDtypeStruct((HOLDERS, KEEP, width), cache.dtype),
-            jax.ShapeDtypeStruct((sources * KEEP, width), cache.dtype),
-        ),
+        out_shape=[block] * CHIPS + [jax.ShapeDtypeStruct((sources * KEEP, width), cache.dtype)],
         grid_spec=pltpu.PrefetchScalarGridSpec(
             num_scalar_prefetch=2,
             grid=(sources // STEP,),
@@ -82,13 +88,45 @@
                 pl.BlockSpec((STEP, 1, KEEP), lambda s, *_: (s, 0, 0)),
                 pl.BlockSpec((STEP, rows, width), lambda s, *_: (s, 0, 0)),
             ],
-            out_specs=[
-                pl.BlockSpec((HOLDERS, KEEP, width), lambda s, *_: (0, 0, 0)),
-                pl.BlockSpec((STEP * KEEP, width), lambda s, *_: (s, 0)),
-            ],
+            out_specs=[pl.BlockSpec(block.shape, lambda s, *_: (0, 0, 0))] * CHIPS
+            + [pl.BlockSpec((STEP * KEEP, width), lambda s, *_: (s, 0))],
         ),
         name="select_rows",
     )(page_count, dest_slot, keep_rows, cache.reshape(sources, rows, width))
+    return results[:CHIPS], results[CHIPS]
+
+
+def pack_kernel(*refs):
+    for d in range(CHIPS):
+        refs[CHIPS][d] = refs[d][1]
+
+
+def pack(got):
+    return pl.pallas_call(
+        pack_kernel,
+        out_shape=jax.ShapeDtypeStruct((CHIPS,) + got[0].shape[1:], got[0].dtype),
+        in_specs=[VMEM] * CHIPS,
+        out_specs=VMEM,
+        name="pack",
+    )(*got)
+
+
+def place_kernel(*refs):
+    got_refs, cross_ref, out_ref = refs[:CHIPS], refs[CHIPS], refs[CHIPS + 1]
+    holder = lax.axis_index("page")
+    for d in range(CHIPS):
+        out_ref[holder ^ (2 * d)] = got_refs[d][0]
+        out_ref[holder ^ (2 * d + 1)] = cross_ref[d]
+
+
+def place_pages(got, cross):
+    return pl.pallas_call(
+        place_kernel,
+        out_shape=jax.ShapeDtypeStruct((HOLDERS,) + cross.shape[1:], cross.dtype),
+        in_specs=[VMEM] * (CHIPS + 1),
+        out_specs=VMEM,
+        name="place_pages",
+    )(*got, cross)
 
 
 def project_kernel(rows_ref, query_ref, pair_ref, out_ref):
@@ -109,7 +147,7 @@
     )(rows, w_query.T, w_keyvalue.T)
 
 
-def pick_kernel(plane_ref, all_ref, out_ref, rows_ref):
+def pick_kernel(all_ref, out_ref, rows_ref):
     half = HEAD_DIM // 2
     for i in range(PLANE):
         block = all_ref[i].astype(jnp.float32)
@@ -124,22 +162,16 @@
             out_ref[2 * h + quad] = piece
 
 
-def pick(plane, everyone):
-    count, rows, width = everyone.shape
-    both = rows // PLANE
-    piece = jax.ShapeDtypeStruct((4, both // 2, HALF_COLUMNS), everyone.dtype)
+def pick(block):
+    count, both, _ = block.shape
     return pl.pallas_call(
         pick_kernel,
-        out_shape=piece,
-        grid_spec=pltpu.PrefetchScalarGridSpec(
-            num_scalar_prefetch=1,
-            grid=(1,),
-            in_specs=[pl.BlockSpec((count, both, width), lambda i, plane: (0, plane[0], 0))],
-            out_specs=pl.BlockSpec(piece.shape, lambda i, *_: (0, 0, 0)),
-            scratch_shapes=[pltpu.VMEM((both, HALF_COLUMNS), jnp.float32)],
-        ),
+        out_shape=jax.ShapeDtypeStruct((4, both // 2, HALF_COLUMNS), block.dtype),
+        in_specs=[VMEM],
+        out_specs=VMEM,
+        scratch_shapes=[pltpu.VMEM((both, HALF_COLUMNS), jnp.float32)],
         name="pick",
-    )(plane, everyone)
+    )(block)
 
 
 def held(rows_ref, holder, half, columns):
@@ -335,28 +367,11 @@
     )(parts, own, value)
 
 
-def settle_kernel(in_ref, out_ref):
-    out_ref[...] = in_ref[...]
-
-
-def settle(pages):
-    block = pl.BlockSpec((4,) + pages.shape[1:], lambda i: (i, 0, 0))
-    return pl.pallas_call(
-        settle_kernel,
-        out_shape=jax.ShapeDtypeStruct(pages.shape, pages.dtype),
-        grid=(pages.shape[0] // 4,),
-        in_specs=[block],
-        out_specs=block,
-        name="settle",
-    )(pages)
-
-
 def per_device(
     tokens, norm_gain, w_query, w_keyvalue, cache, page_count, page_owner, keep_rows, dest_slot
 ):
     holder = lax.axis_index("page")
-    group = lax.axis_index("tensor")
-    half = group % 2
+    half = lax.axis_index("tensor") % 2
     share = tokens.shape[0] // HOLDERS
 
     def normalise(rows):
@@ -373,32 +388,52 @@
 
     mine = normalise(lax.dynamic_slice_in_dim(tokens, holder * share, share, 0))
     across = lax.ppermute(mine, ("page", "tensor"), OTHER_HALF)
-    across, compact = lax.optimization_barrier((across, compact))
-    arrived = lax.all_to_all(compact, "page", 0, 0, tiled=True)
-
+    got = [compact[0]] + [None] * (CHIPS - 1)
+
+    def send(after, steps):
+        blocks, after = lax.optimization_barrier(([compact[d] for d in steps], after))
+        for d, block in zip(steps, blocks):
+            got[d] = lax.ppermute(block, "page", OTHER_CHIP[d])
+        return after
+
+    def receive(before, steps):
+        blocks, before = lax.optimization_barrier(([got[d] for d in steps], before))
+        for d, block in zip(steps, blocks):
+            got[d] = block
+        return before
+
+    across = send(across, (4, 5, 1))
     both = jnp.where(
         half == 0,
         jnp.concatenate([mine, across], axis=0),
         jnp.concatenate([across, mine], axis=0),
     )
-    rows = lax.all_gather(
-        both, "tensor", axis=0, axis_index_groups=PLANE_GROUPS, tiled=True
+    rows = lax.all_to_all(
+        jnp.broadcast_to(both[None], (PLANE,) + both.shape),
+        "tensor",
+        0,
+        0,
+        axis_index_groups=PLANE_GROUPS,
+        tiled=True,
+    ).reshape(PLANE * both.shape[0], -1)
+    rows = send(rows, (2,))
+    projected = project(rows, w_query, w_keyvalue).reshape(PLANE, both.shape[0], -1)
+    back = lax.all_to_all(
+        projected, "tensor", 0, 0, axis_index_groups=PLANE_GROUPS, tiled=True
     )
-    projected = project(rows, w_query, w_keyvalue)
-    everyone = lax.all_gather(
-        projected, "tensor", axis=0, axis_index_groups=PLANE_GROUPS, tiled=False
-    )
-    halves = pick((group // 2).reshape(1), everyone)
-    halves, arrived = lax.optimization_barrier((halves, arrived))
+    halves = receive(pick(back), (4, 5, 1))
+    halves = send(halves, (6, 3))
     quarter = lax.all_to_all(
         halves, ("page", "tensor"), 0, 0, axis_index_groups=FOUR_GROUPS, tiled=True
     )
     rows = lax.all_gather(quarter, "page", axis=0, axis_index_groups=QUAD_GROUPS, tiled=True)
+    rows = receive(rows, (2,))
     part = attend(page_count, page_owner, kept, rows)
     far = lax.ppermute(part, "page", OTHER_QUAD)
     own, value = own_part(rows)
-    settled = settle(arrived)
-    far, own, value, settled = lax.optimization_barrier((far, own, value, settled))
+    own = send(own, (7,))
+    far, own, value = lax.optimization_barrier((far, own, value))
+    far = receive(far, (6, 3))
     parts = lax.all_gather(
         jnp.concatenate([part, far], axis=0),
         "page",
@@ -406,7 +441,10 @@
         axis_index_groups=QUAD_GROUPS,
         tiled=True,
     )
-    return combine(parts, own, value), settled[:, None]
+    parts = receive(parts, (7,))
+    cross = lax.ppermute(pack(got), "page", OTHER_CORE)
+    attended = combine(parts, own, value)
+    return attended, place_pages(got, cross)[:, None]
 
 
 def solution(mesh):

time: 162 us -> 161 us (level)
  starting transfers between devices: 22.5 us -> 63.9 us
  blocking collectives: 99.7 us -> 61.4 us
  waiting for transfers between devices: 11.3 us -> 3.28 us
  Pallas kernels: 22.3 us -> 24.2 us
    all_gather x2 -> x0, blocking collectives: 43 us -> none  [the longest x1 22.1 us: per_device(): lax.all_gather(both, 'tensor', axis=0, axis_index_groups=PLANE_GROUPS, ti...]
    ppermute x0 -> x8, starting transfers between devices: none -> 36 us  [the longest x7 33.9 us: send(): got[d] = lax.ppermute(block, 'page', OTHER_CHIP[d])]
    all_gather x1, blocking collectives: 17.7 us -> 27.7 us  [per_device(): lax.all_gather(quarter, 'page', axis=0, axis_index_groups=QUAD_GROUPS, ti...]
    all_to_all x1, blocking collectives: 23.1 us -> 13.2 us  [per_device(): lax.all_to_all(projected, 'tensor', 0, 0, axis_index_groups=PLANE_GROUPS,...]
    all_to_all x1 -> x2, waiting for transfers between devices: 6.55 us -> 0.08 us  [the longest x1 0.08 us: per_device(): lax.all_to_all(jnp.broadcast_to(both[None], (PLANE,) + both.shape), 'tens...]
    ppermute x1, waiting for transfers between devices: 4.72 us -> 0.01 us  [per_device(): far = lax.ppermute(part, 'page', OTHER_QUAD)]
    all_gather x1, blocking collectives: 15.9 us -> 20.6 us  [per_device(): lax.all_gather(jnp.concatenate([part, far], axis=0), 'page', axis=0, axis...]
    all_to_all x1 -> x2, starting transfers between devices: 7.16 us -> 11.5 us  [the longest x1 6.87 us: per_device(): lax.all_to_all(jnp.broadcast_to(both[None], (PLANE,) + both.shape), 'tens...]
  transfers between devices with their start and end apart: 3 -> 12, of which waited for: 2 -> 2; matrix products, arithmetic and copies ran while one was open for 0% -> 1% of each run, Pallas kernels for 9% -> 12%
where the time goes in v7:
time: 161 us; the launch traced here: 160 us
  starting transfers between devices  63.9 us (40%)
  blocking collectives  61.4 us (38%)
  Pallas kernels  24.2 us (15%)
  waiting for transfers between devices  3.28 us (2%)
  local copies, waits for them, and re-layouts  3.24 us (2%)
  other arithmetic  2.71 us (2%)
    ppermute x7, starting transfers between devices, send(): got[d] = lax.ppermute(block, 'page', OTHER_CHIP[d])  33.9 us
    all_gather x1, blocking collectives, per_device(): lax.all_gather(quarter, 'page', axis=0, axis_index_groups=QUAD_GROUPS, ti...  27.7 us
    all_gather x1, blocking collectives, per_device(): lax.all_gather(jnp.concatenate([part, far], axis=0), 'page', axis=0, axis...  20.6 us
    ppermute x1, starting transfers between devices, per_device(): across = lax.ppermute(mine, ('page', 'tensor'), OTHER_HALF)  13.3 us
    all_to_all x1, blocking collectives, per_device(): lax.all_to_all(projected, 'tensor', 0, 0, axis_index_groups=PLANE_GROUPS,...  13.2 us
    all_to_all x1, starting transfers between devices, per_device(): lax.all_to_all(jnp.broadcast_to(both[None], (PLANE,) + both.shape), 'tens...  6.87 us
    pallas_call x1, Pallas kernels, select_rows(): pl.pallas_call(select_kernel, out_shape=[block] * CHIPS + [jax.ShapeDtype...  5.5 us
    all_to_all x1, starting transfers between devices, per_device(): lax.all_to_all(halves, ('page', 'tensor'), 0, 0, axis_index_groups=FOUR_G...  4.6 us
  transfers between devices with their start and end apart: 12, of which 2 were waited for; matrix products, arithmetic and copies ran while one was open for 1% of the time, Pallas kernels for 12%

profile of v7, /device:TPU:1, one launch (start us, length us, event | category | flops | bytes accessed | tf_op | source)
XLA Modules:
  0.0 160.3 jit_solution(18264886680641055084)
XLA Ops:
  2.4 13.3 %collective-permute-start = (bf16[4,2560]{1,0:T(4,128)(2,1)S(1)}, bf16[4,2560]{1,0:T(4,128)(2,1)S(1)}, u32[]{:S(2)}, u32[]{:S(2)}) collective-permute-start(bf16[4,2560]{1,0:T(4,128)(2,1)S(1)} %fusion.2), channel_id=1, source_target_pairs={{0,257},{1,256},{2,259},{3,258},{4,261},{5,260},{6,263},{7,262},{8... | collective-permute-start | bytes 61448 | tf_op jit(solution)/shard_map/ppermute | solution.py:390
  16.4 5.5 %select_rows.1 = (bf16[2,32,1280]{2,1,0:T(8,128)(2,1)}, bf16[2,32,1280]{2,1,0:T(8,128)(2,1)}, bf16[2,32,1280]{2,1,0:T(8,128)(2,1)}, bf16[2,32,1280]{2,1,0:T(8,12...) custom-call(s32[1]{0:T(128)} %bitcast.11.count_ref, ...), custom_call_target="tpu_custom_call" | custom-call | tf_op jit(solution)/shard_map/select_rows/pallas_call | solution.py:81
  22.9 6.9 %all-to-all-start = ((bf16[16,8,2560]{2,1,0:T(8,128)(2,1)}), bf16[16,8,2560]{2,1,0:T(8,128)(2,1)S(1)}, u32[]{:S(2)}, u32[]{:S(2)}) async-start(bf16[16,8,2560]{2,1,0:T(8,128)(2,1)} %broadcast_in_dim.4), calls=%async_computation | async-start | bytes 1310720 | tf_op jit(solution)/shard_map/all_to_all | solution.py:411
  29.7 5.1 %collective-permute-start.2 = (bf16[2,32,1280]{2,1,0:T(8,128)(2,1)}, bf16[2,32,1280]{2,1,0:T(8,128)(2,1)S(1)}, u32[]{:S(2)}, u32[]{:S(2)}) collective-permute-start(bf16[2,32,1280]{2,1,0:T(8,128)(2,1)} %get-tuple-element.47), channel_id=1, source_target_pairs={{0,256},{32,288},{64,320},{96,352},{128,384},{160,416},{192,448},{... | collective-permute-start | bytes 491528 | tf_op jit(solution)/shard_map/ppermute | solution.py:396
  34.9 4.5 %collective-permute-start.3 = (bf16[2,32,1280]{2,1,0:T(8,128)(2,1)}, bf16[2,32,1280]{2,1,0:T(8,128)(2,1)S(1)}, u32[]{:S(2)}, u32[]{:S(2)}) collective-permute-start(bf16[2,32,1280]{2,1,0:T(8,128)(2,1)} %get-tuple-element.48), channel_id=1, source_target_pairs={{0,320},{32,352},{64,256},{96,288},{128,448},{160,480},{192,384},{... | collective-permute-start | bytes 491528 | tf_op jit(solution)/shard_map/ppermute | solution.py:396
  39.4 1.9 %collective-permute-start.4 = (bf16[2,32,1280]{2,1,0:T(8,128)(2,1)}, bf16[2,32,1280]{2,1,0:T(8,128)(2,1)S(1)}, u32[]{:S(2)}, u32[]{:S(2)}) collective-permute-start(bf16[2,32,1280]{2,1,0:T(8,128)(2,1)} %get-tuple-element.49), channel_id=1, source_target_pairs={{0,64},{32,96},{64,0},{96,32},{128,192},{160,224},{192,128},{224,1... | collective-permute-start | bytes 491528 | tf_op jit(solution)/shard_map/ppermute | solution.py:396
  42.2 2.4 %project.1 = bf16[128,120]{1,0:T(8,128)(2,1)} custom-call(bf16[128,2560]{1,0:T(8,128)(2,1)} %bitcast.14, bf16[80,2560]{1,0:T(8,128)(2,1)} %bitcast.16, bf16[40,2560]{1,0:T(8,128)(2,1)} %bitcast.17), custom_call_target="tpu_custom_call" | custom-call | tf_op jit(solution)/shard_map/project/pallas_call | solution.py:141
  44.6 13.2 %all_to_all.15.all_ref = bf16[16,8,120]{2,1,0:T(8,128)(2,1)} all-to-all(bf16[16,8,120]{2,1,0:T(8,128)(2,1)} %bitcast.18), channel_id=1, replica_groups={{0,2,4,6,8,10,12,14,16,18,20,22,24,26,28,30},{1,3,5,7,9,11,13,15,17,19,..., dimensions={0} | all-to-all | bytes 61440 | tf_op jit(solution)/shard_map/all_to_all | solution.py:421
  57.8 1.5 pick.1
  59.3 3.2 %collective-permute-done.2.refs_4_ = bf16[2,32,1280]{2,1,0:T(8,128)(2,1)S(1)} collective-permute-done((bf16[2,32,1280]{2,1,0:T(8,128)(2,1)}, bf16[2,32,1280]{2,1,0:T(8,128)(2,1)S(1)}, u32[]{:S(2)}, u32[]{:S(2)}) %collective-permute-start.2) | collective-permute-done | bytes 163872 | tf_op jit(solution)/shard_map/ppermute | solution.py:396
  62.5 4.6 %all-to-all-start.2 = ((bf16[4,4,1920]{2,1,0:T(4,128)(2,1)}), bf16[4,4,1920]{2,1,0:T(4,128)(2,1)S(1)}, u32[]{:S(2)}, u32[]{:S(2)}) async-start(bf16[4,4,1920]{2,1,0:T(4,128)(2,1)} %pick.1), calls=%async_computation.2 | async-start | bytes 122880 | tf_op jit(solution)/shard_map/all_to_all | solution.py:426
  67.1 6.1 %collective-permute-start.1 = (bf16[2,32,1280]{2,1,0:T(8,128)(2,1)S(1)}, bf16[2,32,1280]{2,1,0:T(8,128)(2,1)S(1)}, u32[]{:S(2)}, u32[]{:S(2)}) collective-permute-start(bf16[2,32,1280]{2,1,0:T(8,128)(2,1)S(1)} %copy-done.14), channel_id=1, source_target_pairs={{0,128},{32,160},{64,192},{96,224},{128,0},{160,32},{192,64},{224,... | collective-permute-start | bytes 491528 | tf_op jit(solution)/shard_map/ppermute | solution.py:396
  73.2 7.0 %collective-permute-start.6 = (bf16[2,32,1280]{2,1,0:T(8,128)(2,1)S(1)}, bf16[2,32,1280]{2,1,0:T(8,128)(2,1)S(1)}, u32[]{:S(2)}, u32[]{:S(2)}) collective-permute-start(bf16[2,32,1280]{2,1,0:T(8,128)(2,1)S(1)} %copy-done.13), channel_id=1, source_target_pairs={{0,384},{32,416},{64,448},{96,480},{128,256},{160,288},{192,320},{... | collective-permute-start | bytes 491528 | tf_op jit(solution)/shard_map/ppermute | solution.py:396
  80.3 1.9 %collective-permute-start.7 = (bf16[2,32,1280]{2,1,0:T(8,128)(2,1)S(1)}, bf16[2,32,1280]{2,1,0:T(8,128)(2,1)S(1)}, u32[]{:S(2)}, u32[]{:S(2)}) collective-permute-start(bf16[2,32,1280]{2,1,0:T(8,128)(2,1)S(1)} %copy-done.12), channel_id=1, source_target_pairs={{0,192},{32,224},{64,128},{96,160},{128,64},{160,96},{192,0},{224,... | collective-permute-start | bytes 491528 | tf_op jit(solution)/shard_map/ppermute | solution.py:396
  82.2 27.7 %all_gather.6.rows_ref = bf16[32,4,1920]{2,1,0:T(4,128)(2,1)} all-gather(bf16[4,4,1920]{2,1,0:T(4,128)(2,1)S(1)} %all-to-all-done.2), channel_id=1, replica_groups={{0,32,64,96,128,160,192,224},{256,288,320,352,384,416,448,480},{1,33,65..., dimensions={0}, use_global_device_ids=true | all-gather | bytes 552960 | tf_op jit(solution)/shard_map/all_gather | solution.py:429
  109.9 3.9 %attend.1 = bf16[8,2816]{1,0:T(8,128)(2,1)} custom-call(s32[1]{0:T(128)} %bitcast.12.count_ref, s32[8]{0:T(128)} %bitcast.20, bf16[256,1280]{1,0:T(8,128)(2,1)} %get-tuple-element.56.kept_ref, bf16[32,4,1920]{2,1,0:T(4,128)(2,1)} %all_gather.6.rows_ref), custom_call_target="tpu_custom_call" | custom-call | tf_op jit(solution)/shard_map/attend/pallas_call | solution.py:251
  113.8 3.2 %collective-permute-start.8 = (bf16[8,2816]{1,0:T(8,128)(2,1)}, bf16[8,2816]{1,0:T(8,128)(2,1)S(1)}, u32[]{:S(2)}, u32[]{:S(2)}) collective-permute-start(bf16[8,2816]{1,0:T(8,128)(2,1)} %attend.1), channel_id=1, source_target_pairs={{0,256},{32,288},{64,320},{96,352},{128,384},{160,416},{192,448},{... | collective-permute-start | bytes 135176 | tf_op jit(solution)/shard_map/ppermute | solution.py:432
  117.0 2.3 %own_part.1 = (f32[64,32]{1,0:T(8,128)}, f32[64,640]{1,0:T(8,128)}) custom-call(bf16[32,4,1920]{2,1,0:T(4,128)(2,1)} %all_gather.6.rows_ref), custom_call_target="tpu_custom_call" | custom-call | tf_op jit(solution)/shard_map/own_part/pallas_call | solution.py:308
  119.3 7.3 %collective-permute-start.5 = (bf16[2,32,1280]{2,1,0:T(8,128)(2,1)S(1)}, bf16[2,32,1280]{2,1,0:T(8,128)(2,1)S(1)}, u32[]{:S(2)}, u32[]{:S(2)}) collective-permute-start(bf16[2,32,1280]{2,1,0:T(8,128)(2,1)S(1)} %copy-done.11), channel_id=1, source_target_pairs={{0,448},{32,480},{64,384},{96,416},{128,320},{160,352},{192,256},{... | collective-permute-start | bytes 491528 | tf_op jit(solution)/shard_map/ppermute | solution.py:396
  127.5 20.6 %all_gather.7.part_ref = bf16[128,2816]{1,0:T(8,128)(2,1)S(1)} all-gather(bf16[16,2816]{1,0:T(8,128)(2,1)S(1)} %pad_maximum_fusion), channel_id=1, replica_groups={{0,32,64,96,128,160,192,224},{256,288,320,352,384,416,448,480},{1,33,65..., dimensions={0}, use_global_device_ids=true | all-gather | bytes 811008 | tf_op jit(solution)/shard_map/all_gather | solution.py:437
  148.8 2.3 %pack.1 = bf16[8,32,1280]{2,1,0:T(8,128)(2,1)} custom-call(bf16[2,32,1280]{2,1,0:T(8,128)(2,1)} %get-tuple-element.66.refs_0_, bf16[2,32,1280]{2,1,0:T(8,128)(2,1)} %copy-done.5, bf16[2,32,1280]{2,1,0:T(8,128)(2,1)} %copy-done.6, bf16[2,32,1280]{2,1,0:T(8,128)(2,1)} %copy-done.8, bf16[2,32,1280]{2,1,0:T(8,128)(2,1)} %copy-done.3, ...), custom_call_target="tpu_custom_call" | custom-call | tf_op jit(solution)/shard_map/pack/pallas_call | solution.py:105
  151.0 2.1 %collective-permute-start.9 = (bf16[8,32,1280]{2,1,0:T(8,128)(2,1)}, bf16[8,32,1280]{2,1,0:T(8,128)(2,1)S(1)}, u32[]{:S(2)}, u32[]{:S(2)}) collective-permute-start(bf16[8,32,1280]{2,1,0:T(8,128)(2,1)} %pack.1), channel_id=1, source_target_pairs={{0,32},{32,0},{64,96},{96,64},{128,160},{160,128},{192,224},{224,1... | collective-permute-start | bytes 1966088 | tf_op jit(solution)/shard_map/ppermute | solution.py:445
  153.1 3.5 %combine.1 = bf16[64,2560]{1,0:T(8,128)(2,1)} custom-call(bf16[128,2816]{1,0:T(8,128)(2,1)S(1)} %all_gather.7.part_ref, f32[64,32]{1,0:T(8,128)S(1)} %copy-done.1, f32[64,640]{1,0:T(8,128)S(1)} %copy-done), custom_call_target="tpu_custom_call" | custom-call | tf_op jit(solution)/shard_map/combine/pallas_call | solution.py:360
  157.5 2.8 %place_pages.1 = bf16[16,32,1280]{2,1,0:T(8,128)(2,1)} custom-call(bf16[2,32,1280]{2,1,0:T(8,128)(2,1)} %get-tuple-element.66.refs_0_, bf16[2,32,1280]{2,1,0:T(8,128)(2,1)} %copy-done.5, bf16[2,32,1280]{2,1,0:T(8,128)(2,1)} %copy-done.6, bf16[2,32,1280]{2,1,0:T(8,128)(2,1)} %copy-done.8, bf16[2,32,1280]{2,1,0:T(8,128)(2,1)} %copy-done.3, ...), custom_call_target="tpu_custom_call" | custom-call | tf_op jit(solution)/shard_map/place_pages/pallas_call | solution.py:123
  (47 shorter events, 6.1 us)
Async XLA Ops:
  2.4 19.5 %collective-permute-start = (bf16[4,2560]{1,0:T(4,128)(2,1)S(1)}, bf16[4,2560]{1,0:T(4,128)(2,1)S(1)}, u32[]{:S(2)}, u32[]{:S(2)}) collective-permute-start(bf16[4,2560]{1,0:T(4,128)(2,1)S(1)} %fusion.2), channel_id=1, source_target_pairs={{0,257},{1,256},{2,259},{3,258},{4,261},{5,260},{6,263},{7,262},{8... | collective-permute-start | bytes 61448 | tf_op jit(solution)/shard_map/ppermute | solution.py:390
  21.9 45.2 %copy-start.14 = (bf16[2,32,1280]{2,1,0:T(8,128)(2,1)S(1)}, bf16[2,32,1280]{2,1,0:T(8,128)(2,1)}, u32[]{:S(2)}) copy-start(bf16[2,32,1280]{2,1,0:T(8,128)(2,1)} %get-tuple-element.44) | copy-start | bytes 491524
  21.9 51.3 %copy-start.13 = (bf16[2,32,1280]{2,1,0:T(8,128)(2,1)S(1)}, bf16[2,32,1280]{2,1,0:T(8,128)(2,1)}, u32[]{:S(2)}) copy-start(bf16[2,32,1280]{2,1,0:T(8,128)(2,1)} %get-tuple-element.57) | copy-start | bytes 491524
  21.9 58.3 %copy-start.12 = (bf16[2,32,1280]{2,1,0:T(8,128)(2,1)S(1)}, bf16[2,32,1280]{2,1,0:T(8,128)(2,1)}, u32[]{:S(2)}) copy-start(bf16[2,32,1280]{2,1,0:T(8,128)(2,1)} %get-tuple-element.58) | copy-start | bytes 491524
  22.9 96.4 %copy-start.11 = (bf16[2,32,1280]{2,1,0:T(8,128)(2,1)S(1)}, bf16[2,32,1280]{2,1,0:T(8,128)(2,1)}, u32[]{:S(2)}) copy-start(bf16[2,32,1280]{2,1,0:T(8,128)(2,1)} %get-tuple-element.55) | copy-start | bytes 491524
  22.9 18.5 %all-to-all-start = ((bf16[16,8,2560]{2,1,0:T(8,128)(2,1)}), bf16[16,8,2560]{2,1,0:T(8,128)(2,1)S(1)}, u32[]{:S(2)}, u32[]{:S(2)}) async-start(bf16[16,8,2560]{2,1,0:T(8,128)(2,1)} %broadcast_in_dim.4), calls=%async_computation | async-start | bytes 1310720 | tf_op jit(solution)/shard_map/all_to_all | solution.py:411
  29.7 32.7 %collective-permute-start.2 = (bf16[2,32,1280]{2,1,0:T(8,128)(2,1)}, bf16[2,32,1280]{2,1,0:T(8,128)(2,1)S(1)}, u32[]{:S(2)}, u32[]{:S(2)}) collective-permute-start(bf16[2,32,1280]{2,1,0:T(8,128)(2,1)} %get-tuple-element.47), channel_id=1, source_target_pairs={{0,256},{32,288},{64,320},{96,352},{128,384},{160,416},{192,448},{... | collective-permute-start | bytes 491528 | tf_op jit(solution)/shard_map/ppermute | solution.py:396
  34.9 27.6 %collective-permute-start.3 = (bf16[2,32,1280]{2,1,0:T(8,128)(2,1)}, bf16[2,32,1280]{2,1,0:T(8,128)(2,1)S(1)}, u32[]{:S(2)}, u32[]{:S(2)}) collective-permute-start(bf16[2,32,1280]{2,1,0:T(8,128)(2,1)} %get-tuple-element.48), channel_id=1, source_target_pairs={{0,320},{32,352},{64,256},{96,288},{128,448},{160,480},{192,384},{... | collective-permute-start | bytes 491528 | tf_op jit(solution)/shard_map/ppermute | solution.py:396
  39.4 23.1 %collective-permute-start.4 = (bf16[2,32,1280]{2,1,0:T(8,128)(2,1)}, bf16[2,32,1280]{2,1,0:T(8,128)(2,1)S(1)}, u32[]{:S(2)}, u32[]{:S(2)}) collective-permute-start(bf16[2,32,1280]{2,1,0:T(8,128)(2,1)} %get-tuple-element.49), channel_id=1, source_target_pairs={{0,64},{32,96},{64,0},{96,32},{128,192},{160,224},{192,128},{224,1... | collective-permute-start | bytes 491528 | tf_op jit(solution)/shard_map/ppermute | solution.py:396
  62.5 85.6 %copy-start.3 = (bf16[2,32,1280]{2,1,0:T(8,128)(2,1)}, bf16[2,32,1280]{2,1,0:T(8,128)(2,1)S(1)}, u32[]{:S(2)}) copy-start(bf16[2,32,1280]{2,1,0:T(8,128)(2,1)S(1)} %collective-permute-done.2.refs_4_) | copy-start | bytes 491524
  62.5 85.6 %copy-start.4 = (bf16[2,32,1280]{2,1,0:T(8,128)(2,1)}, bf16[2,32,1280]{2,1,0:T(8,128)(2,1)S(1)}, u32[]{:S(2)}) copy-start(bf16[2,32,1280]{2,1,0:T(8,128)(2,1)S(1)} %collective-permute-done.3.refs_5_) | copy-start | bytes 491524
  62.5 85.6 %copy-start.5 = (bf16[2,32,1280]{2,1,0:T(8,128)(2,1)}, bf16[2,32,1280]{2,1,0:T(8,128)(2,1)S(1)}, u32[]{:S(2)}) copy-start(bf16[2,32,1280]{2,1,0:T(8,128)(2,1)S(1)} %collective-permute-done.4.refs_1_) | copy-start | bytes 491524
  62.5 19.7 %all-to-all-start.2 = ((bf16[4,4,1920]{2,1,0:T(4,128)(2,1)}), bf16[4,4,1920]{2,1,0:T(4,128)(2,1)S(1)}, u32[]{:S(2)}, u32[]{:S(2)}) async-start(bf16[4,4,1920]{2,1,0:T(4,128)(2,1)} %pick.1), calls=%async_computation.2 | async-start | bytes 122880 | tf_op jit(solution)/shard_map/all_to_all | solution.py:426
  67.1 42.8 %collective-permute-start.1 = (bf16[2,32,1280]{2,1,0:T(8,128)(2,1)S(1)}, bf16[2,32,1280]{2,1,0:T(8,128)(2,1)S(1)}, u32[]{:S(2)}, u32[]{:S(2)}) collective-permute-start(bf16[2,32,1280]{2,1,0:T(8,128)(2,1)S(1)} %copy-done.14), channel_id=1, source_target_pairs={{0,128},{32,160},{64,192},{96,224},{128,0},{160,32},{192,64},{224,... | collective-permute-start | bytes 491528 | tf_op jit(solution)/shard_map/ppermute | solution.py:396
  73.2 53.4 %collective-permute-start.6 = (bf16[2,32,1280]{2,1,0:T(8,128)(2,1)S(1)}, bf16[2,32,1280]{2,1,0:T(8,128)(2,1)S(1)}, u32[]{:S(2)}, u32[]{:S(2)}) collective-permute-start(bf16[2,32,1280]{2,1,0:T(8,128)(2,1)S(1)} %copy-done.13), channel_id=1, source_target_pairs={{0,384},{32,416},{64,448},{96,480},{128,256},{160,288},{192,320},{... | collective-permute-start | bytes 491528 | tf_op jit(solution)/shard_map/ppermute | solution.py:396
  80.3 46.4 %collective-permute-start.7 = (bf16[2,32,1280]{2,1,0:T(8,128)(2,1)S(1)}, bf16[2,32,1280]{2,1,0:T(8,128)(2,1)S(1)}, u32[]{:S(2)}, u32[]{:S(2)}) collective-permute-start(bf16[2,32,1280]{2,1,0:T(8,128)(2,1)S(1)} %copy-done.12), channel_id=1, source_target_pairs={{0,192},{32,224},{64,128},{96,160},{128,64},{160,96},{192,0},{224,... | collective-permute-start | bytes 491528 | tf_op jit(solution)/shard_map/ppermute | solution.py:396
  109.9 38.2 %copy-start.6 = (bf16[2,32,1280]{2,1,0:T(8,128)(2,1)}, bf16[2,32,1280]{2,1,0:T(8,128)(2,1)S(1)}, u32[]{:S(2)}) copy-start(bf16[2,32,1280]{2,1,0:T(8,128)(2,1)S(1)} %collective-permute-done.1.refs_2_) | copy-start | bytes 491524
  113.8 12.8 %collective-permute-start.8 = (bf16[8,2816]{1,0:T(8,128)(2,1)}, bf16[8,2816]{1,0:T(8,128)(2,1)S(1)}, u32[]{:S(2)}, u32[]{:S(2)}) collective-permute-start(bf16[8,2816]{1,0:T(8,128)(2,1)} %attend.1), channel_id=1, source_target_pairs={{0,256},{32,288},{64,320},{96,352},{128,384},{160,416},{192,448},{... | collective-permute-start | bytes 135176 | tf_op jit(solution)/shard_map/ppermute | solution.py:432
  119.3 33.8 %copy-start = (f32[64,640]{1,0:T(8,128)S(1)}, f32[64,640]{1,0:T(8,128)}, u32[]{:S(2)}) copy-start(f32[64,640]{1,0:T(8,128)} %get-tuple-element.65.value_ref) | copy-start | bytes 491524
  119.3 33.8 %copy-start.1 = (f32[64,32]{1,0:T(8,128)S(1)}, f32[64,32]{1,0:T(8,128)}, u32[]{:S(2)}) copy-start(f32[64,32]{1,0:T(8,128)} %get-tuple-element.64.own_ref) | copy-start | bytes 24580
  119.3 28.8 %collective-permute-start.5 = (bf16[2,32,1280]{2,1,0:T(8,128)(2,1)S(1)}, bf16[2,32,1280]{2,1,0:T(8,128)(2,1)S(1)}, u32[]{:S(2)}, u32[]{:S(2)}) collective-permute-start(bf16[2,32,1280]{2,1,0:T(8,128)(2,1)S(1)} %copy-done.11), channel_id=1, source_target_pairs={{0,448},{32,480},{64,384},{96,416},{128,320},{160,352},{192,256},{... | collective-permute-start | bytes 491528 | tf_op jit(solution)/shard_map/ppermute | solution.py:396
  126.6 21.5 %copy-start.7 = (bf16[2,32,1280]{2,1,0:T(8,128)(2,1)}, bf16[2,32,1280]{2,1,0:T(8,128)(2,1)S(1)}, u32[]{:S(2)}) copy-start(bf16[2,32,1280]{2,1,0:T(8,128)(2,1)S(1)} %collective-permute-done.6.refs_6_) | copy-start | bytes 491524
  126.7 21.5 %copy-start.8 = (bf16[2,32,1280]{2,1,0:T(8,128)(2,1)}, bf16[2,32,1280]{2,1,0:T(8,128)(2,1)S(1)}, u32[]{:S(2)}) copy-start(bf16[2,32,1280]{2,1,0:T(8,128)(2,1)S(1)} %collective-permute-done.7.refs_3_) | copy-start | bytes 491524
  151.0 5.6 %collective-permute-start.9 = (bf16[8,32,1280]{2,1,0:T(8,128)(2,1)}, bf16[8,32,1280]{2,1,0:T(8,128)(2,1)S(1)}, u32[]{:S(2)}, u32[]{:S(2)}) collective-permute-start(bf16[8,32,1280]{2,1,0:T(8,128)(2,1)} %pack.1), channel_id=1, source_target_pairs={{0,32},{32,0},{64,96},{96,64},{128,160},{160,128},{192,224},{224,1... | collective-permute-start | bytes 1966088 | tf_op jit(solution)/shard_map/ppermute | solution.py:445
  (3 other events, 2.4 us)

commit v8 on v7

--- a/solution.py
+++ b/solution.py
@@ -37,8 +37,6 @@
     for core in range(2)
 ]
 QUAD_GROUPS = [[CHIPS * quad + i for i in range(CHIPS)] for quad in range(2)]
-OTHER_CORE = [(i, i ^ 1) for i in range(HOLDERS)]
-OTHER_CHIP = [[(i, i ^ (2 * d)) for i in range(HOLDERS)] for d in range(CHIPS)]
 OTHER_QUAD = [(i, i ^ CHIPS) for i in range(HOLDERS)]
 HALF_COLUMNS = (QUERIES + 2 * KEYS) // 2
 STEP = 4
@@ -47,15 +45,14 @@
 SMEM = pl.BlockSpec(memory_space=pltpu.SMEM)
 
 
-def select_kernel(count_ref, dest_ref, keep_ref, page_ref, *refs):
-    out_refs, kept_ref = refs[:CHIPS], refs[CHIPS]
+def select_kernel(count_ref, dest_ref, keep_ref, page_ref, near_ref, far_ref, kept_ref):
     grid_step = pl.program_id(0)
-    holder = lax.axis_index("page")
+    quad = lax.axis_index("page") // CHIPS
 
     @pl.when(grid_step == 0)
     def _():
-        for ref in out_refs:
-            ref[...] = jnp.zeros_like(ref)
+        near_ref[...] = jnp.zeros_like(near_ref)
+        far_ref[...] = jnp.zeros_like(far_ref)
 
     rows = page_ref.shape[1]
     for i in range(STEP):
@@ -66,21 +63,26 @@
             chosen.T.astype(jnp.bfloat16), page_ref[i], preferred_element_type=jnp.float32
         ).astype(jnp.bfloat16)
         kept_ref[i * KEEP : (i + 1) * KEEP] = kept
-        target = dest_ref[slot] ^ holder
+        target = dest_ref[slot]
         live = slot < count_ref[0]
-        for d in range(CHIPS):
-
-            @pl.when(live & (target // 2 == d))
-            def _():
-                out_refs[d][target % 2] = kept_ref[i * KEEP : (i + 1) * KEEP]
+        same = target // CHIPS == quad
+
+        @pl.when(live & same)
+        def _():
+            near_ref[target % CHIPS] = kept
+
+        @pl.when(live & jnp.logical_not(same))
+        def _():
+            far_ref[target % CHIPS] = kept
 
 
 def select_rows(page_count, dest_slot, keep_rows, cache):
     sources, _, rows, width = cache.shape
-    block = jax.ShapeDtypeStruct((2, KEEP, width), cache.dtype)
-    results = pl.pallas_call(
+    block = jax.ShapeDtypeStruct((CHIPS, KEEP, width), cache.dtype)
+    whole = pl.BlockSpec(block.shape, lambda s, *_: (0, 0, 0))
+    return pl.pallas_call(
         select_kernel,
-        out_shape=[block] * CHIPS + [jax.ShapeDtypeStruct((sources * KEEP, width), cache.dtype)],
+        out_shape=(block, block, jax.ShapeDtypeStruct((sources * KEEP, width), cache.dtype)),
         grid_spec=pltpu.PrefetchScalarGridSpec(
             num_scalar_prefetch=2,
             grid=(sources // STEP,),
@@ -88,45 +90,30 @@
                 pl.BlockSpec((STEP, 1, KEEP), lambda s, *_: (s, 0, 0)),
                 pl.BlockSpec((STEP, rows, width), lambda s, *_: (s, 0, 0)),
             ],
-            out_specs=[pl.BlockSpec(block.shape, lambda s, *_: (0, 0, 0))] * CHIPS
-            + [pl.BlockSpec((STEP * KEEP, width), lambda s, *_: (s, 0))],
+            out_specs=(whole, whole, pl.BlockSpec((STEP * KEEP, width), lambda s, *_: (s, 0))),
         ),
         name="select_rows",
     )(page_count, dest_slot, keep_rows, cache.reshape(sources, rows, width))
-    return results[:CHIPS], results[CHIPS]
-
-
-def pack_kernel(*refs):
-    for d in range(CHIPS):
-        refs[CHIPS][d] = refs[d][1]
-
-
-def pack(got):
-    return pl.pallas_call(
-        pack_kernel,
-        out_shape=jax.ShapeDtypeStruct((CHIPS,) + got[0].shape[1:], got[0].dtype),
-        in_specs=[VMEM] * CHIPS,
-        out_specs=VMEM,
-        name="pack",
-    )(*got)
-
-
-def place_kernel(*refs):
-    got_refs, cross_ref, out_ref = refs[:CHIPS], refs[CHIPS], refs[CHIPS + 1]
-    holder = lax.axis_index("page")
-    for d in range(CHIPS):
-        out_ref[holder ^ (2 * d)] = got_refs[d][0]
-        out_ref[holder ^ (2 * d + 1)] = cross_ref[d]
-
-
-def place_pages(got, cross):
-    return pl.pallas_call(
-        place_kernel,
-        out_shape=jax.ShapeDtypeStruct((HOLDERS,) + cross.shape[1:], cross.dtype),
-        in_specs=[VMEM] * (CHIPS + 1),
-        out_specs=VMEM,
-        name="place_pages",
-    )(*got, cross)
+
+
+def join_kernel(near_ref, far_ref, out_ref):
+    quad = lax.axis_index("page") // CHIPS
+    for i in range(near_ref.shape[0]):
+        out_ref[i, quad] = near_ref[i]
+        out_ref[i, 1 - quad] = far_ref[i]
+
+
+def join(near, far):
+    count, keep, width = near.shape
+    block = pl.BlockSpec((STEP, keep, width), lambda i: (i, 0, 0))
+    return pl.pallas_call(
+        join_kernel,
+        out_shape=jax.ShapeDtypeStruct((count, 2, keep, width), near.dtype),
+        grid=(count // STEP,),
+        in_specs=[block, block],
+        out_specs=pl.BlockSpec((STEP, 2, keep, width), lambda i: (i, 0, 0, 0)),
+        name="join",
+    )(near, far)
 
 
 def project_kernel(rows_ref, query_ref, pair_ref, out_ref):
@@ -384,25 +371,12 @@
 
     page_count = page_count.reshape(1)
     page_owner = page_owner.reshape(SOURCES)
-    compact, kept = select_rows(page_count, dest_slot.reshape(SOURCES), keep_rows, cache)
+    near_pages, far_pages, kept = select_rows(page_count, dest_slot.reshape(SOURCES), keep_rows, cache)
 
     mine = normalise(lax.dynamic_slice_in_dim(tokens, holder * share, share, 0))
     across = lax.ppermute(mine, ("page", "tensor"), OTHER_HALF)
-    got = [compact[0]] + [None] * (CHIPS - 1)
-
-    def send(after, steps):
-        blocks, after = lax.optimization_barrier(([compact[d] for d in steps], after))
-        for d, block in zip(steps, blocks):
-            got[d] = lax.ppermute(block, "page", OTHER_CHIP[d])
-        return after
-
-    def receive(before, steps):
-        blocks, before = lax.optimization_barrier(([got[d] for d in steps], before))
-        for d, block in zip(steps, blocks):
-            got[d] = block
-        return before
-
-    across = send(across, (4, 5, 1))
+    across, far_pages = lax.optimization_barrier((across, far_pages))
+    relayed = lax.ppermute(far_pages, "page", OTHER_QUAD)
     both = jnp.where(
         half == 0,
         jnp.concatenate([mine, across], axis=0),
@@ -416,24 +390,23 @@
         axis_index_groups=PLANE_GROUPS,
         tiled=True,
     ).reshape(PLANE * both.shape[0], -1)
-    rows = send(rows, (2,))
     projected = project(rows, w_query, w_keyvalue).reshape(PLANE, both.shape[0], -1)
     back = lax.all_to_all(
         projected, "tensor", 0, 0, axis_index_groups=PLANE_GROUPS, tiled=True
     )
-    halves = receive(pick(back), (4, 5, 1))
-    halves = send(halves, (6, 3))
+    halves = pick(back)
     quarter = lax.all_to_all(
         halves, ("page", "tensor"), 0, 0, axis_index_groups=FOUR_GROUPS, tiled=True
     )
     rows = lax.all_gather(quarter, "page", axis=0, axis_index_groups=QUAD_GROUPS, tiled=True)
-    rows = receive(rows, (2,))
+    rows, relayed = lax.optimization_barrier((rows, relayed))
+    pages = lax.all_to_all(
+        join(near_pages, relayed), "page", 0, 0, axis_index_groups=QUAD_GROUPS, tiled=True
+    )
     part = attend(page_count, page_owner, kept, rows)
     far = lax.ppermute(part, "page", OTHER_QUAD)
     own, value = own_part(rows)
-    own = send(own, (7,))
     far, own, value = lax.optimization_barrier((far, own, value))
-    far = receive(far, (6, 3))
     parts = lax.all_gather(
         jnp.concatenate([part, far], axis=0),
         "page",
@@ -441,10 +414,8 @@
         axis_index_groups=QUAD_GROUPS,
         tiled=True,
     )
-    parts = receive(parts, (7,))
-    cross = lax.ppermute(pack(got), "page", OTHER_CORE)
-    attended = combine(parts, own, value)
-    return attended, place_pages(got, cross)[:, None]
+    arrived = jnp.swapaxes(pages, 0, 1).reshape((HOLDERS, 1) + pages.shape[2:])
+    return combine(parts, own, value), arrived
 
 
 def solution(mesh):

time: 161 us -> 179 us (1.11)
  blocking collectives: 61.4 us -> 94.5 us
  starting transfers between devices: 63.9 us -> 34.3 us
  waiting for transfers between devices: 3.28 us -> 18.7 us
  Pallas kernels: 24.2 us -> 21 us
  local copies, waits for them, and re-layouts: 3.24 us -> 5.38 us
    all_to_all x0 -> x1, blocking collectives: none -> 39.6 us  [per_device(): lax.all_to_all(halves, ('page', 'tensor'), 0, 0, axis_index_groups=FOUR_G...]
    ppermute x8 -> x1, starting transfers between devices: 36 us -> 5.21 us  [per_device(): relayed = lax.ppermute(far_pages, 'page', OTHER_QUAD)]
    ppermute x1, waiting for transfers between devices: 0.01 us -> 12.3 us  [per_device(): far = lax.ppermute(part, 'page', OTHER_QUAD)]
    all_gather x1, blocking collectives: 27.7 us -> 17.3 us  [per_device(): lax.all_gather(quarter, 'page', axis=0, axis_index_groups=QUAD_GROUPS, ti...]
    all_gather x1, blocking collectives: 20.6 us -> 27 us  [per_device(): lax.all_gather(jnp.concatenate([part, far], axis=0), 'page', axis=0, axis...]
    all_to_all x1, waiting for transfers between devices: 0.08 us -> 6.4 us  [per_device(): lax.all_to_all(jnp.broadcast_to(both[None], (PLANE,) + both.shape), 'tens...]
    ppermute x8 -> x1, waiting for transfers between devices: 3.19 us -> 0.01 us  [per_device(): relayed = lax.ppermute(far_pages, 'page', OTHER_QUAD)]
    pallas_call x3 -> x2, Pallas kernels: 10.5 us -> 7.43 us  [the longest x1 5.25 us: select_rows(): pl.pallas_call(select_kernel, out_shape=(block, block, jax.ShapeDtypeStru...]
  transfers between devices with their start and end apart: 12 -> 5, of which waited for: 2 -> 2; matrix products, arithmetic and copies ran while one was open for 1% -> 0% of each run, Pallas kernels for 12% -> 11%
where the time goes in v8:
time: 179 us; the launch traced here: 178 us
  blocking collectives  94.5 us (53%)
  starting transfers between devices  34.3 us (19%)
  Pallas kernels  21 us (12%)
  waiting for transfers between devices  18.7 us (10%)
  local copies, waits for them, and re-layouts  5.38 us (3%)
  other arithmetic  2.65 us (1%)
    all_to_all x1, blocking collectives, per_device(): lax.all_to_all(halves, ('page', 'tensor'), 0, 0, axis_index_groups=FOUR_G...  39.6 us
    all_gather x1, blocking collectives, per_device(): lax.all_gather(jnp.concatenate([part, far], axis=0), 'page', axis=0, axis...  27 us
    all_gather x1, blocking collectives, per_device(): lax.all_gather(quarter, 'page', axis=0, axis_index_groups=QUAD_GROUPS, ti...  17.3 us
    ppermute x1, starting transfers between devices, per_device(): across = lax.ppermute(mine, ('page', 'tensor'), OTHER_HALF)  13.3 us
    ppermute x1, waiting for transfers between devices, per_device(): far = lax.ppermute(part, 'page', OTHER_QUAD)  12.3 us
    all_to_all x1, blocking collectives, per_device(): lax.all_to_all(projected, 'tensor', 0, 0, axis_index_groups=PLANE_GROUPS,...  10.6 us
    all_to_all x1, starting transfers between devices, per_device(): lax.all_to_all(jnp.broadcast_to(both[None], (PLANE,) + both.shape), 'tens...  6.74 us
    all_to_all x1, waiting for transfers between devices, per_device(): lax.all_to_all(jnp.broadcast_to(both[None], (PLANE,) + both.shape), 'tens...  6.4 us
  transfers between devices with their start and end apart: 5, of which 2 were waited for; matrix products, arithmetic and copies ran while one was open for 0% of the time, Pallas kernels for 11%

profile of v8, /device:TPU:1, one launch (start us, length us, event | category | flops | bytes accessed | tf_op | source)
XLA Modules:
  0.0 177.9 jit_solution(6744171444341986015)
XLA Ops:
  0.6 0.9 fusion
  1.6 0.9 fusion.2
  2.4 13.3 %collective-permute-start = (bf16[4,2560]{1,0:T(4,128)(2,1)S(1)}, bf16[4,2560]{1,0:T(4,128)(2,1)S(1)}, u32[]{:S(2)}, u32[]{:S(2)}) collective-permute-start(bf16[4,2560]{1,0:T(4,128)(2,1)S(1)} %fusion.2), channel_id=1, source_target_pairs={{0,257},{1,256},{2,259},{3,258},{4,261},{5,260},{6,263},{7,262},{8... | collective-permute-start | bytes 61448 | tf_op jit(solution)/shard_map/ppermute | solution.py:377
  16.4 5.2 %select_rows.1 = (bf16[8,32,1280]{2,1,0:T(8,128)(2,1)}, bf16[8,32,1280]{2,1,0:T(8,128)(2,1)}, bf16[256,1280]{1,0:T(8,128)(2,1)}) custom-call(s32[1]{0:T(128)} %bitcast.12.count_ref, s32[8]{0:T(128)} %bitcast.21, s32[8,1,32]{2,1,0:T(1,128)} %keep_ref.1, bf16[8,128,1280]{2,1,0:T(8,128)(2,1)} %bitcast.15), custom_call_target="tpu_custom_call" | custom-call | tf_op jit(solution)/shard_map/select_rows/pallas_call | solution.py:83
  21.7 0.9 broadcast_in_dim.2
  22.6 6.7 %all-to-all-start = ((bf16[16,8,2560]{2,1,0:T(8,128)(2,1)}), bf16[16,8,2560]{2,1,0:T(8,128)(2,1)S(1)}, u32[]{:S(2)}, u32[]{:S(2)}) async-start(bf16[16,8,2560]{2,1,0:T(8,128)(2,1)} %broadcast_in_dim.2), calls=%async_computation | async-start | bytes 1310720 | tf_op jit(solution)/shard_map/all_to_all | solution.py:385
  29.3 5.2 %collective-permute-start.1 = (bf16[8,32,1280]{2,1,0:T(8,128)(2,1)S(1)}, bf16[8,32,1280]{2,1,0:T(8,128)(2,1)S(1)}, u32[]{:S(2)}, u32[]{:S(2)}) collective-permute-start(bf16[8,32,1280]{2,1,0:T(8,128)(2,1)S(1)} %copy-done.4), channel_id=1, source_target_pairs={{0,256},{32,288},{64,320},{96,352},{128,384},{160,416},{192,448},{... | collective-permute-start | bytes 1966088 | tf_op jit(solution)/shard_map/ppermute | solution.py:379
  34.6 6.4 %all-to-all-done = bf16[16,8,2560]{2,1,0:T(8,128)(2,1)S(1)} async-done(((bf16[16,8,2560]{2,1,0:T(8,128)(2,1)}), bf16[16,8,2560]{2,1,0:T(8,128)(2,1)S(1)}, u32[]{:S(2)}, u32[]{:S(2)}) %all-to-all-start) | async-done | bytes 655392 | tf_op jit(solution)/shard_map/all_to_all | solution.py:385
  41.8 2.4 %project.1 = bf16[128,120]{1,0:T(8,128)(2,1)} custom-call(bf16[128,2560]{1,0:T(8,128)(2,1)} %bitcast.16, bf16[80,2560]{1,0:T(8,128)(2,1)} %bitcast.18, bf16[40,2560]{1,0:T(8,128)(2,1)} %bitcast.19), custom_call_target="tpu_custom_call" | custom-call | tf_op jit(solution)/shard_map/project/pallas_call | solution.py:128
  44.2 10.6 %all_to_all.20.all_ref = bf16[16,8,120]{2,1,0:T(8,128)(2,1)} all-to-all(bf16[16,8,120]{2,1,0:T(8,128)(2,1)} %bitcast.20), channel_id=1, replica_groups={{0,2,4,6,8,10,12,14,16,18,20,22,24,26,28,30},{1,3,5,7,9,11,13,15,17,19,..., dimensions={0} | all-to-all | bytes 61440 | tf_op jit(solution)/shard_map/all_to_all | solution.py:394
  54.8 1.5 pick.1
  56.3 39.6 %all_to_all.21 = bf16[4,4,1920]{2,1,0:T(4,128)(2,1)S(1)} all-to-all(bf16[4,4,1920]{2,1,0:T(4,128)(2,1)} %pick.1), channel_id=1, replica_groups={{0,256,1,257},{32,288,33,289},{64,320,65,321},{96,352,97,353},{128,384,..., dimensions={0} | all-to-all | bytes 122880 | tf_op jit(solution)/shard_map/all_to_all | solution.py:398
  95.9 17.3 %all_gather.6.rows_ref = bf16[32,4,1920]{2,1,0:T(4,128)(2,1)} all-gather(bf16[4,4,1920]{2,1,0:T(4,128)(2,1)S(1)} %all_to_all.21), channel_id=1, replica_groups={{0,32,64,96,128,160,192,224},{256,288,320,352,384,416,448,480},{1,33,65..., dimensions={0}, use_global_device_ids=true | all-gather | bytes 552960 | tf_op jit(solution)/shard_map/all_gather | solution.py:401
  113.2 0.8 copy-done.3
  114.0 2.2 %join.1 = bf16[8,2,32,1280]{3,2,1,0:T(8,128)(2,1)} custom-call(bf16[8,32,1280]{2,1,0:T(8,128)(2,1)} %get-tuple-element.24.near_ref, bf16[8,32,1280]{2,1,0:T(8,128)(2,1)} %copy-done.3), custom_call_target="tpu_custom_call" | custom-call | tf_op jit(solution)/shard_map/join/pallas_call | solution.py:109
  116.2 4.8 %all-to-all-start.3 = ((bf16[8,2,32,1280]{3,2,1,0:T(8,128)(2,1)}), bf16[8,2,32,1280]{3,2,1,0:T(8,128)(2,1)S(1)}, u32[]{:S(2)}, u32[]{:S(2)}) async-start(bf16[8,2,32,1280]{3,2,1,0:T(8,128)(2,1)} %join.1), calls=%async_computation.3 | async-start | bytes 2621440 | tf_op jit(solution)/shard_map/all_to_all | solution.py:403
  121.0 3.8 %attend.1 = bf16[8,2816]{1,0:T(8,128)(2,1)} custom-call(s32[1]{0:T(128)} %bitcast.13.count_ref, s32[8]{0:T(128)} %bitcast.22, bf16[256,1280]{1,0:T(8,128)(2,1)} %get-tuple-element.14.kept_ref, bf16[32,4,1920]{2,1,0:T(4,128)(2,1)} %all_gather.6.rows_ref), custom_call_target="tpu_custom_call" | custom-call | tf_op jit(solution)/shard_map/attend/pallas_call | solution.py:238
  124.8 4.3 %collective-permute-start.2 = (bf16[8,2816]{1,0:T(8,128)(2,1)}, bf16[8,2816]{1,0:T(8,128)(2,1)S(1)}, u32[]{:S(2)}, u32[]{:S(2)}) collective-permute-start(bf16[8,2816]{1,0:T(8,128)(2,1)} %attend.1), channel_id=1, source_target_pairs={{0,256},{32,288},{64,320},{96,352},{128,384},{160,416},{192,448},{... | collective-permute-start | bytes 135176 | tf_op jit(solution)/shard_map/ppermute | solution.py:407
  129.1 2.3 %own_part.1 = (f32[64,32]{1,0:T(8,128)}, f32[64,640]{1,0:T(8,128)}) custom-call(bf16[32,4,1920]{2,1,0:T(4,128)(2,1)} %all_gather.6.rows_ref), custom_call_target="tpu_custom_call" | custom-call | tf_op jit(solution)/shard_map/own_part/pallas_call | solution.py:295
  131.4 12.3 %collective-permute-done.2 = bf16[8,2816]{1,0:T(8,128)(2,1)S(1)} collective-permute-done((bf16[8,2816]{1,0:T(8,128)(2,1)}, bf16[8,2816]{1,0:T(8,128)(2,1)S(1)}, u32[]{:S(2)}, u32[]{:S(2)}) %collective-permute-start.2) | collective-permute-done | bytes 45088 | tf_op jit(solution)/shard_map/ppermute | solution.py:407
  144.5 27.0 %all_gather.7.part_ref = bf16[128,2816]{1,0:T(8,128)(2,1)S(1)} all-gather(bf16[16,2816]{1,0:T(8,128)(2,1)S(1)} %pad_maximum_fusion), channel_id=1, replica_groups={{0,32,64,96,128,160,192,224},{256,288,320,352,384,416,448,480},{1,33,65..., dimensions={0}, use_global_device_ids=true | all-gather | bytes 811008 | tf_op jit(solution)/shard_map/all_gather | solution.py:410
  171.6 0.9 copy-done
  173.2 3.5 %combine.1 = bf16[64,2560]{1,0:T(8,128)(2,1)} custom-call(bf16[128,2816]{1,0:T(8,128)(2,1)S(1)} %all_gather.7.part_ref, f32[64,32]{1,0:T(8,128)S(1)} %copy-done.1, f32[64,640]{1,0:T(8,128)S(1)} %copy-done), custom_call_target="tpu_custom_call" | custom-call | tf_op jit(solution)/shard_map/combine/pallas_call | solution.py:347
  176.8 1.2 copy.13
  (14 shorter events, 2.5 us)
Async XLA Ops:
  2.4 19.2 %collective-permute-start = (bf16[4,2560]{1,0:T(4,128)(2,1)S(1)}, bf16[4,2560]{1,0:T(4,128)(2,1)S(1)}, u32[]{:S(2)}, u32[]{:S(2)}) collective-permute-start(bf16[4,2560]{1,0:T(4,128)(2,1)S(1)} %fusion.2), channel_id=1, source_target_pairs={{0,257},{1,256},{2,259},{3,258},{4,261},{5,260},{6,263},{7,262},{8... | collective-permute-start | bytes 61448 | tf_op jit(solution)/shard_map/ppermute | solution.py:377
  21.6 7.7 %copy-start.4 = (bf16[8,32,1280]{2,1,0:T(8,128)(2,1)S(1)}, bf16[8,32,1280]{2,1,0:T(8,128)(2,1)}, u32[]{:S(2)}) copy-start(bf16[8,32,1280]{2,1,0:T(8,128)(2,1)} %get-tuple-element.17) | copy-start | bytes 1966084
  22.6 18.4 %all-to-all-start = ((bf16[16,8,2560]{2,1,0:T(8,128)(2,1)}), bf16[16,8,2560]{2,1,0:T(8,128)(2,1)S(1)}, u32[]{:S(2)}, u32[]{:S(2)}) async-start(bf16[16,8,2560]{2,1,0:T(8,128)(2,1)} %broadcast_in_dim.2), calls=%async_computation | async-start | bytes 1310720 | tf_op jit(solution)/shard_map/all_to_all | solution.py:385
  29.3 83.8 %collective-permute-start.1 = (bf16[8,32,1280]{2,1,0:T(8,128)(2,1)S(1)}, bf16[8,32,1280]{2,1,0:T(8,128)(2,1)S(1)}, u32[]{:S(2)}, u32[]{:S(2)}) collective-permute-start(bf16[8,32,1280]{2,1,0:T(8,128)(2,1)S(1)} %copy-done.4), channel_id=1, source_target_pairs={{0,256},{32,288},{64,320},{96,352},{128,384},{160,416},{192,448},{... | collective-permute-start | bytes 1966088 | tf_op jit(solution)/shard_map/ppermute | solution.py:379
  41.0 0.8 copy-start.2
  113.2 0.8 copy-start.3
  116.2 60.6 %all-to-all-start.3 = ((bf16[8,2,32,1280]{3,2,1,0:T(8,128)(2,1)}), bf16[8,2,32,1280]{3,2,1,0:T(8,128)(2,1)S(1)}, u32[]{:S(2)}, u32[]{:S(2)}) async-start(bf16[8,2,32,1280]{3,2,1,0:T(8,128)(2,1)} %join.1), calls=%async_computation.3 | async-start | bytes 2621440 | tf_op jit(solution)/shard_map/all_to_all | solution.py:403
  124.8 18.9 %collective-permute-start.2 = (bf16[8,2816]{1,0:T(8,128)(2,1)}, bf16[8,2816]{1,0:T(8,128)(2,1)S(1)}, u32[]{:S(2)}, u32[]{:S(2)}) collective-permute-start(bf16[8,2816]{1,0:T(8,128)(2,1)} %attend.1), channel_id=1, source_target_pairs={{0,256},{32,288},{64,320},{96,352},{128,384},{160,416},{192,448},{... | collective-permute-start | bytes 135176 | tf_op jit(solution)/shard_map/ppermute | solution.py:407
  171.6 0.9 copy-start
  172.5 0.8 copy-start.1

commit v9 on v6

--- a/solution.py
+++ b/solution.py
@@ -247,7 +247,7 @@
     return ((lane >= head) & (lane < head + HEAD_DIM)).astype(jnp.float32).astype(jnp.bfloat16)
 
 
-def own_kernel(rows_ref, score_ref, value_ref, query_ref, pair_ref):
+def own_kernel(rows_ref, own_ref, query_ref, pair_ref):
     scale = HEAD_DIM ** (-0.5)
     share = rows_ref.shape[1]
     piece = HEAD_DIM // 2
@@ -266,21 +266,20 @@
             at = KEYS // 2 + g * piece
             values.append(pair_ref[half, :, at : at + piece])
     key = jnp.concatenate(keys, axis=1)
-    value_ref[...] = jnp.concatenate(values, axis=1)
+    own_ref[:, :KEYS] = jnp.concatenate(values, axis=1)
     product = query_ref[...] * jnp.concatenate([key] * REPEAT, axis=1)
-    score_ref[...] = scale * spread_dot(product, head_columns(), ((1,), (1,)), 3)
+    own_ref[:, KEYS:] = jnp.concatenate(
+        [scale * spread_dot(product, head_columns(), ((1,), (1,)), 3)] * 4, axis=1
+    )
 
 
 def own_part(rows):
     requests = HOLDERS * rows.shape[1]
     return pl.pallas_call(
         own_kernel,
-        out_shape=(
-            jax.ShapeDtypeStruct((requests, HEADS), jnp.float32),
-            jax.ShapeDtypeStruct((requests, KEYS), jnp.float32),
-        ),
+        out_shape=jax.ShapeDtypeStruct((requests, KEYS + 4 * HEADS), jnp.float32),
         in_specs=[VMEM],
-        out_specs=(VMEM, VMEM),
+        out_specs=VMEM,
         scratch_shapes=[
             pltpu.VMEM((requests, QUERIES), jnp.float32),
             pltpu.VMEM((2, requests, KEYS), jnp.float32),
@@ -289,7 +288,7 @@
     )(rows)
 
 
-def combine_kernel(part_ref, own_ref, value_ref, out_ref):
+def combine_kernel(part_ref, own_ref, out_ref):
     requests = out_ref.shape[0]
     slots = part_ref.shape[0]
     extra = part_ref[:, QUERIES:].astype(jnp.float32)
@@ -297,18 +296,27 @@
     peaks = column[0] + column[1] + column[2]
     totals = column[3] + column[4] + column[5]
     tag = column[6][:, :1]
-    row = lax.broadcasted_iota(jnp.int32, (requests, 1), 0).astype(jnp.float32)
     member = (
         tag == lax.broadcasted_iota(jnp.int32, (slots, requests), 1).astype(jnp.float32)
     ).astype(jnp.float32).astype(jnp.bfloat16)
     expand = head_columns()
-    own = own_ref[...]
-    tops = [own] + [jnp.full(own.shape, NEGATIVE, jnp.float32)] * 3
-    for s in range(slots):
-        tops[s % 4] = jnp.maximum(
-            tops[s % 4], jnp.where(tag[s : s + 1] == row, peaks[s : s + 1], NEGATIVE)
+    own = own_ref[:, KEYS : KEYS + HEADS]
+    quarter = slots // 4
+    beside = [
+        jnp.concatenate([block[i * quarter : (i + 1) * quarter] for i in range(4)], axis=1)
+        for block in (peaks, column[6])
+    ]
+    row = lax.broadcasted_iota(jnp.int32, (requests, 4 * HEADS), 0).astype(jnp.float32)
+    tops = [jnp.full(row.shape, NEGATIVE, jnp.float32)] * 2
+    for s in range(quarter):
+        tops[s % 2] = jnp.maximum(
+            tops[s % 2],
+            jnp.where(beside[1][s : s + 1] == row, beside[0][s : s + 1], NEGATIVE),
         )
-    top = jnp.maximum(jnp.maximum(tops[0], tops[1]), jnp.maximum(tops[2], tops[3]))
+    wide = jnp.maximum(tops[0], tops[1])
+    top = own
+    for i in range(4):
+        top = jnp.maximum(top, wide[:, i * HEADS : (i + 1) * HEADS])
     own_weight = jnp.exp(own - top)
     weight = jnp.exp(peaks - spread_dot(top, member, ((1,), (0,)), 3, True))
     total = spread_dot(weight * totals, member, ((0,), (0,)), 3, True) + own_weight
@@ -317,38 +325,53 @@
     scaled = part_ref[:, :QUERIES].astype(jnp.float32) * spread_dot(weight, expand, ((1,), (0,)), 2)
     mixed = spread_dot(scaled, member, ((0,), (0,)), 2, True)
     own_share = spread_dot(own_weight * inverse, expand, ((1,), (0,)), 2)
-    mixed = mixed + own_share * jnp.concatenate([value_ref[...]] * REPEAT, axis=1)
+    mixed = mixed + own_share * jnp.concatenate([own_ref[:, :KEYS]] * REPEAT, axis=1)
     mixed = mixed.astype(jnp.bfloat16)
     for h in range(HEADS):
         at = (h % REPEAT * KV_HEADS + h // REPEAT) * HEAD_DIM
         out_ref[:, h * HEAD_DIM : (h + 1) * HEAD_DIM] = mixed[:, at : at + HEAD_DIM]
 
 
-def combine(parts, own, value):
+def combine(parts, own):
     return pl.pallas_call(
         combine_kernel,
         out_shape=jax.ShapeDtypeStruct((own.shape[0], QUERIES), jnp.bfloat16),
-        in_specs=[VMEM] * 3,
+        in_specs=[VMEM] * 2,
         out_specs=VMEM,
         compiler_params=pltpu.CompilerParams(vmem_limit_bytes=48 * 1024 * 1024),
         name="combine",
-    )(parts, own, value)
-
-
-def settle_kernel(in_ref, out_ref):
-    out_ref[...] = in_ref[...]
-
-
-def settle(pages):
-    block = pl.BlockSpec((4,) + pages.shape[1:], lambda i: (i, 0, 0))
-    return pl.pallas_call(
-        settle_kernel,
-        out_shape=jax.ShapeDtypeStruct(pages.shape, pages.dtype),
-        grid=(pages.shape[0] // 4,),
-        in_specs=[block],
-        out_specs=block,
-        name="settle",
-    )(pages)
+    )(parts, own)
+
+
+def normalise_kernel(holder_ref, tokens_ref, gain_ref, out_ref, rows_ref):
+    share = out_ref.shape[0]
+    widened = tokens_ref[...].astype(jnp.float32)
+    mean = jnp.mean(widened * widened, axis=-1, keepdims=True)
+    normed = widened * lax.rsqrt(mean + EPSILON) * gain_ref[...]
+    for i in range(rows_ref.shape[0]):
+        rows_ref[i] = normed[i * share : (i + 1) * share]
+    out_ref[...] = rows_ref[holder_ref[0] % rows_ref.shape[0]].astype(jnp.bfloat16)
+
+
+def normalise(holder, tokens, norm_gain):
+    requests, width = tokens.shape
+    share = requests // HOLDERS
+    shares = 4
+    return pl.pallas_call(
+        normalise_kernel,
+        out_shape=jax.ShapeDtypeStruct((share, width), jnp.bfloat16),
+        grid_spec=pltpu.PrefetchScalarGridSpec(
+            num_scalar_prefetch=1,
+            grid=(1,),
+            in_specs=[
+                pl.BlockSpec((shares * share, width), lambda i, holder: (holder[0] // shares, 0)),
+                pl.BlockSpec((1, width), lambda i, *_: (0, 0)),
+            ],
+            out_specs=pl.BlockSpec((share, width), lambda i, *_: (0, 0)),
+            scratch_shapes=[pltpu.VMEM((shares, share, width), jnp.float32)],
+        ),
+        name="normalise",
+    )(holder.reshape(1), tokens, norm_gain.reshape(1, width))
 
 
 def per_device(
@@ -357,21 +380,11 @@
     holder = lax.axis_index("page")
     group = lax.axis_index("tensor")
     half = group % 2
-    share = tokens.shape[0] // HOLDERS
-
-    def normalise(rows):
-        widened = rows.astype(jnp.float32)
-        return (
-            widened
-            * lax.rsqrt(jnp.mean(widened * widened, axis=-1, keepdims=True) + EPSILON)
-            * norm_gain
-        ).astype(jnp.bfloat16)
-
     page_count = page_count.reshape(1)
     page_owner = page_owner.reshape(SOURCES)
     compact, kept = select_rows(page_count, dest_slot.reshape(SOURCES), keep_rows, cache)
 
-    mine = normalise(lax.dynamic_slice_in_dim(tokens, holder * share, share, 0))
+    mine = normalise(holder, tokens, norm_gain)
     across = lax.ppermute(mine, ("page", "tensor"), OTHER_HALF)
     across, compact = lax.optimization_barrier((across, compact))
     arrived = lax.all_to_all(compact, "page", 0, 0, tiled=True)
@@ -396,9 +409,8 @@
     rows = lax.all_gather(quarter, "page", axis=0, axis_index_groups=QUAD_GROUPS, tiled=True)
     part = attend(page_count, page_owner, kept, rows)
     far = lax.ppermute(part, "page", OTHER_QUAD)
-    own, value = own_part(rows)
-    settled = settle(arrived)
-    far, own, value, settled = lax.optimization_barrier((far, own, value, settled))
+    own = own_part(rows)
+    far, own = lax.optimization_barrier((far, own))
     parts = lax.all_gather(
         jnp.concatenate([part, far], axis=0),
         "page",
@@ -406,7 +418,7 @@
         axis_index_groups=QUAD_GROUPS,
         tiled=True,
     )
-    return combine(parts, own, value), settled[:, None]
+    return combine(parts, own), arrived[:, None]
 
 
 def solution(mesh):

time: 162 us -> 163 us (level)
  waiting for transfers between devices: 11.3 us -> 14.6 us
  Pallas kernels: 22.3 us -> 19.7 us
    ppermute x1, waiting for transfers between devices: 4.72 us -> 8.05 us  [per_device(): far = lax.ppermute(part, 'page', OTHER_QUAD)]
    pallas_call x2, Pallas kernels: 5.74 us -> 4.07 us  [the longest x1 2.42 us: own_part(): pl.pallas_call(own_kernel, out_shape=jax.ShapeDtypeStruct((requests, KEYS...]
  transfers between devices with their start and end apart: 3 -> 3, of which waited for: 2 -> 2; matrix products, arithmetic and copies ran while one was open for 0% -> 0% of each run, Pallas kernels for 9% -> 7%
where the time goes in v9:
time: 163 us; the launch traced here: 162 us
  blocking collectives  99.8 us (61%)
  starting transfers between devices  22.4 us (14%)
  Pallas kernels  19.7 us (12%)
  waiting for transfers between devices  14.6 us (9%)
  local copies, waits for them, and re-layouts  3.3 us (2%)
    all_to_all x1, blocking collectives, per_device(): lax.all_to_all(halves, ('page', 'tensor'), 0, 0, axis_index_groups=FOUR_G...  23.4 us
    all_gather x1, blocking collectives, per_device(): lax.all_gather(both, 'tensor', axis=0, axis_index_groups=PLANE_GROUPS, ti...  22.1 us
    all_gather x1, blocking collectives, per_device(): lax.all_gather(projected, 'tensor', axis=0, axis_index_groups=PLANE_GROUP...  20.9 us
    all_gather x1, blocking collectives, per_device(): lax.all_gather(quarter, 'page', axis=0, axis_index_groups=QUAD_GROUPS, ti...  17.5 us
    all_gather x1, blocking collectives, per_device(): lax.all_gather(jnp.concatenate([part, far], axis=0), 'page', axis=0, axis...  15.8 us
    ppermute x1, starting transfers between devices, per_device(): across = lax.ppermute(mine, ('page', 'tensor'), OTHER_HALF)  13.3 us
    ppermute x1, waiting for transfers between devices, per_device(): far = lax.ppermute(part, 'page', OTHER_QUAD)  8.05 us
    all_to_all x1, starting transfers between devices, per_device(): arrived = lax.all_to_all(compact, 'page', 0, 0, tiled=True)  7.17 us
  transfers between devices with their start and end apart: 3, of which 2 were waited for; matrix products, arithmetic and copies ran while one was open for 0% of the time, Pallas kernels for 7%

profile of v9, /device:TPU:1, one launch (start us, length us, event | category | flops | bytes accessed | tf_op | source)
XLA Modules:
  0.0 161.9 jit_solution(8407893781346821748)
XLA Ops:
  0.6 1.3 reshape.31.gain_ref
  1.9 1.6 %normalise.1 = bf16[4,2560]{1,0:T(4,128)(2,1)} custom-call(s32[1]{0:T(128)} %bitcast.5.holder_ref, bf16[64,2560]{1,0:T(8,128)(2,1)} %tokens_ref.1, f32[1,2560]{1,0:T(1,128)} %reshape.31.gain_ref), custom_call_target="tpu_custom_call" | custom-call | tf_op jit(solution)/shard_map/normalise/pallas_call | solution.py:360
  3.6 13.3 %collective-permute-start = (bf16[4,2560]{1,0:T(4,128)(2,1)}, bf16[4,2560]{1,0:T(4,128)(2,1)S(1)}, u32[]{:S(2)}, u32[]{:S(2)}) collective-permute-start(bf16[4,2560]{1,0:T(4,128)(2,1)} %normalise.1), channel_id=1, source_target_pairs={{0,257},{1,256},{2,259},{3,258},{4,261},{5,260},{6,263},{7,262},{8... | collective-permute-start | bytes 61448 | tf_op jit(solution)/shard_map/ppermute | solution.py:388
  17.5 5.2 %select_rows.1 = (bf16[16,32,1280]{2,1,0:T(8,128)(2,1)}, bf16[256,1280]{1,0:T(8,128)(2,1)}) custom-call(s32[1]{0:T(128)} %bitcast.12.count_ref, s32[8]{0:T(128)} %bitcast.19, s32[8,1,32]{2,1,0:T(1,128)} %keep_ref.1, bf16[8,128,1280]{2,1,0:T(8,128)(2,1)} %bitcast.15), custom_call_target="tpu_custom_call" | custom-call | tf_op jit(solution)/shard_map/select_rows/pallas_call | solution.py:72
  22.7 0.0 collective-permute-done
  22.7 0.0 copy-start.1
  22.8 7.2 %all-to-all-start = ((bf16[16,32,1280]{2,1,0:T(8,128)(2,1)}), bf16[16,32,1280]{2,1,0:T(8,128)(2,1)S(1)}, u32[]{:S(2)}, u32[]{:S(2)}) async-start(bf16[16,32,1280]{2,1,0:T(8,128)(2,1)} %get-tuple-element.13), calls=%async_computation | async-start | bytes 2621440 | tf_op jit(solution)/shard_map/all_to_all | solution.py:390
  29.9 0.0 copy-done.1
  30.0 22.1 %all_gather.15.rows_ref = bf16[128,2560]{1,0:T(8,128)(2,1)} all-gather(bf16[8,2560]{1,0:T(8,128)(2,1)S(1)} %maximum_select_fusion), channel_id=1, replica_groups={{0,2,4,6,8,10,12,14,16,18,20,22,24,26,28,30},{1,3,5,7,9,11,13,15,17,19,..., dimensions={0}, use_global_device_ids=true | all-gather | bytes 696320 | tf_op jit(solution)/shard_map/all_gather | solution.py:397
  52.1 2.4 %project.1 = bf16[128,120]{1,0:T(8,128)(2,1)} custom-call(bf16[128,2560]{1,0:T(8,128)(2,1)} %all_gather.15.rows_ref, bf16[80,2560]{1,0:T(8,128)(2,1)} %bitcast.17, bf16[40,2560]{1,0:T(8,128)(2,1)} %bitcast.18), custom_call_target="tpu_custom_call" | custom-call | tf_op jit(solution)/shard_map/project/pallas_call | solution.py:103
  54.5 20.9 %all-gather = bf16[2048,120]{1,0:T(8,128)(2,1)} all-gather(bf16[128,120]{1,0:T(8,128)(2,1)} %project.1), channel_id=2, replica_groups={{0,2,4,6,8,10,12,14,16,18,20,22,24,26,28,30},{1,3,5,7,9,11,13,15,17,19,..., dimensions={0}, use_global_device_ids=true | all-gather | bytes 522240 | tf_op jit(solution)/shard_map/all_gather | solution.py:401
  75.4 1.5 pick.1
  76.9 6.5 %all-to-all-done = bf16[16,32,1280]{2,1,0:T(8,128)(2,1)S(1)} async-done(((bf16[16,32,1280]{2,1,0:T(8,128)(2,1)}), bf16[16,32,1280]{2,1,0:T(8,128)(2,1)S(1)}, u32[]{:S(2)}, u32[]{:S(2)}) %all-to-all-start) | async-done | bytes 1310752 | tf_op jit(solution)/shard_map/all_to_all | solution.py:390
  83.5 23.4 %all_to_all.10 = bf16[4,4,1920]{2,1,0:T(4,128)(2,1)S(1)} all-to-all(bf16[4,4,1920]{2,1,0:T(4,128)(2,1)} %pick.1), channel_id=1, replica_groups={{0,256,1,257},{32,288,33,289},{64,320,65,321},{96,352,97,353},{128,384,..., dimensions={0} | all-to-all | bytes 122880 | tf_op jit(solution)/shard_map/all_to_all | solution.py:406
  106.9 17.5 %all_gather.18.rows_ref = bf16[32,4,1920]{2,1,0:T(4,128)(2,1)} all-gather(bf16[4,4,1920]{2,1,0:T(4,128)(2,1)S(1)} %all_to_all.10), channel_id=1, replica_groups={{0,32,64,96,128,160,192,224},{256,288,320,352,384,416,448,480},{1,33,65..., dimensions={0}, use_global_device_ids=true | all-gather | bytes 552960 | tf_op jit(solution)/shard_map/all_gather | solution.py:409
  124.4 3.9 %attend.1 = bf16[8,2816]{1,0:T(8,128)(2,1)} custom-call(s32[1]{0:T(128)} %bitcast.13.count_ref, s32[8]{0:T(128)} %bitcast.20, bf16[256,1280]{1,0:T(8,128)(2,1)} %get-tuple-element.10.kept_ref, bf16[32,4,1920]{2,1,0:T(4,128)(2,1)} %all_gather.18.rows_ref), custom_call_target="tpu_custom_call" | custom-call | tf_op jit(solution)/shard_map/attend/pallas_call | solution.py:219
  128.2 1.9 %collective-permute-start.1 = (bf16[8,2816]{1,0:T(8,128)(2,1)}, bf16[8,2816]{1,0:T(8,128)(2,1)S(1)}, u32[]{:S(2)}, u32[]{:S(2)}) collective-permute-start(bf16[8,2816]{1,0:T(8,128)(2,1)} %attend.1), channel_id=1, source_target_pairs={{0,256},{32,288},{64,320},{96,352},{128,384},{160,416},{192,448},{... | collective-permute-start | bytes 135176 | tf_op jit(solution)/shard_map/ppermute | solution.py:411
  130.1 2.4 %own_part.1.own_ref = f32[64,768]{1,0:T(8,128)} custom-call(bf16[32,4,1920]{2,1,0:T(4,128)(2,1)} %all_gather.18.rows_ref), custom_call_target="tpu_custom_call" | custom-call | tf_op jit(solution)/shard_map/own_part/pallas_call | solution.py:278
  132.6 8.1 %collective-permute-done.1 = bf16[8,2816]{1,0:T(8,128)(2,1)S(1)} collective-permute-done((bf16[8,2816]{1,0:T(8,128)(2,1)}, bf16[8,2816]{1,0:T(8,128)(2,1)S(1)}, u32[]{:S(2)}, u32[]{:S(2)}) %collective-permute-start.1) | collective-permute-done | bytes 45088 | tf_op jit(solution)/shard_map/ppermute | solution.py:411
  140.6 0.8 pad_maximum_fusion
  141.4 15.8 %all_gather.19.part_ref = bf16[128,2816]{1,0:T(8,128)(2,1)S(1)} all-gather(bf16[16,2816]{1,0:T(8,128)(2,1)S(1)} %pad_maximum_fusion), channel_id=1, replica_groups={{0,32,64,96,128,160,192,224},{256,288,320,352,384,416,448,480},{1,33,65..., dimensions={0}, use_global_device_ids=true | all-gather | bytes 811008 | tf_op jit(solution)/shard_map/all_gather | solution.py:414
  157.3 0.9 copy-done
  158.2 2.7 %combine.1 = bf16[64,2560]{1,0:T(8,128)(2,1)} custom-call(bf16[128,2816]{1,0:T(8,128)(2,1)S(1)} %all_gather.19.part_ref, f32[64,768]{1,0:T(8,128)S(1)} %copy-done), custom_call_target="tpu_custom_call" | custom-call | tf_op jit(solution)/shard_map/combine/pallas_call | solution.py:336
  160.9 1.1 copy.15
  (2 shorter events, 0.0 us)
Async XLA Ops:
  3.6 19.1 %collective-permute-start = (bf16[4,2560]{1,0:T(4,128)(2,1)}, bf16[4,2560]{1,0:T(4,128)(2,1)S(1)}, u32[]{:S(2)}, u32[]{:S(2)}) collective-permute-start(bf16[4,2560]{1,0:T(4,128)(2,1)} %normalise.1), channel_id=1, source_target_pairs={{0,257},{1,256},{2,259},{3,258},{4,261},{5,260},{6,263},{7,262},{8... | collective-permute-start | bytes 61448 | tf_op jit(solution)/shard_map/ppermute | solution.py:388
  22.7 7.2 %copy-start.1 = (bf16[4,2560]{1,0:T(4,128)(2,1)S(1)}, bf16[4,2560]{1,0:T(4,128)(2,1)}, u32[]{:S(2)}) copy-start(bf16[4,2560]{1,0:T(4,128)(2,1)} %normalise.1) | copy-start | bytes 61444
  22.8 60.7 %all-to-all-start = ((bf16[16,32,1280]{2,1,0:T(8,128)(2,1)}), bf16[16,32,1280]{2,1,0:T(8,128)(2,1)S(1)}, u32[]{:S(2)}, u32[]{:S(2)}) async-start(bf16[16,32,1280]{2,1,0:T(8,128)(2,1)} %get-tuple-element.13), calls=%async_computation | async-start | bytes 2621440 | tf_op jit(solution)/shard_map/all_to_all | solution.py:390
  128.2 12.4 %collective-permute-start.1 = (bf16[8,2816]{1,0:T(8,128)(2,1)}, bf16[8,2816]{1,0:T(8,128)(2,1)S(1)}, u32[]{:S(2)}, u32[]{:S(2)}) collective-permute-start(bf16[8,2816]{1,0:T(8,128)(2,1)} %attend.1), channel_id=1, source_target_pairs={{0,256},{32,288},{64,320},{96,352},{128,384},{160,416},{192,448},{... | collective-permute-start | bytes 135176 | tf_op jit(solution)/shard_map/ppermute | solution.py:411
  157.3 0.9 copy-start

commit v10 on v7

--- a/solution.py
+++ b/solution.py
@@ -279,7 +279,7 @@
     return ((lane >= head) & (lane < head + HEAD_DIM)).astype(jnp.float32).astype(jnp.bfloat16)
 
 
-def own_kernel(rows_ref, score_ref, value_ref, query_ref, pair_ref):
+def own_kernel(rows_ref, own_ref, query_ref, pair_ref):
     scale = HEAD_DIM ** (-0.5)
     share = rows_ref.shape[1]
     piece = HEAD_DIM // 2
@@ -298,21 +298,20 @@
             at = KEYS // 2 + g * piece
             values.append(pair_ref[half, :, at : at + piece])
     key = jnp.concatenate(keys, axis=1)
-    value_ref[...] = jnp.concatenate(values, axis=1)
+    own_ref[:, :KEYS] = jnp.concatenate(values, axis=1)
     product = query_ref[...] * jnp.concatenate([key] * REPEAT, axis=1)
-    score_ref[...] = scale * spread_dot(product, head_columns(), ((1,), (1,)), 3)
+    own_ref[:, KEYS:] = jnp.concatenate(
+        [scale * spread_dot(product, head_columns(), ((1,), (1,)), 3)] * 4, axis=1
+    )
 
 
 def own_part(rows):
     requests = HOLDERS * rows.shape[1]
     return pl.pallas_call(
         own_kernel,
-        out_shape=(
-            jax.ShapeDtypeStruct((requests, HEADS), jnp.float32),
-            jax.ShapeDtypeStruct((requests, KEYS), jnp.float32),
-        ),
+        out_shape=jax.ShapeDtypeStruct((requests, KEYS + 4 * HEADS), jnp.float32),
         in_specs=[VMEM],
-        out_specs=(VMEM, VMEM),
+        out_specs=VMEM,
         scratch_shapes=[
             pltpu.VMEM((requests, QUERIES), jnp.float32),
             pltpu.VMEM((2, requests, KEYS), jnp.float32),
@@ -321,7 +320,7 @@
     )(rows)
 
 
-def combine_kernel(part_ref, own_ref, value_ref, out_ref):
+def combine_kernel(part_ref, own_ref, out_ref):
     requests = out_ref.shape[0]
     slots = part_ref.shape[0]
     extra = part_ref[:, QUERIES:].astype(jnp.float32)
@@ -329,18 +328,27 @@
     peaks = column[0] + column[1] + column[2]
     totals = column[3] + column[4] + column[5]
     tag = column[6][:, :1]
-    row = lax.broadcasted_iota(jnp.int32, (requests, 1), 0).astype(jnp.float32)
     member = (
         tag == lax.broadcasted_iota(jnp.int32, (slots, requests), 1).astype(jnp.float32)
     ).astype(jnp.float32).astype(jnp.bfloat16)
     expand = head_columns()
-    own = own_ref[...]
-    tops = [own] + [jnp.full(own.shape, NEGATIVE, jnp.float32)] * 3
-    for s in range(slots):
-        tops[s % 4] = jnp.maximum(
-            tops[s % 4], jnp.where(tag[s : s + 1] == row, peaks[s : s + 1], NEGATIVE)
+    own = own_ref[:, KEYS : KEYS + HEADS]
+    quarter = slots // 4
+    beside = [
+        jnp.concatenate([block[i * quarter : (i + 1) * quarter] for i in range(4)], axis=1)
+        for block in (peaks, column[6])
+    ]
+    row = lax.broadcasted_iota(jnp.int32, (requests, 4 * HEADS), 0).astype(jnp.float32)
+    tops = [jnp.full(row.shape, NEGATIVE, jnp.float32)] * 2
+    for s in range(quarter):
+        tops[s % 2] = jnp.maximum(
+            tops[s % 2],
+            jnp.where(beside[1][s : s + 1] == row, beside[0][s : s + 1], NEGATIVE),
         )
-    top = jnp.maximum(jnp.maximum(tops[0], tops[1]), jnp.maximum(tops[2], tops[3]))
+    wide = jnp.maximum(tops[0], tops[1])
+    top = own
+    for i in range(4):
+        top = jnp.maximum(top, wide[:, i * HEADS : (i + 1) * HEADS])
     own_weight = jnp.exp(own - top)
     weight = jnp.exp(peaks - spread_dot(top, member, ((1,), (0,)), 3, True))
     total = spread_dot(weight * totals, member, ((0,), (0,)), 3, True) + own_weight
@@ -349,22 +357,22 @@
     scaled = part_ref[:, :QUERIES].astype(jnp.float32) * spread_dot(weight, expand, ((1,), (0,)), 2)
     mixed = spread_dot(scaled, member, ((0,), (0,)), 2, True)
     own_share = spread_dot(own_weight * inverse, expand, ((1,), (0,)), 2)
-    mixed = mixed + own_share * jnp.concatenate([value_ref[...]] * REPEAT, axis=1)
+    mixed = mixed + own_share * jnp.concatenate([own_ref[:, :KEYS]] * REPEAT, axis=1)
     mixed = mixed.astype(jnp.bfloat16)
     for h in range(HEADS):
         at = (h % REPEAT * KV_HEADS + h // REPEAT) * HEAD_DIM
         out_ref[:, h * HEAD_DIM : (h + 1) * HEAD_DIM] = mixed[:, at : at + HEAD_DIM]
 
 
-def combine(parts, own, value):
+def combine(parts, own):
     return pl.pallas_call(
         combine_kernel,
         out_shape=jax.ShapeDtypeStruct((own.shape[0], QUERIES), jnp.bfloat16),
-        in_specs=[VMEM] * 3,
+        in_specs=[VMEM] * 2,
         out_specs=VMEM,
         compiler_params=pltpu.CompilerParams(vmem_limit_bytes=48 * 1024 * 1024),
         name="combine",
-    )(parts, own, value)
+    )(parts, own)
 
 
 def per_device(
@@ -416,24 +424,22 @@
         axis_index_groups=PLANE_GROUPS,
         tiled=True,
     ).reshape(PLANE * both.shape[0], -1)
-    rows = send(rows, (2,))
     projected = project(rows, w_query, w_keyvalue).reshape(PLANE, both.shape[0], -1)
+    projected = send(projected, (2, 3))
     back = lax.all_to_all(
         projected, "tensor", 0, 0, axis_index_groups=PLANE_GROUPS, tiled=True
     )
-    halves = receive(pick(back), (4, 5, 1))
-    halves = send(halves, (6, 3))
+    halves = receive(pick(back), (4, 5, 1, 2, 3))
+    halves = send(halves, (6,))
     quarter = lax.all_to_all(
         halves, ("page", "tensor"), 0, 0, axis_index_groups=FOUR_GROUPS, tiled=True
     )
     rows = lax.all_gather(quarter, "page", axis=0, axis_index_groups=QUAD_GROUPS, tiled=True)
-    rows = receive(rows, (2,))
     part = attend(page_count, page_owner, kept, rows)
     far = lax.ppermute(part, "page", OTHER_QUAD)
-    own, value = own_part(rows)
-    own = send(own, (7,))
-    far, own, value = lax.optimization_barrier((far, own, value))
-    far = receive(far, (6, 3))
+    own = send(own_part(rows), (7,))
+    far, own = lax.optimization_barrier((far, own))
+    far = receive(far, (6,))
     parts = lax.all_gather(
         jnp.concatenate([part, far], axis=0),
         "page",
@@ -443,7 +449,7 @@
     )
     parts = receive(parts, (7,))
     cross = lax.ppermute(pack(got), "page", OTHER_CORE)
-    attended = combine(parts, own, value)
+    attended = combine(parts, own)
     return attended, place_pages(got, cross)[:, None]
 
 

time: 161 us -> 168 us (1.043)
  waiting for transfers between devices: 3.28 us -> 7.72 us
  blocking collectives: 61.4 us -> 63.8 us
    ppermute x7, waiting for transfers between devices: 3.18 us -> 6.58 us  [send(): got[d] = lax.ppermute(block, 'page', OTHER_CHIP[d])]
    ppermute x7, starting transfers between devices: 33.9 us -> 36.5 us  [send(): got[d] = lax.ppermute(block, 'page', OTHER_CHIP[d])]
    all_gather x1, blocking collectives: 27.7 us -> 29.4 us  [per_device(): lax.all_gather(quarter, 'page', axis=0, axis_index_groups=QUAD_GROUPS, ti...]
  transfers between devices with their start and end apart: 12 -> 12, of which waited for: 2 -> 2; matrix products, arithmetic and copies ran while one was open for 1% -> 1% of each run, Pallas kernels for 12% -> 11%
where the time goes in v10:
time: 168 us; the launch traced here: 167 us
  starting transfers between devices  65 us (39%)
  blocking collectives  63.8 us (38%)
  Pallas kernels  23.3 us (14%)
  waiting for transfers between devices  7.72 us (5%)
  local copies, waits for them, and re-layouts  3.26 us (2%)
  other arithmetic  2.7 us (2%)
    ppermute x7, starting transfers between devices, send(): got[d] = lax.ppermute(block, 'page', OTHER_CHIP[d])  36.5 us
    all_gather x1, blocking collectives, per_device(): lax.all_gather(quarter, 'page', axis=0, axis_index_groups=QUAD_GROUPS, ti...  29.4 us
    all_gather x1, blocking collectives, per_device(): lax.all_gather(jnp.concatenate([part, far], axis=0), 'page', axis=0, axis...  21.1 us
    ppermute x1, starting transfers between devices, per_device(): across = lax.ppermute(mine, ('page', 'tensor'), OTHER_HALF)  13.3 us
    all_to_all x1, blocking collectives, per_device(): lax.all_to_all(projected, 'tensor', 0, 0, axis_index_groups=PLANE_GROUPS,...  13.3 us
    all_to_all x1, starting transfers between devices, per_device(): lax.all_to_all(jnp.broadcast_to(both[None], (PLANE,) + both.shape), 'tens...  6.88 us
    ppermute x7, waiting for transfers between devices, send(): got[d] = lax.ppermute(block, 'page', OTHER_CHIP[d])  6.58 us
    pallas_call x1, Pallas kernels, select_rows(): pl.pallas_call(select_kernel, out_shape=[block] * CHIPS + [jax.ShapeDtype...  5.44 us
  transfers between devices with their start and end apart: 12, of which 2 were waited for; matrix products, arithmetic and copies ran while one was open for 1% of the time, Pallas kernels for 11%

profile of v10, /device:TPU:1, one launch (start us, length us, event | category | flops | bytes accessed | tf_op | source)
XLA Modules:
  0.0 167.3 jit_solution(9995842564406655171)
XLA Ops:
  2.4 13.3 %collective-permute-start = (bf16[4,2560]{1,0:T(4,128)(2,1)S(1)}, bf16[4,2560]{1,0:T(4,128)(2,1)S(1)}, u32[]{:S(2)}, u32[]{:S(2)}) collective-permute-start(bf16[4,2560]{1,0:T(4,128)(2,1)S(1)} %fusion.2), channel_id=1, source_target_pairs={{0,257},{1,256},{2,259},{3,258},{4,261},{5,260},{6,263},{7,262},{8... | collective-permute-start | bytes 61448 | tf_op jit(solution)/shard_map/ppermute | solution.py:398
  16.4 5.4 %select_rows.1 = (bf16[2,32,1280]{2,1,0:T(8,128)(2,1)}, bf16[2,32,1280]{2,1,0:T(8,128)(2,1)}, bf16[2,32,1280]{2,1,0:T(8,128)(2,1)}, bf16[2,32,1280]{2,1,0:T(8,12...) custom-call(s32[1]{0:T(128)} %bitcast.11.count_ref, ...), custom_call_target="tpu_custom_call" | custom-call | tf_op jit(solution)/shard_map/select_rows/pallas_call | solution.py:81
  22.8 6.9 %all-to-all-start = ((bf16[16,8,2560]{2,1,0:T(8,128)(2,1)}), bf16[16,8,2560]{2,1,0:T(8,128)(2,1)S(1)}, u32[]{:S(2)}, u32[]{:S(2)}) async-start(bf16[16,8,2560]{2,1,0:T(8,128)(2,1)} %broadcast_in_dim.4), calls=%async_computation | async-start | bytes 1310720 | tf_op jit(solution)/shard_map/all_to_all | solution.py:419
  29.7 5.2 %collective-permute-start.1 = (bf16[2,32,1280]{2,1,0:T(8,128)(2,1)}, bf16[2,32,1280]{2,1,0:T(8,128)(2,1)S(1)}, u32[]{:S(2)}, u32[]{:S(2)}) collective-permute-start(bf16[2,32,1280]{2,1,0:T(8,128)(2,1)} %get-tuple-element.39), channel_id=1, source_target_pairs={{0,256},{32,288},{64,320},{96,352},{128,384},{160,416},{192,448},{... | collective-permute-start | bytes 491528 | tf_op jit(solution)/shard_map/ppermute | solution.py:404
  34.9 4.5 %collective-permute-start.2 = (bf16[2,32,1280]{2,1,0:T(8,128)(2,1)}, bf16[2,32,1280]{2,1,0:T(8,128)(2,1)S(1)}, u32[]{:S(2)}, u32[]{:S(2)}) collective-permute-start(bf16[2,32,1280]{2,1,0:T(8,128)(2,1)} %get-tuple-element.40), channel_id=1, source_target_pairs={{0,320},{32,352},{64,256},{96,288},{128,448},{160,480},{192,384},{... | collective-permute-start | bytes 491528 | tf_op jit(solution)/shard_map/ppermute | solution.py:404
  39.4 1.9 %collective-permute-start.3 = (bf16[2,32,1280]{2,1,0:T(8,128)(2,1)}, bf16[2,32,1280]{2,1,0:T(8,128)(2,1)S(1)}, u32[]{:S(2)}, u32[]{:S(2)}) collective-permute-start(bf16[2,32,1280]{2,1,0:T(8,128)(2,1)} %get-tuple-element.41), channel_id=1, source_target_pairs={{0,64},{32,96},{64,0},{96,32},{128,192},{160,224},{192,128},{224,1... | collective-permute-start | bytes 491528 | tf_op jit(solution)/shard_map/ppermute | solution.py:404
  42.2 2.4 %project.1 = bf16[128,120]{1,0:T(8,128)(2,1)} custom-call(bf16[128,2560]{1,0:T(8,128)(2,1)} %bitcast.14, bf16[80,2560]{1,0:T(8,128)(2,1)} %bitcast.16, bf16[40,2560]{1,0:T(8,128)(2,1)} %bitcast.17), custom_call_target="tpu_custom_call" | custom-call | tf_op jit(solution)/shard_map/project/pallas_call | solution.py:141
  44.6 3.1 %collective-permute-start.4 = (bf16[2,32,1280]{2,1,0:T(8,128)(2,1)S(1)}, bf16[2,32,1280]{2,1,0:T(8,128)(2,1)S(1)}, u32[]{:S(2)}, u32[]{:S(2)}) collective-permute-start(bf16[2,32,1280]{2,1,0:T(8,128)(2,1)S(1)} %copy-done.13), channel_id=1, source_target_pairs={{0,128},{32,160},{64,192},{96,224},{128,0},{160,32},{192,64},{224,... | collective-permute-start | bytes 491528 | tf_op jit(solution)/shard_map/ppermute | solution.py:404
  47.7 4.2 %collective-permute-start.5 = (bf16[2,32,1280]{2,1,0:T(8,128)(2,1)S(1)}, bf16[2,32,1280]{2,1,0:T(8,128)(2,1)S(1)}, u32[]{:S(2)}, u32[]{:S(2)}) collective-permute-start(bf16[2,32,1280]{2,1,0:T(8,128)(2,1)S(1)} %copy-done.12), channel_id=1, source_target_pairs={{0,192},{32,224},{64,128},{96,160},{128,64},{160,96},{192,0},{224,... | collective-permute-start | bytes 491528 | tf_op jit(solution)/shard_map/ppermute | solution.py:404
  52.0 13.3 %all_to_all.15.all_ref = bf16[16,8,120]{2,1,0:T(8,128)(2,1)} all-to-all(bf16[16,8,120]{2,1,0:T(8,128)(2,1)} %bitcast.18), channel_id=1, replica_groups={{0,2,4,6,8,10,12,14,16,18,20,22,24,26,28,30},{1,3,5,7,9,11,13,15,17,19,..., dimensions={0} | all-to-all | bytes 61440 | tf_op jit(solution)/shard_map/all_to_all | solution.py:429
  65.3 1.5 pick.1
  66.8 6.6 %collective-permute-done.5.refs_3_ = bf16[2,32,1280]{2,1,0:T(8,128)(2,1)S(1)} collective-permute-done((bf16[2,32,1280]{2,1,0:T(8,128)(2,1)S(1)}, bf16[2,32,1280]{2,1,0:T(8,128)(2,1)S(1)}, u32[]{:S(2)}, u32[]{:S(2)}) %collective-permute-start.5) | collective-permute-done | bytes 163872 | tf_op jit(solution)/shard_map/ppermute | solution.py:404
  73.4 4.4 %all-to-all-start.2 = ((bf16[4,4,1920]{2,1,0:T(4,128)(2,1)}), bf16[4,4,1920]{2,1,0:T(4,128)(2,1)S(1)}, u32[]{:S(2)}, u32[]{:S(2)}) async-start(bf16[4,4,1920]{2,1,0:T(4,128)(2,1)} %pick.1), calls=%async_computation.2 | async-start | bytes 122880 | tf_op jit(solution)/shard_map/all_to_all | solution.py:434
  77.8 10.7 %collective-permute-start.7 = (bf16[2,32,1280]{2,1,0:T(8,128)(2,1)S(1)}, bf16[2,32,1280]{2,1,0:T(8,128)(2,1)S(1)}, u32[]{:S(2)}, u32[]{:S(2)}) collective-permute-start(bf16[2,32,1280]{2,1,0:T(8,128)(2,1)S(1)} %copy-done.11), channel_id=1, source_target_pairs={{0,384},{32,416},{64,448},{96,480},{128,256},{160,288},{192,320},{... | collective-permute-start | bytes 491528 | tf_op jit(solution)/shard_map/ppermute | solution.py:404
  89.6 29.4 %all_gather.6.rows_ref = bf16[32,4,1920]{2,1,0:T(4,128)(2,1)} all-gather(bf16[4,4,1920]{2,1,0:T(4,128)(2,1)S(1)} %all-to-all-done.2), channel_id=1, replica_groups={{0,32,64,96,128,160,192,224},{256,288,320,352,384,416,448,480},{1,33,65..., dimensions={0}, use_global_device_ids=true | all-gather | bytes 552960 | tf_op jit(solution)/shard_map/all_gather | solution.py:437
  119.0 3.9 %attend.1 = bf16[8,2816]{1,0:T(8,128)(2,1)} custom-call(s32[1]{0:T(128)} %bitcast.12.count_ref, s32[8]{0:T(128)} %bitcast.20, bf16[256,1280]{1,0:T(8,128)(2,1)} %get-tuple-element.51.kept_ref, bf16[32,4,1920]{2,1,0:T(4,128)(2,1)} %all_gather.6.rows_ref), custom_call_target="tpu_custom_call" | custom-call | tf_op jit(solution)/shard_map/attend/pallas_call | solution.py:251
  122.8 1.9 %collective-permute-start.8 = (bf16[8,2816]{1,0:T(8,128)(2,1)}, bf16[8,2816]{1,0:T(8,128)(2,1)S(1)}, u32[]{:S(2)}, u32[]{:S(2)}) collective-permute-start(bf16[8,2816]{1,0:T(8,128)(2,1)} %attend.1), channel_id=1, source_target_pairs={{0,256},{32,288},{64,320},{96,352},{128,384},{160,416},{192,448},{... | collective-permute-start | bytes 135176 | tf_op jit(solution)/shard_map/ppermute | solution.py:439
  124.7 2.4 %own_part.1.own_ref = f32[64,768]{1,0:T(8,128)} custom-call(bf16[32,4,1920]{2,1,0:T(4,128)(2,1)} %all_gather.6.rows_ref), custom_call_target="tpu_custom_call" | custom-call | tf_op jit(solution)/shard_map/own_part/pallas_call | solution.py:310
  127.2 6.8 %collective-permute-start.6 = (bf16[2,32,1280]{2,1,0:T(8,128)(2,1)S(1)}, bf16[2,32,1280]{2,1,0:T(8,128)(2,1)S(1)}, u32[]{:S(2)}, u32[]{:S(2)}) collective-permute-start(bf16[2,32,1280]{2,1,0:T(8,128)(2,1)S(1)} %copy-done.10), channel_id=1, source_target_pairs={{0,448},{32,480},{64,384},{96,416},{128,320},{160,352},{192,256},{... | collective-permute-start | bytes 491528 | tf_op jit(solution)/shard_map/ppermute | solution.py:404
  134.9 21.1 %all_gather.7.part_ref = bf16[128,2816]{1,0:T(8,128)(2,1)S(1)} all-gather(bf16[16,2816]{1,0:T(8,128)(2,1)S(1)} %pad_maximum_fusion), channel_id=1, replica_groups={{0,32,64,96,128,160,192,224},{256,288,320,352,384,416,448,480},{1,33,65..., dimensions={0}, use_global_device_ids=true | all-gather | bytes 811008 | tf_op jit(solution)/shard_map/all_gather | solution.py:443
  156.7 2.3 %pack.1 = bf16[8,32,1280]{2,1,0:T(8,128)(2,1)} custom-call(bf16[2,32,1280]{2,1,0:T(8,128)(2,1)} %get-tuple-element.58.refs_0_, bf16[2,32,1280]{2,1,0:T(8,128)(2,1)} %copy-done.4, bf16[2,32,1280]{2,1,0:T(8,128)(2,1)} %copy-done.5, bf16[2,32,1280]{2,1,0:T(8,128)(2,1)} %copy-done.6, bf16[2,32,1280]{2,1,0:T(8,128)(2,1)} %copy-done.2, ...), custom_call_target="tpu_custom_call" | custom-call | tf_op jit(solution)/shard_map/pack/pallas_call | solution.py:105
  158.9 2.1 %collective-permute-start.9 = (bf16[8,32,1280]{2,1,0:T(8,128)(2,1)}, bf16[8,32,1280]{2,1,0:T(8,128)(2,1)S(1)}, u32[]{:S(2)}, u32[]{:S(2)}) collective-permute-start(bf16[8,32,1280]{2,1,0:T(8,128)(2,1)} %pack.1), channel_id=1, source_target_pairs={{0,32},{32,0},{64,96},{96,64},{128,160},{160,128},{192,224},{224,1... | collective-permute-start | bytes 1966088 | tf_op jit(solution)/shard_map/ppermute | solution.py:451
  161.0 2.7 %combine.1 = bf16[64,2560]{1,0:T(8,128)(2,1)} custom-call(bf16[128,2816]{1,0:T(8,128)(2,1)S(1)} %all_gather.7.part_ref, f32[64,768]{1,0:T(8,128)S(1)} %copy-done), custom_call_target="tpu_custom_call" | custom-call | tf_op jit(solution)/shard_map/combine/pallas_call | solution.py:368
  164.6 2.8 %place_pages.1 = bf16[16,32,1280]{2,1,0:T(8,128)(2,1)} custom-call(bf16[2,32,1280]{2,1,0:T(8,128)(2,1)} %get-tuple-element.58.refs_0_, bf16[2,32,1280]{2,1,0:T(8,128)(2,1)} %copy-done.4, bf16[2,32,1280]{2,1,0:T(8,128)(2,1)} %copy-done.5, bf16[2,32,1280]{2,1,0:T(8,128)(2,1)} %copy-done.6, bf16[2,32,1280]{2,1,0:T(8,128)(2,1)} %copy-done.2, ...), custom_call_target="tpu_custom_call" | custom-call | tf_op jit(solution)/shard_map/place_pages/pallas_call | solution.py:123
  (45 shorter events, 7.1 us)
Async XLA Ops:
  2.4 19.4 %collective-permute-start = (bf16[4,2560]{1,0:T(4,128)(2,1)S(1)}, bf16[4,2560]{1,0:T(4,128)(2,1)S(1)}, u32[]{:S(2)}, u32[]{:S(2)}) collective-permute-start(bf16[4,2560]{1,0:T(4,128)(2,1)S(1)} %fusion.2), channel_id=1, source_target_pairs={{0,257},{1,256},{2,259},{3,258},{4,261},{5,260},{6,263},{7,262},{8... | collective-permute-start | bytes 61448 | tf_op jit(solution)/shard_map/ppermute | solution.py:398
  21.8 22.8 %copy-start.13 = (bf16[2,32,1280]{2,1,0:T(8,128)(2,1)S(1)}, bf16[2,32,1280]{2,1,0:T(8,128)(2,1)}, u32[]{:S(2)}) copy-start(bf16[2,32,1280]{2,1,0:T(8,128)(2,1)} %get-tuple-element.45) | copy-start | bytes 491524
  21.8 25.9 %copy-start.12 = (bf16[2,32,1280]{2,1,0:T(8,128)(2,1)S(1)}, bf16[2,32,1280]{2,1,0:T(8,128)(2,1)}, u32[]{:S(2)}) copy-start(bf16[2,32,1280]{2,1,0:T(8,128)(2,1)} %get-tuple-element.46) | copy-start | bytes 491524
  21.8 55.9 %copy-start.11 = (bf16[2,32,1280]{2,1,0:T(8,128)(2,1)S(1)}, bf16[2,32,1280]{2,1,0:T(8,128)(2,1)}, u32[]{:S(2)}) copy-start(bf16[2,32,1280]{2,1,0:T(8,128)(2,1)} %get-tuple-element.52) | copy-start | bytes 491524
  22.8 104.4 %copy-start.10 = (bf16[2,32,1280]{2,1,0:T(8,128)(2,1)S(1)}, bf16[2,32,1280]{2,1,0:T(8,128)(2,1)}, u32[]{:S(2)}) copy-start(bf16[2,32,1280]{2,1,0:T(8,128)(2,1)} %get-tuple-element.50) | copy-start | bytes 491524
  22.8 18.5 %all-to-all-start = ((bf16[16,8,2560]{2,1,0:T(8,128)(2,1)}), bf16[16,8,2560]{2,1,0:T(8,128)(2,1)S(1)}, u32[]{:S(2)}, u32[]{:S(2)}) async-start(bf16[16,8,2560]{2,1,0:T(8,128)(2,1)} %broadcast_in_dim.4), calls=%async_computation | async-start | bytes 1310720 | tf_op jit(solution)/shard_map/all_to_all | solution.py:419
  29.7 37.0 %collective-permute-start.1 = (bf16[2,32,1280]{2,1,0:T(8,128)(2,1)}, bf16[2,32,1280]{2,1,0:T(8,128)(2,1)S(1)}, u32[]{:S(2)}, u32[]{:S(2)}) collective-permute-start(bf16[2,32,1280]{2,1,0:T(8,128)(2,1)} %get-tuple-element.39), channel_id=1, source_target_pairs={{0,256},{32,288},{64,320},{96,352},{128,384},{160,416},{192,448},{... | collective-permute-start | bytes 491528 | tf_op jit(solution)/shard_map/ppermute | solution.py:404
  34.9 31.8 %collective-permute-start.2 = (bf16[2,32,1280]{2,1,0:T(8,128)(2,1)}, bf16[2,32,1280]{2,1,0:T(8,128)(2,1)S(1)}, u32[]{:S(2)}, u32[]{:S(2)}) collective-permute-start(bf16[2,32,1280]{2,1,0:T(8,128)(2,1)} %get-tuple-element.40), channel_id=1, source_target_pairs={{0,320},{32,352},{64,256},{96,288},{128,448},{160,480},{192,384},{... | collective-permute-start | bytes 491528 | tf_op jit(solution)/shard_map/ppermute | solution.py:404
  39.4 27.3 %collective-permute-start.3 = (bf16[2,32,1280]{2,1,0:T(8,128)(2,1)}, bf16[2,32,1280]{2,1,0:T(8,128)(2,1)S(1)}, u32[]{:S(2)}, u32[]{:S(2)}) collective-permute-start(bf16[2,32,1280]{2,1,0:T(8,128)(2,1)} %get-tuple-element.41), channel_id=1, source_target_pairs={{0,64},{32,96},{64,0},{96,32},{128,192},{160,224},{192,128},{224,1... | collective-permute-start | bytes 491528 | tf_op jit(solution)/shard_map/ppermute | solution.py:404
  41.4 0.9 copy-start.1
  44.6 22.2 %collective-permute-start.4 = (bf16[2,32,1280]{2,1,0:T(8,128)(2,1)S(1)}, bf16[2,32,1280]{2,1,0:T(8,128)(2,1)S(1)}, u32[]{:S(2)}, u32[]{:S(2)}) collective-permute-start(bf16[2,32,1280]{2,1,0:T(8,128)(2,1)S(1)} %copy-done.13), channel_id=1, source_target_pairs={{0,128},{32,160},{64,192},{96,224},{128,0},{160,32},{192,64},{224,... | collective-permute-start | bytes 491528 | tf_op jit(solution)/shard_map/ppermute | solution.py:404
  47.7 25.6 %collective-permute-start.5 = (bf16[2,32,1280]{2,1,0:T(8,128)(2,1)S(1)}, bf16[2,32,1280]{2,1,0:T(8,128)(2,1)S(1)}, u32[]{:S(2)}, u32[]{:S(2)}) collective-permute-start(bf16[2,32,1280]{2,1,0:T(8,128)(2,1)S(1)} %copy-done.12), channel_id=1, source_target_pairs={{0,192},{32,224},{64,128},{96,160},{128,64},{160,96},{192,0},{224,... | collective-permute-start | bytes 491528 | tf_op jit(solution)/shard_map/ppermute | solution.py:404
  66.7 89.2 %copy-start.2 = (bf16[2,32,1280]{2,1,0:T(8,128)(2,1)}, bf16[2,32,1280]{2,1,0:T(8,128)(2,1)S(1)}, u32[]{:S(2)}) copy-start(bf16[2,32,1280]{2,1,0:T(8,128)(2,1)S(1)} %collective-permute-done.1.refs_4_) | copy-start | bytes 491524
  66.7 89.2 %copy-start.3 = (bf16[2,32,1280]{2,1,0:T(8,128)(2,1)}, bf16[2,32,1280]{2,1,0:T(8,128)(2,1)S(1)}, u32[]{:S(2)}) copy-start(bf16[2,32,1280]{2,1,0:T(8,128)(2,1)S(1)} %collective-permute-done.2.refs_5_) | copy-start | bytes 491524
  66.8 89.2 %copy-start.4 = (bf16[2,32,1280]{2,1,0:T(8,128)(2,1)}, bf16[2,32,1280]{2,1,0:T(8,128)(2,1)S(1)}, u32[]{:S(2)}) copy-start(bf16[2,32,1280]{2,1,0:T(8,128)(2,1)S(1)} %collective-permute-done.3.refs_1_) | copy-start | bytes 491524
  66.8 89.2 %copy-start.5 = (bf16[2,32,1280]{2,1,0:T(8,128)(2,1)}, bf16[2,32,1280]{2,1,0:T(8,128)(2,1)S(1)}, u32[]{:S(2)}) copy-start(bf16[2,32,1280]{2,1,0:T(8,128)(2,1)S(1)} %collective-permute-done.4.refs_2_) | copy-start | bytes 491524
  73.4 82.7 %copy-start.6 = (bf16[2,32,1280]{2,1,0:T(8,128)(2,1)}, bf16[2,32,1280]{2,1,0:T(8,128)(2,1)S(1)}, u32[]{:S(2)}) copy-start(bf16[2,32,1280]{2,1,0:T(8,128)(2,1)S(1)} %collective-permute-done.5.refs_3_) | copy-start | bytes 491524
  73.4 16.2 %all-to-all-start.2 = ((bf16[4,4,1920]{2,1,0:T(4,128)(2,1)}), bf16[4,4,1920]{2,1,0:T(4,128)(2,1)S(1)}, u32[]{:S(2)}, u32[]{:S(2)}) async-start(bf16[4,4,1920]{2,1,0:T(4,128)(2,1)} %pick.1), calls=%async_computation.2 | async-start | bytes 122880 | tf_op jit(solution)/shard_map/all_to_all | solution.py:434
  77.8 56.3 %collective-permute-start.7 = (bf16[2,32,1280]{2,1,0:T(8,128)(2,1)S(1)}, bf16[2,32,1280]{2,1,0:T(8,128)(2,1)S(1)}, u32[]{:S(2)}, u32[]{:S(2)}) collective-permute-start(bf16[2,32,1280]{2,1,0:T(8,128)(2,1)S(1)} %copy-done.11), channel_id=1, source_target_pairs={{0,384},{32,416},{64,448},{96,480},{128,256},{160,288},{192,320},{... | collective-permute-start | bytes 491528 | tf_op jit(solution)/shard_map/ppermute | solution.py:404
  122.8 11.2 %collective-permute-start.8 = (bf16[8,2816]{1,0:T(8,128)(2,1)}, bf16[8,2816]{1,0:T(8,128)(2,1)S(1)}, u32[]{:S(2)}, u32[]{:S(2)}) collective-permute-start(bf16[8,2816]{1,0:T(8,128)(2,1)} %attend.1), channel_id=1, source_target_pairs={{0,256},{32,288},{64,320},{96,352},{128,384},{160,416},{192,448},{... | collective-permute-start | bytes 135176 | tf_op jit(solution)/shard_map/ppermute | solution.py:439
  127.2 33.8 %copy-start = (f32[64,768]{1,0:T(8,128)S(1)}, f32[64,768]{1,0:T(8,128)}, u32[]{:S(2)}) copy-start(f32[64,768]{1,0:T(8,128)} %own_part.1.own_ref) | copy-start | bytes 589828
  127.2 28.8 %collective-permute-start.6 = (bf16[2,32,1280]{2,1,0:T(8,128)(2,1)S(1)}, bf16[2,32,1280]{2,1,0:T(8,128)(2,1)S(1)}, u32[]{:S(2)}, u32[]{:S(2)}) collective-permute-start(bf16[2,32,1280]{2,1,0:T(8,128)(2,1)S(1)} %copy-done.10), channel_id=1, source_target_pairs={{0,448},{32,480},{64,384},{96,416},{128,320},{160,352},{192,256},{... | collective-permute-start | bytes 491528 | tf_op jit(solution)/shard_map/ppermute | solution.py:404
  134.0 22.0 %copy-start.7 = (bf16[2,32,1280]{2,1,0:T(8,128)(2,1)}, bf16[2,32,1280]{2,1,0:T(8,128)(2,1)S(1)}, u32[]{:S(2)}) copy-start(bf16[2,32,1280]{2,1,0:T(8,128)(2,1)S(1)} %collective-permute-done.7.refs_6_) | copy-start | bytes 491524
  158.9 4.8 %collective-permute-start.9 = (bf16[8,32,1280]{2,1,0:T(8,128)(2,1)}, bf16[8,32,1280]{2,1,0:T(8,128)(2,1)S(1)}, u32[]{:S(2)}, u32[]{:S(2)}) collective-permute-start(bf16[8,32,1280]{2,1,0:T(8,128)(2,1)} %pack.1), channel_id=1, source_target_pairs={{0,32},{32,0},{64,96},{96,64},{128,160},{160,128},{192,224},{224,1... | collective-permute-start | bytes 1966088 | tf_op jit(solution)/shard_map/ppermute | solution.py:451
  (2 other events, 1.5 us)

commit v11 on v9

--- a/solution.py
+++ b/solution.py
@@ -26,17 +26,13 @@
     (p * 2 * PLANE + t, (p ^ 8) * 2 * PLANE + (t ^ 1)) for p in range(HOLDERS) for t in range(2 * PLANE)
 ]
 
-FOUR_GROUPS = [
-    [
-        (2 * (4 * quad + z) + core) * 2 * PLANE + 2 * xy + half
-        for half in range(2)
-        for quad in range(2)
-    ]
+COLUMN_GROUPS = [
+    [(2 * z + core) * 2 * PLANE + 2 * xy + half for half in range(2) for z in range(CHIPS)]
     for xy in range(PLANE)
-    for z in range(CHIPS // 2)
     for core in range(2)
 ]
 QUAD_GROUPS = [[CHIPS * quad + i for i in range(CHIPS)] for quad in range(2)]
+OTHER_CORE = [(i, i ^ 1) for i in range(HOLDERS)]
 OTHER_QUAD = [(i, i ^ CHIPS) for i in range(HOLDERS)]
 HALF_COLUMNS = (QUERIES + 2 * KEYS) // 2
 STEP = 4
@@ -120,14 +116,14 @@
     share = out_ref.shape[1]
     for h in range(2):
         piece = rows_ref[h * share : (h + 1) * share].astype(jnp.bfloat16)
-        for quad in range(2):
-            out_ref[2 * h + quad] = piece
+        for z in range(CHIPS):
+            out_ref[h * CHIPS + z] = piece
 
 
 def pick(plane, everyone):
     count, rows, width = everyone.shape
     both = rows // PLANE
-    piece = jax.ShapeDtypeStruct((4, both // 2, HALF_COLUMNS), everyone.dtype)
+    piece = jax.ShapeDtypeStruct((2 * CHIPS, both // 2, HALF_COLUMNS), everyone.dtype)
     return pl.pallas_call(
         pick_kernel,
         out_shape=piece,
@@ -142,11 +138,12 @@
     )(plane, everyone)
 
 
-def held(rows_ref, holder, half, columns):
-    quad, inside = holder // CHIPS, holder % CHIPS
-    same = lax.axis_index("tensor") % 2 == half
-    spot = inside * 4 + 2 * half + jnp.where(same, quad, 1 - quad)
-    return rows_ref[spot, :, columns].astype(jnp.float32)
+def held(near_ref, far_ref, holder, half, columns):
+    chip = holder // 2
+    spot = half * CHIPS + jnp.where(lax.axis_index("tensor") % 2 == half, chip, chip ^ 4)
+    near = near_ref[spot, :, columns].astype(jnp.float32)
+    far = far_ref[spot, :, columns].astype(jnp.float32)
+    return jnp.where(lax.axis_index("page") % 2 == holder % 2, near, far)
 
 
 def pieces(value, count):
@@ -159,10 +156,10 @@
 
 
 def attend_kernel(
-    count_ref, owner_ref, kept_ref, rows_ref, out_ref, sum_ref, peak_ref, total_ref
+    count_ref, owner_ref, kept_ref, near_ref, far_ref, out_ref, sum_ref, peak_ref, total_ref
 ):
     scale = HEAD_DIM ** (-0.5)
-    share = rows_ref.shape[1]
+    share = near_ref.shape[1]
     line = lax.broadcasted_iota(jnp.int32, (share, QUERIES // 2), 0)
     head = lax.broadcasted_iota(jnp.int32, (KV_HEADS, KEYS), 0) * HEAD_DIM
     lane = lax.broadcasted_iota(jnp.int32, (KV_HEADS, KEYS), 1)
@@ -172,7 +169,7 @@
         holder = request // share
         query = []
         for half in range(2):
-            block = held(rows_ref, holder, half, pl.ds(0, QUERIES // 2))
+            block = held(near_ref, far_ref, holder, half, pl.ds(0, QUERIES // 2))
             query.append(
                 jnp.sum(jnp.where(line == request % share, block, 0.0), axis=0, keepdims=True)
             )
@@ -215,11 +212,11 @@
     out_ref[:, QUERIES:] = columns
 
 
-def attend(page_count, page_owner, kept, rows):
+def attend(page_count, page_owner, kept, near, far):
     return pl.pallas_call(
         attend_kernel,
         out_shape=jax.ShapeDtypeStruct((SOURCES, QUERIES + EXTRA), jnp.bfloat16),
-        in_specs=[SMEM] * 2 + [VMEM] * 2,
+        in_specs=[SMEM] * 2 + [VMEM] * 3,
         out_specs=VMEM,
         scratch_shapes=[
             pltpu.VMEM((SOURCES, QUERIES), jnp.float32),
@@ -227,7 +224,7 @@
             pltpu.VMEM((SOURCES, HEADS), jnp.float32),
         ],
         name="attend",
-    )(page_count, page_owner, kept, rows)
+    )(page_count, page_owner, kept, near, far)
 
 
 def spread_dot(value, chosen, contract, count, chosen_first=False):
@@ -247,14 +244,14 @@
     return ((lane >= head) & (lane < head + HEAD_DIM)).astype(jnp.float32).astype(jnp.bfloat16)
 
 
-def own_kernel(rows_ref, own_ref, query_ref, pair_ref):
+def own_kernel(near_ref, far_ref, own_ref, query_ref, pair_ref):
     scale = HEAD_DIM ** (-0.5)
-    share = rows_ref.shape[1]
+    share = near_ref.shape[1]
     piece = HEAD_DIM // 2
     for holder in range(HOLDERS):
         rows = slice(holder * share, (holder + 1) * share)
         for half in range(2):
-            block = held(rows_ref, holder, half, pl.ds(0, HALF_COLUMNS))
+            block = held(near_ref, far_ref, holder, half, pl.ds(0, HALF_COLUMNS))
             for k in range(2):
                 at = (2 * k + half) * KEYS
                 query_ref[rows, at : at + KEYS] = block[:, k * KEYS : (k + 1) * KEYS]
@@ -273,19 +270,19 @@
     )
 
 
-def own_part(rows):
-    requests = HOLDERS * rows.shape[1]
+def own_part(near, far):
+    requests = HOLDERS * near.shape[1]
     return pl.pallas_call(
         own_kernel,
         out_shape=jax.ShapeDtypeStruct((requests, KEYS + 4 * HEADS), jnp.float32),
-        in_specs=[VMEM],
+        in_specs=[VMEM, VMEM],
         out_specs=VMEM,
         scratch_shapes=[
             pltpu.VMEM((requests, QUERIES), jnp.float32),
             pltpu.VMEM((2, requests, KEYS), jnp.float32),
         ],
         name="own_part",
-    )(rows)
+    )(near, far)
 
 
 def combine_kernel(part_ref, own_ref, out_ref):
@@ -343,48 +340,27 @@
     )(parts, own)
 
 
-def normalise_kernel(holder_ref, tokens_ref, gain_ref, out_ref, rows_ref):
-    share = out_ref.shape[0]
-    widened = tokens_ref[...].astype(jnp.float32)
-    mean = jnp.mean(widened * widened, axis=-1, keepdims=True)
-    normed = widened * lax.rsqrt(mean + EPSILON) * gain_ref[...]
-    for i in range(rows_ref.shape[0]):
-        rows_ref[i] = normed[i * share : (i + 1) * share]
-    out_ref[...] = rows_ref[holder_ref[0] % rows_ref.shape[0]].astype(jnp.bfloat16)
-
-
-def normalise(holder, tokens, norm_gain):
-    requests, width = tokens.shape
-    share = requests // HOLDERS
-    shares = 4
-    return pl.pallas_call(
-        normalise_kernel,
-        out_shape=jax.ShapeDtypeStruct((share, width), jnp.bfloat16),
-        grid_spec=pltpu.PrefetchScalarGridSpec(
-            num_scalar_prefetch=1,
-            grid=(1,),
-            in_specs=[
-                pl.BlockSpec((shares * share, width), lambda i, holder: (holder[0] // shares, 0)),
-                pl.BlockSpec((1, width), lambda i, *_: (0, 0)),
-            ],
-            out_specs=pl.BlockSpec((share, width), lambda i, *_: (0, 0)),
-            scratch_shapes=[pltpu.VMEM((shares, share, width), jnp.float32)],
-        ),
-        name="normalise",
-    )(holder.reshape(1), tokens, norm_gain.reshape(1, width))
-
-
 def per_device(
     tokens, norm_gain, w_query, w_keyvalue, cache, page_count, page_owner, keep_rows, dest_slot
 ):
     holder = lax.axis_index("page")
     group = lax.axis_index("tensor")
     half = group % 2
+    share = tokens.shape[0] // HOLDERS
+
+    def normalise(rows):
+        widened = rows.astype(jnp.float32)
+        return (
+            widened
+            * lax.rsqrt(jnp.mean(widened * widened, axis=-1, keepdims=True) + EPSILON)
+            * norm_gain
+        ).astype(jnp.bfloat16)
+
     page_count = page_count.reshape(1)
     page_owner = page_owner.reshape(SOURCES)
     compact, kept = select_rows(page_count, dest_slot.reshape(SOURCES), keep_rows, cache)
 
-    mine = normalise(holder, tokens, norm_gain)
+    mine = normalise(lax.dynamic_slice_in_dim(tokens, holder * share, share, 0))
     across = lax.ppermute(mine, ("page", "tensor"), OTHER_HALF)
     across, compact = lax.optimization_barrier((across, compact))
     arrived = lax.all_to_all(compact, "page", 0, 0, tiled=True)
@@ -403,13 +379,13 @@
     )
     halves = pick((group // 2).reshape(1), everyone)
     halves, arrived = lax.optimization_barrier((halves, arrived))
-    quarter = lax.all_to_all(
-        halves, ("page", "tensor"), 0, 0, axis_index_groups=FOUR_GROUPS, tiled=True
-    )
-    rows = lax.all_gather(quarter, "page", axis=0, axis_index_groups=QUAD_GROUPS, tiled=True)
-    part = attend(page_count, page_owner, kept, rows)
+    near = lax.all_to_all(
+        halves, ("page", "tensor"), 0, 0, axis_index_groups=COLUMN_GROUPS, tiled=True
+    )
+    far = lax.ppermute(near, "page", OTHER_CORE)
+    part = attend(page_count, page_owner, kept, near, far)
+    own = own_part(near, far)
     far = lax.ppermute(part, "page", OTHER_QUAD)
-    own = own_part(rows)
     far, own = lax.optimization_barrier((far, own))
     parts = lax.all_gather(
         jnp.concatenate([part, far], axis=0),

time: 163 us -> 154 us (0.945)
  blocking collectives: 99.8 us -> 86.9 us
  starting transfers between devices: 22.4 us -> 32.5 us
  waiting for transfers between devices: 14.6 us -> 8.64 us
  other arithmetic: 0.84 us -> 2.65 us
    all_gather x1 -> x0, blocking collectives: 17.5 us -> none  [per_device(): lax.all_gather(quarter, 'page', axis=0, axis_index_groups=QUAD_GROUPS, ti...]
    ppermute x1, waiting for transfers between devices: 8.05 us -> 1.04 us  [per_device(): far = lax.ppermute(part, 'page', OTHER_QUAD)]
    ppermute x0 -> x1, starting transfers between devices: none -> 6.68 us  [per_device(): far = lax.ppermute(near, 'page', OTHER_CORE)]
    ppermute x1, starting transfers between devices: 1.91 us -> 5.38 us  [per_device(): far = lax.ppermute(part, 'page', OTHER_QUAD)]
    all_to_all x1, blocking collectives: 23.4 us -> 25.7 us  [per_device(): lax.all_to_all(halves, ('page', 'tensor'), 0, 0, axis_index_groups=COLUMN...]
    all_gather x1, blocking collectives: 15.8 us -> 18.1 us  [per_device(): lax.all_gather(jnp.concatenate([part, far], axis=0), 'page', axis=0, axis...]
    pallas_call x1 -> x0, Pallas kernels: 1.65 us -> none  [normalise(): pl.pallas_call(normalise_kernel, out_shape=jax.ShapeDtypeStruct((share, w...]
  transfers between devices with their start and end apart: 3 -> 4, of which waited for: 2 -> 3; matrix products, arithmetic and copies ran while one was open for 0% -> 0% of each run, Pallas kernels for 7% -> 8%
where the time goes in v11:
time: 154 us; the launch traced here: 153 us
  blocking collectives  86.9 us (56%)
  starting transfers between devices  32.5 us (21%)
  Pallas kernels  18.2 us (12%)
  waiting for transfers between devices  8.64 us (6%)
  local copies, waits for them, and re-layouts  2.68 us (2%)
  other arithmetic  2.65 us (2%)
    all_to_all x1, blocking collectives, per_device(): lax.all_to_all(halves, ('page', 'tensor'), 0, 0, axis_index_groups=COLUMN...  25.7 us
    all_gather x1, blocking collectives, per_device(): lax.all_gather(both, 'tensor', axis=0, axis_index_groups=PLANE_GROUPS, ti...  22.1 us
    all_gather x1, blocking collectives, per_device(): lax.all_gather(projected, 'tensor', axis=0, axis_index_groups=PLANE_GROUP...  20.9 us
    all_gather x1, blocking collectives, per_device(): lax.all_gather(jnp.concatenate([part, far], axis=0), 'page', axis=0, axis...  18.1 us
    ppermute x1, starting transfers between devices, per_device(): across = lax.ppermute(mine, ('page', 'tensor'), OTHER_HALF)  13.3 us
    all_to_all x1, starting transfers between devices, per_device(): arrived = lax.all_to_all(compact, 'page', 0, 0, tiled=True)  7.16 us
    ppermute x1, starting transfers between devices, per_device(): far = lax.ppermute(near, 'page', OTHER_CORE)  6.68 us
    all_to_all x1, waiting for transfers between devices, per_device(): arrived = lax.all_to_all(compact, 'page', 0, 0, tiled=True)  6.48 us
  transfers between devices with their start and end apart: 4, of which 3 were waited for; matrix products, arithmetic and copies ran while one was open for 0% of the time, Pallas kernels for 8%

profile of v11, /device:TPU:1, one launch (start us, length us, event | category | flops | bytes accessed | tf_op | source)
XLA Modules:
  0.0 152.9 jit_solution(17325865205593100367)
XLA Ops:
  0.6 0.9 fusion
  1.6 0.9 fusion.2
  2.4 13.3 %collective-permute-start = (bf16[4,2560]{1,0:T(4,128)(2,1)S(1)}, bf16[4,2560]{1,0:T(4,128)(2,1)S(1)}, u32[]{:S(2)}, u32[]{:S(2)}) collective-permute-start(bf16[4,2560]{1,0:T(4,128)(2,1)S(1)} %fusion.2), channel_id=1, source_target_pairs={{0,257},{1,256},{2,259},{3,258},{4,261},{5,260},{6,263},{7,262},{8... | collective-permute-start | bytes 61448 | tf_op jit(solution)/shard_map/ppermute | solution.py:364
  16.4 5.2 %select_rows.1 = (bf16[16,32,1280]{2,1,0:T(8,128)(2,1)}, bf16[256,1280]{1,0:T(8,128)(2,1)}) custom-call(s32[1]{0:T(128)} %bitcast.11.count_ref, s32[8]{0:T(128)} %bitcast.18, s32[8,1,32]{2,1,0:T(1,128)} %keep_ref.1, bf16[8,128,1280]{2,1,0:T(8,128)(2,1)} %bitcast.14), custom_call_target="tpu_custom_call" | custom-call | tf_op jit(solution)/shard_map/select_rows/pallas_call | solution.py:68
  21.6 0.0 collective-permute-done
  21.6 7.2 %all-to-all-start = ((bf16[16,32,1280]{2,1,0:T(8,128)(2,1)}), bf16[16,32,1280]{2,1,0:T(8,128)(2,1)S(1)}, u32[]{:S(2)}, u32[]{:S(2)}) async-start(bf16[16,32,1280]{2,1,0:T(8,128)(2,1)} %get-tuple-element.13), calls=%async_computation | async-start | bytes 2621440 | tf_op jit(solution)/shard_map/all_to_all | solution.py:366
  28.8 22.1 %all_gather.12.rows_ref = bf16[128,2560]{1,0:T(8,128)(2,1)} all-gather(bf16[8,2560]{1,0:T(8,128)(2,1)S(1)} %maximum_select_fusion), channel_id=1, replica_groups={{0,2,4,6,8,10,12,14,16,18,20,22,24,26,28,30},{1,3,5,7,9,11,13,15,17,19,..., dimensions={0}, use_global_device_ids=true | all-gather | bytes 696320 | tf_op jit(solution)/shard_map/all_gather | solution.py:373
  50.9 2.4 %project.1 = bf16[128,120]{1,0:T(8,128)(2,1)} custom-call(bf16[128,2560]{1,0:T(8,128)(2,1)} %all_gather.12.rows_ref, bf16[80,2560]{1,0:T(8,128)(2,1)} %bitcast.16, bf16[40,2560]{1,0:T(8,128)(2,1)} %bitcast.17), custom_call_target="tpu_custom_call" | custom-call | tf_op jit(solution)/shard_map/project/pallas_call | solution.py:99
  53.4 20.9 %all-gather = bf16[2048,120]{1,0:T(8,128)(2,1)} all-gather(bf16[128,120]{1,0:T(8,128)(2,1)} %project.1), channel_id=2, replica_groups={{0,2,4,6,8,10,12,14,16,18,20,22,24,26,28,30},{1,3,5,7,9,11,13,15,17,19,..., dimensions={0}, use_global_device_ids=true | all-gather | bytes 522240 | tf_op jit(solution)/shard_map/all_gather | solution.py:377
  74.3 1.6 %pick.1 = bf16[16,4,1920]{2,1,0:T(4,128)(2,1)} custom-call(s32[1]{0:T(128)} %bitcast.4.plane_ref, bf16[16,128,120]{2,1,0:T(8,128)(2,1)} %bitcast.15), custom_call_target="tpu_custom_call" | custom-call | tf_op jit(solution)/shard_map/pick/pallas_call | solution.py:127
  75.8 6.5 %all-to-all-done = bf16[16,32,1280]{2,1,0:T(8,128)(2,1)S(1)} async-done(((bf16[16,32,1280]{2,1,0:T(8,128)(2,1)}), bf16[16,32,1280]{2,1,0:T(8,128)(2,1)S(1)}, u32[]{:S(2)}, u32[]{:S(2)}) %all-to-all-start) | async-done | bytes 1310752 | tf_op jit(solution)/shard_map/all_to_all | solution.py:366
  82.3 25.7 %all_to_all.10.near_ref = bf16[16,4,1920]{2,1,0:T(4,128)(2,1)S(1)} all-to-all(bf16[16,4,1920]{2,1,0:T(4,128)(2,1)} %pick.1), channel_id=1, replica_groups={{0,64,128,192,256,320,384,448,1,65,129,193,257,321,385,449},{32,96,160,..., dimensions={0} | all-to-all | bytes 491520 | tf_op jit(solution)/shard_map/all_to_all | solution.py:382
  108.0 6.7 %collective-permute-start.1 = (bf16[16,4,1920]{2,1,0:T(4,128)(2,1)S(1)}, bf16[16,4,1920]{2,1,0:T(4,128)(2,1)S(1)}, u32[]{:S(2)}, u32[]{:S(2)}) collective-permute-start(bf16[16,4,1920]{2,1,0:T(4,128)(2,1)S(1)} %all_to_all.10.near_ref), channel_id=1, source_target_pairs={{0,32},{32,0},{64,96},{96,64},{128,160},{160,128},{192,224},{224,1... | collective-permute-start | bytes 737288 | tf_op jit(solution)/shard_map/ppermute | solution.py:385
  114.7 1.1 collective-permute-done.1.far_ref
  115.8 0.7 copy-done.2
  116.5 3.9 %attend.1 = bf16[8,2816]{1,0:T(8,128)(2,1)} custom-call(s32[1]{0:T(128)} %bitcast.12.count_ref, s32[8]{0:T(128)} %bitcast.19, bf16[256,1280]{1,0:T(8,128)(2,1)} %get-tuple-element.10.kept_ref, bf16[16,4,1920]{2,1,0:T(4,128)(2,1)} %copy-done.1, bf16[16,4,1920]{2,1,0:T(4,128)(2,1)} %copy-done.2), custom_call_target="tpu_custom_call" | custom-call | tf_op jit(solution)/shard_map/attend/pallas_call | solution.py:216
  120.4 5.4 %collective-permute-start.2 = (bf16[8,2816]{1,0:T(8,128)(2,1)}, bf16[8,2816]{1,0:T(8,128)(2,1)S(1)}, u32[]{:S(2)}, u32[]{:S(2)}) collective-permute-start(bf16[8,2816]{1,0:T(8,128)(2,1)} %attend.1), channel_id=1, source_target_pairs={{0,256},{32,288},{64,320},{96,352},{128,384},{160,416},{192,448},{... | collective-permute-start | bytes 135176 | tf_op jit(solution)/shard_map/ppermute | solution.py:388
  125.8 2.5 %own_part.1.own_ref = f32[64,768]{1,0:T(8,128)} custom-call(bf16[16,4,1920]{2,1,0:T(4,128)(2,1)} %copy-done.1, bf16[16,4,1920]{2,1,0:T(4,128)(2,1)} %copy-done.2), custom_call_target="tpu_custom_call" | custom-call | tf_op jit(solution)/shard_map/own_part/pallas_call | solution.py:275
  128.3 1.0 collective-permute-done.2
  129.3 0.8 pad_maximum_fusion
  130.1 18.1 %all_gather.15.part_ref = bf16[128,2816]{1,0:T(8,128)(2,1)S(1)} all-gather(bf16[16,2816]{1,0:T(8,128)(2,1)S(1)} %pad_maximum_fusion), channel_id=1, replica_groups={{0,32,64,96,128,160,192,224},{256,288,320,352,384,416,448,480},{1,33,65..., dimensions={0}, use_global_device_ids=true | all-gather | bytes 811008 | tf_op jit(solution)/shard_map/all_gather | solution.py:390
  148.2 0.9 copy-done
  149.2 2.7 %combine.1 = bf16[64,2560]{1,0:T(8,128)(2,1)} custom-call(bf16[128,2816]{1,0:T(8,128)(2,1)S(1)} %all_gather.15.part_ref, f32[64,768]{1,0:T(8,128)S(1)} %copy-done), custom_call_target="tpu_custom_call" | custom-call | tf_op jit(solution)/shard_map/combine/pallas_call | solution.py:333
  151.8 1.1 copy.14
  (6 shorter events, 0.1 us)
Async XLA Ops:
  2.4 19.2 %collective-permute-start = (bf16[4,2560]{1,0:T(4,128)(2,1)S(1)}, bf16[4,2560]{1,0:T(4,128)(2,1)S(1)}, u32[]{:S(2)}, u32[]{:S(2)}) collective-permute-start(bf16[4,2560]{1,0:T(4,128)(2,1)S(1)} %fusion.2), channel_id=1, source_target_pairs={{0,257},{1,256},{2,259},{3,258},{4,261},{5,260},{6,263},{7,262},{8... | collective-permute-start | bytes 61448 | tf_op jit(solution)/shard_map/ppermute | solution.py:364
  21.6 60.7 %all-to-all-start = ((bf16[16,32,1280]{2,1,0:T(8,128)(2,1)}), bf16[16,32,1280]{2,1,0:T(8,128)(2,1)S(1)}, u32[]{:S(2)}, u32[]{:S(2)}) async-start(bf16[16,32,1280]{2,1,0:T(8,128)(2,1)} %get-tuple-element.13), calls=%async_computation | async-start | bytes 2621440 | tf_op jit(solution)/shard_map/all_to_all | solution.py:366
  108.0 7.8 %copy-start.1 = (bf16[16,4,1920]{2,1,0:T(4,128)(2,1)}, bf16[16,4,1920]{2,1,0:T(4,128)(2,1)S(1)}, u32[]{:S(2)}) copy-start(bf16[16,4,1920]{2,1,0:T(4,128)(2,1)S(1)} %all_to_all.10.near_ref) | copy-start | bytes 737284
  108.0 7.8 %collective-permute-start.1 = (bf16[16,4,1920]{2,1,0:T(4,128)(2,1)S(1)}, bf16[16,4,1920]{2,1,0:T(4,128)(2,1)S(1)}, u32[]{:S(2)}, u32[]{:S(2)}) collective-permute-start(bf16[16,4,1920]{2,1,0:T(4,128)(2,1)S(1)} %all_to_all.10.near_ref), channel_id=1, source_target_pairs={{0,32},{32,0},{64,96},{96,64},{128,160},{160,128},{192,224},{224,1... | collective-permute-start | bytes 737288 | tf_op jit(solution)/shard_map/ppermute | solution.py:385
  115.8 0.7 copy-start.2
  120.4 8.9 %collective-permute-start.2 = (bf16[8,2816]{1,0:T(8,128)(2,1)}, bf16[8,2816]{1,0:T(8,128)(2,1)S(1)}, u32[]{:S(2)}, u32[]{:S(2)}) collective-permute-start(bf16[8,2816]{1,0:T(8,128)(2,1)} %attend.1), channel_id=1, source_target_pairs={{0,256},{32,288},{64,320},{96,352},{128,384},{160,416},{192,448},{... | collective-permute-start | bytes 135176 | tf_op jit(solution)/shard_map/ppermute | solution.py:388
  148.2 0.9 copy-start

commit v12 on v11

--- a/solution.py
+++ b/solution.py
@@ -35,7 +35,7 @@
 OTHER_CORE = [(i, i ^ 1) for i in range(HOLDERS)]
 OTHER_QUAD = [(i, i ^ CHIPS) for i in range(HOLDERS)]
 HALF_COLUMNS = (QUERIES + 2 * KEYS) // 2
-STEP = 4
+STEP = 8
 
 VMEM = pl.BlockSpec(memory_space=pltpu.VMEM)
 SMEM = pl.BlockSpec(memory_space=pltpu.SMEM)
@@ -51,10 +51,12 @@
     rows = page_ref.shape[1]
     for i in range(STEP):
         slot = step * STEP + i
-        picks = jnp.broadcast_to(keep_ref[i], (rows, KEEP))
-        chosen = (picks == lax.broadcasted_iota(jnp.int32, (rows, KEEP), 0)).astype(jnp.float32)
-        kept = jnp.dot(
-            chosen.T.astype(jnp.bfloat16), page_ref[i], preferred_element_type=jnp.float32
+        chosen = keep_ref[i] == lax.broadcasted_iota(jnp.int32, (rows, KEEP), 0)
+        kept = lax.dot_general(
+            chosen.astype(jnp.float32).astype(jnp.bfloat16),
+            page_ref[i],
+            (((0,), (0,)), ((), ())),
+            preferred_element_type=jnp.float32,
         ).astype(jnp.bfloat16)
         kept_ref[i * KEEP : (i + 1) * KEEP] = kept
 
@@ -83,6 +85,7 @@
                 pl.BlockSpec((STEP * KEEP, width), lambda s, *_: (s, 0)),
             ],
         ),
+        compiler_params=pltpu.CompilerParams(vmem_limit_bytes=48 * 1024 * 1024),
         name="select_rows",
     )(page_count, dest_slot, keep_rows, cache.reshape(sources, rows, width))
 
@@ -340,6 +343,22 @@
     )(parts, own)
 
 
+def settle_kernel(in_ref, out_ref):
+    out_ref[...] = in_ref[...]
+
+
+def settle(pages):
+    block = pl.BlockSpec((4,) + pages.shape[1:], lambda i: (i, 0, 0))
+    return pl.pallas_call(
+        settle_kernel,
+        out_shape=jax.ShapeDtypeStruct(pages.shape, pages.dtype),
+        grid=(pages.shape[0] // 4,),
+        in_specs=[block],
+        out_specs=block,
+        name="settle",
+    )(pages)
+
+
 def per_device(
     tokens, norm_gain, w_query, w_keyvalue, cache, page_count, page_owner, keep_rows, dest_slot
 ):
@@ -382,6 +401,7 @@
     near = lax.all_to_all(
         halves, ("page", "tensor"), 0, 0, axis_index_groups=COLUMN_GROUPS, tiled=True
     )
+    near, settled = lax.optimization_barrier((near, settle(arrived)))
     far = lax.ppermute(near, "page", OTHER_CORE)
     part = attend(page_count, page_owner, kept, near, far)
     own = own_part(near, far)
@@ -394,7 +414,7 @@
         axis_index_groups=QUAD_GROUPS,
         tiled=True,
     )
-    return combine(parts, own), arrived[:, None]
+    return combine(parts, own), settled[:, None]
 
 
 def solution(mesh):

time: 154 us -> 155 us (level)
  blocking collectives: 86.9 us -> 61.2 us
  starting transfers between devices: 32.5 us -> 44.5 us
  waiting for transfers between devices: 8.64 us -> 18.8 us
  local copies, waits for them, and re-layouts: 2.68 us -> 5.54 us
  Pallas kernels: 18.2 us -> 19.9 us
    all_to_all x1 -> x0, blocking collectives: 25.7 us -> none  [per_device(): lax.all_to_all(halves, ('page', 'tensor'), 0, 0, axis_index_groups=COLUMN...]
    all_to_all x0 -> x1, starting transfers between devices: none -> 12 us  [per_device(): lax.all_to_all(halves, ('page', 'tensor'), 0, 0, axis_index_groups=COLUMN...]
    all_to_all x0 -> x1, waiting for transfers between devices: none -> 10.2 us  [per_device(): lax.all_to_all(halves, ('page', 'tensor'), 0, 0, axis_index_groups=COLUMN...]
    pallas_call x0 -> x1, Pallas kernels: none -> 3.47 us  [settle(): pl.pallas_call(settle_kernel, out_shape=jax.ShapeDtypeStruct(pages.shape,...]
    unnamed x7 -> x16, local copies, waits for them, and re-layouts: 2.68 us -> 5.54 us
    pallas_call x1, Pallas kernels: 5.22 us -> 3.41 us  [select_rows(): pl.pallas_call(select_kernel, out_shape=(jax.ShapeDtypeStruct((HOLDERS, K...]
  transfers between devices with their start and end apart: 4 -> 5, of which waited for: 3 -> 4; matrix products, arithmetic and copies ran while one was open for 0% -> 0% of each run, Pallas kernels for 8% -> 9%
where the time goes in v12:
time: 155 us; the launch traced here: 154 us
  blocking collectives  61.2 us (39%)
  starting transfers between devices  44.5 us (29%)
  Pallas kernels  19.9 us (13%)
  waiting for transfers between devices  18.8 us (12%)
  local copies, waits for them, and re-layouts  5.54 us (4%)
  other arithmetic  2.65 us (2%)
    all_gather x1, blocking collectives, per_device(): lax.all_gather(both, 'tensor', axis=0, axis_index_groups=PLANE_GROUPS, ti...  22.1 us
    all_gather x1, blocking collectives, per_device(): lax.all_gather(projected, 'tensor', axis=0, axis_index_groups=PLANE_GROUP...  20.9 us
    all_gather x1, blocking collectives, per_device(): lax.all_gather(jnp.concatenate([part, far], axis=0), 'page', axis=0, axis...  18.1 us
    ppermute x1, starting transfers between devices, per_device(): across = lax.ppermute(mine, ('page', 'tensor'), OTHER_HALF)  13.3 us
    all_to_all x1, starting transfers between devices, per_device(): lax.all_to_all(halves, ('page', 'tensor'), 0, 0, axis_index_groups=COLUMN...  12 us
    all_to_all x1, waiting for transfers between devices, per_device(): lax.all_to_all(halves, ('page', 'tensor'), 0, 0, axis_index_groups=COLUMN...  10.2 us
    all_to_all x1, starting transfers between devices, per_device(): arrived = lax.all_to_all(compact, 'page', 0, 0, tiled=True)  7.16 us
    ppermute x1, starting transfers between devices, per_device(): far = lax.ppermute(near, 'page', OTHER_CORE)  6.68 us
  transfers between devices with their start and end apart: 5, of which 4 were waited for; matrix products, arithmetic and copies ran while one was open for 0% of the time, Pallas kernels for 9%

profile of v12, /device:TPU:1, one launch (start us, length us, event | category | flops | bytes accessed | tf_op | source)
XLA Modules:
  0.0 154.0 jit_solution(5785820561720906634)
XLA Ops:
  0.6 0.9 fusion
  1.6 0.9 fusion.2
  2.4 13.3 %collective-permute-start = (bf16[4,2560]{1,0:T(4,128)(2,1)S(1)}, bf16[4,2560]{1,0:T(4,128)(2,1)S(1)}, u32[]{:S(2)}, u32[]{:S(2)}) collective-permute-start(bf16[4,2560]{1,0:T(4,128)(2,1)S(1)} %fusion.2), channel_id=1, source_target_pairs={{0,257},{1,256},{2,259},{3,258},{4,261},{5,260},{6,263},{7,262},{8... | collective-permute-start | bytes 61448 | tf_op jit(solution)/shard_map/ppermute | solution.py:383
  16.4 1.7 %copy-done = bf16[8,1,128,1280]{3,2,1,0:T(8,128)(2,1)S(1)} copy-done((bf16[8,1,128,1280]{3,2,1,0:T(8,128)(2,1)S(1)}, bf16[8,1,128,1280]{3,2,1,0:T(8,128)(2,1)}, u32[]{:S(2)}) %copy-start) | copy-done | bytes 2621464
  19.5 3.4 %select_rows.1 = (bf16[16,32,1280]{2,1,0:T(8,128)(2,1)}, bf16[256,1280]{1,0:T(8,128)(2,1)S(1)}) custom-call(s32[1]{0:T(128)} %bitcast.11.count_ref, s32[8]{0:T(128)S(1)} %bitcast.14, s32[8,1,32]{2,1,0:T(1,128)S(1)} %copy-done.3, bf16[8,128,1280]{2,1,0:T(8,128)(2,1)S(1)} %bitcast.13), custom_call_target="tpu_custom_call" | custom-call | tf_op jit(solution)/shard_map/select_rows/pallas_call | solution.py:70
  22.9 0.8 copy-done.2
  23.7 7.2 %all-to-all-start = ((bf16[16,32,1280]{2,1,0:T(8,128)(2,1)}), bf16[16,32,1280]{2,1,0:T(8,128)(2,1)S(1)}, u32[]{:S(2)}, u32[]{:S(2)}) async-start(bf16[16,32,1280]{2,1,0:T(8,128)(2,1)} %get-tuple-element.15), calls=%async_computation | async-start | bytes 2621440 | tf_op jit(solution)/shard_map/all_to_all | solution.py:385
  30.9 22.1 %all_gather.12.rows_ref = bf16[128,2560]{1,0:T(8,128)(2,1)} all-gather(bf16[8,2560]{1,0:T(8,128)(2,1)S(1)} %maximum_select_fusion), channel_id=1, replica_groups={{0,2,4,6,8,10,12,14,16,18,20,22,24,26,28,30},{1,3,5,7,9,11,13,15,17,19,..., dimensions={0}, use_global_device_ids=true | all-gather | bytes 696320 | tf_op jit(solution)/shard_map/all_gather | solution.py:392
  53.1 2.4 %project.1 = bf16[128,120]{1,0:T(8,128)(2,1)} custom-call(bf16[128,2560]{1,0:T(8,128)(2,1)} %all_gather.12.rows_ref, bf16[80,2560]{1,0:T(8,128)(2,1)} %bitcast.17, bf16[40,2560]{1,0:T(8,128)(2,1)} %bitcast.18), custom_call_target="tpu_custom_call" | custom-call | tf_op jit(solution)/shard_map/project/pallas_call | solution.py:102
  55.5 20.9 %all-gather = bf16[2048,120]{1,0:T(8,128)(2,1)} all-gather(bf16[128,120]{1,0:T(8,128)(2,1)} %project.1), channel_id=2, replica_groups={{0,2,4,6,8,10,12,14,16,18,20,22,24,26,28,30},{1,3,5,7,9,11,13,15,17,19,..., dimensions={0}, use_global_device_ids=true | all-gather | bytes 522240 | tf_op jit(solution)/shard_map/all_gather | solution.py:396
  76.4 1.6 %pick.1 = bf16[16,4,1920]{2,1,0:T(4,128)(2,1)} custom-call(s32[1]{0:T(128)} %bitcast.4.plane_ref, bf16[16,128,120]{2,1,0:T(8,128)(2,1)} %bitcast.15), custom_call_target="tpu_custom_call" | custom-call | tf_op jit(solution)/shard_map/pick/pallas_call | solution.py:130
  78.0 6.5 %all-to-all-done.in_ref = bf16[16,32,1280]{2,1,0:T(8,128)(2,1)S(1)} async-done(((bf16[16,32,1280]{2,1,0:T(8,128)(2,1)}), bf16[16,32,1280]{2,1,0:T(8,128)(2,1)S(1)}, u32[]{:S(2)}, u32[]{:S(2)}) %all-to-all-start) | async-done | bytes 1310752 | tf_op jit(solution)/shard_map/all_to_all | solution.py:385
  84.4 12.0 %all-to-all-start.1 = ((bf16[16,4,1920]{2,1,0:T(4,128)(2,1)}), bf16[16,4,1920]{2,1,0:T(4,128)(2,1)S(1)}, u32[]{:S(2)}, u32[]{:S(2)}) async-start(bf16[16,4,1920]{2,1,0:T(4,128)(2,1)} %pick.1), calls=%async_computation.1 | async-start | bytes 491520 | tf_op jit(solution)/shard_map/all_to_all | solution.py:401
  96.5 3.5 %settle.1 = bf16[16,32,1280]{2,1,0:T(8,128)(2,1)} custom-call(bf16[16,32,1280]{2,1,0:T(8,128)(2,1)} %copy-done.5), custom_call_target="tpu_custom_call" | custom-call | tf_op jit(solution)/shard_map/settle/pallas_call | solution.py:352
  99.9 10.2 %all-to-all-done.1.near_ref = bf16[16,4,1920]{2,1,0:T(4,128)(2,1)S(1)} async-done(((bf16[16,4,1920]{2,1,0:T(4,128)(2,1)}), bf16[16,4,1920]{2,1,0:T(4,128)(2,1)S(1)}, u32[]{:S(2)}, u32[]{:S(2)}) %all-to-all-start.1) | async-done | bytes 245792 | tf_op jit(solution)/shard_map/all_to_all | solution.py:401
  110.2 6.7 %collective-permute-start.1 = (bf16[16,4,1920]{2,1,0:T(4,128)(2,1)S(1)}, bf16[16,4,1920]{2,1,0:T(4,128)(2,1)S(1)}, u32[]{:S(2)}, u32[]{:S(2)}) collective-permute-start(bf16[16,4,1920]{2,1,0:T(4,128)(2,1)S(1)} %all-to-all-done.1.near_ref), channel_id=1, source_target_pairs={{0,32},{32,0},{64,96},{96,64},{128,160},{160,128},{192,224},{224,1... | collective-permute-start | bytes 737288 | tf_op jit(solution)/shard_map/ppermute | solution.py:405
  116.8 1.1 collective-permute-done.1.far_ref
  118.7 3.9 %attend.1 = bf16[8,2816]{1,0:T(8,128)(2,1)} custom-call(s32[1]{0:T(128)} %bitcast.12.count_ref, s32[8]{0:T(128)} %bitcast.19, bf16[256,1280]{1,0:T(8,128)(2,1)} %copy-done.2, bf16[16,4,1920]{2,1,0:T(4,128)(2,1)} %copy-done.6, bf16[16,4,1920]{2,1,0:T(4,128)(2,1)} %copy-done.7), custom_call_target="tpu_custom_call" | custom-call | tf_op jit(solution)/shard_map/attend/pallas_call | solution.py:219
  122.6 5.4 %collective-permute-start.2 = (bf16[8,2816]{1,0:T(8,128)(2,1)}, bf16[8,2816]{1,0:T(8,128)(2,1)S(1)}, u32[]{:S(2)}, u32[]{:S(2)}) collective-permute-start(bf16[8,2816]{1,0:T(8,128)(2,1)} %attend.1), channel_id=1, source_target_pairs={{0,256},{32,288},{64,320},{96,352},{128,384},{160,416},{192,448},{... | collective-permute-start | bytes 135176 | tf_op jit(solution)/shard_map/ppermute | solution.py:408
  127.9 2.5 %own_part.1.own_ref = f32[64,768]{1,0:T(8,128)} custom-call(bf16[16,4,1920]{2,1,0:T(4,128)(2,1)} %copy-done.6, bf16[16,4,1920]{2,1,0:T(4,128)(2,1)} %copy-done.7), custom_call_target="tpu_custom_call" | custom-call | tf_op jit(solution)/shard_map/own_part/pallas_call | solution.py:278
  130.4 1.0 collective-permute-done.2
  132.3 18.1 %all_gather.15.part_ref = bf16[128,2816]{1,0:T(8,128)(2,1)S(1)} all-gather(bf16[16,2816]{1,0:T(8,128)(2,1)S(1)} %pad_maximum_fusion), channel_id=1, replica_groups={{0,32,64,96,128,160,192,224},{256,288,320,352,384,416,448,480},{1,33,65..., dimensions={0}, use_global_device_ids=true | all-gather | bytes 811008 | tf_op jit(solution)/shard_map/all_gather | solution.py:410
  150.4 0.9 copy-done.1
  151.3 2.7 %combine.1 = bf16[64,2560]{1,0:T(8,128)(2,1)} custom-call(bf16[128,2816]{1,0:T(8,128)(2,1)S(1)} %all_gather.15.part_ref, f32[64,768]{1,0:T(8,128)S(1)} %copy-done.1), custom_call_target="tpu_custom_call" | custom-call | tf_op jit(solution)/shard_map/combine/pallas_call | solution.py:336
  (17 shorter events, 2.9 us)
Async XLA Ops:
  2.4 21.3 %collective-permute-start = (bf16[4,2560]{1,0:T(4,128)(2,1)S(1)}, bf16[4,2560]{1,0:T(4,128)(2,1)S(1)}, u32[]{:S(2)}, u32[]{:S(2)}) collective-permute-start(bf16[4,2560]{1,0:T(4,128)(2,1)S(1)} %fusion.2), channel_id=1, source_target_pairs={{0,257},{1,256},{2,259},{3,258},{4,261},{5,260},{6,263},{7,262},{8... | collective-permute-start | bytes 61448 | tf_op jit(solution)/shard_map/ppermute | solution.py:383
  16.4 1.7 %copy-start = (bf16[8,1,128,1280]{3,2,1,0:T(8,128)(2,1)S(1)}, bf16[8,1,128,1280]{3,2,1,0:T(8,128)(2,1)}, u32[]{:S(2)}) copy-start(bf16[8,1,128,1280]{3,2,1,0:T(8,128)(2,1)} %param.13) | copy-start | bytes 7864324
  18.1 0.7 copy-start.3
  18.8 0.7 copy-start.4
  22.9 0.8 copy-start.2
  23.7 60.7 %all-to-all-start = ((bf16[16,32,1280]{2,1,0:T(8,128)(2,1)}), bf16[16,32,1280]{2,1,0:T(8,128)(2,1)S(1)}, u32[]{:S(2)}, u32[]{:S(2)}) async-start(bf16[16,32,1280]{2,1,0:T(8,128)(2,1)} %get-tuple-element.15), calls=%async_computation | async-start | bytes 2621440 | tf_op jit(solution)/shard_map/all_to_all | solution.py:385
  84.4 12.0 %copy-start.5 = (bf16[16,32,1280]{2,1,0:T(8,128)(2,1)}, bf16[16,32,1280]{2,1,0:T(8,128)(2,1)S(1)}, u32[]{:S(2)}) copy-start(bf16[16,32,1280]{2,1,0:T(8,128)(2,1)S(1)} %all-to-all-done.in_ref) | copy-start | bytes 3932164
  84.4 25.7 %all-to-all-start.1 = ((bf16[16,4,1920]{2,1,0:T(4,128)(2,1)}), bf16[16,4,1920]{2,1,0:T(4,128)(2,1)S(1)}, u32[]{:S(2)}, u32[]{:S(2)}) async-start(bf16[16,4,1920]{2,1,0:T(4,128)(2,1)} %pick.1), calls=%async_computation.1 | async-start | bytes 491520 | tf_op jit(solution)/shard_map/all_to_all | solution.py:401
  110.2 7.8 %copy-start.6 = (bf16[16,4,1920]{2,1,0:T(4,128)(2,1)}, bf16[16,4,1920]{2,1,0:T(4,128)(2,1)S(1)}, u32[]{:S(2)}) copy-start(bf16[16,4,1920]{2,1,0:T(4,128)(2,1)S(1)} %all-to-all-done.1.near_ref) | copy-start | bytes 737284
  110.2 7.8 %collective-permute-start.1 = (bf16[16,4,1920]{2,1,0:T(4,128)(2,1)S(1)}, bf16[16,4,1920]{2,1,0:T(4,128)(2,1)S(1)}, u32[]{:S(2)}, u32[]{:S(2)}) collective-permute-start(bf16[16,4,1920]{2,1,0:T(4,128)(2,1)S(1)} %all-to-all-done.1.near_ref), channel_id=1, source_target_pairs={{0,32},{32,0},{64,96},{96,64},{128,160},{160,128},{192,224},{224,1... | collective-permute-start | bytes 737288 | tf_op jit(solution)/shard_map/ppermute | solution.py:405
  118.0 0.7 copy-start.7
  122.6 8.9 %collective-permute-start.2 = (bf16[8,2816]{1,0:T(8,128)(2,1)}, bf16[8,2816]{1,0:T(8,128)(2,1)S(1)}, u32[]{:S(2)}, u32[]{:S(2)}) collective-permute-start(bf16[8,2816]{1,0:T(8,128)(2,1)} %attend.1), channel_id=1, source_target_pairs={{0,256},{32,288},{64,320},{96,352},{128,384},{160,416},{192,448},{... | collective-permute-start | bytes 135176 | tf_op jit(solution)/shard_map/ppermute | solution.py:408
  150.4 0.9 copy-start.1

commit v13 on v12

--- a/solution.py
+++ b/solution.py
@@ -35,7 +35,7 @@
 OTHER_CORE = [(i, i ^ 1) for i in range(HOLDERS)]
 OTHER_QUAD = [(i, i ^ CHIPS) for i in range(HOLDERS)]
 HALF_COLUMNS = (QUERIES + 2 * KEYS) // 2
-STEP = 8
+STEP = 4
 
 VMEM = pl.BlockSpec(memory_space=pltpu.VMEM)
 SMEM = pl.BlockSpec(memory_space=pltpu.SMEM)
@@ -85,7 +85,6 @@
                 pl.BlockSpec((STEP * KEEP, width), lambda s, *_: (s, 0)),
             ],
         ),
-        compiler_params=pltpu.CompilerParams(vmem_limit_bytes=48 * 1024 * 1024),
         name="select_rows",
     )(page_count, dest_slot, keep_rows, cache.reshape(sources, rows, width))
 

time: 155 us -> 153 us (0.987)
  local copies, waits for them, and re-layouts: 5.54 us -> 1.62 us
  Pallas kernels: 19.9 us -> 21.6 us
    unnamed x16 -> x8, local copies, waits for them, and re-layouts: 5.54 us -> 1.62 us
    pallas_call x1, Pallas kernels: 3.41 us -> 5.08 us  [select_rows(): pl.pallas_call(select_kernel, out_shape=(jax.ShapeDtypeStruct((HOLDERS, K...]
  transfers between devices with their start and end apart: 5 -> 5, of which waited for: 4 -> 4; matrix products, arithmetic and copies ran while one was open for 0% -> 0% of each run, Pallas kernels for 9% -> 10%
where the time goes in v13:
time: 153 us; the launch traced here: 152 us
  blocking collectives  61.2 us (40%)
  starting transfers between devices  44.5 us (29%)
  Pallas kernels  21.6 us (14%)
  waiting for transfers between devices  18.8 us (12%)
  other arithmetic  2.65 us (2%)
  local copies, waits for them, and re-layouts  1.62 us (1%)
    all_gather x1, blocking collectives, per_device(): lax.all_gather(both, 'tensor', axis=0, axis_index_groups=PLANE_GROUPS, ti...  22.1 us
    all_gather x1, blocking collectives, per_device(): lax.all_gather(projected, 'tensor', axis=0, axis_index_groups=PLANE_GROUP...  20.9 us
    all_gather x1, blocking collectives, per_device(): lax.all_gather(jnp.concatenate([part, far], axis=0), 'page', axis=0, axis...  18.1 us
    ppermute x1, starting transfers between devices, per_device(): across = lax.ppermute(mine, ('page', 'tensor'), OTHER_HALF)  13.3 us
    all_to_all x1, starting transfers between devices, per_device(): lax.all_to_all(halves, ('page', 'tensor'), 0, 0, axis_index_groups=COLUMN...  12 us
    all_to_all x1, waiting for transfers between devices, per_device(): lax.all_to_all(halves, ('page', 'tensor'), 0, 0, axis_index_groups=COLUMN...  10.2 us
    all_to_all x1, starting transfers between devices, per_device(): arrived = lax.all_to_all(compact, 'page', 0, 0, tiled=True)  7.16 us
    ppermute x1, starting transfers between devices, per_device(): far = lax.ppermute(near, 'page', OTHER_CORE)  6.68 us
  transfers between devices with their start and end apart: 5, of which 4 were waited for; matrix products, arithmetic and copies ran while one was open for 0% of the time, Pallas kernels for 10%

profile of v13, /device:TPU:1, one launch (start us, length us, event | category | flops | bytes accessed | tf_op | source)
XLA Modules:
  0.0 151.7 jit_solution(10188602861184007115)
XLA Ops:
  0.6 0.9 fusion
  1.6 0.9 fusion.2
  2.4 13.3 %collective-permute-start = (bf16[4,2560]{1,0:T(4,128)(2,1)S(1)}, bf16[4,2560]{1,0:T(4,128)(2,1)S(1)}, u32[]{:S(2)}, u32[]{:S(2)}) collective-permute-start(bf16[4,2560]{1,0:T(4,128)(2,1)S(1)} %fusion.2), channel_id=1, source_target_pairs={{0,257},{1,256},{2,259},{3,258},{4,261},{5,260},{6,263},{7,262},{8... | collective-permute-start | bytes 61448 | tf_op jit(solution)/shard_map/ppermute | solution.py:382
  16.4 5.1 %select_rows.1 = (bf16[16,32,1280]{2,1,0:T(8,128)(2,1)}, bf16[256,1280]{1,0:T(8,128)(2,1)}) custom-call(s32[1]{0:T(128)} %bitcast.11.count_ref, s32[8]{0:T(128)} %bitcast.18, s32[8,1,32]{2,1,0:T(1,128)} %keep_ref.1, bf16[8,128,1280]{2,1,0:T(8,128)(2,1)} %bitcast.13), custom_call_target="tpu_custom_call" | custom-call | tf_op jit(solution)/shard_map/select_rows/pallas_call | solution.py:70
  21.5 7.2 %all-to-all-start = ((bf16[16,32,1280]{2,1,0:T(8,128)(2,1)}), bf16[16,32,1280]{2,1,0:T(8,128)(2,1)S(1)}, u32[]{:S(2)}, u32[]{:S(2)}) async-start(bf16[16,32,1280]{2,1,0:T(8,128)(2,1)} %get-tuple-element.15), calls=%async_computation | async-start | bytes 2621440 | tf_op jit(solution)/shard_map/all_to_all | solution.py:384
  28.7 22.1 %all_gather.12.rows_ref = bf16[128,2560]{1,0:T(8,128)(2,1)} all-gather(bf16[8,2560]{1,0:T(8,128)(2,1)S(1)} %maximum_select_fusion), channel_id=1, replica_groups={{0,2,4,6,8,10,12,14,16,18,20,22,24,26,28,30},{1,3,5,7,9,11,13,15,17,19,..., dimensions={0}, use_global_device_ids=true | all-gather | bytes 696320 | tf_op jit(solution)/shard_map/all_gather | solution.py:391
  50.8 2.4 %project.1 = bf16[128,120]{1,0:T(8,128)(2,1)} custom-call(bf16[128,2560]{1,0:T(8,128)(2,1)} %all_gather.12.rows_ref, bf16[80,2560]{1,0:T(8,128)(2,1)} %bitcast.16, bf16[40,2560]{1,0:T(8,128)(2,1)} %bitcast.17), custom_call_target="tpu_custom_call" | custom-call | tf_op jit(solution)/shard_map/project/pallas_call | solution.py:101
  53.2 20.9 %all-gather = bf16[2048,120]{1,0:T(8,128)(2,1)} all-gather(bf16[128,120]{1,0:T(8,128)(2,1)} %project.1), channel_id=2, replica_groups={{0,2,4,6,8,10,12,14,16,18,20,22,24,26,28,30},{1,3,5,7,9,11,13,15,17,19,..., dimensions={0}, use_global_device_ids=true | all-gather | bytes 522240 | tf_op jit(solution)/shard_map/all_gather | solution.py:395
  74.1 1.6 %pick.1 = bf16[16,4,1920]{2,1,0:T(4,128)(2,1)} custom-call(s32[1]{0:T(128)} %bitcast.4.plane_ref, bf16[16,128,120]{2,1,0:T(8,128)(2,1)} %bitcast.14), custom_call_target="tpu_custom_call" | custom-call | tf_op jit(solution)/shard_map/pick/pallas_call | solution.py:129
  75.7 6.5 %all-to-all-done.in_ref = bf16[16,32,1280]{2,1,0:T(8,128)(2,1)S(1)} async-done(((bf16[16,32,1280]{2,1,0:T(8,128)(2,1)}), bf16[16,32,1280]{2,1,0:T(8,128)(2,1)S(1)}, u32[]{:S(2)}, u32[]{:S(2)}) %all-to-all-start) | async-done | bytes 1310752 | tf_op jit(solution)/shard_map/all_to_all | solution.py:384
  82.2 12.0 %all-to-all-start.1 = ((bf16[16,4,1920]{2,1,0:T(4,128)(2,1)}), bf16[16,4,1920]{2,1,0:T(4,128)(2,1)S(1)}, u32[]{:S(2)}, u32[]{:S(2)}) async-start(bf16[16,4,1920]{2,1,0:T(4,128)(2,1)} %pick.1), calls=%async_computation.1 | async-start | bytes 491520 | tf_op jit(solution)/shard_map/all_to_all | solution.py:400
  94.2 3.5 %settle.1 = bf16[16,32,1280]{2,1,0:T(8,128)(2,1)} custom-call(bf16[16,32,1280]{2,1,0:T(8,128)(2,1)} %copy-done.1), custom_call_target="tpu_custom_call" | custom-call | tf_op jit(solution)/shard_map/settle/pallas_call | solution.py:351
  97.7 10.2 %all-to-all-done.1.near_ref = bf16[16,4,1920]{2,1,0:T(4,128)(2,1)S(1)} async-done(((bf16[16,4,1920]{2,1,0:T(4,128)(2,1)}), bf16[16,4,1920]{2,1,0:T(4,128)(2,1)S(1)}, u32[]{:S(2)}, u32[]{:S(2)}) %all-to-all-start.1) | async-done | bytes 245792 | tf_op jit(solution)/shard_map/all_to_all | solution.py:400
  107.9 6.7 %collective-permute-start.1 = (bf16[16,4,1920]{2,1,0:T(4,128)(2,1)S(1)}, bf16[16,4,1920]{2,1,0:T(4,128)(2,1)S(1)}, u32[]{:S(2)}, u32[]{:S(2)}) collective-permute-start(bf16[16,4,1920]{2,1,0:T(4,128)(2,1)S(1)} %all-to-all-done.1.near_ref), channel_id=1, source_target_pairs={{0,32},{32,0},{64,96},{96,64},{128,160},{160,128},{192,224},{224,1... | collective-permute-start | bytes 737288 | tf_op jit(solution)/shard_map/ppermute | solution.py:404
  114.6 1.1 collective-permute-done.1.far_ref
  115.7 0.7 copy-done.3
  116.4 3.9 %attend.1 = bf16[8,2816]{1,0:T(8,128)(2,1)} custom-call(s32[1]{0:T(128)} %bitcast.12.count_ref, s32[8]{0:T(128)} %bitcast.19, bf16[256,1280]{1,0:T(8,128)(2,1)} %get-tuple-element.12.kept_ref, bf16[16,4,1920]{2,1,0:T(4,128)(2,1)} %copy-done.2, bf16[16,4,1920]{2,1,0:T(4,128)(2,1)} %copy-done.3), custom_call_target="tpu_custom_call" | custom-call | tf_op jit(solution)/shard_map/attend/pallas_call | solution.py:218
  120.3 5.4 %collective-permute-start.2 = (bf16[8,2816]{1,0:T(8,128)(2,1)}, bf16[8,2816]{1,0:T(8,128)(2,1)S(1)}, u32[]{:S(2)}, u32[]{:S(2)}) collective-permute-start(bf16[8,2816]{1,0:T(8,128)(2,1)} %attend.1), channel_id=1, source_target_pairs={{0,256},{32,288},{64,320},{96,352},{128,384},{160,416},{192,448},{... | collective-permute-start | bytes 135176 | tf_op jit(solution)/shard_map/ppermute | solution.py:407
  125.7 2.5 %own_part.1.own_ref = f32[64,768]{1,0:T(8,128)} custom-call(bf16[16,4,1920]{2,1,0:T(4,128)(2,1)} %copy-done.2, bf16[16,4,1920]{2,1,0:T(4,128)(2,1)} %copy-done.3), custom_call_target="tpu_custom_call" | custom-call | tf_op jit(solution)/shard_map/own_part/pallas_call | solution.py:277
  128.2 1.0 collective-permute-done.2
  129.2 0.8 pad_maximum_fusion
  130.0 18.1 %all_gather.15.part_ref = bf16[128,2816]{1,0:T(8,128)(2,1)S(1)} all-gather(bf16[16,2816]{1,0:T(8,128)(2,1)S(1)} %pad_maximum_fusion), channel_id=1, replica_groups={{0,32,64,96,128,160,192,224},{256,288,320,352,384,416,448,480},{1,33,65..., dimensions={0}, use_global_device_ids=true | all-gather | bytes 811008 | tf_op jit(solution)/shard_map/all_gather | solution.py:409
  148.1 0.9 copy-done
  149.0 2.7 %combine.1 = bf16[64,2560]{1,0:T(8,128)(2,1)} custom-call(bf16[128,2816]{1,0:T(8,128)(2,1)S(1)} %all_gather.15.part_ref, f32[64,768]{1,0:T(8,128)S(1)} %copy-done), custom_call_target="tpu_custom_call" | custom-call | tf_op jit(solution)/shard_map/combine/pallas_call | solution.py:335
  (9 shorter events, 0.1 us)
Async XLA Ops:
  2.4 19.0 %collective-permute-start = (bf16[4,2560]{1,0:T(4,128)(2,1)S(1)}, bf16[4,2560]{1,0:T(4,128)(2,1)S(1)}, u32[]{:S(2)}, u32[]{:S(2)}) collective-permute-start(bf16[4,2560]{1,0:T(4,128)(2,1)S(1)} %fusion.2), channel_id=1, source_target_pairs={{0,257},{1,256},{2,259},{3,258},{4,261},{5,260},{6,263},{7,262},{8... | collective-permute-start | bytes 61448 | tf_op jit(solution)/shard_map/ppermute | solution.py:382
  21.5 60.7 %all-to-all-start = ((bf16[16,32,1280]{2,1,0:T(8,128)(2,1)}), bf16[16,32,1280]{2,1,0:T(8,128)(2,1)S(1)}, u32[]{:S(2)}, u32[]{:S(2)}) async-start(bf16[16,32,1280]{2,1,0:T(8,128)(2,1)} %get-tuple-element.15), calls=%async_computation | async-start | bytes 2621440 | tf_op jit(solution)/shard_map/all_to_all | solution.py:384
  82.2 12.0 %copy-start.1 = (bf16[16,32,1280]{2,1,0:T(8,128)(2,1)}, bf16[16,32,1280]{2,1,0:T(8,128)(2,1)S(1)}, u32[]{:S(2)}) copy-start(bf16[16,32,1280]{2,1,0:T(8,128)(2,1)S(1)} %all-to-all-done.in_ref) | copy-start | bytes 3932164
  82.2 25.7 %all-to-all-start.1 = ((bf16[16,4,1920]{2,1,0:T(4,128)(2,1)}), bf16[16,4,1920]{2,1,0:T(4,128)(2,1)S(1)}, u32[]{:S(2)}, u32[]{:S(2)}) async-start(bf16[16,4,1920]{2,1,0:T(4,128)(2,1)} %pick.1), calls=%async_computation.1 | async-start | bytes 491520 | tf_op jit(solution)/shard_map/all_to_all | solution.py:400
  107.9 7.8 %copy-start.2 = (bf16[16,4,1920]{2,1,0:T(4,128)(2,1)}, bf16[16,4,1920]{2,1,0:T(4,128)(2,1)S(1)}, u32[]{:S(2)}) copy-start(bf16[16,4,1920]{2,1,0:T(4,128)(2,1)S(1)} %all-to-all-done.1.near_ref) | copy-start | bytes 737284
  107.9 7.8 %collective-permute-start.1 = (bf16[16,4,1920]{2,1,0:T(4,128)(2,1)S(1)}, bf16[16,4,1920]{2,1,0:T(4,128)(2,1)S(1)}, u32[]{:S(2)}, u32[]{:S(2)}) collective-permute-start(bf16[16,4,1920]{2,1,0:T(4,128)(2,1)S(1)} %all-to-all-done.1.near_ref), channel_id=1, source_target_pairs={{0,32},{32,0},{64,96},{96,64},{128,160},{160,128},{192,224},{224,1... | collective-permute-start | bytes 737288 | tf_op jit(solution)/shard_map/ppermute | solution.py:404
  115.7 0.7 copy-start.3
  120.3 8.9 %collective-permute-start.2 = (bf16[8,2816]{1,0:T(8,128)(2,1)}, bf16[8,2816]{1,0:T(8,128)(2,1)S(1)}, u32[]{:S(2)}, u32[]{:S(2)}) collective-permute-start(bf16[8,2816]{1,0:T(8,128)(2,1)} %attend.1), channel_id=1, source_target_pairs={{0,256},{32,288},{64,320},{96,352},{128,384},{160,416},{192,448},{... | collective-permute-start | bytes 135176 | tf_op jit(solution)/shard_map/ppermute | solution.py:407
  148.1 0.9 copy-start

commit v14 on v13

--- a/solution.py
+++ b/solution.py
@@ -21,6 +21,8 @@
 EXTRA = 256
 
 CHIPS = 8
+ROW_GROUPS = [[(x * 4 + y) * 2 + half for y in range(4)] for x in range(4) for half in range(2)]
+LINE_GROUPS = [[(x * 4 + y) * 2 + half for x in range(4)] for y in range(4) for half in range(2)]
 PLANE_GROUPS = [[2 * i + half for i in range(PLANE)] for half in range(2)]
 OTHER_HALF = [
     (p * 2 * PLANE + t, (p ^ 8) * 2 * PLANE + (t ^ 1)) for p in range(HOLDERS) for t in range(2 * PLANE)
@@ -388,9 +390,11 @@
         jnp.concatenate([mine, across], axis=0),
         jnp.concatenate([across, mine], axis=0),
     )
-    rows = lax.all_gather(
-        both, "tensor", axis=0, axis_index_groups=PLANE_GROUPS, tiled=True
-    )
+    rows = both
+    for plane_groups in (ROW_GROUPS, LINE_GROUPS):
+        rows = lax.all_gather(
+            rows, "tensor", axis=0, axis_index_groups=plane_groups, tiled=True
+        )
     projected = project(rows, w_query, w_keyvalue)
     everyone = lax.all_gather(
         projected, "tensor", axis=0, axis_index_groups=PLANE_GROUPS, tiled=False

time: 153 us -> 153 us (level)
    all_gather x1 -> x2, blocking collectives: 22.1 us -> 23.2 us  [per_device(): lax.all_gather(rows, 'tensor', axis=0, axis_index_groups=plane_groups, ti...]
where the time goes in v14:
time: 153 us; the launch traced here: 152 us
  blocking collectives  61.8 us (40%)
  starting transfers between devices  45.7 us (30%)
  Pallas kernels  21.6 us (14%)
  waiting for transfers between devices  17.4 us (11%)
  other arithmetic  2.65 us (2%)
  local copies, waits for them, and re-layouts  1.62 us (1%)
    all_gather x2, blocking collectives, per_device(): lax.all_gather(rows, 'tensor', axis=0, axis_index_groups=plane_groups, ti...  23.2 us
    all_gather x1, blocking collectives, per_device(): lax.all_gather(projected, 'tensor', axis=0, axis_index_groups=PLANE_GROUP...  20.6 us
    all_gather x1, blocking collectives, per_device(): lax.all_gather(jnp.concatenate([part, far], axis=0), 'page', axis=0, axis...  18 us
    ppermute x1, starting transfers between devices, per_device(): across = lax.ppermute(mine, ('page', 'tensor'), OTHER_HALF)  13.3 us
    all_to_all x1, starting transfers between devices, per_device(): lax.all_to_all(halves, ('page', 'tensor'), 0, 0, axis_index_groups=COLUMN...  12 us
    all_to_all x1, waiting for transfers between devices, per_device(): lax.all_to_all(halves, ('page', 'tensor'), 0, 0, axis_index_groups=COLUMN...  9.36 us
    ppermute x1, starting transfers between devices, per_device(): far = lax.ppermute(near, 'page', OTHER_CORE)  8.04 us
    all_to_all x1, starting transfers between devices, per_device(): arrived = lax.all_to_all(compact, 'page', 0, 0, tiled=True)  7.16 us
  transfers between devices with their start and end apart: 5, of which 4 were waited for; matrix products, arithmetic and copies ran while one was open for 0% of the time, Pallas kernels for 10%

profile of v14, /device:TPU:1, one launch (start us, length us, event | category | flops | bytes accessed | tf_op | source)
XLA Modules:
  0.0 152.1 jit_solution(12086313456787262713)
XLA Ops:
  0.6 0.9 fusion
  1.6 0.9 fusion.2
  2.4 13.3 %collective-permute-start = (bf16[4,2560]{1,0:T(4,128)(2,1)S(1)}, bf16[4,2560]{1,0:T(4,128)(2,1)S(1)}, u32[]{:S(2)}, u32[]{:S(2)}) collective-permute-start(bf16[4,2560]{1,0:T(4,128)(2,1)S(1)} %fusion.2), channel_id=1, source_target_pairs={{0,257},{1,256},{2,259},{3,258},{4,261},{5,260},{6,263},{7,262},{8... | collective-permute-start | bytes 61448 | tf_op jit(solution)/shard_map/ppermute | solution.py:384
  16.4 5.1 %select_rows.1 = (bf16[16,32,1280]{2,1,0:T(8,128)(2,1)}, bf16[256,1280]{1,0:T(8,128)(2,1)}) custom-call(s32[1]{0:T(128)} %bitcast.11.count_ref, s32[8]{0:T(128)} %bitcast.18, s32[8,1,32]{2,1,0:T(1,128)} %keep_ref.1, bf16[8,128,1280]{2,1,0:T(8,128)(2,1)} %bitcast.13), custom_call_target="tpu_custom_call" | custom-call | tf_op jit(solution)/shard_map/select_rows/pallas_call | solution.py:72
  21.5 7.2 %all-to-all-start = ((bf16[16,32,1280]{2,1,0:T(8,128)(2,1)}), bf16[16,32,1280]{2,1,0:T(8,128)(2,1)S(1)}, u32[]{:S(2)}, u32[]{:S(2)}) async-start(bf16[16,32,1280]{2,1,0:T(8,128)(2,1)} %get-tuple-element.15), calls=%async_computation | async-start | bytes 2621440 | tf_op jit(solution)/shard_map/all_to_all | solution.py:386
  28.7 10.6 %all_gather.15 = bf16[32,2560]{1,0:T(8,128)(2,1)S(1)} all-gather(bf16[8,2560]{1,0:T(8,128)(2,1)S(1)} %maximum_select_fusion), channel_id=1, replica_groups={{0,2,4,6},{1,3,5,7},{8,10,12,14},{9,11,13,15},{16,18,20,22},{17,19,21,2..., dimensions={0}, use_global_device_ids=true | all-gather | bytes 204800 | tf_op jit(solution)/shard_map/all_gather | solution.py:395
  39.3 12.7 %all_gather.16.rows_ref = bf16[128,2560]{1,0:T(8,128)(2,1)} all-gather(bf16[32,2560]{1,0:T(8,128)(2,1)S(1)} %all_gather.15), channel_id=1, replica_groups={{0,8,16,24},{1,9,17,25},{2,10,18,26},{3,11,19,27},{4,12,20,28},{5,13,21..., dimensions={0}, use_global_device_ids=true | all-gather | bytes 819200 | tf_op jit(solution)/shard_map/all_gather | solution.py:395
  51.9 2.4 %project.1 = bf16[128,120]{1,0:T(8,128)(2,1)} custom-call(bf16[128,2560]{1,0:T(8,128)(2,1)} %all_gather.16.rows_ref, bf16[80,2560]{1,0:T(8,128)(2,1)} %bitcast.16, bf16[40,2560]{1,0:T(8,128)(2,1)} %bitcast.17), custom_call_target="tpu_custom_call" | custom-call | tf_op jit(solution)/shard_map/project/pallas_call | solution.py:103
  54.3 20.6 %all-gather = bf16[2048,120]{1,0:T(8,128)(2,1)} all-gather(bf16[128,120]{1,0:T(8,128)(2,1)} %project.1), channel_id=2, replica_groups={{0,2,4,6,8,10,12,14,16,18,20,22,24,26,28,30},{1,3,5,7,9,11,13,15,17,19,..., dimensions={0}, use_global_device_ids=true | all-gather | bytes 522240 | tf_op jit(solution)/shard_map/all_gather | solution.py:399
  74.9 1.6 %pick.1 = bf16[16,4,1920]{2,1,0:T(4,128)(2,1)} custom-call(s32[1]{0:T(128)} %bitcast.4.plane_ref, bf16[16,128,120]{2,1,0:T(8,128)(2,1)} %bitcast.14), custom_call_target="tpu_custom_call" | custom-call | tf_op jit(solution)/shard_map/pick/pallas_call | solution.py:131
  76.5 5.7 %all-to-all-done.in_ref = bf16[16,32,1280]{2,1,0:T(8,128)(2,1)S(1)} async-done(((bf16[16,32,1280]{2,1,0:T(8,128)(2,1)}), bf16[16,32,1280]{2,1,0:T(8,128)(2,1)S(1)}, u32[]{:S(2)}, u32[]{:S(2)}) %all-to-all-start) | async-done | bytes 1310752 | tf_op jit(solution)/shard_map/all_to_all | solution.py:386
  82.2 12.0 %all-to-all-start.1 = ((bf16[16,4,1920]{2,1,0:T(4,128)(2,1)}), bf16[16,4,1920]{2,1,0:T(4,128)(2,1)S(1)}, u32[]{:S(2)}, u32[]{:S(2)}) async-start(bf16[16,4,1920]{2,1,0:T(4,128)(2,1)} %pick.1), calls=%async_computation.1 | async-start | bytes 491520 | tf_op jit(solution)/shard_map/all_to_all | solution.py:404
  94.2 3.5 %settle.1 = bf16[16,32,1280]{2,1,0:T(8,128)(2,1)} custom-call(bf16[16,32,1280]{2,1,0:T(8,128)(2,1)} %copy-done.1), custom_call_target="tpu_custom_call" | custom-call | tf_op jit(solution)/shard_map/settle/pallas_call | solution.py:353
  97.7 9.4 %all-to-all-done.1.near_ref = bf16[16,4,1920]{2,1,0:T(4,128)(2,1)S(1)} async-done(((bf16[16,4,1920]{2,1,0:T(4,128)(2,1)}), bf16[16,4,1920]{2,1,0:T(4,128)(2,1)S(1)}, u32[]{:S(2)}, u32[]{:S(2)}) %all-to-all-start.1) | async-done | bytes 245792 | tf_op jit(solution)/shard_map/all_to_all | solution.py:404
  107.0 8.0 %collective-permute-start.1 = (bf16[16,4,1920]{2,1,0:T(4,128)(2,1)S(1)}, bf16[16,4,1920]{2,1,0:T(4,128)(2,1)S(1)}, u32[]{:S(2)}, u32[]{:S(2)}) collective-permute-start(bf16[16,4,1920]{2,1,0:T(4,128)(2,1)S(1)} %all-to-all-done.1.near_ref), channel_id=1, source_target_pairs={{0,32},{32,0},{64,96},{96,64},{128,160},{160,128},{192,224},{224,1... | collective-permute-start | bytes 737288 | tf_op jit(solution)/shard_map/ppermute | solution.py:408
  115.1 1.1 collective-permute-done.1.far_ref
  116.9 3.9 %attend.1 = bf16[8,2816]{1,0:T(8,128)(2,1)} custom-call(s32[1]{0:T(128)} %bitcast.12.count_ref, s32[8]{0:T(128)} %bitcast.19, bf16[256,1280]{1,0:T(8,128)(2,1)} %get-tuple-element.12.kept_ref, bf16[16,4,1920]{2,1,0:T(4,128)(2,1)} %copy-done.2, bf16[16,4,1920]{2,1,0:T(4,128)(2,1)} %copy-done.3), custom_call_target="tpu_custom_call" | custom-call | tf_op jit(solution)/shard_map/attend/pallas_call | solution.py:220
  120.8 5.2 %collective-permute-start.2 = (bf16[8,2816]{1,0:T(8,128)(2,1)}, bf16[8,2816]{1,0:T(8,128)(2,1)S(1)}, u32[]{:S(2)}, u32[]{:S(2)}) collective-permute-start(bf16[8,2816]{1,0:T(8,128)(2,1)} %attend.1), channel_id=1, source_target_pairs={{0,256},{32,288},{64,320},{96,352},{128,384},{160,416},{192,448},{... | collective-permute-start | bytes 135176 | tf_op jit(solution)/shard_map/ppermute | solution.py:411
  126.0 2.5 %own_part.1.own_ref = f32[64,768]{1,0:T(8,128)} custom-call(bf16[16,4,1920]{2,1,0:T(4,128)(2,1)} %copy-done.2, bf16[16,4,1920]{2,1,0:T(4,128)(2,1)} %copy-done.3), custom_call_target="tpu_custom_call" | custom-call | tf_op jit(solution)/shard_map/own_part/pallas_call | solution.py:279
  128.5 1.2 collective-permute-done.2
  129.7 0.8 pad_maximum_fusion
  130.5 18.0 %all_gather.19.part_ref = bf16[128,2816]{1,0:T(8,128)(2,1)S(1)} all-gather(bf16[16,2816]{1,0:T(8,128)(2,1)S(1)} %pad_maximum_fusion), channel_id=1, replica_groups={{0,32,64,96,128,160,192,224},{256,288,320,352,384,416,448,480},{1,33,65..., dimensions={0}, use_global_device_ids=true | all-gather | bytes 811008 | tf_op jit(solution)/shard_map/all_gather | solution.py:413
  148.5 0.9 copy-done
  149.4 2.7 %combine.1 = bf16[64,2560]{1,0:T(8,128)(2,1)} custom-call(bf16[128,2816]{1,0:T(8,128)(2,1)S(1)} %all_gather.19.part_ref, f32[64,768]{1,0:T(8,128)S(1)} %copy-done), custom_call_target="tpu_custom_call" | custom-call | tf_op jit(solution)/shard_map/combine/pallas_call | solution.py:337
  (10 shorter events, 0.7 us)
Async XLA Ops:
  2.4 19.0 %collective-permute-start = (bf16[4,2560]{1,0:T(4,128)(2,1)S(1)}, bf16[4,2560]{1,0:T(4,128)(2,1)S(1)}, u32[]{:S(2)}, u32[]{:S(2)}) collective-permute-start(bf16[4,2560]{1,0:T(4,128)(2,1)S(1)} %fusion.2), channel_id=1, source_target_pairs={{0,257},{1,256},{2,259},{3,258},{4,261},{5,260},{6,263},{7,262},{8... | collective-permute-start | bytes 61448 | tf_op jit(solution)/shard_map/ppermute | solution.py:384
  21.5 60.7 %all-to-all-start = ((bf16[16,32,1280]{2,1,0:T(8,128)(2,1)}), bf16[16,32,1280]{2,1,0:T(8,128)(2,1)S(1)}, u32[]{:S(2)}, u32[]{:S(2)}) async-start(bf16[16,32,1280]{2,1,0:T(8,128)(2,1)} %get-tuple-element.15), calls=%async_computation | async-start | bytes 2621440 | tf_op jit(solution)/shard_map/all_to_all | solution.py:386
  82.2 12.0 %copy-start.1 = (bf16[16,32,1280]{2,1,0:T(8,128)(2,1)}, bf16[16,32,1280]{2,1,0:T(8,128)(2,1)S(1)}, u32[]{:S(2)}) copy-start(bf16[16,32,1280]{2,1,0:T(8,128)(2,1)S(1)} %all-to-all-done.in_ref) | copy-start | bytes 3932164
  82.2 24.9 %all-to-all-start.1 = ((bf16[16,4,1920]{2,1,0:T(4,128)(2,1)}), bf16[16,4,1920]{2,1,0:T(4,128)(2,1)S(1)}, u32[]{:S(2)}, u32[]{:S(2)}) async-start(bf16[16,4,1920]{2,1,0:T(4,128)(2,1)} %pick.1), calls=%async_computation.1 | async-start | bytes 491520 | tf_op jit(solution)/shard_map/all_to_all | solution.py:404
  107.0 9.2 %copy-start.2 = (bf16[16,4,1920]{2,1,0:T(4,128)(2,1)}, bf16[16,4,1920]{2,1,0:T(4,128)(2,1)S(1)}, u32[]{:S(2)}) copy-start(bf16[16,4,1920]{2,1,0:T(4,128)(2,1)S(1)} %all-to-all-done.1.near_ref) | copy-start | bytes 737284
  107.0 9.2 %collective-permute-start.1 = (bf16[16,4,1920]{2,1,0:T(4,128)(2,1)S(1)}, bf16[16,4,1920]{2,1,0:T(4,128)(2,1)S(1)}, u32[]{:S(2)}, u32[]{:S(2)}) collective-permute-start(bf16[16,4,1920]{2,1,0:T(4,128)(2,1)S(1)} %all-to-all-done.1.near_ref), channel_id=1, source_target_pairs={{0,32},{32,0},{64,96},{96,64},{128,160},{160,128},{192,224},{224,1... | collective-permute-start | bytes 737288 | tf_op jit(solution)/shard_map/ppermute | solution.py:408
  116.2 0.7 copy-start.3
  120.8 8.9 %collective-permute-start.2 = (bf16[8,2816]{1,0:T(8,128)(2,1)}, bf16[8,2816]{1,0:T(8,128)(2,1)S(1)}, u32[]{:S(2)}, u32[]{:S(2)}) collective-permute-start(bf16[8,2816]{1,0:T(8,128)(2,1)} %attend.1), channel_id=1, source_target_pairs={{0,256},{32,288},{64,320},{96,352},{128,384},{160,416},{192,448},{... | collective-permute-start | bytes 135176 | tf_op jit(solution)/shard_map/ppermute | solution.py:411
  148.5 0.9 copy-start
